TPU v7x, 256 devices: a whole 4x4x8 slice. The times are simulated.
256 devices in a mesh: dp: 8 (over z), space: 8 (over x, core), tensor: 4 (over y).
Axes of the slice: x: 4, y: 4, z: 8, core: 2. Of those that a mesh axis runs over, the one named last changes fastest.
Arguments:
- feat_policy: bfloat16 [8, 2, 320, 32, 128], P('dp', None, 'tensor', 'space'), may hold values from -6 to 6
- feat_ref: bfloat16 [8, 2, 320, 32, 128], P('dp', None, 'tensor', 'space'), may hold values from -6 to 6
- noise: float32 [8, 2, 4, 32, 128], P('dp', None, None, 'space'), may hold values from -6 to 6
- w1_policy: bfloat16 [9, 320, 320], P(None, 'tensor'), may hold values from -0.109375 to 0.109375
- w1_ref: bfloat16 [9, 320, 320], P(None, 'tensor'), may hold values from -0.109375 to 0.109375
- b1_policy: float32 [320], P('tensor'), may hold values from -3 to 3
- b1_ref: float32 [320], P('tensor'), may hold values from -3 to 3
- gn_gain_policy: float32 [320], P('tensor'), may hold values from 0.25 to 1.75
- gn_bias_policy: float32 [320], P('tensor'), may hold values from -3 to 3
- gn_gain_ref: float32 [320], P('tensor'), may hold values from 0.25 to 1.75
- gn_bias_ref: float32 [320], P('tensor'), may hold values from -3 to 3
- w2_policy: bfloat16 [9, 4, 320], P(None, None, 'tensor'), may hold values from -0.109375 to 0.109375
- w2_ref: bfloat16 [9, 4, 320], P(None, None, 'tensor'), may hold values from -0.109375 to 0.109375
- time_table: float32 [1000, 320], P(None, 'tensor'), may hold values from -3 to 3
- timestep: int32 [8], P('dp'), may hold values from 0 to 999
- winner: int32 [8], P('dp'), may hold values from 0 to 1
Outputs:
- logits: float32 [8], P('dp')
- grad_w1: float32 [9, 320, 320], P(None, 'tensor', ('dp', 'space'))
- grad_w2: float32 [9, 4, 320], P(None, None, 'tensor')
All inputs are finite; a program needn't handle non-finite values.
Results may differ from a plain program's by a relative error of at most 0.0068.
Values may be sent and summed in bfloat16 or wider, within the bound.
No kernel may reach another device: no remote copies, remote signals or barrier semaphores. Data moves between devices by JAX's collectives and lax.ppermute only.
A program may use at most 64 MiB of HBM per device.

v0:
```python
import jax
import jax.numpy as jnp
from jax import lax
from jax.sharding import PartitionSpec as P

C = 320
GROUPS = 32


dpo_beta = 500.0
norm_eps = 1e-05


def with_halo(cells, sides, width):
    for axis, dim in sides:
        count = lax.axis_size(axis)
        ends = count - 1
        head = lax.slice_in_dim(cells, 0, width, axis=dim)
        tail = lax.slice_in_dim(cells, cells.shape[dim] - width, cells.shape[dim], axis=dim)
        cells = jnp.concatenate(
            [
                lax.ppermute(tail, axis, [(i, (i + 1) % count) for i in range(ends)]),
                cells,
                lax.ppermute(head, axis, [((i + 1) % count, i) for i in range(ends)]),
            ],
            axis=dim,
        )
    return cells


def to_kernel(weights):
    return weights.reshape(3, 3, weights.shape[1], weights.shape[2]).transpose(2, 3, 0, 1)


def flip_kernel(weights):
    shaped = weights.reshape(3, 3, weights.shape[1], weights.shape[2])[::-1, ::-1]
    return shaped.transpose(3, 2, 0, 1)


def conv_rows(inputs, kernel):
    return lax.conv_general_dilated(
        inputs,
        kernel,
        (1, 1),
        ((0, 0), (1, 1)),
        dimension_numbers=("NCHW", "OIHW", "NCHW"),
        preferred_element_type=jnp.float32,
    )


def kernel_grad(inputs, deltas):
    return lax.conv_general_dilated(
        inputs,
        deltas,
        (1, 1),
        ((0, 0), (1, 1)),
        dimension_numbers=("CNHW", "IOHW", "NCHW"),
        preferred_element_type=jnp.float32,
    )


def group_total(values, group_size):
    local_groups = values.shape[-3] // group_size
    shaped = values.reshape(values.shape[:-3] + (local_groups, group_size) + values.shape[-2:])
    return jnp.sum(shaped, axis=(-3, -2, -1))


def spread_back(stat, group_size):
    return jnp.repeat(stat, group_size, axis=-1)[..., None, None]


def body(
    feat_policy,
    feat_ref,
    noise,
    w1_policy,
    w1_ref,
    b1_policy,
    b1_ref,
    gn_gain_policy,
    gn_bias_policy,
    gn_gain_ref,
    gn_bias_ref,
    w2_policy,
    w2_ref,
    time_table,
    timestep,
    winner,
):
    pair_count = feat_policy.shape[0]
    chan_local = feat_policy.shape[2]
    row_count = feat_policy.shape[3]
    col_count = feat_policy.shape[4]
    latent_chans = noise.shape[2]
    images = 2 * pair_count
    group_size = C // GROUPS
    stacked = jnp.stack(
        [
            feat_policy.reshape(images, chan_local, row_count, col_count),
            feat_ref.reshape(images, chan_local, row_count, col_count),
        ]
    )
    stacked_ext = with_halo(stacked, (("space", 3),), 1)
    onehot = (
        timestep[:, None] == jnp.arange(time_table.shape[0], dtype=jnp.int32)[None, :]
    ).astype(jnp.float32)
    shift = jnp.repeat(jnp.dot(onehot, time_table, precision=lax.Precision.HIGHEST), 2, axis=0)
    kernel_policy = to_kernel(w1_policy)
    kernel_frozen = to_kernel(w1_ref)
    zeros = jnp.zeros((images, chan_local, row_count, col_count), jnp.float32)
    block_in = lax.all_gather(stacked_ext, "tensor", axis=2, tiled=True)
    pre_policy = zeros + conv_rows(block_in[0], kernel_policy)
    pre_frozen = zeros + conv_rows(block_in[1], kernel_frozen)
    pre_policy = pre_policy + (b1_policy[None, :] + shift)[:, :, None, None]
    pre_frozen = pre_frozen + (b1_ref[None, :] + shift)[:, :, None, None]
    pre_both = jnp.stack([pre_policy, pre_frozen])
    group_count = group_size * row_count * lax.axis_size("space") * col_count
    sum_values, sum_squares = lax.psum(
        (group_total(pre_both, group_size), group_total(pre_both * pre_both, group_size)), "space"
    )
    group_mean = sum_values / group_count
    inv_std = lax.rsqrt(sum_squares / group_count - group_mean * group_mean + norm_eps)
    centered = (pre_both - spread_back(group_mean, group_size)) * spread_back(inv_std, group_size)
    gains = jnp.stack([gn_gain_policy, gn_gain_ref])[:, None, :, None, None]
    offsets = jnp.stack([gn_bias_policy, gn_bias_ref])[:, None, :, None, None]
    normed = centered * gains + offsets
    hidden = jax.nn.silu(normed).astype(jnp.bfloat16)
    hidden_ext = with_halo(hidden, (("space", 3),), 1)
    part_policy = conv_rows(hidden_ext[0], to_kernel(w2_policy))
    part_frozen = conv_rows(hidden_ext[1], to_kernel(w2_ref))
    noise_img = noise.reshape(images, latent_chans, row_count, col_count)
    cell_total = latent_chans * row_count * lax.axis_size("space") * col_count
    share_policy, share_frozen = (
        lax.psum_scatter(part_policy, "tensor", scatter_dimension=1, tiled=True),
        lax.psum_scatter(part_frozen, "tensor", scatter_dimension=1, tiled=True),
    )
    per_share = latent_chans // lax.axis_size("tensor")
    noise_own = lax.dynamic_slice_in_dim(
        noise_img, lax.axis_index("tensor") * per_share, per_share, 1
    )
    squares = jnp.stack(
        [
            jnp.sum((share_policy - noise_own) ** 2, axis=(1, 2, 3)),
            jnp.sum((share_frozen - noise_own) ** 2, axis=(1, 2, 3)),
        ]
    )
    errors = lax.psum(squares, ("space", "tensor"))
    residual = share_policy - noise_own
    errors = (errors / cell_total).reshape(2, pair_count, 2)
    pair_sign = 1.0 - 2.0 * winner.astype(jnp.float32)
    logits = (
        -0.5
        * dpo_beta
        * pair_sign
        * (errors[0, :, 0] - errors[0, :, 1] - (errors[1, :, 0] - errors[1, :, 1]))
    )
    weight = jax.nn.sigmoid(-logits)
    scaled = (
        (dpo_beta * weight * pair_sign / cell_total)[:, None]
        * jnp.array([1.0, -1.0], jnp.float32)[None, :]
    ).reshape(images)
    dpred = (scaled[:, None, None, None] * residual).astype(jnp.bfloat16)
    dpred = lax.all_gather(dpred, "tensor", axis=1, tiled=True)
    dpred_ext = with_halo(dpred, (("space", 2),), 1)
    head_local = kernel_grad(hidden_ext[0], dpred)
    head_local = head_local.transpose(2, 3, 1, 0).reshape(9, latent_chans, chan_local)
    grad_w2 = lax.psum(head_local, ("dp", "space"))
    dhidden = conv_rows(dpred_ext, flip_kernel(w2_policy))
    normed_policy = normed[0]
    centered_policy = centered[0]
    gate_value = jax.nn.sigmoid(normed_policy)
    gnorm = (
        dhidden
        * gate_value
        * (1.0 + normed_policy * (1.0 - gate_value))
        * gn_gain_policy[None, :, None, None]
    )
    first_sum, second_sum = lax.psum(
        (group_total(gnorm, group_size), group_total(gnorm * centered_policy, group_size)), "space"
    )
    first_mean = spread_back(first_sum / group_count, group_size)
    second_mean = spread_back(second_sum / group_count, group_size)
    delta = (
        spread_back(inv_std[0], group_size) * (gnorm - first_mean - centered_policy * second_mean)
    ).astype(jnp.bfloat16)
    body_local = kernel_grad(lax.all_gather(stacked_ext[0], "tensor", axis=1, tiled=True), delta)
    body_local = body_local.transpose(2, 3, 1, 0).reshape(9, chan_local, body_local.shape[0])
    grad_w1 = lax.psum_scatter(body_local, ("dp", "space"), scatter_dimension=2, tiled=True)
    return (logits, grad_w1, grad_w2)


def solution(mesh):
    in_specs = (
        P("dp", None, "tensor", "space", None),
        P("dp", None, "tensor", "space", None),
        P("dp", None, None, "space", None),
        P(None, "tensor", None),
        P(None, "tensor", None),
        P("tensor"),
        P("tensor"),
        P("tensor"),
        P("tensor"),
        P("tensor"),
        P("tensor"),
        P(None, None, "tensor"),
        P(None, None, "tensor"),
        P(None, "tensor"),
        P("dp"),
        P("dp"),
    )
    out_specs = (P("dp"), P(None, "tensor", ("dp", "space")), P(None, None, "tensor"))
    return jax.shard_map(body, mesh=mesh, in_specs=in_specs, out_specs=out_specs, check_vma=False)
```

profile of v0, /device:TPU:1, one launch (start us, length us, event | category | flops | bytes accessed | tf_op | source)
XLA Modules:
  0.0 512.2 jit_solution(16194882127117866804)
XLA Ops:
  9.8 4.5 collective-permute-start
  16.2 3.8 collective-permute-done.1
  25.7 30.3 %all-gather.3.cloned.1.call-done = bf16[2,2,320,6,128]{4,1,3,0,2:T(2,128)(2,1)} async-done(((bf16[2,2,80,6,128]{4,1,3,0,2:T(2,128)(2,1)}), bf16[2,2,320,6,128]{4,1,3,0,2:T(2,128)(2,1)}) %all-gather.3.cloned.1.call-update) | async-done | bytes 1966096 | tf_op jit(solution)/shard_map/all_gather | solution.py:111
  56.0 3.3 slice_bitcast_fusion.1
  59.3 3.8 copy.156
  65.7 2.1 fusion.13
  68.1 2.0 copy.157
  72.6 2.1 fusion.19
  76.9 12.8 %all-reduce.4 = (f32[2,2,8]{2,1,0:T(2,128)S(1)}, f32[2,2,8]{2,1,0:T(2,128)S(1)}) all-reduce(f32[2,2,8]{2,1,0:T(2,128)S(1)} %get-tuple-element.4, f32[2,2,8]{2,1,0:T(2,128)S(1)} %get-tuple-element.3), channel_id=1, replica_groups=mesh['dp'=8,'space'=8,'tensor'=4] {'space'}, use_global_device_ids=true, to_apply=%region_3.0 | all-reduce | flops 64 | bytes 512 | tf_op jit(solution)/shard_map/psum | solution.py:118
  90.1 2.5 fusion.25
  92.8 2.7 collective-permute-start.2
  95.4 3.1 collective-permute-start.3
  98.6 12.8 %all-gather = bf16[1,2,320,6,128]{4,1,3,0,2:T(2,128)(2,1)S(1)} all-gather(bf16[1,2,80,6,128]{4,1,3,0,2:T(2,128)(2,1)S(1)} %copy-done.2), channel_id=2, replica_groups=mesh['dp'=8,'space'=8,'tensor'=4] {'tensor'}, dimensions={2}, use_global_device_ids=true | all-gather | bytes 1228800 | tf_op jit(solution)/shard_map/all_gather | solution.py:186
  114.6 4.0 convolution_select_fusion.1
  121.3 4.7 convolution_select_fusion.2
  127.3 11.8 %all-reduce.5 = (f32[2,4,4,128]{3,2,0,1:T(4,128)S(1)}, f32[2,4,4,128]{3,2,0,1:T(4,128)S(1)}) all-reduce(f32[2,4,4,128]{3,2,0,1:T(4,128)S(1)} %copy.136, f32[2,4,4,128]{3,2,0,1:T(4,128)S(1)} %copy.140), channel_id=3, replica_groups=mesh['dp'=8,'space'=8,'tensor'=4] {'tensor'}, use_global_device_ids=true, to_apply=%region_4.5.clone | all-reduce | flops 8192 | bytes 65536
  140.6 3.2 copy.141
  143.8 62.8 %psum.44 = f32[2,2]{1,0:T(2,128)S(1)} all-reduce(f32[2,2]{1,0:T(2,128)S(1)} %pad_maximum_fusion.5), channel_id=1, replica_groups=mesh['dp'=8,'space'=8,'tensor'=4] {'space','tensor'}, use_global_device_ids=true, to_apply=%region_8.9 | all-reduce | flops 4 | bytes 32 | tf_op jit(solution)/shard_map/psum | solution.py:147
  211.9 8.1 %all_gather.11 = bf16[2,4,4,128]{3,2,0,1:T(4,128)(2,1)S(1)} all-gather(bf16[2,1,4,128]{3,2,0,1:T(4,128)(2,1)S(1)} %multiply_convert_fusion.2), channel_id=1, replica_groups=mesh['dp'=8,'space'=8,'tensor'=4] {'tensor'}, dimensions={1}, use_global_device_ids=true | all-gather | bytes 10240 | tf_op jit(solution)/shard_map/all_gather | solution.py:163
  220.1 1.9 collective-permute-start.4
  222.0 8.6 %collective-permute-start.5 = (bf16[2,4,1,128]{3,2,0,1:T(2,128)(2,1)S(1)}, bf16[2,4,1,128]{3,2,0,1:T(2,128)(2,1)S(1)}, u32[]{:S(2)}, u32[]{:S(2)}) collective-permute-start(bf16[2,4,1,128]{3,2,0,1:T(2,128)(2,1)S(1)} %get-tuple-element.32), channel_id=1, source_target_pairs={{4,0},{8,4},{12,8},{16,12},{20,16},{24,20},{28,24},{5,1},{9,5},{13... | collective-permute-start | bytes 6152 | tf_op jit(solution)/shard_map/ppermute | solution.py:24
  235.4 12.3 %all-reduce.3 = (f32[2,8]{1,0:T(2,128)S(1)}, f32[2,8]{1,0:T(2,128)S(1)}) all-reduce(f32[2,8]{1,0:T(2,128)S(1)} %reduce_sum.77, f32[2,8]{1,0:T(2,128)S(1)} %reduce_sum.74), channel_id=1, replica_groups=mesh['dp'=8,'space'=8,'tensor'=4] {'space'}, use_global_device_ids=true, to_apply=%region_14.15 | all-reduce | flops 32 | bytes 256 | tf_op jit(solution)/shard_map/psum | solution.py:178
  248.0 7.1 %fusion.22 = f32[3,3,80,320]{2,3,1,0:T(8,128)} fusion(bf16[1,2,320,6,128]{2,1,4,3,0:T(2,128)(2,1)} %copy.141, f32[2,80,4,128]{1,0,3,2:T(2,128)S(1)} %get-tuple-element.15, f32[2,2,80,4,128]{2,1,4,3,0:T(2,128)S(1)} %get-tuple-element.18, f32[2,80]{1,0:T(2,128)S(1)} %mul.129, f32[2,80]{1,0:T(2,128)S(1)} %sub.65, f32[2,80]{1,0:T(2,128)S(1)} %mul.114), kind=kOutput, calls=%fused_computation.16 | convolution fusion | flops 469811200 | bytes 2956288 | tf_op jit(solution)/shard_map/transpose | solution.py:187
  259.0 243.7 %psum.47 = f32[9,4,80]{2,1,0:T(4,128)} all-reduce(f32[9,4,80]{2,1,0:T(4,128)S(1)} %bitcast.159), channel_id=1, replica_groups=mesh['dp'=8,'space'=8,'tensor'=4] {'dp','space'}, use_global_device_ids=true, to_apply=%region_16.17 | all-reduce | flops 2880 | bytes 23040 | tf_op jit(solution)/shard_map/psum | solution.py:167
  (131 shorter events, 37.7 us)
Async XLA Ops:
  7.2 58.5 %copy-start = (bf16[9,80,320]{2,1,0:T(8,128)(2,1)S(1)}, bf16[9,80,320]{2,1,0:T(8,128)(2,1)}, u32[]{:S(2)}) copy-start(bf16[9,80,320]{2,1,0:T(8,128)(2,1)} %param.20) | copy-start | bytes 1382404
  7.2 15.8 %copy-start.15 = (u32[256]{0:T(256)S(1)}, u32[256]{0:T(256)}, u32[]{:S(2)}) copy-start(u32[256]{0:T(256)} %constant.73) | copy-start | bytes 3076
  7.2 16.4 %copy-start.4 = (f32[80]{0:T(128)S(1)}, f32[80]{0:T(128)}, u32[]{:S(2)}) copy-start(f32[80]{0:T(128)} %param.24) | copy-start | bytes 964
  7.2 16.4 %copy-start.8 = (f32[80]{0:T(128)S(1)}, f32[80]{0:T(128)}, u32[]{:S(2)}) copy-start(f32[80]{0:T(128)} %param.26) | copy-start | bytes 964
  7.2 16.4 %copy-start.10 = (f32[80]{0:T(128)S(1)}, f32[80]{0:T(128)}, u32[]{:S(2)}) copy-start(f32[80]{0:T(128)} %param.25) | copy-start | bytes 964
  7.2 16.3 %copy-start.9 = (f32[80]{0:T(128)S(1)}, f32[80]{0:T(128)}, u32[]{:S(2)}) copy-start(f32[80]{0:T(128)} %param.27) | copy-start | bytes 964
  7.2 16.4 %copy-start.6 = (f32[80]{0:T(128)S(1)}, f32[80]{0:T(128)}, u32[]{:S(2)}) copy-start(f32[80]{0:T(128)} %param.22) | copy-start | bytes 964
  7.2 16.4 %copy-start.7 = (f32[80]{0:T(128)S(1)}, f32[80]{0:T(128)}, u32[]{:S(2)}) copy-start(f32[80]{0:T(128)} %param.23) | copy-start | bytes 964
  7.3 16.4 %copy-start.3 = (f32[1000,80]{0,1:T(8,128)S(1)}, f32[1000,80]{0,1:T(8,128)}, u32[]{:S(2)}) copy-start(f32[1000,80]{0,1:T(8,128)} %param.30) | copy-start | bytes 960004
  7.3 48.7 %all-gather.3.cloned.1.call-start = ((), (), s32[]{:S(2)}) async-start(), calls=%async_computation | async-start | bytes 2457600 | tf_op jit(solution)/shard_map/all_gather | solution.py:111
  9.8 6.4 %collective-permute-start = (bf16[2,2,80,1,128]{4,1,3,0,2:T(2,128)(2,1)S(1)}, bf16[2,2,80,1,128]{4,1,3,0,2:T(2,128)(2,1)S(1)}, u32[]{:S(2)}, u32[]{:S(2)}) collective-permute-start(bf16[2,2,80,1,128]{4,1,3,0,2:T(2,128)(2,1)S(1)} %get-tuple-element.29), channel_id=1, source_target_pairs={{0,4},{4,8},{8,12},{12,16},{16,20},{20,24},{24,28},{1,5},{5,9},{9,... | collective-permute-start | bytes 245768 | tf_op jit(solution)/shard_map/ppermute | solution.py:22
  14.3 5.8 %collective-permute-start.1 = (bf16[2,2,80,1,128]{4,1,3,0,2:T(2,128)(2,1)S(1)}, bf16[2,2,80,1,128]{4,1,3,0,2:T(2,128)(2,1)S(1)}, u32[]{:S(2)}, u32[]{:S(2)}) collective-permute-start(bf16[2,2,80,1,128]{4,1,3,0,2:T(2,128)(2,1)S(1)} %get-tuple-element.30), channel_id=1, source_target_pairs={{4,0},{8,4},{12,8},{16,12},{20,16},{24,20},{28,24},{5,1},{9,5},{13... | collective-permute-start | bytes 245768 | tf_op jit(solution)/shard_map/ppermute | solution.py:24
  21.6 481.1 %all-reduce.8.cloned.1.call-start = ((), (), s32[]{:S(2)}) async-start(), calls=%async_computation.1 | async-start | bytes 2949120
  64.3 1.4 copy-start.16
  71.2 1.4 copy-start.11
  90.1 8.5 %copy-start.2 = (bf16[1,2,80,6,128]{4,1,3,0,2:T(2,128)(2,1)S(1)}, bf16[1,2,80,6,128]{4,1,3,0,2:T(2,128)(2,1)}, u32[]{:S(2)}) copy-start(bf16[1,2,80,6,128]{4,1,3,0,2:T(2,128)(2,1)} %slice.99) | copy-start | bytes 737284
  92.8 18.6 %collective-permute-start.2 = (bf16[2,2,80,1,128]{2,1,4,3,0:T(2,128)(2,1)S(1)}, bf16[2,2,80,1,128]{2,1,4,3,0:T(2,128)(2,1)S(1)}, u32[]{:S(2)}, u32[]{:S(2)}) collective-permute-start(bf16[2,2,80,1,128]{2,1,4,3,0:T(2,128)(2,1)S(1)} %get-tuple-element.23), channel_id=1, source_target_pairs={{0,4},{4,8},{8,12},{12,16},{16,20},{20,24},{24,28},{1,5},{5,9},{9,... | collective-permute-start | bytes 245768 | tf_op jit(solution)/shard_map/ppermute | solution.py:22
  95.4 16.0 %collective-permute-start.3 = (bf16[2,2,80,1,128]{2,1,4,3,0:T(2,128)(2,1)S(1)}, bf16[2,2,80,1,128]{2,1,4,3,0:T(2,128)(2,1)S(1)}, u32[]{:S(2)}, u32[]{:S(2)}) collective-permute-start(bf16[2,2,80,1,128]{2,1,4,3,0:T(2,128)(2,1)S(1)} %get-tuple-element.24), channel_id=1, source_target_pairs={{4,0},{8,4},{12,8},{16,12},{20,16},{24,20},{28,24},{5,1},{9,5},{13... | collective-permute-start | bytes 245768 | tf_op jit(solution)/shard_map/ppermute | solution.py:24
  112.8 1.8 copy-start.12
  140.5 91.5 %copy-start.13 = (bf16[9,4,80]{2,1,0:T(4,128)(2,1)S(1)}, bf16[9,4,80]{2,1,0:T(4,128)(2,1)}, u32[]{:S(2)}) copy-start(bf16[9,4,80]{2,1,0:T(4,128)(2,1)} %param.28) | copy-start | bytes 17284
  140.5 91.5 %copy-start.17 = (pred[16,17]{0,1:T(8,128)(4,1)S(1)}, pred[16,17]{0,1:T(8,128)(4,1)}, u32[]{:S(2)}) copy-start(pred[16,17]{0,1:T(8,128)(4,1)} %constant.66) | copy-start | bytes 820
  220.1 10.7 %collective-permute-start.4 = (bf16[2,4,1,128]{3,2,0,1:T(2,128)(2,1)S(1)}, bf16[2,4,1,128]{3,2,0,1:T(2,128)(2,1)S(1)}, u32[]{:S(2)}, u32[]{:S(2)}) collective-permute-start(bf16[2,4,1,128]{3,2,0,1:T(2,128)(2,1)S(1)} %get-tuple-element.31), channel_id=1, source_target_pairs={{0,4},{4,8},{8,12},{12,16},{16,20},{20,24},{24,28},{1,5},{5,9},{9,... | collective-permute-start | bytes 6152 | tf_op jit(solution)/shard_map/ppermute | solution.py:22
  222.0 9.4 %collective-permute-start.5 = (bf16[2,4,1,128]{3,2,0,1:T(2,128)(2,1)S(1)}, bf16[2,4,1,128]{3,2,0,1:T(2,128)(2,1)S(1)}, u32[]{:S(2)}, u32[]{:S(2)}) collective-permute-start(bf16[2,4,1,128]{3,2,0,1:T(2,128)(2,1)S(1)} %get-tuple-element.32), channel_id=1, source_target_pairs={{4,0},{8,4},{12,8},{16,12},{20,16},{24,20},{28,24},{5,1},{9,5},{13... | collective-permute-start | bytes 6152 | tf_op jit(solution)/shard_map/ppermute | solution.py:24
  232.4 1.2 copy-start.1
  (2 other events, 1.9 us)
Sparse Core Ops, SparseCore 0:
  21.7 34.2 all-gather.2
  255.3 186.4 all-reduce.7
where the time goes:
time: 518 us; the launch traced here: 512 us
  blocking collectives  364 us (70%)
  waiting for transfers between devices  34.8 us (7%)
  local copies, waits for them, and re-layouts  33.8 us (7%)
  starting transfers between devices  22.8 us (4%)
  matrix products  22.3 us (4%)
  between operations  20.4 us (4%)
  other arithmetic  13.8 us (3%)
    psum x1, blocking collectives, body(): grad_w2 = lax.psum(head_local, ('dp', 'space'))  244 us
    psum x1, blocking collectives, body(): errors = lax.psum(squares, ('space', 'tensor'))  62.8 us
    all_gather x1, waiting for transfers between devices, body(): block_in = lax.all_gather(stacked_ext, 'tensor', axis=2, tiled=True)  30.3 us
    ppermute x3, starting transfers between devices, with_halo(): lax.ppermute(head, axis, [((i + 1) % count, i) for i in range(ends)])  13.6 us
    conv_general_dilated x5, matrix products, conv_rows(): lax.conv_general_dilated(inputs, kernel, (1, 1), ((0, 0), (1, 1)), dimens...  13.3 us
    psum x1, blocking collectives, body(): lax.psum((group_total(pre_both, group_size), group_total(pre_both * pre_b...  12.8 us
    all_gather x1, blocking collectives, body(): lax.all_gather(stacked_ext[0], 'tensor', axis=1, tiled=True)  12.8 us
    psum x1, blocking collectives, body(): lax.psum((group_total(gnorm, group_size), group_total(gnorm * centered_po...  12.3 us
  transfers between devices with their start and end apart: 8, of which 3 were waited for; matrix products, arithmetic and copies ran while one was open for 1% of the time, Pallas kernels for 0%

commit v1 on v0

v1 whole, which is shorter than its diff:
```python
import functools

import jax
import jax.numpy as jnp
from jax import lax
from jax.experimental import pallas as pl
from jax.experimental.pallas import tpu as pltpu
from jax.sharding import PartitionSpec as P

C = 320
GROUPS = 32
BETA = 500.0
EPS = 1e-05
CH = 80
ROWS = 4
COLS = 128
PIX = ROWS * COLS
GSIZE = C // GROUPS
LOCAL_GROUPS = CH // GSIZE
COUNT = float(GSIZE * 32 * 128)
CELLS = float(4 * 32 * 128)
F32 = jnp.float32
BF16 = jnp.bfloat16
HIGHEST = lax.Precision.HIGHEST

VM = pl.BlockSpec(memory_space=pltpu.VMEM)
SM = pl.BlockSpec(memory_space=pltpu.SMEM)


def call(kernel, ins, outs, name, flops, smem=0, scratch=()):
    in_bytes = sum(a.size * a.dtype.itemsize for a in ins)
    out_bytes = sum(s.size * s.dtype.itemsize for s in outs)
    return pl.pallas_call(
        kernel,
        out_shape=outs,
        in_specs=[SM] * smem + [VM] * (len(ins) - smem),
        out_specs=[VM] * len(outs),
        scratch_shapes=list(scratch),
        name=name,
        cost_estimate=pl.CostEstimate(
            flops=flops, bytes_accessed=in_bytes + out_bytes, transcendentals=0
        ),
        compiler_params=pltpu.CompilerParams(vmem_limit_bytes=40 * 1024 * 1024),
    )(*ins)


def arr(shape, dtype):
    return jax.ShapeDtypeStruct(shape, dtype)


def dot(a, b):
    return lax.dot_general(a, b, (((1,), (0,)), ((), ())), preferred_element_type=F32)


def dot_nt(a, b):
    return lax.dot_general(a, b, (((1,), (1,)), ((), ())), preferred_element_type=F32)


def exact_dot(a, b):
    return lax.dot_general(
        a, b, (((1,), (0,)), ((), ())), preferred_element_type=F32, precision=HIGHEST
    )


def from_left(tile):
    lane = lax.broadcasted_iota(jnp.int32, tile.shape, tile.ndim - 1)
    return jnp.where(lane == 0, 0.0, pltpu.roll(tile, 1, tile.ndim - 1))


def from_right(tile):
    lane = lax.broadcasted_iota(jnp.int32, tile.shape, tile.ndim - 1)
    return jnp.where(lane == COLS - 1, 0.0, pltpu.roll(tile, COLS - 1, tile.ndim - 1))


def row_of(tile, r):
    return tile[:, r * COLS : (r + 1) * COLS]


def members():
    group = lax.broadcasted_iota(jnp.int32, (2 * LOCAL_GROUPS, 2 * CH), 0)
    chan = lax.broadcasted_iota(jnp.int32, (2 * LOCAL_GROUPS, 2 * CH), 1)
    low = group * GSIZE
    return jnp.where((chan >= low) & (chan < low + GSIZE), 1.0, 0.0).astype(F32)


def spread(stat):
    chan = lax.broadcasted_iota(jnp.int32, (2 * CH, 2 * LOCAL_GROUPS), 0)
    group = lax.broadcasted_iota(jnp.int32, (2 * CH, 2 * LOCAL_GROUPS), 1)
    low = group * GSIZE
    pick = jnp.where((chan >= low) & (chan < low + GSIZE), 1.0, 0.0).astype(F32)
    return exact_dot(pick, stat)


def in_lanes(columns):
    rows = columns[0].shape[0]
    lane = lax.broadcasted_iota(jnp.int32, (rows, COLS), 1)
    out = jnp.zeros((rows, COLS), F32)
    for index, column in enumerate(columns):
        out = jnp.where(lane == index, column, out)
    return out


def conv_kernel(halo, t_ref, f0, f1, f2, f3, w_ref, bias_ref, pre_ref, up_ref, dn_ref, fs_ref, *ends):
    t = t_ref[0]
    for k, f in enumerate((f0, f1, f2, f3)):
        owner = lax.rem(t - k + 4, 4)
        base = pl.multiple_of(owner * CH, 16)
        for im in range(2):
            for r in range(ROWS):
                lo = im * PIX + r * COLS
                fs_ref[pl.ds(base, CH), lo : lo + COLS] = f[im, r]
    for im in range(2):
        feats = fs_ref[:, im * PIX : (im + 1) * PIX]
        taps = [dot(w_ref[ky * 3 * CH : (ky + 1) * 3 * CH, :], feats) for ky in range(3)]
        for r in range(-1, ROWS + 1):
            total = None
            for ky in range(3):
                src = r + ky - 1
                if 0 <= src < ROWS:
                    term = row_of(taps[ky], src)
                    total = term if total is None else total + term
            out = (
                total[CH : 2 * CH]
                + from_left(total[0:CH])
                + from_right(total[2 * CH : 3 * CH])
            )
            if r == -1:
                up_ref[im * CH : (im + 1) * CH, :] = out
            elif r == ROWS:
                dn_ref[im * CH : (im + 1) * CH, :] = out
            else:
                pre_ref[im * CH : (im + 1) * CH, r * COLS : (r + 1) * COLS] = (
                    out + bias_ref[im * CH : (im + 1) * CH, :]
                )
    if halo:
        for im in range(2):
            lanes = slice(im * COLS, (im + 1) * COLS)
            ends[0][:, lanes] = fs_ref[:, im * PIX : im * PIX + COLS]
            ends[1][:, lanes] = fs_ref[:, im * PIX + (ROWS - 1) * COLS : (im + 1) * PIX]


def stat_kernel(pre_p, left_p, right_p, pre_r, left_r, right_r, full_p, full_r, out_ref):
    columns = []
    for pre, left, right, full in (
        (pre_p, left_p, right_p, full_p),
        (pre_r, left_r, right_r, full_r),
    ):
        rows = [pre[:, r * COLS : (r + 1) * COLS] for r in range(ROWS)]
        rows[0] = rows[0] + left[...]
        rows[ROWS - 1] = rows[ROWS - 1] + right[...]
        total = rows[0] + rows[1] + rows[2] + rows[3]
        square = (
            rows[0] * rows[0] + rows[1] * rows[1] + rows[2] * rows[2] + rows[3] * rows[3]
        )
        for r in range(ROWS):
            full[:, r * COLS : (r + 1) * COLS] = rows[r]
        columns.append(jnp.sum(total, axis=1, keepdims=True))
        columns.append(jnp.sum(square, axis=1, keepdims=True))
    sums = exact_dot(members(), in_lanes(columns))
    for peer in range(out_ref.shape[0]):
        out_ref[peer] = sums


def moments(total):
    wide = spread(total / COUNT)
    result = []
    for m in range(2):
        mean = wide[:, 2 * m : 2 * m + 1]
        square = wide[:, 2 * m + 1 : 2 * m + 2]
        result.append((mean, lax.rsqrt(square - mean * mean + EPS)))
    return result


def hidden_kernel(full_p, full_r, sums_ref, col_ref, lift_ref, part_ref, hid_ref, stat_ref):
    stats = moments(jnp.sum(sums_ref[...], axis=0))
    stat_ref[...] = in_lanes([stats[0][0], stats[0][1]])
    for m, full in enumerate((full_p, full_r)):
        mean, inv = stats[m]
        gain = col_ref[:, 2 * m : 2 * m + 1]
        shift = col_ref[:, 2 * m + 1 : 2 * m + 2]
        normed = ((full[...] - mean) * inv) * gain + shift
        hidden = (normed * jax.nn.sigmoid(normed)).astype(BF16)
        if m == 0:
            hid_ref[...] = hidden
        taps = dot(lift_ref[m], hidden)
        for r in range(-1, ROWS + 1):
            totals = [None, None, None]
            for kx in range(3):
                for ky in range(3):
                    src = r + ky - 1
                    if 0 <= src < ROWS:
                        tap = 3 * ky + kx
                        term = taps[8 * tap : 8 * tap + 8, src * COLS : (src + 1) * COLS]
                        totals[kx] = term if totals[kx] is None else totals[kx] + term
            part_ref[m, r + 1] = totals[1] + from_left(totals[0]) + from_right(totals[2])


def pred_kernel(p0, p1, p2, p3, noise_ref, own_ref, left_ref, right_ref):
    for m in range(2):
        rows = []
        for r in range(ROWS + 2):
            total = p0[m, r] + p1[m, r] + p2[m, r] + p3[m, r]
            if 1 <= r <= ROWS:
                total = total - noise_ref[r - 1]
            own_ref[m, r] = total
            rows.append(total)
        left_ref[m, 0] = rows[0]
        left_ref[m, 1] = rows[1]
        right_ref[m, 0] = rows[ROWS]
        right_ref[m, 1] = rows[ROWS + 1]


def back_kernel(
    edge_ref, own, left, right, full_p, stat_ref, col_ref, hid_ref, drop_ref, gnorm_ref, out_ref
):
    top = edge_ref[0]
    bottom = edge_ref[1]
    residual = []
    errors = []
    for m in range(2):
        rows = [own[m, r] for r in range(ROWS + 2)]
        rows[0] = rows[0] + left[m, 0]
        rows[1] = rows[1] + left[m, 1]
        rows[ROWS] = rows[ROWS] + right[m, 0]
        rows[ROWS + 1] = rows[ROWS + 1] + right[m, 1]
        square = rows[1] * rows[1]
        for r in range(2, ROWS + 1):
            square = square + rows[r] * rows[r]
        errors.append(jnp.sum(square, axis=1, keepdims=True))
        if m == 0:
            rows[0] = jnp.where(top > 0, 0.0, rows[0])
            rows[ROWS + 1] = jnp.where(bottom > 0, 0.0, rows[ROWS + 1])
            residual = rows
    image = lax.broadcasted_iota(jnp.int32, (8, COLS), 0)
    residual = [jnp.where(image < 4, row, -row) for row in residual]
    moved = [
        [from_right(row) for row in residual],
        residual,
        [from_left(row) for row in residual],
    ]
    blocks = []
    for ky in range(3):
        for kx in range(3):
            blocks.append(
                jnp.concatenate([moved[kx][r + 2 - ky] for r in range(ROWS)], axis=1)
            )
    cot = jnp.concatenate(blocks, axis=0).astype(BF16)
    dhidden = dot(drop_ref[...], cot)
    mean = stat_ref[:, 0:1]
    inv = stat_ref[:, 1:2]
    gain = col_ref[:, 0:1]
    shift = col_ref[:, 1:2]
    centered = (full_p[...] - mean) * inv
    normed = centered * gain + shift
    gate = jax.nn.sigmoid(normed)
    gnorm = dhidden * gate * (1.0 + normed * (1.0 - gate)) * gain
    gnorm_ref[...] = gnorm
    first = jnp.sum(gnorm, axis=1, keepdims=True)
    second = jnp.sum(gnorm * centered, axis=1, keepdims=True)
    sums = exact_dot(members(), in_lanes([first, second]))
    grads = [dot_nt(cot, hid_ref[im * CH : (im + 1) * CH, :]) for im in range(2)]
    error = in_lanes(errors)
    pad = jnp.zeros((4, COLS - CH), F32)
    heads = []
    for tap in range(9):
        head = grads[0][8 * tap : 8 * tap + 4] + grads[1][8 * tap + 4 : 8 * tap + 8]
        heads.append(jnp.concatenate([head, pad], axis=1))
    for peer in range(out_ref.shape[0]):
        out_ref[peer, 0:16, :] = sums
        out_ref[peer, 16:24, :] = error
        out_ref[peer, 24:28, :] = heads[peer]
        out_ref[peer, 28:32, :] = heads[8]


def weight_kernel(
    win_ref, gnorm_ref, full_p, stat_ref, red_ref, fs_ref, above_ref, below_ref,
    out_ref, logit_ref, grad_ref, pack_ref
):
    total = jnp.sum(red_ref[...], axis=0)
    row = lax.broadcasted_iota(jnp.int32, (8, COLS), 0)
    signed = jnp.where(row < 4, total[16:24], -total[16:24])
    gaps = jnp.sum(signed, axis=0, keepdims=True)
    gap = (gaps[:, 0:1] - gaps[:, 1:2]) * (1.0 / CELLS)
    sign = 1.0 - 2.0 * win_ref[0].astype(F32)
    logit = (-0.5 * BETA) * sign * gap
    logit_ref[...] = logit
    scale = (BETA / CELLS) * sign * jax.nn.sigmoid(-logit)
    wide = spread(total[0:16] / COUNT)
    mean = stat_ref[:, 0:1]
    inv = stat_ref[:, 1:2]
    centered = (full_p[...] - mean) * inv
    delta = inv * (gnorm_ref[...] - wide[:, 0:1] - centered * wide[:, 1:2])
    shifted = [[], [], []]
    for im in range(2):
        for r in range(ROWS):
            part = delta[im * CH : (im + 1) * CH, r * COLS : (r + 1) * COLS]
            shifted[0].append(from_right(part))
            shifted[1].append(part)
            shifted[2].append(from_left(part))
    stack = jnp.concatenate(
        [jnp.concatenate(parts, axis=1).astype(BF16) for parts in shifted]
        + [jnp.zeros((16, 2 * PIX), BF16)],
        axis=0,
    )
    for ky in range(3):
        pieces = []
        for im in range(2):
            lanes = slice(im * COLS, (im + 1) * COLS)
            if ky == 0:
                pieces.append(above_ref[:, lanes])
                pieces.append(fs_ref[:, im * PIX : im * PIX + 3 * COLS])
            elif ky == 1:
                pieces.append(fs_ref[:, im * PIX : (im + 1) * PIX])
            else:
                pieces.append(fs_ref[:, im * PIX + COLS : (im + 1) * PIX])
                pieces.append(below_ref[:, lanes])
        feats = jnp.concatenate(pieces, axis=1)
        grad = dot_nt(feats, stack) * scale
        grad_ref[2 * ky] = grad[:, 0:COLS]
        grad_ref[2 * ky + 1] = grad[:, COLS : 2 * COLS]
    peers = out_ref.shape[0]
    chunk = C // peers
    rows = out_ref.shape[1]
    for ii in range(chunk):
        for half in range(6):
            pack_ref[pl.ds(half * chunk + ii, peers, stride=rows), :] = grad_ref[
                half, pl.ds(ii, peers, stride=chunk), :
            ]
    head = total[24:32] * scale
    for peer in range(peers):
        tile = pack_ref[peer * rows : peer * rows + 32, :]
        keep = lax.broadcasted_iota(jnp.int32, (32, COLS), 0) < 6 * chunk
        out_ref[peer, 0:32, :] = jnp.where(keep, tile, 0.0).astype(BF16)
        out_ref[peer, 32:40, :] = head.astype(BF16)


def sum_kernel(space, got_ref, one_ref, two_ref):
    peers = got_ref.shape[0]
    chunk = C // peers
    per_space = []
    for s in range(space):
        total = got_ref[s].astype(F32)
        for d in range(1, peers // space):
            total = total + got_ref[d * space + s].astype(F32)
        per_space.append(total)
        two_ref[s] = total[32:36, 0:CH]
        if s == 0:
            two_ref[8] = total[36:40, 0:CH]
    total = per_space[0]
    for s in range(1, space):
        total = total + per_space[s]
    for ky in range(3):
        lo = 2 * ky * chunk
        wide = jnp.concatenate(
            [total[lo : lo + chunk], total[lo + chunk : lo + 2 * chunk]], axis=1
        )
        for kx in range(3):
            one_ref[3 * ky + kx] = wide[:, kx * CH : (kx + 1) * CH]


def ring(axis, step):
    count = lax.axis_size(axis)
    return [(i, (i + step) % count) for i in range(count)]


def line(axis, step):
    count = lax.axis_size(axis)
    return [(i, i + step) for i in range(count) if 0 <= i + step < count]


def body(
    feat_policy,
    feat_ref,
    noise,
    w1_policy,
    w1_ref,
    b1_policy,
    b1_ref,
    gn_gain_policy,
    gn_bias_policy,
    gn_gain_ref,
    gn_bias_ref,
    w2_policy,
    w2_ref,
    time_table,
    timestep,
    winner,
):
    space = lax.axis_size("space")
    peers = lax.axis_size("dp") * space
    t_index = lax.axis_index("tensor").astype(jnp.int32).reshape(1)
    s_index = lax.axis_index("space")
    edges = jnp.stack([s_index == 0, s_index == space - 1]).astype(jnp.int32)

    def gather(feat):
        own = feat[0].transpose(0, 2, 1, 3)
        return [own] + [lax.ppermute(own, "tensor", ring("tensor", k)) for k in (1, 2, 3)]

    parts_p = gather(feat_policy)
    parts_r = gather(feat_ref)

    shift = lax.dynamic_slice_in_dim(time_table, timestep[0], 1, 0)[0]

    def twice(vec):
        return jnp.concatenate([vec, vec])

    bias_p = twice(b1_policy + shift)[:, None]
    bias_r = twice(b1_ref + shift)[:, None]
    columns = jnp.stack(
        [twice(gn_gain_policy), twice(gn_bias_policy), twice(gn_gain_ref), twice(gn_bias_ref)],
        axis=1,
    )

    def lifted(w2):
        zero = jnp.zeros((9, 4, CH), w2.dtype)
        first = jnp.concatenate([w2, zero], axis=1).reshape(72, CH)
        second = jnp.concatenate([zero, w2], axis=1).reshape(72, CH)
        return jnp.concatenate([first, second], axis=1)

    lift = jnp.stack([lifted(w2_policy), lifted(w2_ref)])
    drop = lift[0].T
    noise_rows = noise[0].transpose(2, 0, 1, 3).reshape(ROWS, 8, COLS)

    conv_flops = 2 * 9 * C * CH * 2 * PIX

    def conv(parts, w1, bias, halo, name):
        outs = [
            arr((2 * CH, PIX), F32),
            arr((2 * CH, COLS), F32),
            arr((2 * CH, COLS), F32),
            arr((C, 2 * PIX), BF16),
        ]
        if halo:
            outs += [arr((C, 2 * COLS), BF16)] * 2
        return call(
            functools.partial(conv_kernel, halo),
            [t_index, *parts, w1.reshape(9 * CH, C), bias],
            outs,
            name,
            conv_flops,
            smem=1,
        )

    pre_p, up_p, dn_p, feats, first_row, last_row = conv(parts_p, w1_policy, bias_p, True, "conv_p")
    right_p = lax.ppermute(up_p, "space", line("space", -1))
    left_p = lax.ppermute(dn_p, "space", line("space", 1))
    pre_r, up_r, dn_r, _ = conv(parts_r, w1_ref, bias_r, False, "conv_r")
    right_r = lax.ppermute(up_r, "space", line("space", -1))
    left_r = lax.ppermute(dn_r, "space", line("space", 1))
    below = lax.ppermute(first_row, "space", line("space", -1))
    above = lax.ppermute(last_row, "space", line("space", 1))

    full_p, full_r, sums = call(
        stat_kernel,
        [pre_p, left_p, right_p, pre_r, left_r, right_r],
        [arr((2 * CH, PIX), F32), arr((2 * CH, PIX), F32), arr((space, 16, COLS), F32)],
        "stats",
        10**6,
    )
    sums = lax.all_to_all(sums, "space", 0, 0, tiled=True)
    part, hidden, stat = call(
        hidden_kernel,
        [full_p, full_r, sums, columns, lift],
        [arr((2, ROWS + 2, 8, COLS), F32), arr((2 * CH, PIX), BF16), arr((2 * CH, COLS), F32)],
        "hidden",
        10**7,
    )
    others = [lax.ppermute(part, "tensor", ring("tensor", k)) for k in (1, 2, 3)]
    own, to_left, to_right = call(
        pred_kernel,
        [part, *others, noise_rows],
        [arr((2, ROWS + 2, 8, COLS), F32), arr((2, 2, 8, COLS), F32), arr((2, 2, 8, COLS), F32)],
        "pred",
        10**5,
    )
    from_l = lax.ppermute(to_right, "space", line("space", 1))
    from_r = lax.ppermute(to_left, "space", line("space", -1))
    gnorm, partial = call(
        back_kernel,
        [edges, own, from_l, from_r, full_p, stat, columns, hidden, drop],
        [arr((2 * CH, PIX), F32), arr((space, 32, COLS), F32)],
        "back",
        10**7,
        smem=1,
    )
    partial = lax.all_to_all(partial, "space", 0, 0, tiled=True)
    packed, logits = call(
        weight_kernel,
        [winner, gnorm, full_p, stat, partial, feats, above, below],
        [arr((peers, 40, COLS), BF16), arr((1, 1), F32)],
        "weight",
        conv_flops,
        smem=1,
        scratch=[pltpu.VMEM((6, C, COLS), F32), pltpu.VMEM((peers * 40, COLS), F32)],
    )
    got = lax.all_to_all(packed, ("dp", "space"), 0, 0, tiled=True)
    grad_one, grad_two = call(
        functools.partial(sum_kernel, space),
        [got],
        [arr((9, C // peers, CH), F32), arr((9, 4, CH), F32)],
        "total",
        10**6,
    )
    return (logits.reshape(1), grad_one.transpose(0, 2, 1), grad_two)


def solution(mesh):
    in_specs = (
        P("dp", None, "tensor", "space", None),
        P("dp", None, "tensor", "space", None),
        P("dp", None, None, "space", None),
        P(None, "tensor", None),
        P(None, "tensor", None),
        P("tensor"),
        P("tensor"),
        P("tensor"),
        P("tensor"),
        P("tensor"),
        P("tensor"),
        P(None, None, "tensor"),
        P(None, None, "tensor"),
        P(None, "tensor"),
        P("dp"),
        P("dp"),
    )
    out_specs = (P("dp"), P(None, "tensor", ("dp", "space")), P(None, None, "tensor"))
    return jax.shard_map(body, mesh=mesh, in_specs=in_specs, out_specs=out_specs, check_vma=False)
```

time: 518 us -> 108 us (0.21); the launches traced: 512 us -> 107 us
  blocking collectives: 364 us -> 30.6 us
  local copies, waits for them, and re-layouts: 33.8 us -> 3.19 us
  matrix products: 22.3 us -> 0 us
  starting transfers between devices: 22.8 us -> 40.9 us
  between operations: 20.4 us -> 2.36 us
  waiting for transfers between devices: 34.8 us -> 20.7 us
  other arithmetic: 13.8 us -> 0.52 us
  Pallas kernels: 0 us -> 9.17 us
    psum x4 -> x0, blocking collectives: 332 us -> none  [the longest x1 244 us: body(): grad_w2 = lax.psum(head_local, ('dp', 'space'))]
    all_to_all x0 -> x1, blocking collectives: none -> 30.6 us  [body(): got = lax.all_to_all(packed, ('dp', 'space'), 0, 0, tiled=True)]
    all_gather x1 -> x0, waiting for transfers between devices: 30.3 us -> none  [body(): block_in = lax.all_gather(stacked_ext, 'tensor', axis=2, tiled=True)]
    all_gather x2 -> x0, blocking collectives: 20.9 us -> none  [the longest x1 12.8 us: body(): lax.all_gather(stacked_ext[0], 'tensor', axis=1, tiled=True)]
    conv_general_dilated x5 -> x0, matrix products: 13.3 us -> none  [conv_rows(): lax.conv_general_dilated(inputs, kernel, (1, 1), ((0, 0), (1, 1)), dimens...]
    unnamed x1 -> x0, blocking collectives: 11.8 us -> none
    ppermute x6 -> x17, starting transfers between devices: 22.7 us -> 33.3 us  [the longest x6 8.23 us: gather(): lax.ppermute(own, 'tensor', ring('tensor', k))]
    all_to_all x0 -> x2, waiting for transfers between devices: none -> 9.29 us  [the longest x1 4.72 us: body(): sums = lax.all_to_all(sums, 'space', 0, 0, tiled=True)]
  transfers between devices with their start and end apart: 8 -> 19, of which waited for: 3 -> 5; matrix products, arithmetic and copies ran while one was open for 1% -> 1% of each run, Pallas kernels for 0% -> 5%
where the time goes in v1:
time: 108 us; the launch traced here: 107 us
  starting transfers between devices  40.9 us (38%)
  blocking collectives  30.6 us (28%)
  waiting for transfers between devices  20.7 us (19%)
  Pallas kernels  9.17 us (8%)
  local copies, waits for them, and re-layouts  3.19 us (3%)
  between operations  2.36 us (2%)
    all_to_all x1, blocking collectives, body(): got = lax.all_to_all(packed, ('dp', 'space'), 0, 0, tiled=True)  30.6 us
    pallas_call x8, Pallas kernels, call(): pl.pallas_call(kernel, out_shape=outs, in_specs=[SM] * smem + [VM] * (len...  9.17 us
    ppermute x6, starting transfers between devices, gather(): lax.ppermute(own, 'tensor', ring('tensor', k))  8.23 us
    all_to_all x1, waiting for transfers between devices, body(): sums = lax.all_to_all(sums, 'space', 0, 0, tiled=True)  4.72 us
    all_to_all x1, waiting for transfers between devices, body(): partial = lax.all_to_all(partial, 'space', 0, 0, tiled=True)  4.57 us
    ppermute x6, waiting for transfers between devices, gather(): lax.ppermute(own, 'tensor', ring('tensor', k))  4.56 us
    ppermute x1, starting transfers between devices, body(): left_r = lax.ppermute(dn_r, 'space', line('space', 1))  4.46 us
    all_to_all x1, starting transfers between devices, body(): sums = lax.all_to_all(sums, 'space', 0, 0, tiled=True)  4.11 us
  transfers between devices with their start and end apart: 19, of which 5 were waited for; matrix products, arithmetic and copies ran while one was open for 1% of the time, Pallas kernels for 5%

profile of v1, /device:TPU:1, one launch (start us, length us, event | category | flops | bytes accessed | tf_op | source)
XLA Modules:
  0.0 107.4 jit_solution(15812720402664271593)
XLA Ops:
  1.7 3.6 %collective-permute-start.7 = (bf16[2,4,80,128]{3,2,1,0:T(8,128)(2,1)S(1)}, bf16[2,4,80,128]{3,2,1,0:T(8,128)(2,1)S(1)}, u32[]{:S(2)}, u32[]{:S(2)}) collective-permute-start(bf16[2,4,80,128]{3,2,1,0:T(8,128)(2,1)S(1)} %bitcast.49), channel_id=1, source_target_pairs={{0,3},{1,0},{2,1},{3,2},{4,7},{5,4},{6,5},{7,6},{8,11},{9,8},{10,9... | collective-permute-start | bytes 491528 | tf_op jit(solution)/shard_map/ppermute | solution.py:397
  6.4 2.1 %collective-permute-start.2 = (bf16[2,4,80,128]{3,2,1,0:T(8,128)(2,1)S(1)}, bf16[2,4,80,128]{3,2,1,0:T(8,128)(2,1)S(1)}, u32[]{:S(2)}, u32[]{:S(2)}) collective-permute-start(bf16[2,4,80,128]{3,2,1,0:T(8,128)(2,1)S(1)} %bitcast.45), channel_id=1, source_target_pairs={{0,3},{1,0},{2,1},{3,2},{4,7},{5,4},{6,5},{7,6},{8,11},{9,8},{10,9... | collective-permute-start | bytes 491528 | tf_op jit(solution)/shard_map/ppermute | solution.py:397
  8.5 1.4 %collective-permute-start.1 = (bf16[2,4,80,128]{3,2,1,0:T(8,128)(2,1)S(1)}, bf16[2,4,80,128]{3,2,1,0:T(8,128)(2,1)S(1)}, u32[]{:S(2)}, u32[]{:S(2)}) collective-permute-start(bf16[2,4,80,128]{3,2,1,0:T(8,128)(2,1)S(1)} %bitcast.46), channel_id=1, source_target_pairs={{0,2},{1,3},{2,0},{3,1},{4,6},{5,7},{6,4},{7,5},{8,10},{9,11},{10,... | collective-permute-start | bytes 491528 | tf_op jit(solution)/shard_map/ppermute | solution.py:397
  13.1 4.5 %collective-permute-done.5.f1 = bf16[2,4,80,128]{3,2,1,0:T(8,128)(2,1)S(1)} collective-permute-done((bf16[2,4,80,128]{3,2,1,0:T(8,128)(2,1)S(1)}, bf16[2,4,80,128]{3,2,1,0:T(8,128)(2,1)S(1)}, u32[]{:S(2)}, u32[]{:S(2)}) %collective-permute-start.5) | collective-permute-done | bytes 163872 | tf_op jit(solution)/shard_map/ppermute | solution.py:397
  17.7 1.9 %conv_r.1 = (f32[160,512]{1,0:T(8,128)S(1)}, f32[160,128]{1,0:T(8,128)S(1)}, f32[160,128]{1,0:T(8,128)S(1)}, bf16[320,1024]{1,0:T(8,128)(2,1)}) custom-call(s32[1]{0:T(128)} %bitcast.2.t_ref, bf16[2,4,80,128]{3,2,1,0:T(8,128)(2,1)S(1)} %bitcast.52, bf16[2,4,80,128]{3,2,1,0:T(8,128)(2,1)S(1)} %collective-permute-done.5.f1, ...), custom_call_target="tpu_custom_call" | custom-call | flops 471859200 | bytes 2263684 | tf_op jit(solution)/shard_map/conv_r/pallas_call | solution.py:33
  19.6 4.5 %collective-permute-start.8 = (f32[160,128]{1,0:T(8,128)S(1)}, f32[160,128]{1,0:T(8,128)S(1)}, u32[]{:S(2)}, u32[]{:S(2)}) collective-permute-start(f32[160,128]{1,0:T(8,128)S(1)} %get-tuple-element.31), channel_id=1, source_target_pairs={{0,4},{4,8},{8,12},{12,16},{16,20},{20,24},{24,28},{1,5},{5,9},{9,... | collective-permute-start | bytes 245768 | tf_op jit(solution)/shard_map/ppermute | solution.py:449
  24.1 1.9 %collective-permute-start.9 = (f32[160,128]{1,0:T(8,128)S(1)}, f32[160,128]{1,0:T(8,128)S(1)}, u32[]{:S(2)}, u32[]{:S(2)}) collective-permute-start(f32[160,128]{1,0:T(8,128)S(1)} %get-tuple-element.32), channel_id=1, source_target_pairs={{4,0},{8,4},{12,8},{16,12},{20,16},{24,20},{28,24},{5,1},{9,5},{13... | collective-permute-start | bytes 245768 | tf_op jit(solution)/shard_map/ppermute | solution.py:448
  26.0 1.2 %conv_p.1 = (f32[160,512]{1,0:T(8,128)S(1)}, f32[160,128]{1,0:T(8,128)S(1)}, f32[160,128]{1,0:T(8,128)S(1)}, bf16[320,1024]{1,0:T(8,128)(2,1)S(1)}, bf16[320,256...) custom-call(s32[1]{0:T(128)} %bitcast.2.t_ref, bf16[2,4,80,128]{3,2,1,0:T(8,128)(2,1)S(1)} %bitcast.48, ...), custom_call_target="tpu_custom_call" | custom-call | flops 471859200 | bytes 2591364 | tf_op jit(solution)/shard_map/conv_p/pallas_call | solution.py:33
  27.3 3.6 %collective-permute-start.3 = (f32[160,128]{1,0:T(8,128)S(1)}, f32[160,128]{1,0:T(8,128)S(1)}, u32[]{:S(2)}, u32[]{:S(2)}) collective-permute-start(f32[160,128]{1,0:T(8,128)S(1)} %get-tuple-element.28), channel_id=1, source_target_pairs={{0,4},{4,8},{8,12},{12,16},{16,20},{20,24},{24,28},{1,5},{5,9},{9,... | collective-permute-start | bytes 245768 | tf_op jit(solution)/shard_map/ppermute | solution.py:446
  30.9 1.9 %collective-permute-start.4 = (f32[160,128]{1,0:T(8,128)S(1)}, f32[160,128]{1,0:T(8,128)S(1)}, u32[]{:S(2)}, u32[]{:S(2)}) collective-permute-start(f32[160,128]{1,0:T(8,128)S(1)} %get-tuple-element.29), channel_id=1, source_target_pairs={{4,0},{8,4},{12,8},{16,12},{20,16},{24,20},{28,24},{5,1},{9,5},{13... | collective-permute-start | bytes 245768 | tf_op jit(solution)/shard_map/ppermute | solution.py:445
  33.0 3.7 %collective-permute-done.4.right_p = f32[160,128]{1,0:T(8,128)S(1)} collective-permute-done((f32[160,128]{1,0:T(8,128)S(1)}, f32[160,128]{1,0:T(8,128)S(1)}, u32[]{:S(2)}, u32[]{:S(2)}) %collective-permute-start.4) | collective-permute-done | bytes 81952 | tf_op jit(solution)/shard_map/ppermute | solution.py:445
  37.7 4.1 %all-to-all-start = ((f32[8,16,128]{2,1,0:T(8,128)}), f32[8,16,128]{2,1,0:T(8,128)S(1)}, u32[]{:S(2)}, u32[]{:S(2)}) async-start(f32[8,16,128]{2,1,0:T(8,128)} %get-tuple-element.35), calls=%async_computation | async-start | bytes 131072 | tf_op jit(solution)/shard_map/all_to_all | solution.py:460
  41.9 4.7 %all-to-all-done.sums_ref = f32[8,16,128]{2,1,0:T(8,128)S(1)} async-done(((f32[8,16,128]{2,1,0:T(8,128)}), f32[8,16,128]{2,1,0:T(8,128)S(1)}, u32[]{:S(2)}, u32[]{:S(2)}) %all-to-all-start) | async-done | bytes 65568 | tf_op jit(solution)/shard_map/all_to_all | solution.py:460
  47.5 1.2 %collective-permute-start.11 = (f32[2,6,8,128]{3,2,1,0:T(8,128)S(1)}, f32[2,6,8,128]{3,2,1,0:T(8,128)S(1)}, u32[]{:S(2)}, u32[]{:S(2)}) collective-permute-start(f32[2,6,8,128]{3,2,1,0:T(8,128)S(1)} %get-tuple-element.36.p0), channel_id=1, source_target_pairs={{0,2},{1,3},{2,0},{3,1},{4,6},{5,7},{6,4},{7,5},{8,10},{9,11},{10,... | collective-permute-start | bytes 147464 | tf_op jit(solution)/shard_map/ppermute | solution.py:468
  49.4 3.7 %collective-permute-start.15 = (bf16[320,256]{1,0:T(8,128)(2,1)S(1)}, bf16[320,256]{1,0:T(8,128)(2,1)S(1)}, u32[]{:S(2)}, u32[]{:S(2)}) collective-permute-start(bf16[320,256]{1,0:T(8,128)(2,1)S(1)} %get-tuple-element.45), channel_id=1, source_target_pairs={{0,4},{4,8},{8,12},{12,16},{16,20},{20,24},{24,28},{1,5},{5,9},{9,... | collective-permute-start | bytes 491528 | tf_op jit(solution)/shard_map/ppermute | solution.py:451
  53.1 1.9 %collective-permute-start.16 = (bf16[320,256]{1,0:T(8,128)(2,1)S(1)}, bf16[320,256]{1,0:T(8,128)(2,1)S(1)}, u32[]{:S(2)}, u32[]{:S(2)}) collective-permute-start(bf16[320,256]{1,0:T(8,128)(2,1)S(1)} %get-tuple-element.46), channel_id=1, source_target_pairs={{4,0},{8,4},{12,8},{16,12},{20,16},{24,20},{28,24},{5,1},{9,5},{13... | collective-permute-start | bytes 491528 | tf_op jit(solution)/shard_map/ppermute | solution.py:450
  55.1 3.6 %collective-permute-start.13 = (f32[2,2,8,128]{3,2,1,0:T(8,128)S(1)}, f32[2,2,8,128]{3,2,1,0:T(8,128)S(1)}, u32[]{:S(2)}, u32[]{:S(2)}) collective-permute-start(f32[2,2,8,128]{3,2,1,0:T(8,128)S(1)} %get-tuple-element.38), channel_id=1, source_target_pairs={{0,4},{4,8},{8,12},{12,16},{16,20},{20,24},{24,28},{1,5},{5,9},{9,... | collective-permute-start | bytes 49160 | tf_op jit(solution)/shard_map/ppermute | solution.py:476
  58.8 1.9 %collective-permute-start.14 = (f32[2,2,8,128]{3,2,1,0:T(8,128)S(1)}, f32[2,2,8,128]{3,2,1,0:T(8,128)S(1)}, u32[]{:S(2)}, u32[]{:S(2)}) collective-permute-start(f32[2,2,8,128]{3,2,1,0:T(8,128)S(1)} %get-tuple-element.39), channel_id=1, source_target_pairs={{4,0},{8,4},{12,8},{16,12},{20,16},{24,20},{28,24},{5,1},{9,5},{13... | collective-permute-start | bytes 49160 | tf_op jit(solution)/shard_map/ppermute | solution.py:477
  60.8 3.0 %collective-permute-done.14.right = f32[2,2,8,128]{3,2,1,0:T(8,128)S(1)} collective-permute-done((f32[2,2,8,128]{3,2,1,0:T(8,128)S(1)}, f32[2,2,8,128]{3,2,1,0:T(8,128)S(1)}, u32[]{:S(2)}, u32[]{:S(2)}) %collective-permute-start.14) | collective-permute-done | bytes 16416 | tf_op jit(solution)/shard_map/ppermute | solution.py:477
  63.8 1.8 %back.1 = (f32[160,512]{1,0:T(8,128)S(1)}, f32[8,32,128]{2,1,0:T(8,128)}) custom-call(s32[2]{0:T(128)S(1)} %add_convert_fusion.edge_ref, f32[2,6,8,128]{3,2,1,0:T(8,128)S(1)} %get-tuple-element.37.own, f32[2,2,8,128]{3,2,1,0:T(8,128)S(1)} %collective-permute-done.13.left, f32[2,2,8,128]{3,2,1,0:T(8,128)S(1)} %collective-permute-done.14.right, ...), custom_call_target="tpu_custom_call" | custom-call | flops 10000000 | bytes 1139720 | tf_op jit(solution)/shard_map/back/pallas_call | solution.py:33
  65.6 3.4 %all-to-all-start.1 = ((f32[8,32,128]{2,1,0:T(8,128)}), f32[8,32,128]{2,1,0:T(8,128)S(1)}, u32[]{:S(2)}, u32[]{:S(2)}) async-start(f32[8,32,128]{2,1,0:T(8,128)} %get-tuple-element.43), calls=%async_computation.1 | async-start | bytes 262144 | tf_op jit(solution)/shard_map/all_to_all | solution.py:486
  69.7 4.6 %all-to-all-done.1.red_ref = f32[8,32,128]{2,1,0:T(8,128)S(1)} async-done(((f32[8,32,128]{2,1,0:T(8,128)}), f32[8,32,128]{2,1,0:T(8,128)S(1)}, u32[]{:S(2)}, u32[]{:S(2)}) %all-to-all-start.1) | async-done | bytes 131104 | tf_op jit(solution)/shard_map/all_to_all | solution.py:486
  74.3 1.7 %weight.1 = (bf16[64,40,128]{2,1,0:T(8,128)(2,1)S(1)}, f32[1,1]{1,0:T(1,128)}) custom-call(s32[1]{0:T(128)S(6)} %copy.58.win_ref, f32[160,512]{1,0:T(8,128)S(1)} %get-tuple-element.42.gnorm_ref, f32[160,512]{1,0:T(8,128)S(1)} %get-tuple-element.33.full_p, f32[160,128]{1,0:T(8,128)S(1)} %get-tuple-element.40.stat_ref, ...), custom_call_target="tpu_custom_call" | custom-call | flops 471859200 | bytes 2506760 | tf_op jit(solution)/shard_map/weight/pallas_call | solution.py:33
  76.0 30.6 %all_to_all.15.got_ref = bf16[64,40,128]{2,1,0:T(8,128)(2,1)S(1)} all-to-all(bf16[64,40,128]{2,1,0:T(8,128)(2,1)S(1)} %get-tuple-element.48), channel_id=1, replica_groups=mesh['dp'=8,'space'=8,'tensor'=4] {'dp','space'}, dimensions={0} | all-to-all | bytes 1310720 | tf_op jit(solution)/shard_map/all_to_all | solution.py:496
  (74 shorter events, 8.2 us)
Async XLA Ops:
  0.6 10.4 %copy-start = (f32[1000,80]{0,1:T(8,128)S(1)}, f32[1000,80]{0,1:T(8,128)}, u32[]{:S(2)}) copy-start(f32[1000,80]{0,1:T(8,128)} %param.29) | copy-start | bytes 960004
  0.6 5.7 %copy-start.3 = (bf16[1,2,80,4,128]{4,3,2,1,0:T(4,128)(2,1)S(1)}, bf16[1,2,80,4,128]{4,3,2,1,0:T(4,128)(2,1)}, u32[]{:S(2)}) copy-start(bf16[1,2,80,4,128]{4,3,2,1,0:T(4,128)(2,1)} %param.16) | copy-start | bytes 491524
  1.7 9.8 %collective-permute-start.7 = (bf16[2,4,80,128]{3,2,1,0:T(8,128)(2,1)S(1)}, bf16[2,4,80,128]{3,2,1,0:T(8,128)(2,1)S(1)}, u32[]{:S(2)}, u32[]{:S(2)}) collective-permute-start(bf16[2,4,80,128]{3,2,1,0:T(8,128)(2,1)S(1)} %bitcast.49), channel_id=1, source_target_pairs={{0,3},{1,0},{2,1},{3,2},{4,7},{5,4},{6,5},{7,6},{8,11},{9,8},{10,9... | collective-permute-start | bytes 491528 | tf_op jit(solution)/shard_map/ppermute | solution.py:397
  5.3 7.9 %collective-permute-start.6 = (bf16[2,4,80,128]{3,2,1,0:T(8,128)(2,1)S(1)}, bf16[2,4,80,128]{3,2,1,0:T(8,128)(2,1)S(1)}, u32[]{:S(2)}, u32[]{:S(2)}) collective-permute-start(bf16[2,4,80,128]{3,2,1,0:T(8,128)(2,1)S(1)} %bitcast.50), channel_id=1, source_target_pairs={{0,2},{1,3},{2,0},{3,1},{4,6},{5,7},{6,4},{7,5},{8,10},{9,11},{10,... | collective-permute-start | bytes 491528 | tf_op jit(solution)/shard_map/ppermute | solution.py:397
  5.6 12.1 %collective-permute-start.5 = (bf16[2,4,80,128]{3,2,1,0:T(8,128)(2,1)S(1)}, bf16[2,4,80,128]{3,2,1,0:T(8,128)(2,1)S(1)}, u32[]{:S(2)}, u32[]{:S(2)}) collective-permute-start(bf16[2,4,80,128]{3,2,1,0:T(8,128)(2,1)S(1)} %bitcast.51), channel_id=1, source_target_pairs={{0,1},{1,2},{2,3},{3,0},{4,5},{5,6},{6,7},{7,4},{8,9},{9,10},{10,1... | collective-permute-start | bytes 491528 | tf_op jit(solution)/shard_map/ppermute | solution.py:397
  6.4 11.3 %copy-start.1 = (bf16[9,80,320]{2,1,0:T(8,128)(2,1)S(1)}, bf16[9,80,320]{2,1,0:T(8,128)(2,1)}, u32[]{:S(2)}) copy-start(bf16[9,80,320]{2,1,0:T(8,128)(2,1)} %param.20) | copy-start | bytes 1382404
  6.4 19.6 %collective-permute-start.2 = (bf16[2,4,80,128]{3,2,1,0:T(8,128)(2,1)S(1)}, bf16[2,4,80,128]{3,2,1,0:T(8,128)(2,1)S(1)}, u32[]{:S(2)}, u32[]{:S(2)}) collective-permute-start(bf16[2,4,80,128]{3,2,1,0:T(8,128)(2,1)S(1)} %bitcast.45), channel_id=1, source_target_pairs={{0,3},{1,0},{2,1},{3,2},{4,7},{5,4},{6,5},{7,6},{8,11},{9,8},{10,9... | collective-permute-start | bytes 491528 | tf_op jit(solution)/shard_map/ppermute | solution.py:397
  8.5 17.5 %collective-permute-start.1 = (bf16[2,4,80,128]{3,2,1,0:T(8,128)(2,1)S(1)}, bf16[2,4,80,128]{3,2,1,0:T(8,128)(2,1)S(1)}, u32[]{:S(2)}, u32[]{:S(2)}) collective-permute-start(bf16[2,4,80,128]{3,2,1,0:T(8,128)(2,1)S(1)} %bitcast.46), channel_id=1, source_target_pairs={{0,2},{1,3},{2,0},{3,1},{4,6},{5,7},{6,4},{7,5},{8,10},{9,11},{10,... | collective-permute-start | bytes 491528 | tf_op jit(solution)/shard_map/ppermute | solution.py:397
  11.5 14.5 %collective-permute-start = (bf16[2,4,80,128]{3,2,1,0:T(8,128)(2,1)S(1)}, bf16[2,4,80,128]{3,2,1,0:T(8,128)(2,1)S(1)}, u32[]{:S(2)}, u32[]{:S(2)}) collective-permute-start(bf16[2,4,80,128]{3,2,1,0:T(8,128)(2,1)S(1)} %bitcast.47), channel_id=1, source_target_pairs={{0,1},{1,2},{2,3},{3,0},{4,5},{5,6},{6,7},{7,4},{8,9},{9,10},{10,1... | collective-permute-start | bytes 491528 | tf_op jit(solution)/shard_map/ppermute | solution.py:397
  17.7 8.3 %copy-start.2 = (bf16[9,80,320]{2,1,0:T(8,128)(2,1)S(1)}, bf16[9,80,320]{2,1,0:T(8,128)(2,1)}, u32[]{:S(2)}) copy-start(bf16[9,80,320]{2,1,0:T(8,128)(2,1)} %param.19) | copy-start | bytes 1382404
  19.6 13.3 %collective-permute-start.8 = (f32[160,128]{1,0:T(8,128)S(1)}, f32[160,128]{1,0:T(8,128)S(1)}, u32[]{:S(2)}, u32[]{:S(2)}) collective-permute-start(f32[160,128]{1,0:T(8,128)S(1)} %get-tuple-element.31), channel_id=1, source_target_pairs={{0,4},{4,8},{8,12},{12,16},{16,20},{20,24},{24,28},{1,5},{5,9},{9,... | collective-permute-start | bytes 245768 | tf_op jit(solution)/shard_map/ppermute | solution.py:449
  24.1 8.9 %collective-permute-start.9 = (f32[160,128]{1,0:T(8,128)S(1)}, f32[160,128]{1,0:T(8,128)S(1)}, u32[]{:S(2)}, u32[]{:S(2)}) collective-permute-start(f32[160,128]{1,0:T(8,128)S(1)} %get-tuple-element.32), channel_id=1, source_target_pairs={{4,0},{8,4},{12,8},{16,12},{20,16},{24,20},{28,24},{5,1},{9,5},{13... | collective-permute-start | bytes 245768 | tf_op jit(solution)/shard_map/ppermute | solution.py:448
  27.3 5.6 %copy-start.12 = (f32[80]{0:T(128)S(1)}, f32[80]{0:T(128)}, u32[]{:S(2)}) copy-start(f32[80]{0:T(128)} %param.26) | copy-start | bytes 964
  27.3 5.7 %collective-permute-start.3 = (f32[160,128]{1,0:T(8,128)S(1)}, f32[160,128]{1,0:T(8,128)S(1)}, u32[]{:S(2)}, u32[]{:S(2)}) collective-permute-start(f32[160,128]{1,0:T(8,128)S(1)} %get-tuple-element.28), channel_id=1, source_target_pairs={{0,4},{4,8},{8,12},{12,16},{16,20},{20,24},{24,28},{1,5},{5,9},{9,... | collective-permute-start | bytes 245768 | tf_op jit(solution)/shard_map/ppermute | solution.py:446
  30.9 5.8 %collective-permute-start.4 = (f32[160,128]{1,0:T(8,128)S(1)}, f32[160,128]{1,0:T(8,128)S(1)}, u32[]{:S(2)}, u32[]{:S(2)}) collective-permute-start(f32[160,128]{1,0:T(8,128)S(1)} %get-tuple-element.29), channel_id=1, source_target_pairs={{4,0},{8,4},{12,8},{16,12},{20,16},{24,20},{28,24},{5,1},{9,5},{13... | collective-permute-start | bytes 245768 | tf_op jit(solution)/shard_map/ppermute | solution.py:445
  37.7 9.0 %all-to-all-start = ((f32[8,16,128]{2,1,0:T(8,128)}), f32[8,16,128]{2,1,0:T(8,128)S(1)}, u32[]{:S(2)}, u32[]{:S(2)}) async-start(f32[8,16,128]{2,1,0:T(8,128)} %get-tuple-element.35), calls=%async_computation | async-start | bytes 131072 | tf_op jit(solution)/shard_map/all_to_all | solution.py:460
  47.4 7.6 %collective-permute-start.12 = (f32[2,6,8,128]{3,2,1,0:T(8,128)S(1)}, f32[2,6,8,128]{3,2,1,0:T(8,128)S(1)}, u32[]{:S(2)}, u32[]{:S(2)}) collective-permute-start(f32[2,6,8,128]{3,2,1,0:T(8,128)S(1)} %get-tuple-element.36.p0), channel_id=1, source_target_pairs={{0,3},{1,0},{2,1},{3,2},{4,7},{5,4},{6,5},{7,6},{8,11},{9,8},{10,9... | collective-permute-start | bytes 147464 | tf_op jit(solution)/shard_map/ppermute | solution.py:468
  47.5 7.6 %collective-permute-start.11 = (f32[2,6,8,128]{3,2,1,0:T(8,128)S(1)}, f32[2,6,8,128]{3,2,1,0:T(8,128)S(1)}, u32[]{:S(2)}, u32[]{:S(2)}) collective-permute-start(f32[2,6,8,128]{3,2,1,0:T(8,128)S(1)} %get-tuple-element.36.p0), channel_id=1, source_target_pairs={{0,2},{1,3},{2,0},{3,1},{4,6},{5,7},{6,4},{7,5},{8,10},{9,11},{10,... | collective-permute-start | bytes 147464 | tf_op jit(solution)/shard_map/ppermute | solution.py:468
  48.6 6.4 %collective-permute-start.10 = (f32[2,6,8,128]{3,2,1,0:T(8,128)S(1)}, f32[2,6,8,128]{3,2,1,0:T(8,128)S(1)}, u32[]{:S(2)}, u32[]{:S(2)}) collective-permute-start(f32[2,6,8,128]{3,2,1,0:T(8,128)S(1)} %get-tuple-element.36.p0), channel_id=1, source_target_pairs={{0,1},{1,2},{2,3},{3,0},{4,5},{5,6},{6,7},{7,4},{8,9},{9,10},{10,1... | collective-permute-start | bytes 147464 | tf_op jit(solution)/shard_map/ppermute | solution.py:468
  49.4 20.3 %collective-permute-start.15 = (bf16[320,256]{1,0:T(8,128)(2,1)S(1)}, bf16[320,256]{1,0:T(8,128)(2,1)S(1)}, u32[]{:S(2)}, u32[]{:S(2)}) collective-permute-start(bf16[320,256]{1,0:T(8,128)(2,1)S(1)} %get-tuple-element.45), channel_id=1, source_target_pairs={{0,4},{4,8},{8,12},{12,16},{16,20},{20,24},{24,28},{1,5},{5,9},{9,... | collective-permute-start | bytes 491528 | tf_op jit(solution)/shard_map/ppermute | solution.py:451
  53.1 16.6 %collective-permute-start.16 = (bf16[320,256]{1,0:T(8,128)(2,1)S(1)}, bf16[320,256]{1,0:T(8,128)(2,1)S(1)}, u32[]{:S(2)}, u32[]{:S(2)}) collective-permute-start(bf16[320,256]{1,0:T(8,128)(2,1)S(1)} %get-tuple-element.46), channel_id=1, source_target_pairs={{4,0},{8,4},{12,8},{16,12},{20,16},{24,20},{28,24},{5,1},{9,5},{13... | collective-permute-start | bytes 491528 | tf_op jit(solution)/shard_map/ppermute | solution.py:450
  55.1 5.7 %collective-permute-start.13 = (f32[2,2,8,128]{3,2,1,0:T(8,128)S(1)}, f32[2,2,8,128]{3,2,1,0:T(8,128)S(1)}, u32[]{:S(2)}, u32[]{:S(2)}) collective-permute-start(f32[2,2,8,128]{3,2,1,0:T(8,128)S(1)} %get-tuple-element.38), channel_id=1, source_target_pairs={{0,4},{4,8},{8,12},{12,16},{16,20},{20,24},{24,28},{1,5},{5,9},{9,... | collective-permute-start | bytes 49160 | tf_op jit(solution)/shard_map/ppermute | solution.py:476
  58.8 5.1 %collective-permute-start.14 = (f32[2,2,8,128]{3,2,1,0:T(8,128)S(1)}, f32[2,2,8,128]{3,2,1,0:T(8,128)S(1)}, u32[]{:S(2)}, u32[]{:S(2)}) collective-permute-start(f32[2,2,8,128]{3,2,1,0:T(8,128)S(1)} %get-tuple-element.39), channel_id=1, source_target_pairs={{4,0},{8,4},{12,8},{16,12},{20,16},{24,20},{28,24},{5,1},{9,5},{13... | collective-permute-start | bytes 49160 | tf_op jit(solution)/shard_map/ppermute | solution.py:477
  65.6 8.7 %all-to-all-start.1 = ((f32[8,32,128]{2,1,0:T(8,128)}), f32[8,32,128]{2,1,0:T(8,128)S(1)}, u32[]{:S(2)}, u32[]{:S(2)}) async-start(f32[8,32,128]{2,1,0:T(8,128)} %get-tuple-element.43), calls=%async_computation.1 | async-start | bytes 262144 | tf_op jit(solution)/shard_map/all_to_all | solution.py:486
  (8 other events, 27.5 us)

commit v2 on v1

v2 whole, which is shorter than its diff:
```python
import functools

import jax
import jax.numpy as jnp
from jax import lax
from jax.experimental import pallas as pl
from jax.experimental.pallas import tpu as pltpu
from jax.sharding import PartitionSpec as P

C = 320
GROUPS = 32
BETA = 500.0
EPS = 1e-05
CH = 80
ROWS = 4
COLS = 128
PIX = ROWS * COLS
GSIZE = C // GROUPS
LOCAL_GROUPS = CH // GSIZE
COUNT = float(GSIZE * 32 * 128)
CELLS = float(4 * 32 * 128)
F32 = jnp.float32
BF16 = jnp.bfloat16
HIGHEST = lax.Precision.HIGHEST

VM = pl.BlockSpec(memory_space=pltpu.VMEM)
SM = pl.BlockSpec(memory_space=pltpu.SMEM)


def call(kernel, ins, outs, name, flops, smem=0, scratch=()):
    in_bytes = sum(a.size * a.dtype.itemsize for a in ins)
    out_bytes = sum(s.size * s.dtype.itemsize for s in outs)
    return pl.pallas_call(
        kernel,
        out_shape=outs,
        in_specs=[SM] * smem + [VM] * (len(ins) - smem),
        out_specs=[VM] * len(outs),
        scratch_shapes=list(scratch),
        name=name,
        cost_estimate=pl.CostEstimate(
            flops=flops, bytes_accessed=in_bytes + out_bytes, transcendentals=0
        ),
        compiler_params=pltpu.CompilerParams(vmem_limit_bytes=12 * 1024 * 1024),
    )(*ins)


def arr(shape, dtype):
    return jax.ShapeDtypeStruct(shape, dtype)


def dot(a, b):
    return lax.dot_general(a, b, (((1,), (0,)), ((), ())), preferred_element_type=F32)


def dot_nt(a, b):
    return lax.dot_general(a, b, (((1,), (1,)), ((), ())), preferred_element_type=F32)


def exact_dot(a, b):
    return lax.dot_general(
        a, b, (((1,), (0,)), ((), ())), preferred_element_type=F32, precision=HIGHEST
    )


def from_left(tile):
    lane = lax.broadcasted_iota(jnp.int32, tile.shape, tile.ndim - 1)
    return jnp.where(lane == 0, 0.0, pltpu.roll(tile, 1, tile.ndim - 1))


def from_right(tile):
    lane = lax.broadcasted_iota(jnp.int32, tile.shape, tile.ndim - 1)
    return jnp.where(lane == COLS - 1, 0.0, pltpu.roll(tile, COLS - 1, tile.ndim - 1))


def row_of(tile, r):
    return tile[:, r * COLS : (r + 1) * COLS]


def members():
    group = lax.broadcasted_iota(jnp.int32, (2 * LOCAL_GROUPS, 2 * CH), 0)
    chan = lax.broadcasted_iota(jnp.int32, (2 * LOCAL_GROUPS, 2 * CH), 1)
    low = group * GSIZE
    return jnp.where((chan >= low) & (chan < low + GSIZE), 1.0, 0.0).astype(F32)


def spread(stat):
    chan = lax.broadcasted_iota(jnp.int32, (2 * CH, 2 * LOCAL_GROUPS), 0)
    group = lax.broadcasted_iota(jnp.int32, (2 * CH, 2 * LOCAL_GROUPS), 1)
    low = group * GSIZE
    pick = jnp.where((chan >= low) & (chan < low + GSIZE), 1.0, 0.0).astype(F32)
    return exact_dot(pick, stat)


def in_lanes(columns):
    rows = columns[0].shape[0]
    lane = lax.broadcasted_iota(jnp.int32, (rows, COLS), 1)
    out = jnp.zeros((rows, COLS), F32)
    for index, column in enumerate(columns):
        out = jnp.where(lane == index, column, out)
    return out


def prep_kernel(
    place_ref, b_p, b_r, gain_p, off_p, gain_r, off_r, w2_p, w2_r, table_ref, noise_ref,
    col_ref, lift_ref, drop_ref, rows_ref
):
    lane = lax.broadcasted_iota(jnp.int32, table_ref.shape, 1)
    shift = jnp.sum(
        jnp.where(lane == place_ref[6], table_ref[...], 0.0), axis=1, keepdims=True
    )
    eye = lax.broadcasted_iota(jnp.int32, (CH, CH), 0) == lax.broadcasted_iota(
        jnp.int32, (CH, CH), 1
    )

    def upright(ref):
        return jnp.sum(jnp.where(eye, ref[...], 0.0), axis=1, keepdims=True)

    block = in_lanes(
        [
            upright(gain_p),
            upright(off_p),
            upright(gain_r),
            upright(off_r),
            upright(b_p) + shift,
            upright(b_r) + shift,
        ]
    )
    col_ref[0:CH, :] = block
    col_ref[CH : 2 * CH, :] = block
    one = jnp.where(eye, 1.0, 0.0).astype(BF16)
    zero = jnp.zeros((4, CH), F32)
    for m, ref in enumerate((w2_p, w2_r)):
        for im in range(2):
            pieces = []
            for tap in range(9):
                rows = ref[tap].astype(F32)
                pieces += [rows, zero] if im == 0 else [zero, rows]
            padded = jnp.concatenate(pieces, axis=0).astype(BF16)
            lift_ref[m, im] = padded
            if m == 0:
                drop_ref[im * CH : (im + 1) * CH, :] = dot_nt(one, padded).astype(BF16)
    for im in range(2):
        for o in range(4):
            slot = im * 4 + o
            for r in range(ROWS):
                rows_ref[r, slot : slot + 1, :] = noise_ref[im, o, r : r + 1, :]


def conv_kernel(last, t_ref, f0, f1, f2a, f2b, f3, w_ref, col_ref, *refs):
    if last:
        side_l, side_r, noise_ref, pre_ref, up_ref, dn_ref, send_l, send_r, fs_ref = refs
    else:
        pre_ref, up_ref, dn_ref, send_l, send_r, fs_ref = refs
    t = t_ref[5]
    bias = 5 if last else 4
    for k in range(4):
        base = pl.multiple_of(lax.rem(t - k + 4, 4) * CH, 16)
        for im in range(2):
            for r in range(ROWS):
                lo = im * PIX + r * COLS
                if k == 2:
                    piece = f2a[r] if im == 0 else f2b[r]
                else:
                    piece = (f0, f1, None, f3)[k][im, r]
                fs_ref[pl.ds(base, CH), lo : lo + COLS] = piece
    if last:
        send_l[0:960, :] = side_l[...]
        send_r[0:960, :] = side_r[...]
        for ref, rows in ((send_l, (0, 1)), (send_r, (2, 3))):
            for index, r in enumerate(rows):
                value = noise_ref[r]
                high = value.astype(BF16).astype(F32)
                both = jnp.concatenate([high, value - high], axis=0).astype(BF16)
                ref[1600 + 16 * index : 1616 + 16 * index, :] = both
        start, keep_l, keep_r = 960, (-1, 0), (ROWS - 1, ROWS)
    else:
        start, keep_l, keep_r = 0, (-1, 0, 1, 2), (1, 2, 3, 4)
    for im in range(2):
        feats = fs_ref[:, im * PIX : (im + 1) * PIX]
        taps = [dot(w_ref[ky * 3 * CH : (ky + 1) * 3 * CH, :], feats) for ky in range(3)]
        chans = slice(im * CH, (im + 1) * CH)
        for r in range(-1, ROWS + 1):
            total = None
            for ky in range(3):
                src = r + ky - 1
                if 0 <= src < ROWS:
                    term = row_of(taps[ky], src)
                    total = term if total is None else total + term
            out = (
                total[CH : 2 * CH]
                + from_left(total[0:CH])
                + from_right(total[2 * CH : 3 * CH])
            )
            if r == -1:
                up_ref[chans, :] = out
            elif r == ROWS:
                dn_ref[chans, :] = out
            else:
                out = out + col_ref[chans, bias : bias + 1]
                pre_ref[chans, r * COLS : (r + 1) * COLS] = out
            for keep, ref in ((keep_l, send_l), (keep_r, send_r)):
                if r in keep:
                    lo = start + keep.index(r) * 2 * CH + im * CH
                    high = out.astype(BF16)
                    ref[lo : lo + CH, :] = high
                    if r in (-1, 0, ROWS - 1, ROWS):
                        near = 0 if r < 1 else 2 - len(keep)
                        slot = keep.index(r) + near + len(keep)
                        lo = start + slot * 2 * CH + im * CH
                        ref[lo : lo + CH, :] = (out - high.astype(F32)).astype(BF16)


def stat_kernel(
    pre_p, up_p, dn_p, pre_r, up_r, dn_r, left, right, noise_ref, ext_p, ext_r, noise_ext, out_ref
):
    def got(ref, index):
        return ref[index * 2 * CH : (index + 1) * 2 * CH, :].astype(F32)

    def near(ref, index, low):
        return got(ref, index) + got(ref, low)

    columns = []
    for pre, up, dn, ext, first, halo in (
        (pre_p, up_p, dn_p, ext_p, 0, 3),
        (pre_r, up_r, dn_r, ext_r, 6, 1),
    ):
        low = first + halo + 1
        rows = [pre[:, r * COLS : (r + 1) * COLS] for r in range(ROWS)]
        rows[0] = rows[0] + near(left, first + halo, low + 1)
        rows[ROWS - 1] = rows[ROWS - 1] + near(right, first, low)
        total = rows[0] + rows[1] + rows[2] + rows[3]
        square = (
            rows[0] * rows[0] + rows[1] * rows[1] + rows[2] * rows[2] + rows[3] * rows[3]
        )
        before = [got(left, first + index) for index in range(halo)]
        before[-1] = near(left, first + halo - 1, low) + up[...]
        after = [got(right, first + 1 + index) for index in range(halo)]
        after[0] = near(right, first + 1, low + 1) + dn[...]
        for index, row in enumerate(before + rows + after):
            ext[:, index * COLS : (index + 1) * COLS] = row
        columns.append(jnp.sum(total, axis=1, keepdims=True))
        columns.append(jnp.sum(square, axis=1, keepdims=True))
    for index in range(2):
        lo = 1600 + 16 * index
        pair = left[lo : lo + 16, :].astype(F32)
        noise_ext[index] = pair[0:8] + pair[8:16]
        pair = right[lo : lo + 16, :].astype(F32)
        noise_ext[ROWS + 2 + index] = pair[0:8] + pair[8:16]
    for r in range(ROWS):
        noise_ext[2 + r] = noise_ref[r]
    sums = exact_dot(members(), in_lanes(columns))
    for peer in range(out_ref.shape[0]):
        out_ref[peer] = sums


def moments(total):
    wide = spread(total / COUNT)
    result = []
    for m in range(2):
        mean = wide[:, 2 * m : 2 * m + 1]
        square = wide[:, 2 * m + 1 : 2 * m + 2]
        result.append((mean, lax.rsqrt(square - mean * mean + EPS)))
    return result


def hidden_kernel(
    edge_ref, ext_p, ext_r, sums_ref, col_ref, lift_ref, part_ref, hid_ref, stat_ref
):
    stats = moments(jnp.sum(sums_ref[...], axis=0))
    stat_ref[...] = in_lanes([stats[0][0], stats[0][1]])
    for m, (ext, halo, start) in enumerate(((ext_p, 3, 0), (ext_r, 1, 8))):
        mean, inv = stats[m]
        gain = col_ref[:, 2 * m : 2 * m + 1]
        shift = col_ref[:, 2 * m + 1 : 2 * m + 2]
        pieces = []
        for index in range(ROWS + 2 * halo):
            value = ext[:, index * COLS : (index + 1) * COLS]
            normed = ((value - mean) * inv) * gain + shift
            hidden = normed * jax.nn.sigmoid(normed)
            if index < halo:
                hidden = jnp.where(edge_ref[1] > 0, 0.0, hidden)
            if index >= ROWS + halo:
                hidden = jnp.where(edge_ref[2] > 0, 0.0, hidden)
            hidden = hidden.astype(BF16)
            if m == 0 and halo <= index < halo + ROWS:
                hid_ref[:, (index - halo) * COLS : (index - halo + 1) * COLS] = hidden
            pieces.append(hidden)
        joined = jnp.concatenate(pieces, axis=1)
        taps = dot(lift_ref[m, 0], joined[0:CH]) + dot(lift_ref[m, 1], joined[CH : 2 * CH])
        for index in range(ROWS + 2 * halo - 2):
            totals = [None, None, None]
            for kx in range(3):
                for ky in range(3):
                    tap = 3 * ky + kx
                    lo = (index + ky) * COLS
                    term = taps[8 * tap : 8 * tap + 8, lo : lo + COLS]
                    totals[kx] = term if totals[kx] is None else totals[kx] + term
            part_ref[start + index] = (
                totals[1] + from_left(totals[0]) + from_right(totals[2])
            )


def back_kernel(
    edge_ref, p0, p1, p2, p3, noise_ext, ext_p, stat_ref, col_ref, hid_ref, drop_ref,
    gnorm_ref, head_ref, out_ref
):
    def pred(index):
        return (p0[index] + p1[index]) + (p2[index] + p3[index])

    residual = [pred(index) - noise_ext[index] for index in range(ROWS + 4)]
    frozen = [pred(8 + r) - noise_ext[2 + r] for r in range(ROWS)]
    errors = []
    for rows in (residual[2 : 2 + ROWS], frozen):
        square = rows[0] * rows[0]
        for row in rows[1:]:
            square = square + row * row
        errors.append(jnp.sum(square, axis=1, keepdims=True))
    image = lax.broadcasted_iota(jnp.int32, (8, COLS), 0)
    residual = [jnp.where(image < 4, row, -row) for row in residual]
    for index in range(2):
        residual[index] = jnp.where(edge_ref[1] > 0, 0.0, residual[index])
        residual[ROWS + 2 + index] = jnp.where(edge_ref[2] > 0, 0.0, residual[ROWS + 2 + index])
    moved = [
        [from_right(row) for row in residual],
        residual,
        [from_left(row) for row in residual],
    ]
    blocks = []
    for ky in range(3):
        for kx in range(3):
            blocks.append(
                jnp.concatenate([moved[kx][r + 2 - ky] for r in range(ROWS + 2)], axis=1)
            )
    cot = jnp.concatenate(blocks, axis=0).astype(BF16)
    dhidden = dot(drop_ref[...], cot)
    mean = stat_ref[:, 0:1]
    inv = stat_ref[:, 1:2]
    gain = col_ref[:, 0:1]
    shift = col_ref[:, 1:2]
    first = None
    second = None
    for index in range(ROWS + 2):
        lanes = slice(index * COLS, (index + 1) * COLS)
        centered = (ext_p[:, (index + 2) * COLS : (index + 3) * COLS] - mean) * inv
        normed = centered * gain + shift
        gate = jax.nn.sigmoid(normed)
        gnorm = dhidden[:, lanes] * gate * (1.0 + normed * (1.0 - gate)) * gain
        gnorm_ref[:, lanes] = gnorm
        if 1 <= index <= ROWS:
            first = gnorm if first is None else first + gnorm
            extra = gnorm * centered
            second = extra if second is None else second + extra
    first = jnp.sum(first, axis=1, keepdims=True)
    second = jnp.sum(second, axis=1, keepdims=True)
    sums = exact_dot(members(), in_lanes([first, second]))
    mine = cot[:, COLS : (ROWS + 1) * COLS]
    grads = [dot_nt(mine, hid_ref[im * CH : (im + 1) * CH, :]) for im in range(2)]
    error = in_lanes(errors)
    head_ref[...] = jnp.zeros(head_ref.shape, F32)
    for tap in range(9):
        head = grads[0][8 * tap : 8 * tap + 4] + grads[1][8 * tap + 4 : 8 * tap + 8]
        head_ref[4 * tap : 4 * tap + 4, 0:CH] = head
    for peer in range(out_ref.shape[0]):
        out_ref[peer, 0:16, :] = sums
        out_ref[peer, 16:24, :] = error


def weight_kernel(
    place_ref, gnorm_ref, ext_p, stat_ref, red_ref, fs_ref, head_ref,
    keep_ref, send_ref, both_ref, logit_ref, grad_ref, pack_ref
):
    total = jnp.sum(red_ref[...], axis=0)
    row = lax.broadcasted_iota(jnp.int32, (8, COLS), 0)
    signed = jnp.where(row < 4, total[16:24], -total[16:24])
    gaps = jnp.sum(signed, axis=0, keepdims=True)
    gap = (gaps[:, 0:1] - gaps[:, 1:2]) * (1.0 / CELLS)
    sign = 1.0 - 2.0 * place_ref[0].astype(F32)
    logit = (-0.5 * BETA) * sign * gap
    logit_ref[...] = logit
    scale = (BETA / CELLS) * sign * jax.nn.sigmoid(-logit)
    wide = spread(total[0:16] / COUNT)
    mean = stat_ref[:, 0:1]
    inv = stat_ref[:, 1:2]
    parts = []
    for index in range(ROWS + 2):
        centered = (ext_p[:, (index + 2) * COLS : (index + 3) * COLS] - mean) * inv
        gnorm = gnorm_ref[:, index * COLS : (index + 1) * COLS]
        delta = inv * (gnorm - wide[:, 0:1] - centered * wide[:, 1:2])
        if index == 0:
            delta = jnp.where(place_ref[1] > 0, 0.0, delta)
        if index == ROWS + 1:
            delta = jnp.where(place_ref[2] > 0, 0.0, delta)
        parts.append(
            [from_right(delta).astype(BF16), delta.astype(BF16), from_left(delta).astype(BF16)]
        )
    blank = jnp.zeros((16, 2 * PIX), BF16)
    for ky in range(3):
        rows = []
        for kx in range(3):
            tiles = []
            for im in range(2):
                for r in range(ROWS):
                    tiles.append(parts[r + 2 - ky][kx][im * CH : (im + 1) * CH])
            rows.append(jnp.concatenate(tiles, axis=1))
        stack = jnp.concatenate(rows + [blank], axis=0)
        grad = dot_nt(fs_ref[...], stack) * scale
        grad_ref[2 * ky] = grad[:, 0:COLS]
        grad_ref[2 * ky + 1] = grad[:, COLS : 2 * COLS]
    chunk = 5
    peers = C // chunk
    for ii in range(chunk):
        for half in range(6):
            pack_ref[pl.ds(half * chunk + ii, peers, stride=32), :] = grad_ref[
                half, pl.ds(ii, peers, stride=chunk), :
            ]
    core = place_ref[3]
    used = lax.broadcasted_iota(jnp.int32, (32, COLS), 0) < 6 * chunk
    for x in range(4):
        for d in range(8):
            lo = (x * 8 + d) * 32
            mine = pl.multiple_of((d * 8 + 2 * x + core) * 32, 32)
            keep_ref[lo : lo + 32, :] = jnp.where(used, pack_ref[pl.ds(mine, 32), :], 0.0)
            his = pl.multiple_of((d * 8 + 2 * x + 1 - core) * 32, 32)
            tile = jnp.where(used, pack_ref[pl.ds(his, 32), :], 0.0)
            send_ref[lo : lo + 32, :] = tile.astype(BF16)
    head = head_ref[...] * scale
    both_ref[...] = head
    send_ref[1024:1072, :] = head.astype(BF16)


def core_kernel(x_ref, keep_ref, both_ref, got_ref, own_ref, s1, s2, s3):
    x = x_ref[4]
    head = both_ref[...] + got_ref[1024:1072, :].astype(F32)
    for k, ref in enumerate((own_ref, s1, s2, s3)):
        lo = pl.multiple_of(lax.rem(x + k, 4) * 256, 256)
        block = keep_ref[pl.ds(lo, 256), :] + got_ref[pl.ds(lo, 256), :].astype(F32)
        ref[0:256, :] = block.astype(ref.dtype)
        ref[256:304, :] = head.astype(ref.dtype)


def cross_kernel(own_ref, r1, r2, r3, out_ref):
    def total(lo, hi):
        return (own_ref[lo:hi, :] + r1[lo:hi, :].astype(F32)) + (
            r2[lo:hi, :].astype(F32) + r3[lo:hi, :].astype(F32)
        )

    head = total(256, 304).astype(BF16)
    for d in range(8):
        out_ref[d, 0:32, :] = total(32 * d, 32 * d + 32).astype(BF16)
        out_ref[d, 32:80, :] = head


def sum_kernel(got_ref, one_ref, two_ref):
    total = got_ref[0].astype(F32)
    for d in range(1, got_ref.shape[0]):
        total = total + got_ref[d].astype(F32)
    chunk = 5
    for tap in range(9):
        two_ref[tap] = total[32 + 4 * tap : 36 + 4 * tap, 0:CH]
    for ky in range(3):
        lo = 2 * ky * chunk
        wide = jnp.concatenate(
            [total[lo : lo + chunk], total[lo + chunk : lo + 2 * chunk]], axis=1
        )
        for kx in range(3):
            one_ref[3 * ky + kx] = wide[:, kx * CH : (kx + 1) * CH]


def ring(axis, step):
    count = lax.axis_size(axis)
    return [(i, (i + step) % count) for i in range(count)]


def line(axis, step):
    count = lax.axis_size(axis)
    return [(i, i + step) for i in range(count) if 0 <= i + step < count]


def body(
    feat_policy,
    feat_ref,
    noise,
    w1_policy,
    w1_ref,
    b1_policy,
    b1_ref,
    gn_gain_policy,
    gn_bias_policy,
    gn_gain_ref,
    gn_bias_ref,
    w2_policy,
    w2_ref,
    time_table,
    timestep,
    winner,
):
    space = lax.axis_size("space")
    s_index = lax.axis_index("space").astype(jnp.int32)
    is_top = (s_index == 0).astype(jnp.int32)
    is_bottom = (s_index == space - 1).astype(jnp.int32)
    place = jnp.stack(
        [
            winner[0].astype(jnp.int32),
            is_top,
            is_bottom,
            s_index & 1,
            s_index >> 1,
            lax.axis_index("tensor").astype(jnp.int32),
            timestep[0].astype(jnp.int32),
        ]
    )

    def gather(own):
        left = lax.ppermute(own, "tensor", ring("tensor", 1))
        right = lax.ppermute(own, "tensor", ring("tensor", -1))
        return own, left, right

    def relay(own, left, right):
        far_a = lax.ppermute(left[0], "tensor", ring("tensor", 1))
        far_b = lax.ppermute(right[1], "tensor", ring("tensor", -1))
        return own, left, far_a, far_b, right

    own_p = feat_policy[0].transpose(0, 2, 1, 3)
    feat_ref, own_p = lax.optimization_barrier((feat_ref, own_p))
    own_r = feat_ref[0].transpose(0, 2, 1, 3)
    parts_p = relay(*gather(own_p))
    parts_r = relay(*gather(own_r))

    vectors = [b1_policy, b1_ref, gn_gain_policy, gn_bias_policy, gn_gain_ref, gn_bias_ref]
    columns, lift, drop, noise_rows = call(
        prep_kernel,
        [place, *[v[None, :] for v in vectors], w2_policy, w2_ref, time_table.T, noise[0]],
        [
            arr((2 * CH, COLS), F32),
            arr((2, 2, 72, CH), BF16),
            arr((2 * CH, 72), BF16),
            arr((ROWS, 8, COLS), F32),
        ],
        "prep",
        10**6,
        smem=1,
    )

    conv_flops = 2 * 9 * C * CH * 2 * PIX
    wide = arr((2 * CH, PIX), F32)
    thin = arr((2 * CH, COLS), F32)

    pre_p, up_p, dn_p, side_l, side_r, feats = call(
        functools.partial(conv_kernel, False),
        [place, *parts_p, w1_policy.reshape(9 * CH, C), columns],
        [wide, thin, thin, arr((960, COLS), BF16), arr((960, COLS), BF16), arr((C, 2 * PIX), BF16)],
        "conv_p",
        conv_flops,
        smem=1,
    )
    pre_r, up_r, dn_r, to_left, to_right = call(
        functools.partial(conv_kernel, True),
        [place, *parts_r, w1_ref.reshape(9 * CH, C), columns, side_l, side_r, noise_rows],
        [wide, thin, thin, arr((1632, COLS), BF16), arr((1632, COLS), BF16)],
        "conv_r",
        conv_flops,
        smem=1,
        scratch=[pltpu.VMEM((C, 2 * PIX), BF16)],
    )
    left = lax.ppermute(to_right, "space", line("space", 1))
    right = lax.ppermute(to_left, "space", line("space", -1))

    ext_p, ext_r, noise_ext, sums = call(
        stat_kernel,
        [pre_p, up_p, dn_p, pre_r, up_r, dn_r, left, right, noise_rows],
        [
            arr((2 * CH, 10 * COLS), F32),
            arr((2 * CH, 6 * COLS), F32),
            arr((8, 8, COLS), F32),
            arr((space, 16, COLS), F32),
        ],
        "stats",
        10**6,
    )
    sums = lax.all_to_all(sums, "space", 0, 0, tiled=True)
    part, hidden, stat = call(
        hidden_kernel,
        [place, ext_p, ext_r, sums, columns, lift],
        [arr((12, 8, COLS), F32), arr((2 * CH, PIX), BF16), thin],
        "hidden",
        10**7,
        smem=1,
    )
    others = [lax.ppermute(part, "tensor", ring("tensor", k)) for k in (1, 2, 3)]
    gnorm, head, partial = call(
        back_kernel,
        [place, part, *others, noise_ext, ext_p, stat, columns, hidden, drop],
        [arr((2 * CH, 6 * COLS), F32), arr((48, COLS), F32), arr((space, 24, COLS), F32)],
        "back",
        10**7,
        smem=1,
    )
    partial = lax.all_to_all(partial, "space", 0, 0, tiled=True)
    keep, send, both, logits = call(
        weight_kernel,
        [place, gnorm, ext_p, stat, partial, feats, head],
        [arr((1024, COLS), F32), arr((1072, COLS), BF16), arr((48, COLS), F32), arr((1, 1), F32)],
        "weight",
        conv_flops,
        smem=1,
        scratch=[pltpu.VMEM((6, C, COLS), F32), pltpu.VMEM((64 * 32, COLS), F32)],
    )
    got = lax.ppermute(send, "space", [(i, i ^ 1) for i in range(space)])
    own, s1, s2, s3 = call(
        core_kernel,
        [place, keep, both, got],
        [arr((304, COLS), F32)] + [arr((304, COLS), BF16)] * 3,
        "core",
        10**6,
        smem=1,
    )
    back = [
        lax.ppermute(sent, "space", ring("space", 2 * k)) for k, sent in ((1, s1), (2, s2), (3, s3))
    ]
    (packed,) = call(cross_kernel, [own, *back], [arr((8, 80, COLS), BF16)], "cross", 10**6)
    packed = lax.all_to_all(packed, "dp", 0, 0, tiled=True)
    grad_one, grad_two = call(
        sum_kernel, [packed], [arr((9, 5, CH), F32), arr((9, 4, CH), F32)], "total", 10**6
    )
    return (logits.reshape(1), grad_one.transpose(0, 2, 1), grad_two)


def solution(mesh):
    in_specs = (
        P("dp", None, "tensor", "space", None),
        P("dp", None, "tensor", "space", None),
        P("dp", None, None, "space", None),
        P(None, "tensor", None),
        P(None, "tensor", None),
        P("tensor"),
        P("tensor"),
        P("tensor"),
        P("tensor"),
        P("tensor"),
        P("tensor"),
        P(None, None, "tensor"),
        P(None, None, "tensor"),
        P(None, "tensor"),
        P("dp"),
        P("dp"),
    )
    out_specs = (P("dp"), P(None, "tensor", ("dp", "space")), P(None, None, "tensor"))
    return jax.shard_map(body, mesh=mesh, in_specs=in_specs, out_specs=out_specs, check_vma=False)
```

time: 108 us -> 97.5 us (0.903)
  starting transfers between devices: 40.9 us -> 28 us
  blocking collectives: 30.6 us -> 33.9 us
  Pallas kernels: 9.17 us -> 11.2 us
  waiting for transfers between devices: 20.7 us -> 18.7 us
  local copies, waits for them, and re-layouts: 3.19 us -> 1.81 us
    all_to_all x2 -> x0, waiting for transfers between devices: 9.29 us -> none  [the longest x1 4.72 us: body(): sums = lax.all_to_all(sums, 'space', 0, 0, tiled=True)]
    all_to_all x2 -> x0, starting transfers between devices: 7.56 us -> none  [the longest x1 4.11 us: body(): sums = lax.all_to_all(sums, 'space', 0, 0, tiled=True)]
    ppermute x14, starting transfers between devices: 31.3 us -> 25.3 us  [the longest x2 6.82 us: relay(): far_b = lax.ppermute(right[1], 'tensor', ring('tensor', -1))]
    ppermute x3, waiting for transfers between devices: 0.01 us -> 4.12 us  [body(): lax.ppermute(part, 'tensor', ring('tensor', k))]
    all_to_all x1 -> x3, blocking collectives: 30.6 us -> 33.9 us  [the longest x1 16.3 us: body(): packed = lax.all_to_all(packed, 'dp', 0, 0, tiled=True)]
    ppermute x14, waiting for transfers between devices: 11.4 us -> 14.6 us  [the longest x1 4.4 us: body(): right = lax.ppermute(to_left, 'space', line('space', -1))]
    pallas_call x8 -> x10, Pallas kernels: 9.17 us -> 11.2 us  [call(): pl.pallas_call(kernel, out_shape=outs, in_specs=[SM] * smem + [VM] * (len...]
  transfers between devices with their start and end apart: 19 -> 17, of which waited for: 5 -> 12; matrix products, arithmetic and copies ran while one was open for 1% -> 0% of each run, Pallas kernels for 5% -> 3%
where the time goes in v2:
time: 97.5 us; the launch traced here: 95.8 us
  blocking collectives  33.9 us (35%)
  starting transfers between devices  28 us (29%)
  waiting for transfers between devices  18.7 us (19%)
  Pallas kernels  11.2 us (11%)
  between operations  2.21 us (2%)
  local copies, waits for them, and re-layouts  1.81 us (2%)
    all_to_all x1, blocking collectives, body(): packed = lax.all_to_all(packed, 'dp', 0, 0, tiled=True)  16.3 us
    pallas_call x10, Pallas kernels, call(): pl.pallas_call(kernel, out_shape=outs, in_specs=[SM] * smem + [VM] * (len...  11.2 us
    all_to_all x1, blocking collectives, body(): partial = lax.all_to_all(partial, 'space', 0, 0, tiled=True)  8.84 us
    all_to_all x1, blocking collectives, body(): sums = lax.all_to_all(sums, 'space', 0, 0, tiled=True)  8.77 us
    ppermute x2, starting transfers between devices, relay(): far_b = lax.ppermute(right[1], 'tensor', ring('tensor', -1))  6.82 us
    ppermute x1, starting transfers between devices, body(): left = lax.ppermute(to_right, 'space', line('space', 1))  6.41 us
    ppermute x2, starting transfers between devices, gather(): right = lax.ppermute(own, 'tensor', ring('tensor', -1))  6.3 us
    ppermute x1, waiting for transfers between devices, body(): right = lax.ppermute(to_left, 'space', line('space', -1))  4.4 us
  transfers between devices with their start and end apart: 17, of which 12 were waited for; matrix products, arithmetic and copies ran while one was open for 0% of the time, Pallas kernels for 3%

profile of v2, /device:TPU:1, one launch (start us, length us, event | category | flops | bytes accessed | tf_op | source)
XLA Modules:
  0.0 95.8 jit_solution(9269362135581237167)
XLA Ops:
  0.6 1.0 %copy.24 = bf16[1,2,80,4,128]{4,2,3,1,0:T(8,128)(2,1)S(1)} copy(bf16[1,2,80,4,128]{4,3,2,1,0:T(4,128)(2,1)} %param.16) | data formatting | bytes 327680 | tf_op args[0]
  1.7 3.6 %collective-permute-start.6 = (bf16[2,4,80,128]{3,2,1,0:T(8,128)(2,1)S(1)}, bf16[2,4,80,128]{3,2,1,0:T(8,128)(2,1)S(1)}, u32[]{:S(2)}, u32[]{:S(2)}) collective-permute-start(bf16[2,4,80,128]{3,2,1,0:T(8,128)(2,1)S(1)} %bitcast.35), channel_id=1, source_target_pairs={{0,3},{1,0},{2,1},{3,2},{4,7},{5,4},{6,5},{7,6},{8,11},{9,8},{10,9... | collective-permute-start | bytes 491528 | tf_op jit(solution)/shard_map/ppermute | solution.py:515
  5.3 2.7 %collective-permute-start.2 = (bf16[2,4,80,128]{3,2,1,0:T(8,128)(2,1)S(1)}, bf16[2,4,80,128]{3,2,1,0:T(8,128)(2,1)S(1)}, u32[]{:S(2)}, u32[]{:S(2)}) collective-permute-start(bf16[2,4,80,128]{3,2,1,0:T(8,128)(2,1)S(1)} %bitcast.40), channel_id=1, source_target_pairs={{0,3},{1,0},{2,1},{3,2},{4,7},{5,4},{6,5},{7,6},{8,11},{9,8},{10,9... | collective-permute-start | bytes 491528 | tf_op jit(solution)/shard_map/ppermute | solution.py:515
  8.2 3.4 %collective-permute-start.7 = (bf16[4,80,128]{2,1,0:T(8,128)(2,1)S(1)}, bf16[4,80,128]{2,1,0:T(8,128)(2,1)S(1)}, u32[]{:S(2)}, u32[]{:S(2)}) collective-permute-start(bf16[4,80,128]{2,1,0:T(8,128)(2,1)S(1)} %slice_bitcast_fusion), channel_id=1, source_target_pairs={{0,3},{1,0},{2,1},{3,2},{4,7},{5,4},{6,5},{7,6},{8,11},{9,8},{10,9... | collective-permute-start | bytes 245768 | tf_op jit(solution)/shard_map/ppermute | solution.py:520
  12.0 3.4 %collective-permute-start.3 = (bf16[4,80,128]{2,1,0:T(8,128)(2,1)S(1)}, bf16[4,80,128]{2,1,0:T(8,128)(2,1)S(1)}, u32[]{:S(2)}, u32[]{:S(2)}) collective-permute-start(bf16[4,80,128]{2,1,0:T(8,128)(2,1)S(1)} %slice_bitcast_fusion.2), channel_id=1, source_target_pairs={{0,3},{1,0},{2,1},{3,2},{4,7},{5,4},{6,5},{7,6},{8,11},{9,8},{10,9... | collective-permute-start | bytes 245768 | tf_op jit(solution)/shard_map/ppermute | solution.py:520
  18.5 1.5 %collective-permute-done.1.f2a = bf16[4,80,128]{2,1,0:T(8,128)(2,1)S(1)} collective-permute-done((bf16[4,80,128]{2,1,0:T(8,128)(2,1)S(1)}, bf16[4,80,128]{2,1,0:T(8,128)(2,1)S(1)}, u32[]{:S(2)}, u32[]{:S(2)}) %collective-permute-start.1) | collective-permute-done | bytes 81952 | tf_op jit(solution)/shard_map/ppermute | solution.py:519
  20.0 1.7 %conv_p.1 = (f32[160,512]{1,0:T(8,128)S(1)}, f32[160,128]{1,0:T(8,128)S(1)}, f32[160,128]{1,0:T(8,128)S(1)}, bf16[960,128]{1,0:T(8,128)(2,1)S(1)}, bf16[960,128]...) custom-call(s32[7]{0:T(128)S(1)} %stack.31.place_ref.t_ref.edge_ref.x_ref, bf16[2,4,80,128]{3,2,1,0:T(8,128)(2,1)S(1)} %bitcast.42, ...), custom_call_target="tpu_custom_call" | custom-call | flops 471859200 | bytes 2836508 | tf_op jit(solution)/shard_map/conv_p/pallas_call | solution.py:33
  21.7 1.7 %conv_r.1 = (f32[160,512]{1,0:T(8,128)S(1)}, f32[160,128]{1,0:T(8,128)S(1)}, f32[160,128]{1,0:T(8,128)S(1)}, bf16[1632,128]{1,0:T(8,128)(2,1)S(1)}, bf16[1632,128]{1,0:T(8,128)(2,1)S(1)}) custom-call(s32[7]{0:T(128)S(1)} %stack.31.place_ref.t_ref.edge_ref.x_ref, bf16[2,4,80,128]{3,2,1,0:T(8,128)(2,1)S(1)} %bitcast.37, ...), custom_call_target="tpu_custom_call" | custom-call | flops 471859200 | bytes 3033116 | tf_op jit(solution)/shard_map/conv_r/pallas_call | solution.py:33
  23.4 6.4 %collective-permute-start.8 = (bf16[1632,128]{1,0:T(8,128)(2,1)S(1)}, bf16[1632,128]{1,0:T(8,128)(2,1)S(1)}, u32[]{:S(2)}, u32[]{:S(2)}) collective-permute-start(bf16[1632,128]{1,0:T(8,128)(2,1)S(1)} %get-tuple-element.52), channel_id=1, source_target_pairs={{0,4},{4,8},{8,12},{12,16},{16,20},{20,24},{24,28},{1,5},{5,9},{9,... | collective-permute-start | bytes 1253384 | tf_op jit(solution)/shard_map/ppermute | solution.py:565
  29.9 1.9 %collective-permute-start.9 = (bf16[1632,128]{1,0:T(8,128)(2,1)S(1)}, bf16[1632,128]{1,0:T(8,128)(2,1)S(1)}, u32[]{:S(2)}, u32[]{:S(2)}) collective-permute-start(bf16[1632,128]{1,0:T(8,128)(2,1)S(1)} %get-tuple-element.53), channel_id=1, source_target_pairs={{4,0},{8,4},{12,8},{16,12},{20,16},{24,20},{28,24},{5,1},{9,5},{13... | collective-permute-start | bytes 1253384 | tf_op jit(solution)/shard_map/ppermute | solution.py:566
  31.8 3.0 %collective-permute-done.8.left = bf16[1632,128]{1,0:T(8,128)(2,1)S(1)} collective-permute-done((bf16[1632,128]{1,0:T(8,128)(2,1)S(1)}, bf16[1632,128]{1,0:T(8,128)(2,1)S(1)}, u32[]{:S(2)}, u32[]{:S(2)}) %collective-permute-start.8) | collective-permute-done | bytes 417824 | tf_op jit(solution)/shard_map/ppermute | solution.py:565
  34.8 4.4 %collective-permute-done.9.right = bf16[1632,128]{1,0:T(8,128)(2,1)S(1)} collective-permute-done((bf16[1632,128]{1,0:T(8,128)(2,1)S(1)}, bf16[1632,128]{1,0:T(8,128)(2,1)S(1)}, u32[]{:S(2)}, u32[]{:S(2)}) %collective-permute-start.9) | collective-permute-done | bytes 417824 | tf_op jit(solution)/shard_map/ppermute | solution.py:566
  39.6 8.8 %all_to_all.15.sums_ref = f32[8,16,128]{2,1,0:T(8,128)S(1)} all-to-all(f32[8,16,128]{2,1,0:T(8,128)S(1)} %get-tuple-element.56), channel_id=1, replica_groups=mesh['dp'=8,'space'=8,'tensor'=4] {'space'}, dimensions={0} | all-to-all | bytes 131072 | tf_op jit(solution)/shard_map/all_to_all | solution.py:580
  48.3 1.5 %hidden.1 = (f32[12,8,128]{2,1,0:T(8,128)S(1)}, bf16[160,512]{1,0:T(8,128)(2,1)S(1)}, f32[160,128]{1,0:T(8,128)S(1)}) custom-call(s32[7]{0:T(128)S(1)} %stack.31.place_ref.t_ref.edge_ref.x_ref, f32[160,1280]{1,0:T(8,128)S(1)} %get-tuple-element.54.ext_p, f32[160,768]{1,0:T(8,128)S(1)} %get-tuple-element.55.ext_r, f32[8,16,128]{2,1,0:T(8,128)S(1)} %all_to_all.15.sums_ref, ...), custom_call_target="tpu_custom_call" | custom-call | flops 10000000 | bytes 1799196 | tf_op jit(solution)/shard_map/hidden/pallas_call | solution.py:33
  50.3 1.5 %collective-permute-start.11 = (f32[12,8,128]{2,1,0:T(8,128)S(1)}, f32[12,8,128]{2,1,0:T(8,128)S(1)}, u32[]{:S(2)}, u32[]{:S(2)}) collective-permute-start(f32[12,8,128]{2,1,0:T(8,128)S(1)} %get-tuple-element.58.p0), channel_id=1, source_target_pairs={{0,2},{1,3},{2,0},{3,1},{4,6},{5,7},{6,4},{7,5},{8,10},{9,11},{10,... | collective-permute-start | bytes 147464 | tf_op jit(solution)/shard_map/ppermute | solution.py:589
  52.9 1.9 %collective-permute-done.11.p2 = f32[12,8,128]{2,1,0:T(8,128)S(1)} collective-permute-done((f32[12,8,128]{2,1,0:T(8,128)S(1)}, f32[12,8,128]{2,1,0:T(8,128)S(1)}, u32[]{:S(2)}, u32[]{:S(2)}) %collective-permute-start.11) | collective-permute-done | bytes 49184 | tf_op jit(solution)/shard_map/ppermute | solution.py:589
  54.8 2.0 %collective-permute-done.10.p1 = f32[12,8,128]{2,1,0:T(8,128)S(1)} collective-permute-done((f32[12,8,128]{2,1,0:T(8,128)S(1)}, f32[12,8,128]{2,1,0:T(8,128)S(1)}, u32[]{:S(2)}, u32[]{:S(2)}) %collective-permute-start.10) | collective-permute-done | bytes 49184 | tf_op jit(solution)/shard_map/ppermute | solution.py:589
  56.7 1.2 %back.1 = (f32[160,768]{1,0:T(8,128)S(1)}, f32[48,128]{1,0:T(8,128)S(1)}, f32[8,24,128]{2,1,0:T(8,128)S(1)}) custom-call(s32[7]{0:T(128)S(1)} %stack.31.place_ref.t_ref.edge_ref.x_ref, f32[12,8,128]{2,1,0:T(8,128)S(1)} %get-tuple-element.58.p0, f32[12,8,128]{2,1,0:T(8,128)S(1)} %collective-permute-done.10.p1, f32[12,8,128]{2,1,0:T(8,128)S(1)} %collective-permute-done.11.p2, ...), custom_call_target="tpu_custom_call" | custom-call | flops 10000000 | bytes 2013724 | tf_op jit(solution)/shard_map/back/pallas_call | solution.py:33
  58.0 8.8 %all_to_all.16.red_ref = f32[8,24,128]{2,1,0:T(8,128)S(1)} all-to-all(f32[8,24,128]{2,1,0:T(8,128)S(1)} %get-tuple-element.64), channel_id=1, replica_groups=mesh['dp'=8,'space'=8,'tensor'=4] {'space'}, dimensions={0} | all-to-all | bytes 196608 | tf_op jit(solution)/shard_map/all_to_all | solution.py:598
  66.8 2.6 %weight.1 = (f32[1024,128]{1,0:T(8,128)S(1)}, bf16[1072,128]{1,0:T(8,128)(2,1)S(1)}, f32[48,128]{1,0:T(8,128)S(1)}, f32[1,1]{1,0:T(1,128)}) custom-call(s32[7]{0:T(128)S(1)} %stack.31.place_ref.t_ref.edge_ref.x_ref, f32[160,768]{1,0:T(8,128)S(1)} %get-tuple-element.63.gnorm_ref, f32[160,1280]{1,0:T(8,128)S(1)} %get-tuple-element.54.ext_p, ...), custom_call_target="tpu_custom_call" | custom-call | flops 471859200 | bytes 2994208 | tf_op jit(solution)/shard_map/weight/pallas_call | solution.py:33
  70.2 1.2 %collective-permute-done.13.got_ref = bf16[1072,128]{1,0:T(8,128)(2,1)S(1)} collective-permute-done((bf16[1072,128]{1,0:T(8,128)(2,1)S(1)}, bf16[1072,128]{1,0:T(8,128)(2,1)S(1)}, u32[]{:S(2)}, u32[]{:S(2)}) %collective-permute-start.13) | collective-permute-done | bytes 274464 | tf_op jit(solution)/shard_map/ppermute | solution.py:608
  72.3 1.8 %collective-permute-start.15 = (bf16[304,128]{1,0:T(8,128)(2,1)S(1)}, bf16[304,128]{1,0:T(8,128)(2,1)S(1)}, u32[]{:S(2)}, u32[]{:S(2)}) collective-permute-start(bf16[304,128]{1,0:T(8,128)(2,1)S(1)} %get-tuple-element.73), channel_id=1, source_target_pairs={{0,16},{4,20},{8,24},{12,28},{16,0},{20,4},{24,8},{28,12},{1,17},{... | collective-permute-start | bytes 233480 | tf_op jit(solution)/shard_map/ppermute | solution.py:618
  74.8 2.5 %collective-permute-done.14.r1 = bf16[304,128]{1,0:T(8,128)(2,1)S(1)} collective-permute-done((bf16[304,128]{1,0:T(8,128)(2,1)S(1)}, bf16[304,128]{1,0:T(8,128)(2,1)S(1)}, u32[]{:S(2)}, u32[]{:S(2)}) %collective-permute-start.14) | collective-permute-done | bytes 77856 | tf_op jit(solution)/shard_map/ppermute | solution.py:618
  78.8 16.3 %all_to_all.17.got_ref = bf16[8,80,128]{2,1,0:T(8,128)(2,1)S(1)} all-to-all(bf16[8,80,128]{2,1,0:T(8,128)(2,1)S(1)} %cross.1), channel_id=1, replica_groups=mesh['dp'=8,'space'=8,'tensor'=4] {'dp'}, dimensions={0} | all-to-all | bytes 327680 | tf_op jit(solution)/shard_map/all_to_all | solution.py:621
  (56 shorter events, 8.9 us)
Async XLA Ops:
  0.6 1.0 %copy-start.12 = (bf16[1,2,80,4,128]{4,3,2,1,0:T(4,128)(2,1)S(1)}, bf16[1,2,80,4,128]{4,3,2,1,0:T(4,128)(2,1)}, u32[]{:S(2)}) copy-start(bf16[1,2,80,4,128]{4,3,2,1,0:T(4,128)(2,1)} %param.17) | copy-start | bytes 491524
  1.6 18.4 %copy-start.11 = (bf16[9,80,320]{2,1,0:T(8,128)(2,1)S(1)}, bf16[9,80,320]{2,1,0:T(8,128)(2,1)}, u32[]{:S(2)}) copy-start(bf16[9,80,320]{2,1,0:T(8,128)(2,1)} %param.19) | copy-start | bytes 1382404
  1.7 15.4 %copy-start.1 = (f32[1000,80]{0,1:T(8,128)S(1)}, f32[1000,80]{0,1:T(8,128)}, u32[]{:S(2)}) copy-start(f32[1000,80]{0,1:T(8,128)} %param.29) | copy-start | bytes 960004
  1.7 6.5 %collective-permute-start.6 = (bf16[2,4,80,128]{3,2,1,0:T(8,128)(2,1)S(1)}, bf16[2,4,80,128]{3,2,1,0:T(8,128)(2,1)S(1)}, u32[]{:S(2)}, u32[]{:S(2)}) collective-permute-start(bf16[2,4,80,128]{3,2,1,0:T(8,128)(2,1)S(1)} %bitcast.35), channel_id=1, source_target_pairs={{0,3},{1,0},{2,1},{3,2},{4,7},{5,4},{6,5},{7,6},{8,11},{9,8},{10,9... | collective-permute-start | bytes 491528 | tf_op jit(solution)/shard_map/ppermute | solution.py:515
  5.3 10.2 %collective-permute-start.4 = (bf16[2,4,80,128]{3,2,1,0:T(8,128)(2,1)S(1)}, bf16[2,4,80,128]{3,2,1,0:T(8,128)(2,1)S(1)}, u32[]{:S(2)}, u32[]{:S(2)}) collective-permute-start(bf16[2,4,80,128]{3,2,1,0:T(8,128)(2,1)S(1)} %bitcast.36), channel_id=1, source_target_pairs={{0,1},{1,2},{2,3},{3,0},{4,5},{5,6},{6,7},{7,4},{8,9},{9,10},{10,1... | collective-permute-start | bytes 491528 | tf_op jit(solution)/shard_map/ppermute | solution.py:514
  5.3 6.7 %collective-permute-start.2 = (bf16[2,4,80,128]{3,2,1,0:T(8,128)(2,1)S(1)}, bf16[2,4,80,128]{3,2,1,0:T(8,128)(2,1)S(1)}, u32[]{:S(2)}, u32[]{:S(2)}) collective-permute-start(bf16[2,4,80,128]{3,2,1,0:T(8,128)(2,1)S(1)} %bitcast.40), channel_id=1, source_target_pairs={{0,3},{1,0},{2,1},{3,2},{4,7},{5,4},{6,5},{7,6},{8,11},{9,8},{10,9... | collective-permute-start | bytes 491528 | tf_op jit(solution)/shard_map/ppermute | solution.py:515
  8.0 7.4 %collective-permute-start = (bf16[2,4,80,128]{3,2,1,0:T(8,128)(2,1)S(1)}, bf16[2,4,80,128]{3,2,1,0:T(8,128)(2,1)S(1)}, u32[]{:S(2)}, u32[]{:S(2)}) collective-permute-start(bf16[2,4,80,128]{3,2,1,0:T(8,128)(2,1)S(1)} %bitcast.41), channel_id=1, source_target_pairs={{0,1},{1,2},{2,3},{3,0},{4,5},{5,6},{6,7},{7,4},{8,9},{9,10},{10,1... | collective-permute-start | bytes 491528 | tf_op jit(solution)/shard_map/ppermute | solution.py:514
  8.2 13.5 %collective-permute-start.7 = (bf16[4,80,128]{2,1,0:T(8,128)(2,1)S(1)}, bf16[4,80,128]{2,1,0:T(8,128)(2,1)S(1)}, u32[]{:S(2)}, u32[]{:S(2)}) collective-permute-start(bf16[4,80,128]{2,1,0:T(8,128)(2,1)S(1)} %slice_bitcast_fusion), channel_id=1, source_target_pairs={{0,3},{1,0},{2,1},{3,2},{4,7},{5,4},{6,5},{7,6},{8,11},{9,8},{10,9... | collective-permute-start | bytes 245768 | tf_op jit(solution)/shard_map/ppermute | solution.py:520
  12.0 6.5 %collective-permute-start.3 = (bf16[4,80,128]{2,1,0:T(8,128)(2,1)S(1)}, bf16[4,80,128]{2,1,0:T(8,128)(2,1)S(1)}, u32[]{:S(2)}, u32[]{:S(2)}) collective-permute-start(bf16[4,80,128]{2,1,0:T(8,128)(2,1)S(1)} %slice_bitcast_fusion.2), channel_id=1, source_target_pairs={{0,3},{1,0},{2,1},{3,2},{4,7},{5,4},{6,5},{7,6},{8,11},{9,8},{10,9... | collective-permute-start | bytes 245768 | tf_op jit(solution)/shard_map/ppermute | solution.py:520
  15.4 4.6 %collective-permute-start.1 = (bf16[4,80,128]{2,1,0:T(8,128)(2,1)S(1)}, bf16[4,80,128]{2,1,0:T(8,128)(2,1)S(1)}, u32[]{:S(2)}, u32[]{:S(2)}) collective-permute-start(bf16[4,80,128]{2,1,0:T(8,128)(2,1)S(1)} %slice_bitcast_fusion.3), channel_id=1, source_target_pairs={{0,1},{1,2},{2,3},{3,0},{4,5},{5,6},{6,7},{7,4},{8,9},{9,10},{10,1... | collective-permute-start | bytes 245768 | tf_op jit(solution)/shard_map/ppermute | solution.py:519
  15.5 6.2 %collective-permute-start.5 = (bf16[4,80,128]{2,1,0:T(8,128)(2,1)S(1)}, bf16[4,80,128]{2,1,0:T(8,128)(2,1)S(1)}, u32[]{:S(2)}, u32[]{:S(2)}) collective-permute-start(bf16[4,80,128]{2,1,0:T(8,128)(2,1)S(1)} %slice_bitcast_fusion.1), channel_id=1, source_target_pairs={{0,1},{1,2},{2,3},{3,0},{4,5},{5,6},{6,7},{7,4},{8,9},{9,10},{10,1... | collective-permute-start | bytes 245768 | tf_op jit(solution)/shard_map/ppermute | solution.py:519
  15.6 1.5 %copy-start.4 = (bf16[9,4,80]{2,1,0:T(4,128)(2,1)S(1)}, bf16[9,4,80]{2,1,0:T(4,128)(2,1)}, u32[]{:S(2)}) copy-start(bf16[9,4,80]{2,1,0:T(4,128)(2,1)} %w2_r.1) | copy-start | bytes 17284
  15.6 1.5 %copy-start.2 = (f32[1,2,4,4,128]{4,3,2,1,0:T(4,128)S(1)}, f32[1,2,4,4,128]{4,3,2,1,0:T(4,128)}, u32[]{:S(2)}) copy-start(f32[1,2,4,4,128]{4,3,2,1,0:T(4,128)} %param.18) | copy-start | bytes 49156
  17.0 0.7 copy-start.3
  20.0 1.7 %copy-start = (bf16[9,80,320]{2,1,0:T(8,128)(2,1)S(1)}, bf16[9,80,320]{2,1,0:T(8,128)(2,1)}, u32[]{:S(2)}) copy-start(bf16[9,80,320]{2,1,0:T(8,128)(2,1)} %param.20) | copy-start | bytes 1382404
  23.4 11.4 %collective-permute-start.8 = (bf16[1632,128]{1,0:T(8,128)(2,1)S(1)}, bf16[1632,128]{1,0:T(8,128)(2,1)S(1)}, u32[]{:S(2)}, u32[]{:S(2)}) collective-permute-start(bf16[1632,128]{1,0:T(8,128)(2,1)S(1)} %get-tuple-element.52), channel_id=1, source_target_pairs={{0,4},{4,8},{8,12},{12,16},{16,20},{20,24},{24,28},{1,5},{5,9},{9,... | collective-permute-start | bytes 1253384 | tf_op jit(solution)/shard_map/ppermute | solution.py:565
  29.9 9.4 %collective-permute-start.9 = (bf16[1632,128]{1,0:T(8,128)(2,1)S(1)}, bf16[1632,128]{1,0:T(8,128)(2,1)S(1)}, u32[]{:S(2)}, u32[]{:S(2)}) collective-permute-start(bf16[1632,128]{1,0:T(8,128)(2,1)S(1)} %get-tuple-element.53), channel_id=1, source_target_pairs={{4,0},{8,4},{12,8},{16,12},{20,16},{24,20},{28,24},{5,1},{9,5},{13... | collective-permute-start | bytes 1253384 | tf_op jit(solution)/shard_map/ppermute | solution.py:566
  49.9 3.0 %collective-permute-start.12 = (f32[12,8,128]{2,1,0:T(8,128)S(1)}, f32[12,8,128]{2,1,0:T(8,128)S(1)}, u32[]{:S(2)}, u32[]{:S(2)}) collective-permute-start(f32[12,8,128]{2,1,0:T(8,128)S(1)} %get-tuple-element.58.p0), channel_id=1, source_target_pairs={{0,3},{1,0},{2,1},{3,2},{4,7},{5,4},{6,5},{7,6},{8,11},{9,8},{10,9... | collective-permute-start | bytes 147464 | tf_op jit(solution)/shard_map/ppermute | solution.py:589
  50.3 4.4 %collective-permute-start.11 = (f32[12,8,128]{2,1,0:T(8,128)S(1)}, f32[12,8,128]{2,1,0:T(8,128)S(1)}, u32[]{:S(2)}, u32[]{:S(2)}) collective-permute-start(f32[12,8,128]{2,1,0:T(8,128)S(1)} %get-tuple-element.58.p0), channel_id=1, source_target_pairs={{0,2},{1,3},{2,0},{3,1},{4,6},{5,7},{6,4},{7,5},{8,10},{9,11},{10,... | collective-permute-start | bytes 147464 | tf_op jit(solution)/shard_map/ppermute | solution.py:589
  51.9 4.9 %collective-permute-start.10 = (f32[12,8,128]{2,1,0:T(8,128)S(1)}, f32[12,8,128]{2,1,0:T(8,128)S(1)}, u32[]{:S(2)}, u32[]{:S(2)}) collective-permute-start(f32[12,8,128]{2,1,0:T(8,128)S(1)} %get-tuple-element.58.p0), channel_id=1, source_target_pairs={{0,1},{1,2},{2,3},{3,0},{4,5},{5,6},{6,7},{7,4},{8,9},{9,10},{10,1... | collective-permute-start | bytes 147464 | tf_op jit(solution)/shard_map/ppermute | solution.py:589
  69.4 2.0 %collective-permute-start.13 = (bf16[1072,128]{1,0:T(8,128)(2,1)S(1)}, bf16[1072,128]{1,0:T(8,128)(2,1)S(1)}, u32[]{:S(2)}, u32[]{:S(2)}) collective-permute-start(bf16[1072,128]{1,0:T(8,128)(2,1)S(1)} %get-tuple-element.70), channel_id=1, source_target_pairs={{0,4},{4,0},{8,12},{12,8},{16,20},{20,16},{24,28},{28,24},{1,5},{5... | collective-permute-start | bytes 823304 | tf_op jit(solution)/shard_map/ppermute | solution.py:608
  72.0 5.3 %collective-permute-start.14 = (bf16[304,128]{1,0:T(8,128)(2,1)S(1)}, bf16[304,128]{1,0:T(8,128)(2,1)S(1)}, u32[]{:S(2)}, u32[]{:S(2)}) collective-permute-start(bf16[304,128]{1,0:T(8,128)(2,1)S(1)} %get-tuple-element.72), channel_id=1, source_target_pairs={{0,8},{4,12},{8,16},{12,20},{16,24},{20,28},{24,0},{28,4},{1,9},{5... | collective-permute-start | bytes 233480 | tf_op jit(solution)/shard_map/ppermute | solution.py:618
  72.3 5.7 %collective-permute-start.15 = (bf16[304,128]{1,0:T(8,128)(2,1)S(1)}, bf16[304,128]{1,0:T(8,128)(2,1)S(1)}, u32[]{:S(2)}, u32[]{:S(2)}) collective-permute-start(bf16[304,128]{1,0:T(8,128)(2,1)S(1)} %get-tuple-element.73), channel_id=1, source_target_pairs={{0,16},{4,20},{8,24},{12,28},{16,0},{20,4},{24,8},{28,12},{1,17},{... | collective-permute-start | bytes 233480 | tf_op jit(solution)/shard_map/ppermute | solution.py:618
  74.1 4.7 %collective-permute-start.16 = (bf16[304,128]{1,0:T(8,128)(2,1)S(1)}, bf16[304,128]{1,0:T(8,128)(2,1)S(1)}, u32[]{:S(2)}, u32[]{:S(2)}) collective-permute-start(bf16[304,128]{1,0:T(8,128)(2,1)S(1)} %get-tuple-element.74), channel_id=1, source_target_pairs={{0,24},{4,28},{8,0},{12,4},{16,8},{20,12},{24,16},{28,20},{1,25},{... | collective-permute-start | bytes 233480 | tf_op jit(solution)/shard_map/ppermute | solution.py:618
  (6 other events, 4.1 us)

commit v3 on v2

--- a/solution.py
+++ b/solution.py
@@ -146,11 +146,11 @@
                 rows_ref[r, slot : slot + 1, :] = noise_ref[im, o, r : r + 1, :]
 
 
-def conv_kernel(last, t_ref, f0, f1, f2a, f2b, f3, w_ref, col_ref, *refs):
+def conv_kernel(last, t_ref, f0, f1, f2, f3, w_ref, col_ref, *refs):
     if last:
-        side_l, side_r, noise_ref, pre_ref, up_ref, dn_ref, send_l, send_r, fs_ref = refs
+        side_a, side_b, noise_ref, pre_ref, up_ref, dn_ref, send_a, send_b, fs_ref = refs
     else:
-        pre_ref, up_ref, dn_ref, send_l, send_r, fs_ref = refs
+        pre_ref, up_ref, dn_ref, send_a, send_b, fs_ref = refs
     t = t_ref[5]
     bias = 5 if last else 4
     for k in range(4):
@@ -158,27 +158,28 @@
         for im in range(2):
             for r in range(ROWS):
                 lo = im * PIX + r * COLS
-                if k == 2:
-                    piece = f2a[r] if im == 0 else f2b[r]
-                else:
-                    piece = (f0, f1, None, f3)[k][im, r]
-                fs_ref[pl.ds(base, CH), lo : lo + COLS] = piece
+                fs_ref[pl.ds(base, CH), lo : lo + COLS] = (f0, f1, f2, f3)[k][im, r]
+    odd = t_ref[3] > 0
     if last:
-        send_l[0:960, :] = side_l[...]
-        send_r[0:960, :] = side_r[...]
-        for ref, rows in ((send_l, (0, 1)), (send_r, (2, 3))):
-            for index, r in enumerate(rows):
-                value = noise_ref[r]
+        send_a[0:960, :] = side_a[...]
+        send_b[0:960, :] = side_b[...]
+        for index in range(2):
+            first, second = noise_ref[index], noise_ref[2 + index]
+            for ref, value in (
+                (send_a, jnp.where(odd, first, second)),
+                (send_b, jnp.where(odd, second, first)),
+            ):
                 high = value.astype(BF16).astype(F32)
                 both = jnp.concatenate([high, value - high], axis=0).astype(BF16)
                 ref[1600 + 16 * index : 1616 + 16 * index, :] = both
-        start, keep_l, keep_r = 960, (-1, 0), (ROWS - 1, ROWS)
+        start, count = 960, 2
     else:
-        start, keep_l, keep_r = 0, (-1, 0, 1, 2), (1, 2, 3, 4)
+        start, count = 0, 4
     for im in range(2):
         feats = fs_ref[:, im * PIX : (im + 1) * PIX]
         taps = [dot(w_ref[ky * 3 * CH : (ky + 1) * 3 * CH, :], feats) for ky in range(3)]
         chans = slice(im * CH, (im + 1) * CH)
+        outs = []
         for r in range(-1, ROWS + 1):
             total = None
             for ky in range(3):
@@ -198,23 +199,45 @@
             else:
                 out = out + col_ref[chans, bias : bias + 1]
                 pre_ref[chans, r * COLS : (r + 1) * COLS] = out
-            for keep, ref in ((keep_l, send_l), (keep_r, send_r)):
-                if r in keep:
-                    lo = start + keep.index(r) * 2 * CH + im * CH
-                    high = out.astype(BF16)
-                    ref[lo : lo + CH, :] = high
-                    if r in (-1, 0, ROWS - 1, ROWS):
-                        near = 0 if r < 1 else 2 - len(keep)
-                        slot = keep.index(r) + near + len(keep)
-                        lo = start + slot * 2 * CH + im * CH
-                        ref[lo : lo + CH, :] = (out - high.astype(F32)).astype(BF16)
+            outs.append(out)
+        for index in range(count):
+            upper, lower = outs[index], outs[ROWS + 2 - count + index]
+            for ref, value in (
+                (send_a, jnp.where(odd, upper, lower)),
+                (send_b, jnp.where(odd, lower, upper)),
+            ):
+                high = value.astype(BF16)
+                lo = start + index * 2 * CH + im * CH
+                ref[lo : lo + CH, :] = high
+                ref_low = start + (count + index) * 2 * CH + im * CH
+                if count == 2:
+                    ref[ref_low : ref_low + CH, :] = (value - high.astype(F32)).astype(BF16)
+        if count == 4:
+            for index in range(2):
+                upper, lower = outs[index], outs[ROWS + index]
+                for ref, value in (
+                    (send_a, jnp.where(odd, upper, lower)),
+                    (send_b, jnp.where(odd, lower, upper)),
+                ):
+                    rest = value - value.astype(BF16).astype(F32)
+                    lo = start + (count + index) * 2 * CH + im * CH
+                    ref[lo : lo + CH, :] = rest.astype(BF16)
 
 
 def stat_kernel(
-    pre_p, up_p, dn_p, pre_r, up_r, dn_r, left, right, noise_ref, ext_p, ext_r, noise_ext, out_ref
+    place_ref, pre_p, up_p, dn_p, pre_r, up_r, dn_r, got_a, got_b, noise_ref,
+    ext_p, ext_r, noise_ext, out_ref
 ):
-    def got(ref, index):
-        return ref[index * 2 * CH : (index + 1) * 2 * CH, :].astype(F32)
+    odd = place_ref[3] > 0
+    top = place_ref[1] > 0
+    bottom = place_ref[2] > 0
+    left, right = (got_a, got_b), (got_b, got_a)
+
+    def rows_at(side, lo, hi):
+        return jnp.where(odd, side[0][lo:hi, :].astype(F32), side[1][lo:hi, :].astype(F32))
+
+    def got(side, index):
+        return rows_at(side, index * 2 * CH, (index + 1) * 2 * CH)
 
     def near(ref, index, low):
         return got(ref, index) + got(ref, low)
@@ -226,8 +249,8 @@
     ):
         low = first + halo + 1
         rows = [pre[:, r * COLS : (r + 1) * COLS] for r in range(ROWS)]
-        rows[0] = rows[0] + near(left, first + halo, low + 1)
-        rows[ROWS - 1] = rows[ROWS - 1] + near(right, first, low)
+        rows[0] = rows[0] + jnp.where(top, 0.0, near(left, first + halo, low + 1))
+        rows[ROWS - 1] = rows[ROWS - 1] + jnp.where(bottom, 0.0, near(right, first, low))
         total = rows[0] + rows[1] + rows[2] + rows[3]
         square = (
             rows[0] * rows[0] + rows[1] * rows[1] + rows[2] * rows[2] + rows[3] * rows[3]
@@ -242,9 +265,9 @@
         columns.append(jnp.sum(square, axis=1, keepdims=True))
     for index in range(2):
         lo = 1600 + 16 * index
-        pair = left[lo : lo + 16, :].astype(F32)
+        pair = rows_at(left, lo, lo + 16)
         noise_ext[index] = pair[0:8] + pair[8:16]
-        pair = right[lo : lo + 16, :].astype(F32)
+        pair = rows_at(right, lo, lo + 16)
         noise_ext[ROWS + 2 + index] = pair[0:8] + pair[8:16]
     for r in range(ROWS):
         noise_ext[2 + r] = noise_ref[r]
@@ -359,7 +382,12 @@
     head_ref[...] = jnp.zeros(head_ref.shape, F32)
     for tap in range(9):
         head = grads[0][8 * tap : 8 * tap + 4] + grads[1][8 * tap + 4 : 8 * tap + 8]
-        head_ref[4 * tap : 4 * tap + 4, 0:CH] = head
+        if tap < 6:
+            head_ref[4 * tap : 4 * tap + 4, 0:CH] = head
+        else:
+            lo = 4 * tap - 24
+            head_ref[lo : lo + 4, CH:COLS] = head[:, 0 : COLS - CH]
+            head_ref[lo + 12 : lo + 16, CH : 3 * CH - COLS] = head[:, COLS - CH : CH]
     for peer in range(out_ref.shape[0]):
         out_ref[peer, 0:16, :] = sums
         out_ref[peer, 16:24, :] = error
@@ -407,35 +435,30 @@
         grad_ref[2 * ky] = grad[:, 0:COLS]
         grad_ref[2 * ky + 1] = grad[:, COLS : 2 * COLS]
     chunk = 5
-    peers = C // chunk
-    for ii in range(chunk):
-        for half in range(6):
-            pack_ref[pl.ds(half * chunk + ii, peers, stride=32), :] = grad_ref[
-                half, pl.ds(ii, peers, stride=chunk), :
-            ]
     core = place_ref[3]
-    used = lax.broadcasted_iota(jnp.int32, (32, COLS), 0) < 6 * chunk
-    for x in range(4):
-        for d in range(8):
-            lo = (x * 8 + d) * 32
-            mine = pl.multiple_of((d * 8 + 2 * x + core) * 32, 32)
-            keep_ref[lo : lo + 32, :] = jnp.where(used, pack_ref[pl.ds(mine, 32), :], 0.0)
-            his = pl.multiple_of((d * 8 + 2 * x + 1 - core) * 32, 32)
-            tile = jnp.where(used, pack_ref[pl.ds(his, 32), :], 0.0)
-            send_ref[lo : lo + 32, :] = tile.astype(BF16)
+    for ref, who in ((keep_ref, core), (pack_ref, 1 - core)):
+        for x in range(4):
+            for ii in range(chunk):
+                for half in range(6):
+                    ref[pl.ds(x * 256 + half * chunk + ii, 8, stride=32), :] = grad_ref[
+                        half, pl.ds(who * chunk + 2 * chunk * x + ii, 8, stride=8 * chunk), :
+                    ]
+            for spare in (30, 31):
+                ref[pl.ds(x * 256 + spare, 8, stride=32), :] = jnp.zeros((8, COLS), F32)
+    send_ref[0:1024, :] = pack_ref[...].astype(BF16)
     head = head_ref[...] * scale
     both_ref[...] = head
-    send_ref[1024:1072, :] = head.astype(BF16)
+    send_ref[1024:1056, :] = head.astype(BF16)
 
 
 def core_kernel(x_ref, keep_ref, both_ref, got_ref, own_ref, s1, s2, s3):
     x = x_ref[4]
-    head = both_ref[...] + got_ref[1024:1072, :].astype(F32)
+    head = both_ref[...] + got_ref[1024:1056, :].astype(F32)
     for k, ref in enumerate((own_ref, s1, s2, s3)):
         lo = pl.multiple_of(lax.rem(x + k, 4) * 256, 256)
         block = keep_ref[pl.ds(lo, 256), :] + got_ref[pl.ds(lo, 256), :].astype(F32)
         ref[0:256, :] = block.astype(ref.dtype)
-        ref[256:304, :] = head.astype(ref.dtype)
+        ref[256:288, :] = head.astype(ref.dtype)
 
 
 def cross_kernel(own_ref, r1, r2, r3, out_ref):
@@ -444,10 +467,10 @@
             r2[lo:hi, :].astype(F32) + r3[lo:hi, :].astype(F32)
         )
 
-    head = total(256, 304).astype(BF16)
+    head = total(256, 288).astype(BF16)
     for d in range(8):
         out_ref[d, 0:32, :] = total(32 * d, 32 * d + 32).astype(BF16)
-        out_ref[d, 32:80, :] = head
+        out_ref[d, 32:56, :] = head[0:24]
 
 
 def sum_kernel(got_ref, one_ref, two_ref):
@@ -455,8 +478,13 @@
     for d in range(1, got_ref.shape[0]):
         total = total + got_ref[d].astype(F32)
     chunk = 5
-    for tap in range(9):
+    for tap in range(6):
         two_ref[tap] = total[32 + 4 * tap : 36 + 4 * tap, 0:CH]
+    for tap in range(6, 9):
+        lo = 8 + 4 * tap
+        two_ref[tap] = jnp.concatenate(
+            [total[lo : lo + 4, CH:COLS], total[lo + 12 : lo + 16, CH : 3 * CH - COLS]], axis=1
+        )
     for ky in range(3):
         lo = 2 * ky * chunk
         wide = jnp.concatenate(
@@ -469,11 +497,6 @@
 def ring(axis, step):
     count = lax.axis_size(axis)
     return [(i, (i + step) % count) for i in range(count)]
-
-
-def line(axis, step):
-    count = lax.axis_size(axis)
-    return [(i, i + step) for i in range(count) if 0 <= i + step < count]
 
 
 def body(
@@ -511,20 +534,13 @@
     )
 
     def gather(own):
-        left = lax.ppermute(own, "tensor", ring("tensor", 1))
-        right = lax.ppermute(own, "tensor", ring("tensor", -1))
-        return own, left, right
-
-    def relay(own, left, right):
-        far_a = lax.ppermute(left[0], "tensor", ring("tensor", 1))
-        far_b = lax.ppermute(right[1], "tensor", ring("tensor", -1))
-        return own, left, far_a, far_b, right
+        return [own] + [lax.ppermute(own, "tensor", ring("tensor", k)) for k in (1, 2, 3)]
 
     own_p = feat_policy[0].transpose(0, 2, 1, 3)
     feat_ref, own_p = lax.optimization_barrier((feat_ref, own_p))
     own_r = feat_ref[0].transpose(0, 2, 1, 3)
-    parts_p = relay(*gather(own_p))
-    parts_r = relay(*gather(own_r))
+    parts_p = gather(own_p)
+    parts_r = gather(own_r)
 
     vectors = [b1_policy, b1_ref, gn_gain_policy, gn_bias_policy, gn_gain_ref, gn_bias_ref]
     columns, lift, drop, noise_rows = call(
@@ -545,7 +561,7 @@
     wide = arr((2 * CH, PIX), F32)
     thin = arr((2 * CH, COLS), F32)
 
-    pre_p, up_p, dn_p, side_l, side_r, feats = call(
+    pre_p, up_p, dn_p, side_a, side_b, feats = call(
         functools.partial(conv_kernel, False),
         [place, *parts_p, w1_policy.reshape(9 * CH, C), columns],
         [wide, thin, thin, arr((960, COLS), BF16), arr((960, COLS), BF16), arr((C, 2 * PIX), BF16)],
@@ -553,21 +569,23 @@
         conv_flops,
         smem=1,
     )
-    pre_r, up_r, dn_r, to_left, to_right = call(
+    pre_r, up_r, dn_r, to_a, to_b = call(
         functools.partial(conv_kernel, True),
-        [place, *parts_r, w1_ref.reshape(9 * CH, C), columns, side_l, side_r, noise_rows],
+        [place, *parts_r, w1_ref.reshape(9 * CH, C), columns, side_a, side_b, noise_rows],
         [wide, thin, thin, arr((1632, COLS), BF16), arr((1632, COLS), BF16)],
         "conv_r",
         conv_flops,
         smem=1,
         scratch=[pltpu.VMEM((C, 2 * PIX), BF16)],
     )
-    left = lax.ppermute(to_right, "space", line("space", 1))
-    right = lax.ppermute(to_left, "space", line("space", -1))
+    partner = [(i, i ^ 1) for i in range(space)]
+    across = [(i, (i + 1 if i % 2 else i - 1) % space) for i in range(space)]
+    got_b = lax.ppermute(to_b, "space", across)
+    got_a = lax.ppermute(to_a, "space", partner)
 
     ext_p, ext_r, noise_ext, sums = call(
         stat_kernel,
-        [pre_p, up_p, dn_p, pre_r, up_r, dn_r, left, right, noise_rows],
+        [place, pre_p, up_p, dn_p, pre_r, up_r, dn_r, got_a, got_b, noise_rows],
         [
             arr((2 * CH, 10 * COLS), F32),
             arr((2 * CH, 6 * COLS), F32),
@@ -576,6 +594,7 @@
         ],
         "stats",
         10**6,
+        smem=1,
     )
     sums = lax.all_to_all(sums, "space", 0, 0, tiled=True)
     part, hidden, stat = call(
@@ -590,7 +609,7 @@
     gnorm, head, partial = call(
         back_kernel,
         [place, part, *others, noise_ext, ext_p, stat, columns, hidden, drop],
-        [arr((2 * CH, 6 * COLS), F32), arr((48, COLS), F32), arr((space, 24, COLS), F32)],
+        [arr((2 * CH, 6 * COLS), F32), arr((32, COLS), F32), arr((space, 24, COLS), F32)],
         "back",
         10**7,
         smem=1,
@@ -599,17 +618,17 @@
     keep, send, both, logits = call(
         weight_kernel,
         [place, gnorm, ext_p, stat, partial, feats, head],
-        [arr((1024, COLS), F32), arr((1072, COLS), BF16), arr((48, COLS), F32), arr((1, 1), F32)],
+        [arr((1024, COLS), F32), arr((1056, COLS), BF16), arr((32, COLS), F32), arr((1, 1), F32)],
         "weight",
         conv_flops,
         smem=1,
-        scratch=[pltpu.VMEM((6, C, COLS), F32), pltpu.VMEM((64 * 32, COLS), F32)],
-    )
-    got = lax.ppermute(send, "space", [(i, i ^ 1) for i in range(space)])
+        scratch=[pltpu.VMEM((6, C, COLS), F32), pltpu.VMEM((1024, COLS), F32)],
+    )
+    got = lax.ppermute(send, "space", partner)
     own, s1, s2, s3 = call(
         core_kernel,
         [place, keep, both, got],
-        [arr((304, COLS), F32)] + [arr((304, COLS), BF16)] * 3,
+        [arr((288, COLS), F32)] + [arr((288, COLS), BF16)] * 3,
         "core",
         10**6,
         smem=1,
@@ -617,7 +636,7 @@
     back = [
         lax.ppermute(sent, "space", ring("space", 2 * k)) for k, sent in ((1, s1), (2, s2), (3, s3))
     ]
-    (packed,) = call(cross_kernel, [own, *back], [arr((8, 80, COLS), BF16)], "cross", 10**6)
+    (packed,) = call(cross_kernel, [own, *back], [arr((8, 56, COLS), BF16)], "cross", 10**6)
     packed = lax.all_to_all(packed, "dp", 0, 0, tiled=True)
     grad_one, grad_two = call(
         sum_kernel, [packed], [arr((9, 5, CH), F32), arr((9, 4, CH), F32)], "total", 10**6

time: 97.5 us -> 92.4 us (0.948)
  starting transfers between devices: 28 us -> 15.5 us
  waiting for transfers between devices: 18.7 us -> 22.9 us
  blocking collectives: 33.9 us -> 35.2 us
  Pallas kernels: 11.2 us -> 12.3 us
  local copies, waits for them, and re-layouts: 1.81 us -> 2.85 us
    ppermute x11 -> x9, starting transfers between devices: 22.5 us -> 10.7 us  [the longest x6 8.15 us: gather(): lax.ppermute(own, 'tensor', ring('tensor', k))]
    ppermute x11 -> x9, waiting for transfers between devices: 10.6 us -> 15.7 us  [the longest x6 7.92 us: gather(): lax.ppermute(own, 'tensor', ring('tensor', k))]
    pallas_call x10, Pallas kernels: 11.2 us -> 12.3 us  [call(): pl.pallas_call(kernel, out_shape=outs, in_specs=[SM] * smem + [VM] * (len...]
    unnamed x27, local copies, waits for them, and re-layouts: 1.68 us -> 2.74 us
  transfers between devices with their start and end apart: 17 -> 15, of which waited for: 12 -> 12; matrix products, arithmetic and copies ran while one was open for 0% -> 0% of each run, Pallas kernels for 3% -> 3%
where the time goes in v3:
time: 92.4 us; the launch traced here: 90.8 us
  blocking collectives  35.2 us (38%)
  waiting for transfers between devices  22.9 us (25%)
  starting transfers between devices  15.5 us (17%)
  Pallas kernels  12.3 us (13%)
  local copies, waits for them, and re-layouts  2.85 us (3%)
  between operations  2.12 us (2%)
    all_to_all x1, blocking collectives, body(): packed = lax.all_to_all(packed, 'dp', 0, 0, tiled=True)  15.7 us
    pallas_call x10, Pallas kernels, call(): pl.pallas_call(kernel, out_shape=outs, in_specs=[SM] * smem + [VM] * (len...  12.3 us
    all_to_all x1, blocking collectives, body(): sums = lax.all_to_all(sums, 'space', 0, 0, tiled=True)  9.71 us
    all_to_all x1, blocking collectives, body(): partial = lax.all_to_all(partial, 'space', 0, 0, tiled=True)  9.7 us
    ppermute x6, starting transfers between devices, gather(): lax.ppermute(own, 'tensor', ring('tensor', k))  8.15 us
    ppermute x6, waiting for transfers between devices, gather(): lax.ppermute(own, 'tensor', ring('tensor', k))  7.92 us
    ppermute x1, waiting for transfers between devices, body(): got_b = lax.ppermute(to_b, 'space', across)  6.37 us
    ppermute x3, waiting for transfers between devices, body(): lax.ppermute(sent, 'space', ring('space', 2 * k))  3.75 us
  transfers between devices with their start and end apart: 15, of which 12 were waited for; matrix products, arithmetic and copies ran while one was open for 0% of the time, Pallas kernels for 3%

profile of v3, /device:TPU:1, one launch (start us, length us, event | category | flops | bytes accessed | tf_op | source)
XLA Modules:
  0.0 90.8 jit_solution(3749012226186748844)
XLA Ops:
  0.7 1.0 %copy.24 = bf16[1,2,80,4,128]{4,2,3,1,0:T(8,128)(2,1)S(1)} copy(bf16[1,2,80,4,128]{4,3,2,1,0:T(4,128)(2,1)} %param.16) | data formatting | bytes 327680 | tf_op args[0]
  1.6 3.6 %collective-permute-start.2 = (bf16[2,4,80,128]{3,2,1,0:T(8,128)(2,1)S(1)}, bf16[2,4,80,128]{3,2,1,0:T(8,128)(2,1)S(1)}, u32[]{:S(2)}, u32[]{:S(2)}) collective-permute-start(bf16[2,4,80,128]{3,2,1,0:T(8,128)(2,1)S(1)} %bitcast.33), channel_id=1, source_target_pairs={{0,3},{1,0},{2,1},{3,2},{4,7},{5,4},{6,5},{7,6},{8,11},{9,8},{10,9... | collective-permute-start | bytes 491528 | tf_op jit(solution)/shard_map/ppermute | solution.py:537
  6.3 2.1 %collective-permute-start.5 = (bf16[2,4,80,128]{3,2,1,0:T(8,128)(2,1)S(1)}, bf16[2,4,80,128]{3,2,1,0:T(8,128)(2,1)S(1)}, u32[]{:S(2)}, u32[]{:S(2)}) collective-permute-start(bf16[2,4,80,128]{3,2,1,0:T(8,128)(2,1)S(1)} %bitcast.27), channel_id=1, source_target_pairs={{0,3},{1,0},{2,1},{3,2},{4,7},{5,4},{6,5},{7,6},{8,11},{9,8},{10,9... | collective-permute-start | bytes 491528 | tf_op jit(solution)/shard_map/ppermute | solution.py:537
  8.4 1.4 %collective-permute-start.4 = (bf16[2,4,80,128]{3,2,1,0:T(8,128)(2,1)S(1)}, bf16[2,4,80,128]{3,2,1,0:T(8,128)(2,1)S(1)}, u32[]{:S(2)}, u32[]{:S(2)}) collective-permute-start(bf16[2,4,80,128]{3,2,1,0:T(8,128)(2,1)S(1)} %bitcast.28), channel_id=1, source_target_pairs={{0,2},{1,3},{2,0},{3,1},{4,6},{5,7},{6,4},{7,5},{8,10},{9,11},{10,... | collective-permute-start | bytes 491528 | tf_op jit(solution)/shard_map/ppermute | solution.py:537
  13.0 4.7 %collective-permute-done.f1 = bf16[2,4,80,128]{3,2,1,0:T(8,128)(2,1)S(1)} collective-permute-done((bf16[2,4,80,128]{3,2,1,0:T(8,128)(2,1)S(1)}, bf16[2,4,80,128]{3,2,1,0:T(8,128)(2,1)S(1)}, u32[]{:S(2)}, u32[]{:S(2)}) %collective-permute-start) | collective-permute-done | bytes 163872 | tf_op jit(solution)/shard_map/ppermute | solution.py:537
  17.7 1.1 %copy-done.11 = bf16[9,80,320]{2,1,0:T(8,128)(2,1)S(1)} copy-done((bf16[9,80,320]{2,1,0:T(8,128)(2,1)S(1)}, bf16[9,80,320]{2,1,0:T(8,128)(2,1)}, u32[]{:S(2)}) %copy-start.11) | copy-done | bytes 460824
  18.7 1.7 %conv_p.1 = (f32[160,512]{1,0:T(8,128)S(1)}, f32[160,128]{1,0:T(8,128)S(1)}, f32[160,128]{1,0:T(8,128)S(1)}, bf16[960,128]{1,0:T(8,128)(2,1)S(1)}, bf16[960,128]...) custom-call(s32[7]{0:T(128)S(1)} %stack.31.place_ref.t_ref.edge_ref.x_ref, bf16[2,4,80,128]{3,2,1,0:T(8,128)(2,1)S(1)} %bitcast.36, ...), custom_call_target="tpu_custom_call" | custom-call | flops 471859200 | bytes 2836508 | tf_op jit(solution)/shard_map/conv_p/pallas_call | solution.py:33
  20.5 3.0 %collective-permute-done.3.f1 = bf16[2,4,80,128]{3,2,1,0:T(8,128)(2,1)S(1)} collective-permute-done((bf16[2,4,80,128]{3,2,1,0:T(8,128)(2,1)S(1)}, bf16[2,4,80,128]{3,2,1,0:T(8,128)(2,1)S(1)}, u32[]{:S(2)}, u32[]{:S(2)}) %collective-permute-start.3) | collective-permute-done | bytes 163872 | tf_op jit(solution)/shard_map/ppermute | solution.py:537
  23.4 1.7 %conv_r.1 = (f32[160,512]{1,0:T(8,128)S(1)}, f32[160,128]{1,0:T(8,128)S(1)}, f32[160,128]{1,0:T(8,128)S(1)}, bf16[1632,128]{1,0:T(8,128)(2,1)S(1)}, bf16[1632,128]{1,0:T(8,128)(2,1)S(1)}) custom-call(s32[7]{0:T(128)S(1)} %stack.31.place_ref.t_ref.edge_ref.x_ref, bf16[2,4,80,128]{3,2,1,0:T(8,128)(2,1)S(1)} %bitcast.30, ...), custom_call_target="tpu_custom_call" | custom-call | flops 471859200 | bytes 3033116 | tf_op jit(solution)/shard_map/conv_r/pallas_call | solution.py:33
  25.7 1.2 %collective-permute-start.7 = (bf16[1632,128]{1,0:T(8,128)(2,1)S(1)}, bf16[1632,128]{1,0:T(8,128)(2,1)S(1)}, u32[]{:S(2)}, u32[]{:S(2)}) collective-permute-start(bf16[1632,128]{1,0:T(8,128)(2,1)S(1)} %get-tuple-element.53), channel_id=1, source_target_pairs={{0,28},{4,8},{8,4},{12,16},{16,12},{20,24},{24,20},{28,0},{1,29},{... | collective-permute-start | bytes 1253384 | tf_op jit(solution)/shard_map/ppermute | solution.py:583
  27.1 6.4 %collective-permute-done.7.got_b = bf16[1632,128]{1,0:T(8,128)(2,1)S(1)} collective-permute-done((bf16[1632,128]{1,0:T(8,128)(2,1)S(1)}, bf16[1632,128]{1,0:T(8,128)(2,1)S(1)}, u32[]{:S(2)}, u32[]{:S(2)}) %collective-permute-start.7) | collective-permute-done | bytes 417824 | tf_op jit(solution)/shard_map/ppermute | solution.py:583
  33.5 1.0 %stats.1 = (f32[160,1280]{1,0:T(8,128)S(1)}, f32[160,768]{1,0:T(8,128)S(1)}, f32[8,8,128]{2,1,0:T(8,128)S(1)}, f32[8,16,128]{2,1,0:T(8,128)S(1)}) custom-call(s32[7]{0:T(128)S(1)} %stack.31.place_ref.t_ref.edge_ref.x_ref, f32[160,512]{1,0:T(8,128)S(1)} %get-tuple-element.42.pre_p, f32[160,128]{1,0:T(8,128)S(1)} %get-tuple-element.43.up_p, ...), custom_call_target="tpu_custom_call" | custom-call | flops 1000000 | bytes 3244060 | tf_op jit(solution)/shard_map/stats/pallas_call | solution.py:33
  34.5 9.7 %all_to_all.15.sums_ref = f32[8,16,128]{2,1,0:T(8,128)S(1)} all-to-all(f32[8,16,128]{2,1,0:T(8,128)S(1)} %get-tuple-element.56), channel_id=1, replica_groups=mesh['dp'=8,'space'=8,'tensor'=4] {'space'}, dimensions={0} | all-to-all | bytes 131072 | tf_op jit(solution)/shard_map/all_to_all | solution.py:599
  44.2 1.6 %hidden.1 = (f32[12,8,128]{2,1,0:T(8,128)S(1)}, bf16[160,512]{1,0:T(8,128)(2,1)S(1)}, f32[160,128]{1,0:T(8,128)S(1)}) custom-call(s32[7]{0:T(128)S(1)} %stack.31.place_ref.t_ref.edge_ref.x_ref, f32[160,1280]{1,0:T(8,128)S(1)} %get-tuple-element.54.ext_p, f32[160,768]{1,0:T(8,128)S(1)} %get-tuple-element.55.ext_r, f32[8,16,128]{2,1,0:T(8,128)S(1)} %all_to_all.15.sums_ref, ...), custom_call_target="tpu_custom_call" | custom-call | flops 10000000 | bytes 1799196 | tf_op jit(solution)/shard_map/hidden/pallas_call | solution.py:33
  47.7 1.1 %collective-permute-done.10.p3 = f32[12,8,128]{2,1,0:T(8,128)S(1)} collective-permute-done((f32[12,8,128]{2,1,0:T(8,128)S(1)}, f32[12,8,128]{2,1,0:T(8,128)S(1)}, u32[]{:S(2)}, u32[]{:S(2)}) %collective-permute-start.10) | collective-permute-done | bytes 49184 | tf_op jit(solution)/shard_map/ppermute | solution.py:608
  48.8 1.8 %collective-permute-done.9.p2 = f32[12,8,128]{2,1,0:T(8,128)S(1)} collective-permute-done((f32[12,8,128]{2,1,0:T(8,128)S(1)}, f32[12,8,128]{2,1,0:T(8,128)S(1)}, u32[]{:S(2)}, u32[]{:S(2)}) %collective-permute-start.9) | collective-permute-done | bytes 49184 | tf_op jit(solution)/shard_map/ppermute | solution.py:608
  51.2 1.2 %back.1 = (f32[160,768]{1,0:T(8,128)S(1)}, f32[32,128]{1,0:T(8,128)S(1)}, f32[8,24,128]{2,1,0:T(8,128)S(1)}) custom-call(s32[7]{0:T(128)S(1)} %stack.31.place_ref.t_ref.edge_ref.x_ref, f32[12,8,128]{2,1,0:T(8,128)S(1)} %get-tuple-element.58.p0, f32[12,8,128]{2,1,0:T(8,128)S(1)} %collective-permute-done.8.p1, f32[12,8,128]{2,1,0:T(8,128)S(1)} %collective-permute-done.9.p2, ...), custom_call_target="tpu_custom_call" | custom-call | flops 10000000 | bytes 2005532 | tf_op jit(solution)/shard_map/back/pallas_call | solution.py:33
  52.4 9.7 %all_to_all.16.red_ref = f32[8,24,128]{2,1,0:T(8,128)S(1)} all-to-all(f32[8,24,128]{2,1,0:T(8,128)S(1)} %get-tuple-element.64), channel_id=1, replica_groups=mesh['dp'=8,'space'=8,'tensor'=4] {'space'}, dimensions={0} | all-to-all | bytes 196608 | tf_op jit(solution)/shard_map/all_to_all | solution.py:617
  62.1 3.0 %weight.1 = (f32[1024,128]{1,0:T(8,128)S(1)}, bf16[1056,128]{1,0:T(8,128)(2,1)S(1)}, f32[32,128]{1,0:T(8,128)S(1)}, f32[1,1]{1,0:T(1,128)}) custom-call(s32[7]{0:T(128)S(1)} %stack.31.place_ref.t_ref.edge_ref.x_ref, f32[160,768]{1,0:T(8,128)S(1)} %get-tuple-element.63.gnorm_ref, f32[160,1280]{1,0:T(8,128)S(1)} %get-tuple-element.54.ext_p, ...), custom_call_target="tpu_custom_call" | custom-call | flops 471859200 | bytes 2973728 | tf_op jit(solution)/shard_map/weight/pallas_call | solution.py:33
  65.1 0.8 collective-permute-start.11
  65.9 1.2 %collective-permute-done.11.got_ref = bf16[1056,128]{1,0:T(8,128)(2,1)S(1)} collective-permute-done((bf16[1056,128]{1,0:T(8,128)(2,1)S(1)}, bf16[1056,128]{1,0:T(8,128)(2,1)S(1)}, u32[]{:S(2)}, u32[]{:S(2)}) %collective-permute-start.11) | collective-permute-done | bytes 270368 | tf_op jit(solution)/shard_map/ppermute | solution.py:627
  68.1 1.8 %collective-permute-start.13 = (bf16[288,128]{1,0:T(8,128)(2,1)S(1)}, bf16[288,128]{1,0:T(8,128)(2,1)S(1)}, u32[]{:S(2)}, u32[]{:S(2)}) collective-permute-start(bf16[288,128]{1,0:T(8,128)(2,1)S(1)} %get-tuple-element.73), channel_id=1, source_target_pairs={{0,16},{4,20},{8,24},{12,28},{16,0},{20,4},{24,8},{28,12},{1,17},{... | collective-permute-start | bytes 221192 | tf_op jit(solution)/shard_map/ppermute | solution.py:637
  70.6 2.3 %collective-permute-done.12.r1 = bf16[288,128]{1,0:T(8,128)(2,1)S(1)} collective-permute-done((bf16[288,128]{1,0:T(8,128)(2,1)S(1)}, bf16[288,128]{1,0:T(8,128)(2,1)S(1)}, u32[]{:S(2)}, u32[]{:S(2)}) %collective-permute-start.12) | collective-permute-done | bytes 73760 | tf_op jit(solution)/shard_map/ppermute | solution.py:637
  74.3 15.7 %all_to_all.17.got_ref = bf16[8,56,128]{2,1,0:T(8,128)(2,1)S(1)} all-to-all(bf16[8,56,128]{2,1,0:T(8,128)(2,1)S(1)} %cross.1), channel_id=1, replica_groups=mesh['dp'=8,'space'=8,'tensor'=4] {'dp'}, dimensions={0} | all-to-all | bytes 229376 | tf_op jit(solution)/shard_map/all_to_all | solution.py:640
  (48 shorter events, 9.9 us)
Async XLA Ops:
  0.6 5.7 %copy-start.12 = (bf16[1,2,80,4,128]{4,3,2,1,0:T(4,128)(2,1)S(1)}, bf16[1,2,80,4,128]{4,3,2,1,0:T(4,128)(2,1)}, u32[]{:S(2)}) copy-start(bf16[1,2,80,4,128]{4,3,2,1,0:T(4,128)(2,1)} %param.17) | copy-start | bytes 491524
  0.6 10.9 %copy-start.1 = (f32[1000,80]{0,1:T(8,128)S(1)}, f32[1000,80]{0,1:T(8,128)}, u32[]{:S(2)}) copy-start(f32[1000,80]{0,1:T(8,128)} %param.29) | copy-start | bytes 960004
  1.6 8.4 %collective-permute-start.2 = (bf16[2,4,80,128]{3,2,1,0:T(8,128)(2,1)S(1)}, bf16[2,4,80,128]{3,2,1,0:T(8,128)(2,1)S(1)}, u32[]{:S(2)}, u32[]{:S(2)}) collective-permute-start(bf16[2,4,80,128]{3,2,1,0:T(8,128)(2,1)S(1)} %bitcast.33), channel_id=1, source_target_pairs={{0,3},{1,0},{2,1},{3,2},{4,7},{5,4},{6,5},{7,6},{8,11},{9,8},{10,9... | collective-permute-start | bytes 491528 | tf_op jit(solution)/shard_map/ppermute | solution.py:537
  5.3 7.7 %collective-permute-start.1 = (bf16[2,4,80,128]{3,2,1,0:T(8,128)(2,1)S(1)}, bf16[2,4,80,128]{3,2,1,0:T(8,128)(2,1)S(1)}, u32[]{:S(2)}, u32[]{:S(2)}) collective-permute-start(bf16[2,4,80,128]{3,2,1,0:T(8,128)(2,1)S(1)} %bitcast.34), channel_id=1, source_target_pairs={{0,2},{1,3},{2,0},{3,1},{4,6},{5,7},{6,4},{7,5},{8,10},{9,11},{10,... | collective-permute-start | bytes 491528 | tf_op jit(solution)/shard_map/ppermute | solution.py:537
  5.6 12.1 %collective-permute-start = (bf16[2,4,80,128]{3,2,1,0:T(8,128)(2,1)S(1)}, bf16[2,4,80,128]{3,2,1,0:T(8,128)(2,1)S(1)}, u32[]{:S(2)}, u32[]{:S(2)}) collective-permute-start(bf16[2,4,80,128]{3,2,1,0:T(8,128)(2,1)S(1)} %bitcast.35), channel_id=1, source_target_pairs={{0,1},{1,2},{2,3},{3,0},{4,5},{5,6},{6,7},{7,4},{8,9},{9,10},{10,1... | collective-permute-start | bytes 491528 | tf_op jit(solution)/shard_map/ppermute | solution.py:537
  6.3 14.1 %collective-permute-start.5 = (bf16[2,4,80,128]{3,2,1,0:T(8,128)(2,1)S(1)}, bf16[2,4,80,128]{3,2,1,0:T(8,128)(2,1)S(1)}, u32[]{:S(2)}, u32[]{:S(2)}) collective-permute-start(bf16[2,4,80,128]{3,2,1,0:T(8,128)(2,1)S(1)} %bitcast.27), channel_id=1, source_target_pairs={{0,3},{1,0},{2,1},{3,2},{4,7},{5,4},{6,5},{7,6},{8,11},{9,8},{10,9... | collective-permute-start | bytes 491528 | tf_op jit(solution)/shard_map/ppermute | solution.py:537
  8.4 12.0 %collective-permute-start.4 = (bf16[2,4,80,128]{3,2,1,0:T(8,128)(2,1)S(1)}, bf16[2,4,80,128]{3,2,1,0:T(8,128)(2,1)S(1)}, u32[]{:S(2)}, u32[]{:S(2)}) collective-permute-start(bf16[2,4,80,128]{3,2,1,0:T(8,128)(2,1)S(1)} %bitcast.28), channel_id=1, source_target_pairs={{0,2},{1,3},{2,0},{3,1},{4,6},{5,7},{6,4},{7,5},{8,10},{9,11},{10,... | collective-permute-start | bytes 491528 | tf_op jit(solution)/shard_map/ppermute | solution.py:537
  10.0 13.4 %collective-permute-start.3 = (bf16[2,4,80,128]{3,2,1,0:T(8,128)(2,1)S(1)}, bf16[2,4,80,128]{3,2,1,0:T(8,128)(2,1)S(1)}, u32[]{:S(2)}, u32[]{:S(2)}) collective-permute-start(bf16[2,4,80,128]{3,2,1,0:T(8,128)(2,1)S(1)} %bitcast.29), channel_id=1, source_target_pairs={{0,1},{1,2},{2,3},{3,0},{4,5},{5,6},{6,7},{7,4},{8,9},{9,10},{10,1... | collective-permute-start | bytes 491528 | tf_op jit(solution)/shard_map/ppermute | solution.py:537
  10.1 1.5 %copy-start.4 = (bf16[9,4,80]{2,1,0:T(4,128)(2,1)S(1)}, bf16[9,4,80]{2,1,0:T(4,128)(2,1)}, u32[]{:S(2)}) copy-start(bf16[9,4,80]{2,1,0:T(4,128)(2,1)} %w2_r.1) | copy-start | bytes 17284
  10.1 1.5 %copy-start.2 = (f32[1,2,4,4,128]{4,3,2,1,0:T(4,128)S(1)}, f32[1,2,4,4,128]{4,3,2,1,0:T(4,128)}, u32[]{:S(2)}) copy-start(f32[1,2,4,4,128]{4,3,2,1,0:T(4,128)} %param.18) | copy-start | bytes 49156
  11.4 0.7 copy-start.3
  11.5 0.7 copy-start.6
  11.5 0.7 copy-start.7
  17.7 1.1 %copy-start.11 = (bf16[9,80,320]{2,1,0:T(8,128)(2,1)S(1)}, bf16[9,80,320]{2,1,0:T(8,128)(2,1)}, u32[]{:S(2)}) copy-start(bf16[9,80,320]{2,1,0:T(8,128)(2,1)} %param.19) | copy-start | bytes 1382404
  18.7 4.7 %copy-start = (bf16[9,80,320]{2,1,0:T(8,128)(2,1)S(1)}, bf16[9,80,320]{2,1,0:T(8,128)(2,1)}, u32[]{:S(2)}) copy-start(bf16[9,80,320]{2,1,0:T(8,128)(2,1)} %param.20) | copy-start | bytes 1382404
  25.2 2.0 %collective-permute-start.6 = (bf16[1632,128]{1,0:T(8,128)(2,1)S(1)}, bf16[1632,128]{1,0:T(8,128)(2,1)S(1)}, u32[]{:S(2)}, u32[]{:S(2)}) collective-permute-start(bf16[1632,128]{1,0:T(8,128)(2,1)S(1)} %get-tuple-element.52), channel_id=1, source_target_pairs={{0,4},{4,0},{8,12},{12,8},{16,20},{20,16},{24,28},{28,24},{1,5},{5... | collective-permute-start | bytes 1253384 | tf_op jit(solution)/shard_map/ppermute | solution.py:584
  25.7 7.8 %collective-permute-start.7 = (bf16[1632,128]{1,0:T(8,128)(2,1)S(1)}, bf16[1632,128]{1,0:T(8,128)(2,1)S(1)}, u32[]{:S(2)}, u32[]{:S(2)}) collective-permute-start(bf16[1632,128]{1,0:T(8,128)(2,1)S(1)} %get-tuple-element.53), channel_id=1, source_target_pairs={{0,28},{4,8},{8,4},{12,16},{16,12},{20,24},{24,20},{28,0},{1,29},{... | collective-permute-start | bytes 1253384 | tf_op jit(solution)/shard_map/ppermute | solution.py:583
  45.8 3.0 %collective-permute-start.10 = (f32[12,8,128]{2,1,0:T(8,128)S(1)}, f32[12,8,128]{2,1,0:T(8,128)S(1)}, u32[]{:S(2)}, u32[]{:S(2)}) collective-permute-start(f32[12,8,128]{2,1,0:T(8,128)S(1)} %get-tuple-element.58.p0), channel_id=1, source_target_pairs={{0,3},{1,0},{2,1},{3,2},{4,7},{5,4},{6,5},{7,6},{8,11},{9,8},{10,9... | collective-permute-start | bytes 147464 | tf_op jit(solution)/shard_map/ppermute | solution.py:608
  46.2 4.4 %collective-permute-start.9 = (f32[12,8,128]{2,1,0:T(8,128)S(1)}, f32[12,8,128]{2,1,0:T(8,128)S(1)}, u32[]{:S(2)}, u32[]{:S(2)}) collective-permute-start(f32[12,8,128]{2,1,0:T(8,128)S(1)} %get-tuple-element.58.p0), channel_id=1, source_target_pairs={{0,2},{1,3},{2,0},{3,1},{4,6},{5,7},{6,4},{7,5},{8,10},{9,11},{10,... | collective-permute-start | bytes 147464 | tf_op jit(solution)/shard_map/ppermute | solution.py:608
  46.9 4.3 %collective-permute-start.8 = (f32[12,8,128]{2,1,0:T(8,128)S(1)}, f32[12,8,128]{2,1,0:T(8,128)S(1)}, u32[]{:S(2)}, u32[]{:S(2)}) collective-permute-start(f32[12,8,128]{2,1,0:T(8,128)S(1)} %get-tuple-element.58.p0), channel_id=1, source_target_pairs={{0,1},{1,2},{2,3},{3,0},{4,5},{5,6},{6,7},{7,4},{8,9},{9,10},{10,1... | collective-permute-start | bytes 147464 | tf_op jit(solution)/shard_map/ppermute | solution.py:608
  65.1 2.0 %collective-permute-start.11 = (bf16[1056,128]{1,0:T(8,128)(2,1)S(1)}, bf16[1056,128]{1,0:T(8,128)(2,1)S(1)}, u32[]{:S(2)}, u32[]{:S(2)}) collective-permute-start(bf16[1056,128]{1,0:T(8,128)(2,1)S(1)} %get-tuple-element.70), channel_id=1, source_target_pairs={{0,4},{4,0},{8,12},{12,8},{16,20},{20,16},{24,28},{28,24},{1,5},{5... | collective-permute-start | bytes 811016 | tf_op jit(solution)/shard_map/ppermute | solution.py:627
  67.7 5.2 %collective-permute-start.12 = (bf16[288,128]{1,0:T(8,128)(2,1)S(1)}, bf16[288,128]{1,0:T(8,128)(2,1)S(1)}, u32[]{:S(2)}, u32[]{:S(2)}) collective-permute-start(bf16[288,128]{1,0:T(8,128)(2,1)S(1)} %get-tuple-element.72), channel_id=1, source_target_pairs={{0,8},{4,12},{8,16},{12,20},{16,24},{20,28},{24,0},{28,4},{1,9},{5... | collective-permute-start | bytes 221192 | tf_op jit(solution)/shard_map/ppermute | solution.py:637
  68.1 5.5 %collective-permute-start.13 = (bf16[288,128]{1,0:T(8,128)(2,1)S(1)}, bf16[288,128]{1,0:T(8,128)(2,1)S(1)}, u32[]{:S(2)}, u32[]{:S(2)}) collective-permute-start(bf16[288,128]{1,0:T(8,128)(2,1)S(1)} %get-tuple-element.73), channel_id=1, source_target_pairs={{0,16},{4,20},{8,24},{12,28},{16,0},{20,4},{24,8},{28,12},{1,17},{... | collective-permute-start | bytes 221192 | tf_op jit(solution)/shard_map/ppermute | solution.py:637
  69.8 4.5 %collective-permute-start.14 = (bf16[288,128]{1,0:T(8,128)(2,1)S(1)}, bf16[288,128]{1,0:T(8,128)(2,1)S(1)}, u32[]{:S(2)}, u32[]{:S(2)}) collective-permute-start(bf16[288,128]{1,0:T(8,128)(2,1)S(1)} %get-tuple-element.74), channel_id=1, source_target_pairs={{0,24},{4,28},{8,0},{12,4},{16,8},{20,12},{24,16},{28,20},{1,25},{... | collective-permute-start | bytes 221192 | tf_op jit(solution)/shard_map/ppermute | solution.py:637
  (4 other events, 2.7 us)

commit v4 on v3

--- a/solution.py
+++ b/solution.py
@@ -27,7 +27,7 @@
 SM = pl.BlockSpec(memory_space=pltpu.SMEM)
 
 
-def call(kernel, ins, outs, name, flops, smem=0, scratch=()):
+def call(kernel, ins, outs, flops, smem=0, scratch=()):
     in_bytes = sum(a.size * a.dtype.itemsize for a in ins)
     out_bytes = sum(s.size * s.dtype.itemsize for s in outs)
     return pl.pallas_call(
@@ -36,7 +36,6 @@
         in_specs=[SM] * smem + [VM] * (len(ins) - smem),
         out_specs=[VM] * len(outs),
         scratch_shapes=list(scratch),
-        name=name,
         cost_estimate=pl.CostEstimate(
             flops=flops, bytes_accessed=in_bytes + out_bytes, transcendentals=0
         ),
@@ -74,6 +73,10 @@
 
 def row_of(tile, r):
     return tile[:, r * COLS : (r + 1) * COLS]
+
+
+def sigmoid(value):
+    return 0.5 + 0.5 * jnp.tanh(0.5 * value)
 
 
 def members():
@@ -101,9 +104,11 @@
 
 
 def prep_kernel(
-    place_ref, b_p, b_r, gain_p, off_p, gain_r, off_r, w2_p, w2_r, table_ref, noise_ref,
-    col_ref, lift_ref, drop_ref, rows_ref
+    place_ref, b_p, b_r, gain_p, off_p, gain_r, off_r, w2_p, w2_r, table_ref, noise_ref, w1_p, w1_r,
+    col_ref, lift_ref, drop_ref, rows_ref, w1_p_out, w1_r_out
 ):
+    w1_p_out[...] = w1_p[...]
+    w1_r_out[...] = w1_r[...]
     lane = lax.broadcasted_iota(jnp.int32, table_ref.shape, 1)
     shift = jnp.sum(
         jnp.where(lane == place_ref[6], table_ref[...], 0.0), axis=1, keepdims=True
@@ -148,9 +153,9 @@
 
 def conv_kernel(last, t_ref, f0, f1, f2, f3, w_ref, col_ref, *refs):
     if last:
-        side_a, side_b, noise_ref, pre_ref, up_ref, dn_ref, send_a, send_b, fs_ref = refs
+        pre_ref, up_ref, dn_ref, send_a, send_b, fs_ref = refs
     else:
-        pre_ref, up_ref, dn_ref, send_a, send_b, fs_ref = refs
+        noise_ref, pre_ref, up_ref, dn_ref, send_a, send_b, perm_ref, fs_ref = refs
     t = t_ref[5]
     bias = 5 if last else 4
     for k in range(4):
@@ -160,9 +165,8 @@
                 lo = im * PIX + r * COLS
                 fs_ref[pl.ds(base, CH), lo : lo + COLS] = (f0, f1, f2, f3)[k][im, r]
     odd = t_ref[3] > 0
-    if last:
-        send_a[0:960, :] = side_a[...]
-        send_b[0:960, :] = side_b[...]
+    count = 2 if last else 4
+    if not last:
         for index in range(2):
             first, second = noise_ref[index], noise_ref[2 + index]
             for ref, value in (
@@ -171,10 +175,13 @@
             ):
                 high = value.astype(BF16).astype(F32)
                 both = jnp.concatenate([high, value - high], axis=0).astype(BF16)
-                ref[1600 + 16 * index : 1616 + 16 * index, :] = both
-        start, count = 960, 2
-    else:
-        start, count = 0, 4
+                ref[960 + 16 * index : 976 + 16 * index, :] = both
+        row = lax.broadcasted_iota(jnp.int32, (C, C), 0)
+        chan = lax.broadcasted_iota(jnp.int32, (C, C), 1)
+        core, rest = row // 160, row % 160
+        want = 40 * (rest % 8) + 10 * (rest // 40) + 5 * core + (rest % 40) // 8
+        pick = jnp.where(chan == want, 1.0, 0.0).astype(BF16)
+        perm_ref[...] = dot(pick, fs_ref[...]).astype(BF16)
     for im in range(2):
         feats = fs_ref[:, im * PIX : (im + 1) * PIX]
         taps = [dot(w_ref[ky * 3 * CH : (ky + 1) * 3 * CH, :], feats) for ky in range(3)]
@@ -207,9 +214,9 @@
                 (send_b, jnp.where(odd, lower, upper)),
             ):
                 high = value.astype(BF16)
-                lo = start + index * 2 * CH + im * CH
+                lo = index * 2 * CH + im * CH
                 ref[lo : lo + CH, :] = high
-                ref_low = start + (count + index) * 2 * CH + im * CH
+                ref_low = (count + index) * 2 * CH + im * CH
                 if count == 2:
                     ref[ref_low : ref_low + CH, :] = (value - high.astype(F32)).astype(BF16)
         if count == 4:
@@ -220,18 +227,17 @@
                     (send_b, jnp.where(odd, lower, upper)),
                 ):
                     rest = value - value.astype(BF16).astype(F32)
-                    lo = start + (count + index) * 2 * CH + im * CH
+                    lo = (count + index) * 2 * CH + im * CH
                     ref[lo : lo + CH, :] = rest.astype(BF16)
 
 
 def stat_kernel(
-    place_ref, pre_p, up_p, dn_p, pre_r, up_r, dn_r, got_a, got_b, noise_ref,
+    place_ref, pre_p, up_p, dn_p, pre_r, up_r, dn_r, got_ap, got_bp, got_ar, got_br, noise_ref,
     ext_p, ext_r, noise_ext, out_ref
 ):
     odd = place_ref[3] > 0
     top = place_ref[1] > 0
     bottom = place_ref[2] > 0
-    left, right = (got_a, got_b), (got_b, got_a)
 
     def rows_at(side, lo, hi):
         return jnp.where(odd, side[0][lo:hi, :].astype(F32), side[1][lo:hi, :].astype(F32))
@@ -243,10 +249,12 @@
         return got(ref, index) + got(ref, low)
 
     columns = []
-    for pre, up, dn, ext, first, halo in (
-        (pre_p, up_p, dn_p, ext_p, 0, 3),
-        (pre_r, up_r, dn_r, ext_r, 6, 1),
+    first = 0
+    for pre, up, dn, ext, got_a, got_b, halo in (
+        (pre_p, up_p, dn_p, ext_p, got_ap, got_bp, 3),
+        (pre_r, up_r, dn_r, ext_r, got_ar, got_br, 1),
     ):
+        left, right = (got_a, got_b), (got_b, got_a)
         low = first + halo + 1
         rows = [pre[:, r * COLS : (r + 1) * COLS] for r in range(ROWS)]
         rows[0] = rows[0] + jnp.where(top, 0.0, near(left, first + halo, low + 1))
@@ -264,7 +272,8 @@
         columns.append(jnp.sum(total, axis=1, keepdims=True))
         columns.append(jnp.sum(square, axis=1, keepdims=True))
     for index in range(2):
-        lo = 1600 + 16 * index
+        lo = 960 + 16 * index
+        left, right = (got_ap, got_bp), (got_bp, got_ap)
         pair = rows_at(left, lo, lo + 16)
         noise_ext[index] = pair[0:8] + pair[8:16]
         pair = rows_at(right, lo, lo + 16)
@@ -299,7 +308,7 @@
         for index in range(ROWS + 2 * halo):
             value = ext[:, index * COLS : (index + 1) * COLS]
             normed = ((value - mean) * inv) * gain + shift
-            hidden = normed * jax.nn.sigmoid(normed)
+            hidden = normed * sigmoid(normed)
             if index < halo:
                 hidden = jnp.where(edge_ref[1] > 0, 0.0, hidden)
             if index >= ROWS + halo:
@@ -366,7 +375,7 @@
         lanes = slice(index * COLS, (index + 1) * COLS)
         centered = (ext_p[:, (index + 2) * COLS : (index + 3) * COLS] - mean) * inv
         normed = centered * gain + shift
-        gate = jax.nn.sigmoid(normed)
+        gate = sigmoid(normed)
         gnorm = dhidden[:, lanes] * gate * (1.0 + normed * (1.0 - gate)) * gain
         gnorm_ref[:, lanes] = gnorm
         if 1 <= index <= ROWS:
@@ -395,7 +404,7 @@
 
 def weight_kernel(
     place_ref, gnorm_ref, ext_p, stat_ref, red_ref, fs_ref, head_ref,
-    keep_ref, send_ref, both_ref, logit_ref, grad_ref, pack_ref
+    keep_ref, send_ref, both_ref, logit_ref, grad_ref
 ):
     total = jnp.sum(red_ref[...], axis=0)
     row = lax.broadcasted_iota(jnp.int32, (8, COLS), 0)
@@ -432,45 +441,46 @@
             rows.append(jnp.concatenate(tiles, axis=1))
         stack = jnp.concatenate(rows + [blank], axis=0)
         grad = dot_nt(fs_ref[...], stack) * scale
-        grad_ref[2 * ky] = grad[:, 0:COLS]
-        grad_ref[2 * ky + 1] = grad[:, COLS : 2 * COLS]
-    chunk = 5
+        grad_ref[:, 256 * ky : 256 * ky + 256] = grad
     core = place_ref[3]
-    for ref, who in ((keep_ref, core), (pack_ref, 1 - core)):
-        for x in range(4):
-            for ii in range(chunk):
-                for half in range(6):
-                    ref[pl.ds(x * 256 + half * chunk + ii, 8, stride=32), :] = grad_ref[
-                        half, pl.ds(who * chunk + 2 * chunk * x + ii, 8, stride=8 * chunk), :
-                    ]
-            for spare in (30, 31):
-                ref[pl.ds(x * 256 + spare, 8, stride=32), :] = jnp.zeros((8, COLS), F32)
-    send_ref[0:1024, :] = pack_ref[...].astype(BF16)
     head = head_ref[...] * scale
     both_ref[...] = head
-    send_ref[1024:1056, :] = head.astype(BF16)
+    for x in range(4):
+        mine = pl.multiple_of(core * 160 + 40 * x, 8)
+        his = pl.multiple_of((1 - core) * 160 + 40 * x, 8)
+        keep_ref[x] = grad_ref[pl.ds(mine, 40), :]
+        tail = [head[8 * j : 8 * j + 8] for j in range(3)] + [jnp.zeros((8, 3 * COLS), F32)]
+        block = jnp.concatenate(
+            [grad_ref[pl.ds(his, 40), :], jnp.concatenate(tail, axis=1)], axis=0
+        )
+        send_ref[x] = block.astype(BF16)
 
 
 def core_kernel(x_ref, keep_ref, both_ref, got_ref, own_ref, s1, s2, s3):
     x = x_ref[4]
-    head = both_ref[...] + got_ref[1024:1056, :].astype(F32)
+    tail = [both_ref[8 * j : 8 * j + 8, :] for j in range(3)] + [jnp.zeros((8, 3 * COLS), F32)]
+    tail = jnp.concatenate(tail, axis=1)
     for k, ref in enumerate((own_ref, s1, s2, s3)):
-        lo = pl.multiple_of(lax.rem(x + k, 4) * 256, 256)
-        block = keep_ref[pl.ds(lo, 256), :] + got_ref[pl.ds(lo, 256), :].astype(F32)
-        ref[0:256, :] = block.astype(ref.dtype)
-        ref[256:288, :] = head.astype(ref.dtype)
-
-
-def cross_kernel(own_ref, r1, r2, r3, out_ref):
-    def total(lo, hi):
-        return (own_ref[lo:hi, :] + r1[lo:hi, :].astype(F32)) + (
-            r2[lo:hi, :].astype(F32) + r3[lo:hi, :].astype(F32)
-        )
-
-    head = total(256, 288).astype(BF16)
+        where = lax.rem(x + k, 4)
+        got = got_ref[where].astype(F32)
+        block = jnp.concatenate([keep_ref[where] + got[0:40], tail + got[40:48]], axis=0)
+        ref[...] = block.astype(ref.dtype)
+
+
+def cross_kernel(own_ref, r1, r2, r3, out_ref, pack_ref):
+    total = (own_ref[...] + r1[...].astype(F32)) + (r2[...].astype(F32) + r3[...].astype(F32))
+    for half in range(6):
+        lanes = slice(half * COLS, (half + 1) * COLS)
+        for ii in range(5):
+            pack_ref[pl.ds(half * 5 + ii, 8, stride=56), :] = total[8 * ii : 8 * ii + 8, lanes]
+    for spare in (30, 31):
+        pack_ref[pl.ds(spare, 8, stride=56), :] = jnp.zeros((8, COLS), F32)
     for d in range(8):
-        out_ref[d, 0:32, :] = total(32 * d, 32 * d + 32).astype(BF16)
-        out_ref[d, 32:56, :] = head[0:24]
+        for j in range(3):
+            pack_ref[56 * d + 32 + 8 * j : 56 * d + 40 + 8 * j, :] = total[
+                40:48, j * COLS : (j + 1) * COLS
+            ]
+        out_ref[d] = pack_ref[56 * d : 56 * d + 56, :].astype(BF16)
 
 
 def sum_kernel(got_ref, one_ref, two_ref):
@@ -543,16 +553,18 @@
     parts_r = gather(own_r)
 
     vectors = [b1_policy, b1_ref, gn_gain_policy, gn_bias_policy, gn_gain_ref, gn_bias_ref]
-    columns, lift, drop, noise_rows = call(
+    columns, lift, drop, noise_rows, near_p, near_r = call(
         prep_kernel,
-        [place, *[v[None, :] for v in vectors], w2_policy, w2_ref, time_table.T, noise[0]],
+        [place, *[v[None, :] for v in vectors], w2_policy, w2_ref, time_table.T, noise[0],
+         w1_policy.reshape(9 * CH, C), w1_ref.reshape(9 * CH, C)],
         [
             arr((2 * CH, COLS), F32),
             arr((2, 2, 72, CH), BF16),
             arr((2 * CH, 72), BF16),
             arr((ROWS, 8, COLS), F32),
+            arr((9 * CH, C), BF16),
+            arr((9 * CH, C), BF16),
         ],
-        "prep",
         10**6,
         smem=1,
     )
@@ -561,38 +573,39 @@
     wide = arr((2 * CH, PIX), F32)
     thin = arr((2 * CH, COLS), F32)
 
-    pre_p, up_p, dn_p, side_a, side_b, feats = call(
-        functools.partial(conv_kernel, False),
-        [place, *parts_p, w1_policy.reshape(9 * CH, C), columns],
-        [wide, thin, thin, arr((960, COLS), BF16), arr((960, COLS), BF16), arr((C, 2 * PIX), BF16)],
-        "conv_p",
-        conv_flops,
-        smem=1,
-    )
-    pre_r, up_r, dn_r, to_a, to_b = call(
-        functools.partial(conv_kernel, True),
-        [place, *parts_r, w1_ref.reshape(9 * CH, C), columns, side_a, side_b, noise_rows],
-        [wide, thin, thin, arr((1632, COLS), BF16), arr((1632, COLS), BF16)],
-        "conv_r",
-        conv_flops,
-        smem=1,
-        scratch=[pltpu.VMEM((C, 2 * PIX), BF16)],
-    )
     partner = [(i, i ^ 1) for i in range(space)]
     across = [(i, (i + 1 if i % 2 else i - 1) % space) for i in range(space)]
-    got_b = lax.ppermute(to_b, "space", across)
-    got_a = lax.ppermute(to_a, "space", partner)
+    pre_p, up_p, dn_p, to_ap, to_bp, feats = call(
+        functools.partial(conv_kernel, False),
+        [place, *parts_p, near_p, columns, noise_rows],
+        [wide, thin, thin, arr((992, COLS), BF16), arr((992, COLS), BF16), arr((C, 2 * PIX), BF16)],
+        conv_flops,
+        smem=1,
+        scratch=[pltpu.VMEM((C, 2 * PIX), BF16)],
+    )
+    got_bp = lax.ppermute(to_bp, "space", across)
+    got_ap = lax.ppermute(to_ap, "space", partner)
+    own_r, pre_p = lax.optimization_barrier((parts_r[0], pre_p))
+    pre_r, up_r, dn_r, to_ar, to_br = call(
+        functools.partial(conv_kernel, True),
+        [place, own_r, *parts_r[1:], near_r, columns],
+        [wide, thin, thin, arr((640, COLS), BF16), arr((640, COLS), BF16)],
+        conv_flops,
+        smem=1,
+        scratch=[pltpu.VMEM((C, 2 * PIX), BF16)],
+    )
+    got_br = lax.ppermute(to_br, "space", across)
+    got_ar = lax.ppermute(to_ar, "space", partner)
 
     ext_p, ext_r, noise_ext, sums = call(
         stat_kernel,
-        [place, pre_p, up_p, dn_p, pre_r, up_r, dn_r, got_a, got_b, noise_rows],
+        [place, pre_p, up_p, dn_p, pre_r, up_r, dn_r, got_ap, got_bp, got_ar, got_br, noise_rows],
         [
             arr((2 * CH, 10 * COLS), F32),
             arr((2 * CH, 6 * COLS), F32),
             arr((8, 8, COLS), F32),
             arr((space, 16, COLS), F32),
         ],
-        "stats",
         10**6,
         smem=1,
     )
@@ -601,7 +614,6 @@
         hidden_kernel,
         [place, ext_p, ext_r, sums, columns, lift],
         [arr((12, 8, COLS), F32), arr((2 * CH, PIX), BF16), thin],
-        "hidden",
         10**7,
         smem=1,
     )
@@ -610,7 +622,6 @@
         back_kernel,
         [place, part, *others, noise_ext, ext_p, stat, columns, hidden, drop],
         [arr((2 * CH, 6 * COLS), F32), arr((32, COLS), F32), arr((space, 24, COLS), F32)],
-        "back",
         10**7,
         smem=1,
     )
@@ -618,28 +629,32 @@
     keep, send, both, logits = call(
         weight_kernel,
         [place, gnorm, ext_p, stat, partial, feats, head],
-        [arr((1024, COLS), F32), arr((1056, COLS), BF16), arr((32, COLS), F32), arr((1, 1), F32)],
-        "weight",
+        [arr((4, 40, 768), F32), arr((4, 48, 768), BF16), arr((32, COLS), F32), arr((1, 1), F32)],
         conv_flops,
         smem=1,
-        scratch=[pltpu.VMEM((6, C, COLS), F32), pltpu.VMEM((1024, COLS), F32)],
+        scratch=[pltpu.VMEM((C, 768), F32)],
     )
     got = lax.ppermute(send, "space", partner)
     own, s1, s2, s3 = call(
         core_kernel,
         [place, keep, both, got],
-        [arr((288, COLS), F32)] + [arr((288, COLS), BF16)] * 3,
-        "core",
+        [arr((48, 768), F32)] + [arr((48, 768), BF16)] * 3,
         10**6,
         smem=1,
     )
     back = [
         lax.ppermute(sent, "space", ring("space", 2 * k)) for k, sent in ((1, s1), (2, s2), (3, s3))
     ]
-    (packed,) = call(cross_kernel, [own, *back], [arr((8, 56, COLS), BF16)], "cross", 10**6)
+    (packed,) = call(
+        cross_kernel,
+        [own, *back],
+        [arr((8, 56, COLS), BF16)],
+        10**6,
+        scratch=[pltpu.VMEM((8 * 56, COLS), F32)],
+    )
     packed = lax.all_to_all(packed, "dp", 0, 0, tiled=True)
     grad_one, grad_two = call(
-        sum_kernel, [packed], [arr((9, 5, CH), F32), arr((9, 4, CH), F32)], "total", 10**6
+        sum_kernel, [packed], [arr((9, 5, CH), F32), arr((9, 4, CH), F32)], 10**6
     )
     return (logits.reshape(1), grad_one.transpose(0, 2, 1), grad_two)
 

time: 92.4 us -> 89.1 us (0.964)
  waiting for transfers between devices: 22.9 us -> 12.5 us
  starting transfers between devices: 15.5 us -> 22.3 us
  local copies, waits for them, and re-layouts: 2.85 us -> 4.72 us
  blocking collectives: 35.2 us -> 33.4 us
    ppermute x6, waiting for transfers between devices: 7.92 us -> 0.02 us  [gather(): lax.ppermute(own, 'tensor', ring('tensor', k))]
    ppermute x2 -> x4, starting transfers between devices: 1.78 us -> 5.31 us  [the longest x1 3.39 us: body(): got_ap = lax.ppermute(to_ap, 'space', partner)]
    ppermute x3, starting transfers between devices: 1.89 us -> 4.48 us  [body(): lax.ppermute(part, 'tensor', ring('tensor', k))]
    ppermute x2 -> x4, waiting for transfers between devices: 6.56 us -> 4.84 us  [the longest x1 4.01 us: body(): got_br = lax.ppermute(to_br, 'space', across)]
    all_to_all x1, blocking collectives: 9.71 us -> 8.35 us  [body(): sums = lax.all_to_all(sums, 'space', 0, 0, tiled=True)]
    unnamed x27 -> x25, local copies, waits for them, and re-layouts: 2.74 us -> 3.69 us
  transfers between devices with their start and end apart: 15 -> 17, of which waited for: 12 -> 8; matrix products, arithmetic and copies ran while one was open for 0% -> 1% of each run, Pallas kernels for 3% -> 6%
where the time goes in v4:
time: 89.1 us; the launch traced here: 87.5 us
  blocking collectives  33.4 us (37%)
  starting transfers between devices  22.3 us (25%)
  waiting for transfers between devices  12.5 us (14%)
  Pallas kernels  12.4 us (14%)
  local copies, waits for them, and re-layouts  4.72 us (5%)
  between operations  2.19 us (2%)
    all_to_all x1, blocking collectives, body(): packed = lax.all_to_all(packed, 'dp', 0, 0, tiled=True)  15.7 us
    pallas_call x10, Pallas kernels, call(): pl.pallas_call(kernel, out_shape=outs, in_specs=[SM] * smem + [VM] * (len...  12.4 us
    all_to_all x1, blocking collectives, body(): partial = lax.all_to_all(partial, 'space', 0, 0, tiled=True)  9.29 us
    ppermute x6, starting transfers between devices, gather(): lax.ppermute(own, 'tensor', ring('tensor', k))  8.85 us
    all_to_all x1, blocking collectives, body(): sums = lax.all_to_all(sums, 'space', 0, 0, tiled=True)  8.35 us
    ppermute x3, starting transfers between devices, body(): lax.ppermute(part, 'tensor', ring('tensor', k))  4.48 us
    ppermute x1, waiting for transfers between devices, body(): got_br = lax.ppermute(to_br, 'space', across)  4.01 us
    ppermute x3, waiting for transfers between devices, body(): lax.ppermute(sent, 'space', ring('space', 2 * k))  3.75 us
  transfers between devices with their start and end apart: 17, of which 8 were waited for; matrix products, arithmetic and copies ran while one was open for 1% of the time, Pallas kernels for 6%

profile of v4, /device:TPU:1, one launch (start us, length us, event | category | flops | bytes accessed | tf_op | source)
XLA Modules:
  0.0 87.5 jit_solution(16779156422028775281)
XLA Ops:
  0.6 1.0 %copy.24 = bf16[1,2,80,4,128]{4,2,3,1,0:T(8,128)(2,1)S(1)} copy(bf16[1,2,80,4,128]{4,3,2,1,0:T(4,128)(2,1)} %param.16) | data formatting | bytes 327680 | tf_op args[0]
  1.6 2.2 %collective-permute-start = (bf16[2,4,80,128]{3,2,1,0:T(8,128)(2,1)S(1)}, bf16[2,4,80,128]{3,2,1,0:T(8,128)(2,1)S(1)}, u32[]{:S(2)}, u32[]{:S(2)}) collective-permute-start(bf16[2,4,80,128]{3,2,1,0:T(8,128)(2,1)S(1)} %bitcast.34), channel_id=1, source_target_pairs={{0,1},{1,2},{2,3},{3,0},{4,5},{5,6},{6,7},{7,4},{8,9},{9,10},{10,1... | collective-permute-start | bytes 491528 | tf_op jit(solution)/shard_map/ppermute | solution.py:547
  3.8 2.6 %collective-permute-start.1 = (bf16[2,4,80,128]{3,2,1,0:T(8,128)(2,1)S(1)}, bf16[2,4,80,128]{3,2,1,0:T(8,128)(2,1)S(1)}, u32[]{:S(2)}, u32[]{:S(2)}) collective-permute-start(bf16[2,4,80,128]{3,2,1,0:T(8,128)(2,1)S(1)} %bitcast.35), channel_id=1, source_target_pairs={{0,2},{1,3},{2,0},{3,1},{4,6},{5,7},{6,4},{7,5},{8,10},{9,11},{10,... | collective-permute-start | bytes 491528 | tf_op jit(solution)/shard_map/ppermute | solution.py:547
  6.5 1.1 %collective-permute-start.2 = (bf16[2,4,80,128]{3,2,1,0:T(8,128)(2,1)S(1)}, bf16[2,4,80,128]{3,2,1,0:T(8,128)(2,1)S(1)}, u32[]{:S(2)}, u32[]{:S(2)}) collective-permute-start(bf16[2,4,80,128]{3,2,1,0:T(8,128)(2,1)S(1)} %bitcast.36), channel_id=1, source_target_pairs={{0,3},{1,0},{2,1},{3,2},{4,7},{5,4},{6,5},{7,6},{8,11},{9,8},{10,9... | collective-permute-start | bytes 491528 | tf_op jit(solution)/shard_map/ppermute | solution.py:547
  9.7 1.7 %collective-permute-start.5 = (bf16[2,4,80,128]{3,2,1,0:T(8,128)(2,1)S(1)}, bf16[2,4,80,128]{3,2,1,0:T(8,128)(2,1)S(1)}, u32[]{:S(2)}, u32[]{:S(2)}) collective-permute-start(bf16[2,4,80,128]{3,2,1,0:T(8,128)(2,1)S(1)} %bitcast.32), channel_id=1, source_target_pairs={{0,3},{1,0},{2,1},{3,2},{4,7},{5,4},{6,5},{7,6},{8,11},{9,8},{10,9... | collective-permute-start | bytes 491528 | tf_op jit(solution)/shard_map/ppermute | solution.py:547
  13.7 1.0 %copy-done.1 = bf16[9,80,320]{2,1,0:T(8,128)(2,1)S(1)} copy-done((bf16[9,80,320]{2,1,0:T(8,128)(2,1)S(1)}, bf16[9,80,320]{2,1,0:T(8,128)(2,1)}, u32[]{:S(2)}) %copy-start.1) | copy-done | bytes 460824
  16.5 2.3 %shard_map.176 = (f32[160,512]{1,0:T(8,128)S(1)}, f32[160,128]{1,0:T(8,128)S(1)}, f32[160,128]{1,0:T(8,128)S(1)}, bf16[992,128]{1,0:T(8,128)(2,1)S(1)}, bf16[992...) custom-call(s32[7]{0:T(128)S(1)} %stack.31.place_ref.t_ref.edge_ref.x_ref, bf16[2,4,80,128]{3,2,1,0:T(8,128)(2,1)S(1)} %bitcast.37, ...), custom_call_target="tpu_custom_call" | custom-call | flops 471859200 | bytes 2869276 | tf_op jit(solution)/shard_map/pallas_call | solution.py:33
  18.9 3.4 %collective-permute-start.6 = (bf16[992,128]{1,0:T(8,128)(2,1)S(1)}, bf16[992,128]{1,0:T(8,128)(2,1)S(1)}, u32[]{:S(2)}, u32[]{:S(2)}) collective-permute-start(bf16[992,128]{1,0:T(8,128)(2,1)S(1)} %get-tuple-element.58), channel_id=1, source_target_pairs={{0,4},{4,0},{8,12},{12,8},{16,20},{20,16},{24,28},{28,24},{1,5},{5... | collective-permute-start | bytes 761864 | tf_op jit(solution)/shard_map/ppermute | solution.py:587
  22.3 1.7 %shard_map.177 = (f32[160,512]{1,0:T(8,128)S(1)}, f32[160,128]{1,0:T(8,128)S(1)}, f32[160,128]{1,0:T(8,128)S(1)}, bf16[640,128]{1,0:T(8,128)(2,1)S(1)}, bf16[640,128]{1,0:T(8,128)(2,1)S(1)}) custom-call(s32[7]{0:T(128)S(1)} %stack.31.place_ref.t_ref.edge_ref.x_ref, bf16[2,4,80,128]{3,2,1,0:T(8,128)(2,1)S(1)} %bitcast.33, ...), custom_call_target="tpu_custom_call" | custom-call | flops 471859200 | bytes 2017308 | tf_op jit(solution)/shard_map/pallas_call | solution.py:33
  24.0 1.7 %collective-permute-start.8 = (bf16[640,128]{1,0:T(8,128)(2,1)S(1)}, bf16[640,128]{1,0:T(8,128)(2,1)S(1)}, u32[]{:S(2)}, u32[]{:S(2)}) collective-permute-start(bf16[640,128]{1,0:T(8,128)(2,1)S(1)} %get-tuple-element.60), channel_id=1, source_target_pairs={{0,4},{4,0},{8,12},{12,8},{16,20},{20,16},{24,28},{28,24},{1,5},{5... | collective-permute-start | bytes 491528 | tf_op jit(solution)/shard_map/ppermute | solution.py:598
  26.7 4.0 %collective-permute-done.9.got_br = bf16[640,128]{1,0:T(8,128)(2,1)S(1)} collective-permute-done((bf16[640,128]{1,0:T(8,128)(2,1)S(1)}, bf16[640,128]{1,0:T(8,128)(2,1)S(1)}, u32[]{:S(2)}, u32[]{:S(2)}) %collective-permute-start.9) | collective-permute-done | bytes 163872 | tf_op jit(solution)/shard_map/ppermute | solution.py:597
  30.7 1.0 %shard_map.178 = (f32[160,1280]{1,0:T(8,128)S(1)}, f32[160,768]{1,0:T(8,128)S(1)}, f32[8,8,128]{2,1,0:T(8,128)S(1)}, f32[8,16,128]{2,1,0:T(8,128)S(1)}) custom-call(s32[7]{0:T(128)S(1)} %stack.31.place_ref.t_ref.edge_ref.x_ref, f32[160,512]{1,0:T(8,128)S(1)} %get-tuple-element.50.pre_p, f32[160,128]{1,0:T(8,128)S(1)} %get-tuple-element.51.up_p, ...), custom_call_target="tpu_custom_call" | custom-call | flops 1000000 | bytes 3244060 | tf_op jit(solution)/shard_map/pallas_call | solution.py:33
  31.8 8.3 %all_to_all.15.sums_ref = f32[8,16,128]{2,1,0:T(8,128)S(1)} all-to-all(f32[8,16,128]{2,1,0:T(8,128)S(1)} %get-tuple-element.64), channel_id=1, replica_groups=mesh['dp'=8,'space'=8,'tensor'=4] {'space'}, dimensions={0} | all-to-all | bytes 131072 | tf_op jit(solution)/shard_map/all_to_all | solution.py:612
  40.1 1.6 %shard_map.179 = (f32[12,8,128]{2,1,0:T(8,128)S(1)}, bf16[160,512]{1,0:T(8,128)(2,1)S(1)}, f32[160,128]{1,0:T(8,128)S(1)}) custom-call(s32[7]{0:T(128)S(1)} %stack.31.place_ref.t_ref.edge_ref.x_ref, f32[160,1280]{1,0:T(8,128)S(1)} %get-tuple-element.62.ext_p, f32[160,768]{1,0:T(8,128)S(1)} %get-tuple-element.63.ext_r, ...), custom_call_target="tpu_custom_call" | custom-call | flops 10000000 | bytes 1799196 | tf_op jit(solution)/shard_map/pallas_call | solution.py:33
  42.4 3.0 %collective-permute-start.11 = (f32[12,8,128]{2,1,0:T(8,128)S(1)}, f32[12,8,128]{2,1,0:T(8,128)S(1)}, u32[]{:S(2)}, u32[]{:S(2)}) collective-permute-start(f32[12,8,128]{2,1,0:T(8,128)S(1)} %get-tuple-element.66.p0), channel_id=1, source_target_pairs={{0,2},{1,3},{2,0},{3,1},{4,6},{5,7},{6,4},{7,5},{8,10},{9,11},{10,... | collective-permute-start | bytes 147464 | tf_op jit(solution)/shard_map/ppermute | solution.py:620
  46.2 1.3 %collective-permute-done.11.p2 = f32[12,8,128]{2,1,0:T(8,128)S(1)} collective-permute-done((f32[12,8,128]{2,1,0:T(8,128)S(1)}, f32[12,8,128]{2,1,0:T(8,128)S(1)}, u32[]{:S(2)}, u32[]{:S(2)}) %collective-permute-start.11) | collective-permute-done | bytes 49184 | tf_op jit(solution)/shard_map/ppermute | solution.py:620
  47.5 1.4 %collective-permute-done.12.p3 = f32[12,8,128]{2,1,0:T(8,128)S(1)} collective-permute-done((f32[12,8,128]{2,1,0:T(8,128)S(1)}, f32[12,8,128]{2,1,0:T(8,128)S(1)}, u32[]{:S(2)}, u32[]{:S(2)}) %collective-permute-start.12) | collective-permute-done | bytes 49184 | tf_op jit(solution)/shard_map/ppermute | solution.py:620
  48.9 1.2 %shard_map.180 = (f32[160,768]{1,0:T(8,128)S(1)}, f32[32,128]{1,0:T(8,128)S(1)}, f32[8,24,128]{2,1,0:T(8,128)S(1)}) custom-call(s32[7]{0:T(128)S(1)} %stack.31.place_ref.t_ref.edge_ref.x_ref, f32[12,8,128]{2,1,0:T(8,128)S(1)} %get-tuple-element.66.p0, f32[12,8,128]{2,1,0:T(8,128)S(1)} %collective-permute-done.10.p1, ...), custom_call_target="tpu_custom_call" | custom-call | flops 10000000 | bytes 2005532 | tf_op jit(solution)/shard_map/pallas_call | solution.py:33
  50.2 9.3 %all_to_all.16.red_ref = f32[8,24,128]{2,1,0:T(8,128)S(1)} all-to-all(f32[8,24,128]{2,1,0:T(8,128)S(1)} %get-tuple-element.72), channel_id=1, replica_groups=mesh['dp'=8,'space'=8,'tensor'=4] {'space'}, dimensions={0} | all-to-all | bytes 196608 | tf_op jit(solution)/shard_map/all_to_all | solution.py:628
  59.4 2.2 %shard_map.181 = (f32[4,40,768]{2,1,0:T(8,128)S(1)}, bf16[4,48,768]{2,1,0:T(8,128)(2,1)S(1)}, f32[32,128]{1,0:T(8,128)S(1)}, f32[1,1]{1,0:T(1,128)}) custom-call(s32[7]{0:T(128)S(1)} %stack.31.place_ref.t_ref.edge_ref.x_ref, f32[160,768]{1,0:T(8,128)S(1)} %get-tuple-element.71.gnorm_ref, f32[160,1280]{1,0:T(8,128)S(1)} %get-tuple-element.62.ext_p, ...), custom_call_target="tpu_custom_call" | custom-call | flops 471859200 | bytes 2965536 | tf_op jit(solution)/shard_map/pallas_call | solution.py:33
  62.5 1.2 %collective-permute-done.13.got_ref = bf16[4,48,768]{2,1,0:T(8,128)(2,1)S(1)} collective-permute-done((bf16[4,48,768]{2,1,0:T(8,128)(2,1)S(1)}, bf16[4,48,768]{2,1,0:T(8,128)(2,1)S(1)}, u32[]{:S(2)}, u32[]{:S(2)}) %collective-permute-start.13) | collective-permute-done | bytes 294944 | tf_op jit(solution)/shard_map/ppermute | solution.py:637
  64.7 1.8 %collective-permute-start.15 = (bf16[48,768]{1,0:T(8,128)(2,1)S(1)}, bf16[48,768]{1,0:T(8,128)(2,1)S(1)}, u32[]{:S(2)}, u32[]{:S(2)}) collective-permute-start(bf16[48,768]{1,0:T(8,128)(2,1)S(1)} %get-tuple-element.81), channel_id=1, source_target_pairs={{0,16},{4,20},{8,24},{12,28},{16,0},{20,4},{24,8},{28,12},{1,17},{... | collective-permute-start | bytes 221192 | tf_op jit(solution)/shard_map/ppermute | solution.py:646
  67.2 2.3 %collective-permute-done.14.r1 = bf16[48,768]{1,0:T(8,128)(2,1)S(1)} collective-permute-done((bf16[48,768]{1,0:T(8,128)(2,1)S(1)}, bf16[48,768]{1,0:T(8,128)(2,1)S(1)}, u32[]{:S(2)}, u32[]{:S(2)}) %collective-permute-start.14) | collective-permute-done | bytes 73760 | tf_op jit(solution)/shard_map/ppermute | solution.py:646
  71.0 15.7 %all_to_all.17.got_ref = bf16[8,56,128]{2,1,0:T(8,128)(2,1)S(1)} all-to-all(bf16[8,56,128]{2,1,0:T(8,128)(2,1)S(1)} %shard_map.183), channel_id=1, replica_groups=mesh['dp'=8,'space'=8,'tensor'=4] {'dp'}, dimensions={0} | all-to-all | bytes 229376 | tf_op jit(solution)/shard_map/all_to_all | solution.py:655
  (50 shorter events, 12.0 us)
Async XLA Ops:
  0.6 12.3 %copy-start = (bf16[9,80,320]{2,1,0:T(8,128)(2,1)S(1)}, bf16[9,80,320]{2,1,0:T(8,128)(2,1)}, u32[]{:S(2)}) copy-start(bf16[9,80,320]{2,1,0:T(8,128)(2,1)} %param.19) | copy-start | bytes 1382404
  1.6 8.1 %collective-permute-start = (bf16[2,4,80,128]{3,2,1,0:T(8,128)(2,1)S(1)}, bf16[2,4,80,128]{3,2,1,0:T(8,128)(2,1)S(1)}, u32[]{:S(2)}, u32[]{:S(2)}) collective-permute-start(bf16[2,4,80,128]{3,2,1,0:T(8,128)(2,1)S(1)} %bitcast.34), channel_id=1, source_target_pairs={{0,1},{1,2},{2,3},{3,0},{4,5},{5,6},{6,7},{7,4},{8,9},{9,10},{10,1... | collective-permute-start | bytes 491528 | tf_op jit(solution)/shard_map/ppermute | solution.py:547
  3.8 12.7 %collective-permute-start.1 = (bf16[2,4,80,128]{3,2,1,0:T(8,128)(2,1)S(1)}, bf16[2,4,80,128]{3,2,1,0:T(8,128)(2,1)S(1)}, u32[]{:S(2)}, u32[]{:S(2)}) collective-permute-start(bf16[2,4,80,128]{3,2,1,0:T(8,128)(2,1)S(1)} %bitcast.35), channel_id=1, source_target_pairs={{0,2},{1,3},{2,0},{3,1},{4,6},{5,7},{6,4},{7,5},{8,10},{9,11},{10,... | collective-permute-start | bytes 491528 | tf_op jit(solution)/shard_map/ppermute | solution.py:547
  6.5 10.1 %collective-permute-start.2 = (bf16[2,4,80,128]{3,2,1,0:T(8,128)(2,1)S(1)}, bf16[2,4,80,128]{3,2,1,0:T(8,128)(2,1)S(1)}, u32[]{:S(2)}, u32[]{:S(2)}) collective-permute-start(bf16[2,4,80,128]{3,2,1,0:T(8,128)(2,1)S(1)} %bitcast.36), channel_id=1, source_target_pairs={{0,3},{1,0},{2,1},{3,2},{4,7},{5,4},{6,5},{7,6},{8,11},{9,8},{10,9... | collective-permute-start | bytes 491528 | tf_op jit(solution)/shard_map/ppermute | solution.py:547
  8.5 13.8 %collective-permute-start.3 = (bf16[2,4,80,128]{3,2,1,0:T(8,128)(2,1)S(1)}, bf16[2,4,80,128]{3,2,1,0:T(8,128)(2,1)S(1)}, u32[]{:S(2)}, u32[]{:S(2)}) collective-permute-start(bf16[2,4,80,128]{3,2,1,0:T(8,128)(2,1)S(1)} %bitcast.30), channel_id=1, source_target_pairs={{0,1},{1,2},{2,3},{3,0},{4,5},{5,6},{6,7},{7,4},{8,9},{9,10},{10,1... | collective-permute-start | bytes 491528 | tf_op jit(solution)/shard_map/ppermute | solution.py:547
  8.9 13.3 %collective-permute-start.4 = (bf16[2,4,80,128]{3,2,1,0:T(8,128)(2,1)S(1)}, bf16[2,4,80,128]{3,2,1,0:T(8,128)(2,1)S(1)}, u32[]{:S(2)}, u32[]{:S(2)}) collective-permute-start(bf16[2,4,80,128]{3,2,1,0:T(8,128)(2,1)S(1)} %bitcast.31), channel_id=1, source_target_pairs={{0,2},{1,3},{2,0},{3,1},{4,6},{5,7},{6,4},{7,5},{8,10},{9,11},{10,... | collective-permute-start | bytes 491528 | tf_op jit(solution)/shard_map/ppermute | solution.py:547
  9.7 12.5 %collective-permute-start.5 = (bf16[2,4,80,128]{3,2,1,0:T(8,128)(2,1)S(1)}, bf16[2,4,80,128]{3,2,1,0:T(8,128)(2,1)S(1)}, u32[]{:S(2)}, u32[]{:S(2)}) collective-permute-start(bf16[2,4,80,128]{3,2,1,0:T(8,128)(2,1)S(1)} %bitcast.32), channel_id=1, source_target_pairs={{0,3},{1,0},{2,1},{3,2},{4,7},{5,4},{6,5},{7,6},{8,11},{9,8},{10,9... | collective-permute-start | bytes 491528 | tf_op jit(solution)/shard_map/ppermute | solution.py:547
  11.4 1.5 %copy-start.6 = (f32[80]{0:T(128)S(1)}, f32[80]{0:T(128)}, u32[]{:S(2)}) copy-start(f32[80]{0:T(128)} %param.21) | copy-start | bytes 964
  11.4 1.5 %copy-start.7 = (f32[80]{0:T(128)S(1)}, f32[80]{0:T(128)}, u32[]{:S(2)}) copy-start(f32[80]{0:T(128)} %param.22) | copy-start | bytes 964
  11.4 1.5 %copy-start.8 = (f32[80]{0:T(128)S(1)}, f32[80]{0:T(128)}, u32[]{:S(2)}) copy-start(f32[80]{0:T(128)} %param.23) | copy-start | bytes 964
  11.4 1.5 %copy-start.9 = (f32[80]{0:T(128)S(1)}, f32[80]{0:T(128)}, u32[]{:S(2)}) copy-start(f32[80]{0:T(128)} %param.24) | copy-start | bytes 964
  11.4 1.6 %copy-start.10 = (f32[80]{0:T(128)S(1)}, f32[80]{0:T(128)}, u32[]{:S(2)}) copy-start(f32[80]{0:T(128)} %param.25) | copy-start | bytes 964
  11.5 1.5 %copy-start.11 = (f32[80]{0:T(128)S(1)}, f32[80]{0:T(128)}, u32[]{:S(2)}) copy-start(f32[80]{0:T(128)} %param.26) | copy-start | bytes 964
  18.9 11.9 %collective-permute-start.6 = (bf16[992,128]{1,0:T(8,128)(2,1)S(1)}, bf16[992,128]{1,0:T(8,128)(2,1)S(1)}, u32[]{:S(2)}, u32[]{:S(2)}) collective-permute-start(bf16[992,128]{1,0:T(8,128)(2,1)S(1)} %get-tuple-element.58), channel_id=1, source_target_pairs={{0,4},{4,0},{8,12},{12,8},{16,20},{20,16},{24,28},{28,24},{1,5},{5... | collective-permute-start | bytes 761864 | tf_op jit(solution)/shard_map/ppermute | solution.py:587
  22.3 8.5 %collective-permute-start.7 = (bf16[992,128]{1,0:T(8,128)(2,1)S(1)}, bf16[992,128]{1,0:T(8,128)(2,1)S(1)}, u32[]{:S(2)}, u32[]{:S(2)}) collective-permute-start(bf16[992,128]{1,0:T(8,128)(2,1)S(1)} %get-tuple-element.59), channel_id=1, source_target_pairs={{0,28},{4,8},{8,4},{12,16},{16,12},{20,24},{24,20},{28,0},{1,29},{... | collective-permute-start | bytes 761864 | tf_op jit(solution)/shard_map/ppermute | solution.py:586
  24.0 2.7 %collective-permute-start.8 = (bf16[640,128]{1,0:T(8,128)(2,1)S(1)}, bf16[640,128]{1,0:T(8,128)(2,1)S(1)}, u32[]{:S(2)}, u32[]{:S(2)}) collective-permute-start(bf16[640,128]{1,0:T(8,128)(2,1)S(1)} %get-tuple-element.60), channel_id=1, source_target_pairs={{0,4},{4,0},{8,12},{12,8},{16,20},{20,16},{24,28},{28,24},{1,5},{5... | collective-permute-start | bytes 491528 | tf_op jit(solution)/shard_map/ppermute | solution.py:598
  25.7 5.0 %collective-permute-start.9 = (bf16[640,128]{1,0:T(8,128)(2,1)S(1)}, bf16[640,128]{1,0:T(8,128)(2,1)S(1)}, u32[]{:S(2)}, u32[]{:S(2)}) collective-permute-start(bf16[640,128]{1,0:T(8,128)(2,1)S(1)} %get-tuple-element.61), channel_id=1, source_target_pairs={{0,28},{4,8},{8,4},{12,16},{16,12},{20,24},{24,20},{28,0},{1,29},{... | collective-permute-start | bytes 491528 | tf_op jit(solution)/shard_map/ppermute | solution.py:597
  41.8 4.5 %collective-permute-start.10 = (f32[12,8,128]{2,1,0:T(8,128)S(1)}, f32[12,8,128]{2,1,0:T(8,128)S(1)}, u32[]{:S(2)}, u32[]{:S(2)}) collective-permute-start(f32[12,8,128]{2,1,0:T(8,128)S(1)} %get-tuple-element.66.p0), channel_id=1, source_target_pairs={{0,1},{1,2},{2,3},{3,0},{4,5},{5,6},{6,7},{7,4},{8,9},{9,10},{10,1... | collective-permute-start | bytes 147464 | tf_op jit(solution)/shard_map/ppermute | solution.py:620
  42.4 5.1 %collective-permute-start.11 = (f32[12,8,128]{2,1,0:T(8,128)S(1)}, f32[12,8,128]{2,1,0:T(8,128)S(1)}, u32[]{:S(2)}, u32[]{:S(2)}) collective-permute-start(f32[12,8,128]{2,1,0:T(8,128)S(1)} %get-tuple-element.66.p0), channel_id=1, source_target_pairs={{0,2},{1,3},{2,0},{3,1},{4,6},{5,7},{6,4},{7,5},{8,10},{9,11},{10,... | collective-permute-start | bytes 147464 | tf_op jit(solution)/shard_map/ppermute | solution.py:620
  45.4 3.5 %collective-permute-start.12 = (f32[12,8,128]{2,1,0:T(8,128)S(1)}, f32[12,8,128]{2,1,0:T(8,128)S(1)}, u32[]{:S(2)}, u32[]{:S(2)}) collective-permute-start(f32[12,8,128]{2,1,0:T(8,128)S(1)} %get-tuple-element.66.p0), channel_id=1, source_target_pairs={{0,3},{1,0},{2,1},{3,2},{4,7},{5,4},{6,5},{7,6},{8,11},{9,8},{10,9... | collective-permute-start | bytes 147464 | tf_op jit(solution)/shard_map/ppermute | solution.py:620
  61.7 2.0 %collective-permute-start.13 = (bf16[4,48,768]{2,1,0:T(8,128)(2,1)S(1)}, bf16[4,48,768]{2,1,0:T(8,128)(2,1)S(1)}, u32[]{:S(2)}, u32[]{:S(2)}) collective-permute-start(bf16[4,48,768]{2,1,0:T(8,128)(2,1)S(1)} %get-tuple-element.78), channel_id=1, source_target_pairs={{0,4},{4,0},{8,12},{12,8},{16,20},{20,16},{24,28},{28,24},{1,5},{5... | collective-permute-start | bytes 884744 | tf_op jit(solution)/shard_map/ppermute | solution.py:637
  64.3 5.2 %collective-permute-start.14 = (bf16[48,768]{1,0:T(8,128)(2,1)S(1)}, bf16[48,768]{1,0:T(8,128)(2,1)S(1)}, u32[]{:S(2)}, u32[]{:S(2)}) collective-permute-start(bf16[48,768]{1,0:T(8,128)(2,1)S(1)} %get-tuple-element.80), channel_id=1, source_target_pairs={{0,8},{4,12},{8,16},{12,20},{16,24},{20,28},{24,0},{28,4},{1,9},{5... | collective-permute-start | bytes 221192 | tf_op jit(solution)/shard_map/ppermute | solution.py:646
  64.7 5.5 %collective-permute-start.15 = (bf16[48,768]{1,0:T(8,128)(2,1)S(1)}, bf16[48,768]{1,0:T(8,128)(2,1)S(1)}, u32[]{:S(2)}, u32[]{:S(2)}) collective-permute-start(bf16[48,768]{1,0:T(8,128)(2,1)S(1)} %get-tuple-element.81), channel_id=1, source_target_pairs={{0,16},{4,20},{8,24},{12,28},{16,0},{20,4},{24,8},{28,12},{1,17},{... | collective-permute-start | bytes 221192 | tf_op jit(solution)/shard_map/ppermute | solution.py:646
  66.5 4.5 %collective-permute-start.16 = (bf16[48,768]{1,0:T(8,128)(2,1)S(1)}, bf16[48,768]{1,0:T(8,128)(2,1)S(1)}, u32[]{:S(2)}, u32[]{:S(2)}) collective-permute-start(bf16[48,768]{1,0:T(8,128)(2,1)S(1)} %get-tuple-element.82), channel_id=1, source_target_pairs={{0,24},{4,28},{8,0},{12,4},{16,8},{20,12},{24,16},{28,20},{1,25},{... | collective-permute-start | bytes 221192 | tf_op jit(solution)/shard_map/ppermute | solution.py:646
  (5 other events, 4.3 us)

commit v5 on v4

--- a/solution.py
+++ b/solution.py
@@ -240,7 +240,7 @@
     bottom = place_ref[2] > 0
 
     def rows_at(side, lo, hi):
-        return jnp.where(odd, side[0][lo:hi, :].astype(F32), side[1][lo:hi, :].astype(F32))
+        return jnp.where(odd, side[0][lo:hi, :], side[1][lo:hi, :]).astype(F32)
 
     def got(side, index):
         return rows_at(side, index * 2 * CH, (index + 1) * 2 * CH)
@@ -280,9 +280,11 @@
         noise_ext[ROWS + 2 + index] = pair[0:8] + pair[8:16]
     for r in range(ROWS):
         noise_ext[2 + r] = noise_ref[r]
-    sums = exact_dot(members(), in_lanes(columns))
-    for peer in range(out_ref.shape[0]):
-        out_ref[peer] = sums
+    out_ref[...] = exact_dot(members(), in_lanes(columns))
+
+
+def add_kernel(one_ref, two_ref, out_ref):
+    out_ref[...] = one_ref[...] + two_ref[...]
 
 
 def moments(total):
@@ -296,18 +298,20 @@
 
 
 def hidden_kernel(
-    edge_ref, ext_p, ext_r, sums_ref, col_ref, lift_ref, part_ref, hid_ref, stat_ref
+    edge_ref, ext_p, ext_r, sums_ref, more_ref, col_ref, lift_ref, part_ref, hid_ref, stat_ref
 ):
-    stats = moments(jnp.sum(sums_ref[...], axis=0))
+    stats = moments(sums_ref[...] + more_ref[...])
     stat_ref[...] = in_lanes([stats[0][0], stats[0][1]])
     for m, (ext, halo, start) in enumerate(((ext_p, 3, 0), (ext_r, 1, 8))):
         mean, inv = stats[m]
         gain = col_ref[:, 2 * m : 2 * m + 1]
         shift = col_ref[:, 2 * m + 1 : 2 * m + 2]
+        slope = jnp.broadcast_to(inv * gain, (2 * CH, COLS))
+        offset = jnp.broadcast_to(shift - mean * (inv * gain), (2 * CH, COLS))
         pieces = []
         for index in range(ROWS + 2 * halo):
             value = ext[:, index * COLS : (index + 1) * COLS]
-            normed = ((value - mean) * inv) * gain + shift
+            normed = value * slope + offset
             hidden = normed * sigmoid(normed)
             if index < halo:
                 hidden = jnp.where(edge_ref[1] > 0, 0.0, hidden)
@@ -366,14 +370,15 @@
     cot = jnp.concatenate(blocks, axis=0).astype(BF16)
     dhidden = dot(drop_ref[...], cot)
     mean = stat_ref[:, 0:1]
-    inv = stat_ref[:, 1:2]
-    gain = col_ref[:, 0:1]
-    shift = col_ref[:, 1:2]
+    inv = jnp.broadcast_to(stat_ref[:, 1:2], (2 * CH, COLS))
+    base = jnp.broadcast_to(-mean * stat_ref[:, 1:2], (2 * CH, COLS))
+    gain = jnp.broadcast_to(col_ref[:, 0:1], (2 * CH, COLS))
+    shift = jnp.broadcast_to(col_ref[:, 1:2], (2 * CH, COLS))
     first = None
     second = None
     for index in range(ROWS + 2):
         lanes = slice(index * COLS, (index + 1) * COLS)
-        centered = (ext_p[:, (index + 2) * COLS : (index + 3) * COLS] - mean) * inv
+        centered = ext_p[:, (index + 2) * COLS : (index + 3) * COLS] * inv + base
         normed = centered * gain + shift
         gate = sigmoid(normed)
         gnorm = dhidden[:, lanes] * gate * (1.0 + normed * (1.0 - gate)) * gain
@@ -397,16 +402,15 @@
             lo = 4 * tap - 24
             head_ref[lo : lo + 4, CH:COLS] = head[:, 0 : COLS - CH]
             head_ref[lo + 12 : lo + 16, CH : 3 * CH - COLS] = head[:, COLS - CH : CH]
-    for peer in range(out_ref.shape[0]):
-        out_ref[peer, 0:16, :] = sums
-        out_ref[peer, 16:24, :] = error
+    out_ref[0:16, :] = sums
+    out_ref[16:24, :] = error
 
 
 def weight_kernel(
-    place_ref, gnorm_ref, ext_p, stat_ref, red_ref, fs_ref, head_ref,
+    place_ref, gnorm_ref, ext_p, stat_ref, red_ref, more_ref, fs_ref, head_ref,
     keep_ref, send_ref, both_ref, logit_ref, grad_ref
 ):
-    total = jnp.sum(red_ref[...], axis=0)
+    total = red_ref[...] + more_ref[...]
     row = lax.broadcasted_iota(jnp.int32, (8, COLS), 0)
     signed = jnp.where(row < 4, total[16:24], -total[16:24])
     gaps = jnp.sum(signed, axis=0, keepdims=True)
@@ -418,11 +422,15 @@
     wide = spread(total[0:16] / COUNT)
     mean = stat_ref[:, 0:1]
     inv = stat_ref[:, 1:2]
+    tilt = inv * inv * wide[:, 1:2]
+    base = jnp.broadcast_to(tilt * mean - inv * wide[:, 0:1], (2 * CH, COLS))
+    tilt = jnp.broadcast_to(tilt, (2 * CH, COLS))
+    inv = jnp.broadcast_to(inv, (2 * CH, COLS))
     parts = []
     for index in range(ROWS + 2):
-        centered = (ext_p[:, (index + 2) * COLS : (index + 3) * COLS] - mean) * inv
+        value = ext_p[:, (index + 2) * COLS : (index + 3) * COLS]
         gnorm = gnorm_ref[:, index * COLS : (index + 1) * COLS]
-        delta = inv * (gnorm - wide[:, 0:1] - centered * wide[:, 1:2])
+        delta = inv * gnorm - tilt * value + base
         if index == 0:
             delta = jnp.where(place_ref[1] > 0, 0.0, delta)
         if index == ROWS + 1:
@@ -575,6 +583,16 @@
 
     partner = [(i, i ^ 1) for i in range(space)]
     across = [(i, (i + 1 if i % 2 else i - 1) % space) for i in range(space)]
+    chips = space // 2
+    beside = [(i, 2 * ((i // 2) ^ 1) + i % 2) for i in range(space)]
+    facing = [(i, 2 * (chips - 1 - i // 2) + i % 2) for i in range(space)]
+
+    def spread_sum(value):
+        for pairs in (partner, beside):
+            other = lax.ppermute(value, "space", pairs)
+            (value,) = call(add_kernel, [value, other], [arr(value.shape, F32)], 10**4)
+        return value, lax.ppermute(value, "space", facing)
+
     pre_p, up_p, dn_p, to_ap, to_bp, feats = call(
         functools.partial(conv_kernel, False),
         [place, *parts_p, near_p, columns, noise_rows],
@@ -604,15 +622,15 @@
             arr((2 * CH, 10 * COLS), F32),
             arr((2 * CH, 6 * COLS), F32),
             arr((8, 8, COLS), F32),
-            arr((space, 16, COLS), F32),
+            arr((16, COLS), F32),
         ],
         10**6,
         smem=1,
     )
-    sums = lax.all_to_all(sums, "space", 0, 0, tiled=True)
+    sums, more = spread_sum(sums)
     part, hidden, stat = call(
         hidden_kernel,
-        [place, ext_p, ext_r, sums, columns, lift],
+        [place, ext_p, ext_r, sums, more, columns, lift],
         [arr((12, 8, COLS), F32), arr((2 * CH, PIX), BF16), thin],
         10**7,
         smem=1,
@@ -621,14 +639,14 @@
     gnorm, head, partial = call(
         back_kernel,
         [place, part, *others, noise_ext, ext_p, stat, columns, hidden, drop],
-        [arr((2 * CH, 6 * COLS), F32), arr((32, COLS), F32), arr((space, 24, COLS), F32)],
+        [arr((2 * CH, 6 * COLS), F32), arr((32, COLS), F32), arr((24, COLS), F32)],
         10**7,
         smem=1,
     )
-    partial = lax.all_to_all(partial, "space", 0, 0, tiled=True)
+    partial, extra = spread_sum(partial)
     keep, send, both, logits = call(
         weight_kernel,
-        [place, gnorm, ext_p, stat, partial, feats, head],
+        [place, gnorm, ext_p, stat, partial, extra, feats, head],
         [arr((4, 40, 768), F32), arr((4, 48, 768), BF16), arr((32, COLS), F32), arr((1, 1), F32)],
         conv_flops,
         smem=1,

time: 89.1 us -> 92.3 us (1.036)
  blocking collectives: 33.4 us -> 15.7 us
  waiting for transfers between devices: 12.5 us -> 24.2 us
  starting transfers between devices: 22.3 us -> 31.5 us
    all_to_all x2 -> x0, blocking collectives: 17.6 us -> none  [the longest x1 9.29 us: body(): partial = lax.all_to_all(partial, 'space', 0, 0, tiled=True)]
    ppermute x0 -> x6, waiting for transfers between devices: none -> 12.2 us  [the longest x4 6.7 us: spread_sum(): other = lax.ppermute(value, 'space', pairs)]
    ppermute x0 -> x6, starting transfers between devices: none -> 7.38 us  [the longest x4 5.4 us: spread_sum(): other = lax.ppermute(value, 'space', pairs)]
    ppermute x1, starting transfers between devices: 0.83 us -> 2.64 us  [body(): got = lax.ppermute(send, 'space', partner)]
    pallas_call x10 -> x14, Pallas kernels: 12.4 us -> 12.5 us  [call(): pl.pallas_call(kernel, out_shape=outs, in_specs=[SM] * smem + [VM] * (len...]
  transfers between devices with their start and end apart: 17 -> 23, of which waited for: 8 -> 13; matrix products, arithmetic and copies ran while one was open for 1% -> 1% of each run, Pallas kernels for 6% -> 5%
where the time goes in v5:
time: 92.3 us; the launch traced here: 90.9 us
  starting transfers between devices  31.5 us (34%)
  waiting for transfers between devices  24.2 us (26%)
  blocking collectives  15.7 us (17%)
  Pallas kernels  12.5 us (14%)
  local copies, waits for them, and re-layouts  4.72 us (5%)
  between operations  2.21 us (2%)
    all_to_all x1, blocking collectives, body(): packed = lax.all_to_all(packed, 'dp', 0, 0, tiled=True)  15.7 us
    pallas_call x14, Pallas kernels, call(): pl.pallas_call(kernel, out_shape=outs, in_specs=[SM] * smem + [VM] * (len...  12.5 us
    ppermute x6, starting transfers between devices, gather(): lax.ppermute(own, 'tensor', ring('tensor', k))  8.85 us
    ppermute x4, waiting for transfers between devices, spread_sum(): other = lax.ppermute(value, 'space', pairs)  6.7 us
    ppermute x2, waiting for transfers between devices, spread_sum(): return (value, lax.ppermute(value, 'space', facing))  5.49 us
    ppermute x4, starting transfers between devices, spread_sum(): other = lax.ppermute(value, 'space', pairs)  5.4 us
    ppermute x3, starting transfers between devices, body(): lax.ppermute(part, 'tensor', ring('tensor', k))  4.58 us
    ppermute x1, waiting for transfers between devices, body(): got_br = lax.ppermute(to_br, 'space', across)  4.01 us
  transfers between devices with their start and end apart: 23, of which 13 were waited for; matrix products, arithmetic and copies ran while one was open for 1% of the time, Pallas kernels for 5%

profile of v5, /device:TPU:1, one launch (start us, length us, event | category | flops | bytes accessed | tf_op | source)
XLA Modules:
  0.0 90.9 jit_solution(16482329436932153302)
XLA Ops:
  1.6 2.2 %collective-permute-start = (bf16[2,4,80,128]{3,2,1,0:T(8,128)(2,1)S(1)}, bf16[2,4,80,128]{3,2,1,0:T(8,128)(2,1)S(1)}, u32[]{:S(2)}, u32[]{:S(2)}) collective-permute-start(bf16[2,4,80,128]{3,2,1,0:T(8,128)(2,1)S(1)} %bitcast.34), channel_id=1, source_target_pairs={{0,1},{1,2},{2,3},{3,0},{4,5},{5,6},{6,7},{7,4},{8,9},{9,10},{10,1... | collective-permute-start | bytes 491528 | tf_op jit(solution)/shard_map/ppermute | solution.py:555
  3.8 2.6 %collective-permute-start.1 = (bf16[2,4,80,128]{3,2,1,0:T(8,128)(2,1)S(1)}, bf16[2,4,80,128]{3,2,1,0:T(8,128)(2,1)S(1)}, u32[]{:S(2)}, u32[]{:S(2)}) collective-permute-start(bf16[2,4,80,128]{3,2,1,0:T(8,128)(2,1)S(1)} %bitcast.35), channel_id=1, source_target_pairs={{0,2},{1,3},{2,0},{3,1},{4,6},{5,7},{6,4},{7,5},{8,10},{9,11},{10,... | collective-permute-start | bytes 491528 | tf_op jit(solution)/shard_map/ppermute | solution.py:555
  9.7 1.7 %collective-permute-start.5 = (bf16[2,4,80,128]{3,2,1,0:T(8,128)(2,1)S(1)}, bf16[2,4,80,128]{3,2,1,0:T(8,128)(2,1)S(1)}, u32[]{:S(2)}, u32[]{:S(2)}) collective-permute-start(bf16[2,4,80,128]{3,2,1,0:T(8,128)(2,1)S(1)} %bitcast.32), channel_id=1, source_target_pairs={{0,3},{1,0},{2,1},{3,2},{4,7},{5,4},{6,5},{7,6},{8,11},{9,8},{10,9... | collective-permute-start | bytes 491528 | tf_op jit(solution)/shard_map/ppermute | solution.py:555
  16.5 2.3 %shard_map.176 = (f32[160,512]{1,0:T(8,128)S(1)}, f32[160,128]{1,0:T(8,128)S(1)}, f32[160,128]{1,0:T(8,128)S(1)}, bf16[992,128]{1,0:T(8,128)(2,1)S(1)}, bf16[992...) custom-call(s32[7]{0:T(128)S(1)} %stack.31.place_ref.t_ref.edge_ref.x_ref, bf16[2,4,80,128]{3,2,1,0:T(8,128)(2,1)S(1)} %bitcast.37, ...), custom_call_target="tpu_custom_call" | custom-call | flops 471859200 | bytes 2869276 | tf_op jit(solution)/shard_map/pallas_call | solution.py:33
  18.9 3.4 %collective-permute-start.6 = (bf16[992,128]{1,0:T(8,128)(2,1)S(1)}, bf16[992,128]{1,0:T(8,128)(2,1)S(1)}, u32[]{:S(2)}, u32[]{:S(2)}) collective-permute-start(bf16[992,128]{1,0:T(8,128)(2,1)S(1)} %get-tuple-element.58), channel_id=1, source_target_pairs={{0,4},{4,0},{8,12},{12,8},{16,20},{20,16},{24,28},{28,24},{1,5},{5... | collective-permute-start | bytes 761864 | tf_op jit(solution)/shard_map/ppermute | solution.py:605
  22.3 1.7 %shard_map.177 = (f32[160,512]{1,0:T(8,128)S(1)}, f32[160,128]{1,0:T(8,128)S(1)}, f32[160,128]{1,0:T(8,128)S(1)}, bf16[640,128]{1,0:T(8,128)(2,1)S(1)}, bf16[640,128]{1,0:T(8,128)(2,1)S(1)}) custom-call(s32[7]{0:T(128)S(1)} %stack.31.place_ref.t_ref.edge_ref.x_ref, bf16[2,4,80,128]{3,2,1,0:T(8,128)(2,1)S(1)} %bitcast.33, ...), custom_call_target="tpu_custom_call" | custom-call | flops 471859200 | bytes 2017308 | tf_op jit(solution)/shard_map/pallas_call | solution.py:33
  24.0 1.7 %collective-permute-start.8 = (bf16[640,128]{1,0:T(8,128)(2,1)S(1)}, bf16[640,128]{1,0:T(8,128)(2,1)S(1)}, u32[]{:S(2)}, u32[]{:S(2)}) collective-permute-start(bf16[640,128]{1,0:T(8,128)(2,1)S(1)} %get-tuple-element.60), channel_id=1, source_target_pairs={{0,4},{4,0},{8,12},{12,8},{16,20},{20,16},{24,28},{28,24},{1,5},{5... | collective-permute-start | bytes 491528 | tf_op jit(solution)/shard_map/ppermute | solution.py:616
  26.7 4.0 %collective-permute-done.9.got_br = bf16[640,128]{1,0:T(8,128)(2,1)S(1)} collective-permute-done((bf16[640,128]{1,0:T(8,128)(2,1)S(1)}, bf16[640,128]{1,0:T(8,128)(2,1)S(1)}, u32[]{:S(2)}, u32[]{:S(2)}) %collective-permute-start.9) | collective-permute-done | bytes 163872 | tf_op jit(solution)/shard_map/ppermute | solution.py:615
  33.6 2.5 %collective-permute-done.11.two_ref = f32[16,128]{1,0:T(8,128)S(1)} collective-permute-done((f32[16,128]{1,0:T(8,128)S(1)}, f32[16,128]{1,0:T(8,128)S(1)}, u32[]{:S(2)}, u32[]{:S(2)}) %collective-permute-start.11) | collective-permute-done | bytes 8224 | tf_op jit(solution)/shard_map/ppermute | solution.py:592
  36.2 1.4 %collective-permute-start.12 = (f32[16,128]{1,0:T(8,128)S(1)}, f32[16,128]{1,0:T(8,128)S(1)}, u32[]{:S(2)}, u32[]{:S(2)}) collective-permute-start(f32[16,128]{1,0:T(8,128)S(1)} %shard_map.180.sums_ref), channel_id=1, source_target_pairs={{0,24},{4,28},{8,16},{12,20},{16,8},{20,12},{24,0},{28,4},{1,25},{... | collective-permute-start | bytes 24584 | tf_op jit(solution)/shard_map/ppermute | solution.py:594
  37.5 2.4 %collective-permute-done.12.more_ref = f32[16,128]{1,0:T(8,128)S(1)} collective-permute-done((f32[16,128]{1,0:T(8,128)S(1)}, f32[16,128]{1,0:T(8,128)S(1)}, u32[]{:S(2)}, u32[]{:S(2)}) %collective-permute-start.12) | collective-permute-done | bytes 8224 | tf_op jit(solution)/shard_map/ppermute | solution.py:594
  39.9 1.7 %shard_map.181 = (f32[12,8,128]{2,1,0:T(8,128)S(1)}, bf16[160,512]{1,0:T(8,128)(2,1)S(1)}, f32[160,128]{1,0:T(8,128)S(1)}) custom-call(s32[7]{0:T(128)S(1)} %stack.31.place_ref.t_ref.edge_ref.x_ref, f32[160,1280]{1,0:T(8,128)S(1)} %get-tuple-element.62.ext_p, f32[160,768]{1,0:T(8,128)S(1)} %get-tuple-element.63.ext_r, f32[16,128]{1,0:T(8,128)S(1)} %shard_map.180.sums_ref, ...), custom_call_target="tpu_custom_call" | custom-call | flops 10000000 | bytes 1750044 | tf_op jit(solution)/shard_map/pallas_call | solution.py:33
  42.0 3.3 %collective-permute-start.14 = (f32[12,8,128]{2,1,0:T(8,128)S(1)}, f32[12,8,128]{2,1,0:T(8,128)S(1)}, u32[]{:S(2)}, u32[]{:S(2)}) collective-permute-start(f32[12,8,128]{2,1,0:T(8,128)S(1)} %get-tuple-element.66.p0), channel_id=1, source_target_pairs={{0,2},{1,3},{2,0},{3,1},{4,6},{5,7},{6,4},{7,5},{8,10},{9,11},{10,... | collective-permute-start | bytes 147464 | tf_op jit(solution)/shard_map/ppermute | solution.py:638
  46.2 1.2 %collective-permute-done.14.p2 = f32[12,8,128]{2,1,0:T(8,128)S(1)} collective-permute-done((f32[12,8,128]{2,1,0:T(8,128)S(1)}, f32[12,8,128]{2,1,0:T(8,128)S(1)}, u32[]{:S(2)}, u32[]{:S(2)}) %collective-permute-start.14) | collective-permute-done | bytes 49184 | tf_op jit(solution)/shard_map/ppermute | solution.py:638
  48.3 1.3 %shard_map.182 = (f32[160,768]{1,0:T(8,128)S(1)}, f32[32,128]{1,0:T(8,128)S(1)}, f32[24,128]{1,0:T(8,128)S(1)}) custom-call(s32[7]{0:T(128)S(1)} %stack.31.place_ref.t_ref.edge_ref.x_ref, f32[12,8,128]{2,1,0:T(8,128)S(1)} %get-tuple-element.66.p0, f32[12,8,128]{2,1,0:T(8,128)S(1)} %collective-permute-done.13.p1, ...), custom_call_target="tpu_custom_call" | custom-call | flops 10000000 | bytes 1919516 | tf_op jit(solution)/shard_map/pallas_call | solution.py:33
  49.6 4.4 %collective-permute-start.16 = (f32[24,128]{1,0:T(8,128)S(1)}, f32[24,128]{1,0:T(8,128)S(1)}, u32[]{:S(2)}, u32[]{:S(2)}) collective-permute-start(f32[24,128]{1,0:T(8,128)S(1)} %get-tuple-element.72.one_ref), channel_id=1, source_target_pairs={{0,4},{4,0},{8,12},{12,8},{16,20},{20,16},{24,28},{28,24},{1,5},{5... | collective-permute-start | bytes 36872 | tf_op jit(solution)/shard_map/ppermute | solution.py:592
  54.8 2.5 %collective-permute-done.17.two_ref = f32[24,128]{1,0:T(8,128)S(1)} collective-permute-done((f32[24,128]{1,0:T(8,128)S(1)}, f32[24,128]{1,0:T(8,128)S(1)}, u32[]{:S(2)}, u32[]{:S(2)}) %collective-permute-start.17) | collective-permute-done | bytes 12320 | tf_op jit(solution)/shard_map/ppermute | solution.py:592
  57.9 3.1 %collective-permute-done.18.more_ref = f32[24,128]{1,0:T(8,128)S(1)} collective-permute-done((f32[24,128]{1,0:T(8,128)S(1)}, f32[24,128]{1,0:T(8,128)S(1)}, u32[]{:S(2)}, u32[]{:S(2)}) %collective-permute-start.18) | collective-permute-done | bytes 12320 | tf_op jit(solution)/shard_map/ppermute | solution.py:594
  61.1 2.3 %shard_map.185 = (f32[4,40,768]{2,1,0:T(8,128)S(1)}, bf16[4,48,768]{2,1,0:T(8,128)(2,1)S(1)}, f32[32,128]{1,0:T(8,128)S(1)}, f32[1,1]{1,0:T(1,128)}) custom-call(s32[7]{0:T(128)S(1)} %stack.31.place_ref.t_ref.edge_ref.x_ref, f32[160,768]{1,0:T(8,128)S(1)} %get-tuple-element.71.gnorm_ref, f32[160,1280]{1,0:T(8,128)S(1)} %get-tuple-element.62.ext_p, ...), custom_call_target="tpu_custom_call" | custom-call | flops 471859200 | bytes 2891808 | tf_op jit(solution)/shard_map/pallas_call | solution.py:33
  63.3 2.6 %collective-permute-start.19 = (bf16[4,48,768]{2,1,0:T(8,128)(2,1)S(1)}, bf16[4,48,768]{2,1,0:T(8,128)(2,1)S(1)}, u32[]{:S(2)}, u32[]{:S(2)}) collective-permute-start(bf16[4,48,768]{2,1,0:T(8,128)(2,1)S(1)} %get-tuple-element.78), channel_id=1, source_target_pairs={{0,4},{4,0},{8,12},{12,8},{16,20},{20,16},{24,28},{28,24},{1,5},{5... | collective-permute-start | bytes 884744 | tf_op jit(solution)/shard_map/ppermute | solution.py:655
  66.0 1.2 %collective-permute-done.19.got_ref = bf16[4,48,768]{2,1,0:T(8,128)(2,1)S(1)} collective-permute-done((bf16[4,48,768]{2,1,0:T(8,128)(2,1)S(1)}, bf16[4,48,768]{2,1,0:T(8,128)(2,1)S(1)}, u32[]{:S(2)}, u32[]{:S(2)}) %collective-permute-start.19) | collective-permute-done | bytes 294944 | tf_op jit(solution)/shard_map/ppermute | solution.py:655
  67.9 1.8 %collective-permute-start.21 = (bf16[48,768]{1,0:T(8,128)(2,1)S(1)}, bf16[48,768]{1,0:T(8,128)(2,1)S(1)}, u32[]{:S(2)}, u32[]{:S(2)}) collective-permute-start(bf16[48,768]{1,0:T(8,128)(2,1)S(1)} %get-tuple-element.81), channel_id=1, source_target_pairs={{0,16},{4,20},{8,24},{12,28},{16,0},{20,4},{24,8},{28,12},{1,17},{... | collective-permute-start | bytes 221192 | tf_op jit(solution)/shard_map/ppermute | solution.py:664
  70.5 3.8 %collective-permute-done.20.r1 = bf16[48,768]{1,0:T(8,128)(2,1)S(1)} collective-permute-done((bf16[48,768]{1,0:T(8,128)(2,1)S(1)}, bf16[48,768]{1,0:T(8,128)(2,1)S(1)}, u32[]{:S(2)}, u32[]{:S(2)}) %collective-permute-start.20) | collective-permute-done | bytes 73760 | tf_op jit(solution)/shard_map/ppermute | solution.py:664
  74.5 15.7 %all_to_all.5.got_ref = bf16[8,56,128]{2,1,0:T(8,128)(2,1)S(1)} all-to-all(bf16[8,56,128]{2,1,0:T(8,128)(2,1)S(1)} %shard_map.187), channel_id=1, replica_groups=mesh['dp'=8,'space'=8,'tensor'=4] {'dp'}, dimensions={0} | all-to-all | bytes 229376 | tf_op jit(solution)/shard_map/all_to_all | solution.py:673
  (64 shorter events, 17.9 us)
Async XLA Ops:
  0.6 12.3 %copy-start = (bf16[9,80,320]{2,1,0:T(8,128)(2,1)S(1)}, bf16[9,80,320]{2,1,0:T(8,128)(2,1)}, u32[]{:S(2)}) copy-start(bf16[9,80,320]{2,1,0:T(8,128)(2,1)} %param.19) | copy-start | bytes 1382404
  1.6 8.1 %collective-permute-start = (bf16[2,4,80,128]{3,2,1,0:T(8,128)(2,1)S(1)}, bf16[2,4,80,128]{3,2,1,0:T(8,128)(2,1)S(1)}, u32[]{:S(2)}, u32[]{:S(2)}) collective-permute-start(bf16[2,4,80,128]{3,2,1,0:T(8,128)(2,1)S(1)} %bitcast.34), channel_id=1, source_target_pairs={{0,1},{1,2},{2,3},{3,0},{4,5},{5,6},{6,7},{7,4},{8,9},{9,10},{10,1... | collective-permute-start | bytes 491528 | tf_op jit(solution)/shard_map/ppermute | solution.py:555
  3.8 12.7 %collective-permute-start.1 = (bf16[2,4,80,128]{3,2,1,0:T(8,128)(2,1)S(1)}, bf16[2,4,80,128]{3,2,1,0:T(8,128)(2,1)S(1)}, u32[]{:S(2)}, u32[]{:S(2)}) collective-permute-start(bf16[2,4,80,128]{3,2,1,0:T(8,128)(2,1)S(1)} %bitcast.35), channel_id=1, source_target_pairs={{0,2},{1,3},{2,0},{3,1},{4,6},{5,7},{6,4},{7,5},{8,10},{9,11},{10,... | collective-permute-start | bytes 491528 | tf_op jit(solution)/shard_map/ppermute | solution.py:555
  6.5 10.1 %collective-permute-start.2 = (bf16[2,4,80,128]{3,2,1,0:T(8,128)(2,1)S(1)}, bf16[2,4,80,128]{3,2,1,0:T(8,128)(2,1)S(1)}, u32[]{:S(2)}, u32[]{:S(2)}) collective-permute-start(bf16[2,4,80,128]{3,2,1,0:T(8,128)(2,1)S(1)} %bitcast.36), channel_id=1, source_target_pairs={{0,3},{1,0},{2,1},{3,2},{4,7},{5,4},{6,5},{7,6},{8,11},{9,8},{10,9... | collective-permute-start | bytes 491528 | tf_op jit(solution)/shard_map/ppermute | solution.py:555
  8.5 13.8 %collective-permute-start.3 = (bf16[2,4,80,128]{3,2,1,0:T(8,128)(2,1)S(1)}, bf16[2,4,80,128]{3,2,1,0:T(8,128)(2,1)S(1)}, u32[]{:S(2)}, u32[]{:S(2)}) collective-permute-start(bf16[2,4,80,128]{3,2,1,0:T(8,128)(2,1)S(1)} %bitcast.30), channel_id=1, source_target_pairs={{0,1},{1,2},{2,3},{3,0},{4,5},{5,6},{6,7},{7,4},{8,9},{9,10},{10,1... | collective-permute-start | bytes 491528 | tf_op jit(solution)/shard_map/ppermute | solution.py:555
  8.9 13.3 %collective-permute-start.4 = (bf16[2,4,80,128]{3,2,1,0:T(8,128)(2,1)S(1)}, bf16[2,4,80,128]{3,2,1,0:T(8,128)(2,1)S(1)}, u32[]{:S(2)}, u32[]{:S(2)}) collective-permute-start(bf16[2,4,80,128]{3,2,1,0:T(8,128)(2,1)S(1)} %bitcast.31), channel_id=1, source_target_pairs={{0,2},{1,3},{2,0},{3,1},{4,6},{5,7},{6,4},{7,5},{8,10},{9,11},{10,... | collective-permute-start | bytes 491528 | tf_op jit(solution)/shard_map/ppermute | solution.py:555
  9.7 12.5 %collective-permute-start.5 = (bf16[2,4,80,128]{3,2,1,0:T(8,128)(2,1)S(1)}, bf16[2,4,80,128]{3,2,1,0:T(8,128)(2,1)S(1)}, u32[]{:S(2)}, u32[]{:S(2)}) collective-permute-start(bf16[2,4,80,128]{3,2,1,0:T(8,128)(2,1)S(1)} %bitcast.32), channel_id=1, source_target_pairs={{0,3},{1,0},{2,1},{3,2},{4,7},{5,4},{6,5},{7,6},{8,11},{9,8},{10,9... | collective-permute-start | bytes 491528 | tf_op jit(solution)/shard_map/ppermute | solution.py:555
  18.9 11.9 %collective-permute-start.6 = (bf16[992,128]{1,0:T(8,128)(2,1)S(1)}, bf16[992,128]{1,0:T(8,128)(2,1)S(1)}, u32[]{:S(2)}, u32[]{:S(2)}) collective-permute-start(bf16[992,128]{1,0:T(8,128)(2,1)S(1)} %get-tuple-element.58), channel_id=1, source_target_pairs={{0,4},{4,0},{8,12},{12,8},{16,20},{20,16},{24,28},{28,24},{1,5},{5... | collective-permute-start | bytes 761864 | tf_op jit(solution)/shard_map/ppermute | solution.py:605
  22.3 8.5 %collective-permute-start.7 = (bf16[992,128]{1,0:T(8,128)(2,1)S(1)}, bf16[992,128]{1,0:T(8,128)(2,1)S(1)}, u32[]{:S(2)}, u32[]{:S(2)}) collective-permute-start(bf16[992,128]{1,0:T(8,128)(2,1)S(1)} %get-tuple-element.59), channel_id=1, source_target_pairs={{0,28},{4,8},{8,4},{12,16},{16,12},{20,24},{24,20},{28,0},{1,29},{... | collective-permute-start | bytes 761864 | tf_op jit(solution)/shard_map/ppermute | solution.py:604
  24.0 2.8 %collective-permute-start.8 = (bf16[640,128]{1,0:T(8,128)(2,1)S(1)}, bf16[640,128]{1,0:T(8,128)(2,1)S(1)}, u32[]{:S(2)}, u32[]{:S(2)}) collective-permute-start(bf16[640,128]{1,0:T(8,128)(2,1)S(1)} %get-tuple-element.60), channel_id=1, source_target_pairs={{0,4},{4,0},{8,12},{12,8},{16,20},{20,16},{24,28},{28,24},{1,5},{5... | collective-permute-start | bytes 491528 | tf_op jit(solution)/shard_map/ppermute | solution.py:616
  25.7 5.0 %collective-permute-start.9 = (bf16[640,128]{1,0:T(8,128)(2,1)S(1)}, bf16[640,128]{1,0:T(8,128)(2,1)S(1)}, u32[]{:S(2)}, u32[]{:S(2)}) collective-permute-start(bf16[640,128]{1,0:T(8,128)(2,1)S(1)} %get-tuple-element.61), channel_id=1, source_target_pairs={{0,28},{4,8},{8,4},{12,16},{16,12},{20,24},{24,20},{28,0},{1,29},{... | collective-permute-start | bytes 491528 | tf_op jit(solution)/shard_map/ppermute | solution.py:615
  31.8 1.9 %collective-permute-start.10 = (f32[16,128]{1,0:T(8,128)S(1)}, f32[16,128]{1,0:T(8,128)S(1)}, u32[]{:S(2)}, u32[]{:S(2)}) collective-permute-start(f32[16,128]{1,0:T(8,128)S(1)} %get-tuple-element.64.one_ref), channel_id=1, source_target_pairs={{0,4},{4,0},{8,12},{12,8},{16,20},{20,16},{24,28},{28,24},{1,5},{5... | collective-permute-start | bytes 24584 | tf_op jit(solution)/shard_map/ppermute | solution.py:592
  33.6 2.5 %collective-permute-start.11 = (f32[16,128]{1,0:T(8,128)S(1)}, f32[16,128]{1,0:T(8,128)S(1)}, u32[]{:S(2)}, u32[]{:S(2)}) collective-permute-start(f32[16,128]{1,0:T(8,128)S(1)} %shard_map.179.one_ref), channel_id=1, source_target_pairs={{0,8},{4,12},{8,0},{12,4},{16,24},{20,28},{24,16},{28,20},{1,9},{5... | collective-permute-start | bytes 24584 | tf_op jit(solution)/shard_map/ppermute | solution.py:592
  36.2 3.7 %collective-permute-start.12 = (f32[16,128]{1,0:T(8,128)S(1)}, f32[16,128]{1,0:T(8,128)S(1)}, u32[]{:S(2)}, u32[]{:S(2)}) collective-permute-start(f32[16,128]{1,0:T(8,128)S(1)} %shard_map.180.sums_ref), channel_id=1, source_target_pairs={{0,24},{4,28},{8,16},{12,20},{16,8},{20,12},{24,0},{28,4},{1,25},{... | collective-permute-start | bytes 24584 | tf_op jit(solution)/shard_map/ppermute | solution.py:594
  41.6 4.6 %collective-permute-start.13 = (f32[12,8,128]{2,1,0:T(8,128)S(1)}, f32[12,8,128]{2,1,0:T(8,128)S(1)}, u32[]{:S(2)}, u32[]{:S(2)}) collective-permute-start(f32[12,8,128]{2,1,0:T(8,128)S(1)} %get-tuple-element.66.p0), channel_id=1, source_target_pairs={{0,1},{1,2},{2,3},{3,0},{4,5},{5,6},{6,7},{7,4},{8,9},{9,10},{10,1... | collective-permute-start | bytes 147464 | tf_op jit(solution)/shard_map/ppermute | solution.py:638
  42.0 5.3 %collective-permute-start.14 = (f32[12,8,128]{2,1,0:T(8,128)S(1)}, f32[12,8,128]{2,1,0:T(8,128)S(1)}, u32[]{:S(2)}, u32[]{:S(2)}) collective-permute-start(f32[12,8,128]{2,1,0:T(8,128)S(1)} %get-tuple-element.66.p0), channel_id=1, source_target_pairs={{0,2},{1,3},{2,0},{3,1},{4,6},{5,7},{6,4},{7,5},{8,10},{9,11},{10,... | collective-permute-start | bytes 147464 | tf_op jit(solution)/shard_map/ppermute | solution.py:638
  45.3 2.9 %collective-permute-start.15 = (f32[12,8,128]{2,1,0:T(8,128)S(1)}, f32[12,8,128]{2,1,0:T(8,128)S(1)}, u32[]{:S(2)}, u32[]{:S(2)}) collective-permute-start(f32[12,8,128]{2,1,0:T(8,128)S(1)} %get-tuple-element.66.p0), channel_id=1, source_target_pairs={{0,3},{1,0},{2,1},{3,2},{4,7},{5,4},{6,5},{7,6},{8,11},{9,8},{10,9... | collective-permute-start | bytes 147464 | tf_op jit(solution)/shard_map/ppermute | solution.py:638
  49.6 5.2 %collective-permute-start.16 = (f32[24,128]{1,0:T(8,128)S(1)}, f32[24,128]{1,0:T(8,128)S(1)}, u32[]{:S(2)}, u32[]{:S(2)}) collective-permute-start(f32[24,128]{1,0:T(8,128)S(1)} %get-tuple-element.72.one_ref), channel_id=1, source_target_pairs={{0,4},{4,0},{8,12},{12,8},{16,20},{20,16},{24,28},{28,24},{1,5},{5... | collective-permute-start | bytes 36872 | tf_op jit(solution)/shard_map/ppermute | solution.py:592
  54.8 2.5 %collective-permute-start.17 = (f32[24,128]{1,0:T(8,128)S(1)}, f32[24,128]{1,0:T(8,128)S(1)}, u32[]{:S(2)}, u32[]{:S(2)}) collective-permute-start(f32[24,128]{1,0:T(8,128)S(1)} %shard_map.183.one_ref), channel_id=1, source_target_pairs={{0,8},{4,12},{8,0},{12,4},{16,24},{20,28},{24,16},{28,20},{1,9},{5... | collective-permute-start | bytes 36872 | tf_op jit(solution)/shard_map/ppermute | solution.py:592
  57.3 3.8 %collective-permute-start.18 = (f32[24,128]{1,0:T(8,128)S(1)}, f32[24,128]{1,0:T(8,128)S(1)}, u32[]{:S(2)}, u32[]{:S(2)}) collective-permute-start(f32[24,128]{1,0:T(8,128)S(1)} %shard_map.184.red_ref), channel_id=1, source_target_pairs={{0,24},{4,28},{8,16},{12,20},{16,8},{20,12},{24,0},{28,4},{1,25},{... | collective-permute-start | bytes 36872 | tf_op jit(solution)/shard_map/ppermute | solution.py:594
  63.3 3.9 %collective-permute-start.19 = (bf16[4,48,768]{2,1,0:T(8,128)(2,1)S(1)}, bf16[4,48,768]{2,1,0:T(8,128)(2,1)S(1)}, u32[]{:S(2)}, u32[]{:S(2)}) collective-permute-start(bf16[4,48,768]{2,1,0:T(8,128)(2,1)S(1)} %get-tuple-element.78), channel_id=1, source_target_pairs={{0,4},{4,0},{8,12},{12,8},{16,20},{20,16},{24,28},{28,24},{1,5},{5... | collective-permute-start | bytes 884744 | tf_op jit(solution)/shard_map/ppermute | solution.py:655
  67.8 6.5 %collective-permute-start.20 = (bf16[48,768]{1,0:T(8,128)(2,1)S(1)}, bf16[48,768]{1,0:T(8,128)(2,1)S(1)}, u32[]{:S(2)}, u32[]{:S(2)}) collective-permute-start(bf16[48,768]{1,0:T(8,128)(2,1)S(1)} %get-tuple-element.80), channel_id=1, source_target_pairs={{0,8},{4,12},{8,16},{12,20},{16,24},{20,28},{24,0},{28,4},{1,9},{5... | collective-permute-start | bytes 221192 | tf_op jit(solution)/shard_map/ppermute | solution.py:664
  67.9 6.5 %collective-permute-start.21 = (bf16[48,768]{1,0:T(8,128)(2,1)S(1)}, bf16[48,768]{1,0:T(8,128)(2,1)S(1)}, u32[]{:S(2)}, u32[]{:S(2)}) collective-permute-start(bf16[48,768]{1,0:T(8,128)(2,1)S(1)} %get-tuple-element.81), channel_id=1, source_target_pairs={{0,16},{4,20},{8,24},{12,28},{16,0},{20,4},{24,8},{28,12},{1,17},{... | collective-permute-start | bytes 221192 | tf_op jit(solution)/shard_map/ppermute | solution.py:664
  69.7 4.7 %collective-permute-start.22 = (bf16[48,768]{1,0:T(8,128)(2,1)S(1)}, bf16[48,768]{1,0:T(8,128)(2,1)S(1)}, u32[]{:S(2)}, u32[]{:S(2)}) collective-permute-start(bf16[48,768]{1,0:T(8,128)(2,1)S(1)} %get-tuple-element.82), channel_id=1, source_target_pairs={{0,24},{4,28},{8,0},{12,4},{16,8},{20,12},{24,16},{28,20},{1,25},{... | collective-permute-start | bytes 221192 | tf_op jit(solution)/shard_map/ppermute | solution.py:664
  (11 other events, 13.5 us)

commit v6 on v4

--- a/solution.py
+++ b/solution.py
@@ -543,14 +543,17 @@
         ]
     )
 
-    def gather(own):
-        return [own] + [lax.ppermute(own, "tensor", ring("tensor", k)) for k in (1, 2, 3)]
+    def gather(own, way):
+        left = lax.ppermute(own, "tensor", ring("tensor", 1))
+        right = lax.ppermute(own, "tensor", ring("tensor", -1))
+        far = lax.ppermute(left if way > 0 else right, "tensor", ring("tensor", way))
+        return [own, left, far, right]
 
     own_p = feat_policy[0].transpose(0, 2, 1, 3)
     feat_ref, own_p = lax.optimization_barrier((feat_ref, own_p))
     own_r = feat_ref[0].transpose(0, 2, 1, 3)
-    parts_p = gather(own_p)
-    parts_r = gather(own_r)
+    parts_p = gather(own_p, -1)
+    parts_r = gather(own_r, 1)
 
     vectors = [b1_policy, b1_ref, gn_gain_policy, gn_bias_policy, gn_gain_ref, gn_bias_ref]
     columns, lift, drop, noise_rows, near_p, near_r = call(

time: 89.1 us -> 91.5 us (1.027)
  waiting for transfers between devices: 12.5 us -> 15.7 us
    ppermute x6, waiting for transfers between devices: 0.02 us -> 2.49 us  [the longest x2 1.76 us: gather(): right = lax.ppermute(own, 'tensor', ring('tensor', -1))]
    ppermute x1, starting transfers between devices: 0.01 us -> 1.2 us  [body(): got_bp = lax.ppermute(to_bp, 'space', across)]
  transfers between devices with their start and end apart: 17 -> 17, of which waited for: 8 -> 11; matrix products, arithmetic and copies ran while one was open for 1% -> 1% of each run, Pallas kernels for 6% -> 5%
where the time goes in v6:
time: 91.5 us; the launch traced here: 89.9 us
  blocking collectives  33.5 us (37%)
  starting transfers between devices  21.4 us (23%)
  waiting for transfers between devices  15.7 us (17%)
  Pallas kernels  12.4 us (14%)
  local copies, waits for them, and re-layouts  4.72 us (5%)
  between operations  2.2 us (2%)
    all_to_all x1, blocking collectives, body(): packed = lax.all_to_all(packed, 'dp', 0, 0, tiled=True)  15.7 us
    pallas_call x10, Pallas kernels, call(): pl.pallas_call(kernel, out_shape=outs, in_specs=[SM] * smem + [VM] * (len...  12.4 us
    all_to_all x1, blocking collectives, body(): partial = lax.all_to_all(partial, 'space', 0, 0, tiled=True)  9.55 us
    all_to_all x1, blocking collectives, body(): sums = lax.all_to_all(sums, 'space', 0, 0, tiled=True)  8.24 us
    ppermute x3, starting transfers between devices, body(): lax.ppermute(part, 'tensor', ring('tensor', k))  4.21 us
    ppermute x2, starting transfers between devices, gather(): lax.ppermute(left if way > 0 else right, 'tensor', ring('tensor', way))  4.14 us
    ppermute x1, waiting for transfers between devices, body(): got_br = lax.ppermute(to_br, 'space', across)  4.01 us
    ppermute x3, waiting for transfers between devices, body(): lax.ppermute(sent, 'space', ring('space', 2 * k))  3.76 us
  transfers between devices with their start and end apart: 17, of which 11 were waited for; matrix products, arithmetic and copies ran while one was open for 1% of the time, Pallas kernels for 5%

profile of v6, /device:TPU:1, one launch (start us, length us, event | category | flops | bytes accessed | tf_op | source)
XLA Modules:
  0.0 89.9 jit_solution(5389931274166532530)
XLA Ops:
  1.6 3.6 %collective-permute-start.1 = (bf16[2,4,80,128]{3,2,1,0:T(8,128)(2,1)S(1)}, bf16[2,4,80,128]{3,2,1,0:T(8,128)(2,1)S(1)}, u32[]{:S(2)}, u32[]{:S(2)}) collective-permute-start(bf16[2,4,80,128]{3,2,1,0:T(8,128)(2,1)S(1)} %bitcast.33), channel_id=1, source_target_pairs={{0,3},{1,0},{2,1},{3,2},{4,7},{5,4},{6,5},{7,6},{8,11},{9,8},{10,9... | collective-permute-start | bytes 491528 | tf_op jit(solution)/shard_map/ppermute | solution.py:548
  6.4 1.8 %collective-permute-done.1.f3 = bf16[2,4,80,128]{3,2,1,0:T(8,128)(2,1)S(1)} collective-permute-done((bf16[2,4,80,128]{3,2,1,0:T(8,128)(2,1)S(1)}, bf16[2,4,80,128]{3,2,1,0:T(8,128)(2,1)S(1)}, u32[]{:S(2)}, u32[]{:S(2)}) %collective-permute-start.1) | collective-permute-done | bytes 163872 | tf_op jit(solution)/shard_map/ppermute | solution.py:548
  8.2 3.4 %collective-permute-start.2 = (bf16[2,4,80,128]{3,2,1,0:T(8,128)(2,1)S(1)}, bf16[2,4,80,128]{3,2,1,0:T(8,128)(2,1)S(1)}, u32[]{:S(2)}, u32[]{:S(2)}) collective-permute-start(bf16[2,4,80,128]{3,2,1,0:T(8,128)(2,1)S(1)} %collective-permute-done.1.f3), channel_id=1, source_target_pairs={{0,3},{1,0},{2,1},{3,2},{4,7},{5,4},{6,5},{7,6},{8,11},{9,8},{10,9... | collective-permute-start | bytes 491528 | tf_op jit(solution)/shard_map/ppermute | solution.py:549
  15.3 1.0 %copy-done.1 = bf16[9,80,320]{2,1,0:T(8,128)(2,1)S(1)} copy-done((bf16[9,80,320]{2,1,0:T(8,128)(2,1)S(1)}, bf16[9,80,320]{2,1,0:T(8,128)(2,1)}, u32[]{:S(2)}) %copy-start.1) | copy-done | bytes 460824
  18.1 2.3 %shard_map.176 = (f32[160,512]{1,0:T(8,128)S(1)}, f32[160,128]{1,0:T(8,128)S(1)}, f32[160,128]{1,0:T(8,128)S(1)}, bf16[992,128]{1,0:T(8,128)(2,1)S(1)}, bf16[992...) custom-call(s32[7]{0:T(128)S(1)} %stack.31.place_ref.t_ref.edge_ref.x_ref, bf16[2,4,80,128]{3,2,1,0:T(8,128)(2,1)S(1)} %bitcast.35, ...), custom_call_target="tpu_custom_call" | custom-call | flops 471859200 | bytes 2869276 | tf_op jit(solution)/shard_map/pallas_call | solution.py:33
  20.5 2.6 %collective-permute-start.6 = (bf16[992,128]{1,0:T(8,128)(2,1)S(1)}, bf16[992,128]{1,0:T(8,128)(2,1)S(1)}, u32[]{:S(2)}, u32[]{:S(2)}) collective-permute-start(bf16[992,128]{1,0:T(8,128)(2,1)S(1)} %get-tuple-element.58), channel_id=1, source_target_pairs={{0,4},{4,0},{8,12},{12,8},{16,20},{20,16},{24,28},{28,24},{1,5},{5... | collective-permute-start | bytes 761864 | tf_op jit(solution)/shard_map/ppermute | solution.py:590
  23.0 1.2 %collective-permute-start.7 = (bf16[992,128]{1,0:T(8,128)(2,1)S(1)}, bf16[992,128]{1,0:T(8,128)(2,1)S(1)}, u32[]{:S(2)}, u32[]{:S(2)}) collective-permute-start(bf16[992,128]{1,0:T(8,128)(2,1)S(1)} %get-tuple-element.59), channel_id=1, source_target_pairs={{0,28},{4,8},{8,4},{12,16},{16,12},{20,24},{24,20},{28,0},{1,29},{... | collective-permute-start | bytes 761864 | tf_op jit(solution)/shard_map/ppermute | solution.py:589
  24.2 1.7 %shard_map.177 = (f32[160,512]{1,0:T(8,128)S(1)}, f32[160,128]{1,0:T(8,128)S(1)}, f32[160,128]{1,0:T(8,128)S(1)}, bf16[640,128]{1,0:T(8,128)(2,1)S(1)}, bf16[640,128]{1,0:T(8,128)(2,1)S(1)}) custom-call(s32[7]{0:T(128)S(1)} %stack.31.place_ref.t_ref.edge_ref.x_ref, bf16[2,4,80,128]{3,2,1,0:T(8,128)(2,1)S(1)} %bitcast.32, ...), custom_call_target="tpu_custom_call" | custom-call | flops 471859200 | bytes 2017308 | tf_op jit(solution)/shard_map/pallas_call | solution.py:33
  25.9 1.8 %collective-permute-start.8 = (bf16[640,128]{1,0:T(8,128)(2,1)S(1)}, bf16[640,128]{1,0:T(8,128)(2,1)S(1)}, u32[]{:S(2)}, u32[]{:S(2)}) collective-permute-start(bf16[640,128]{1,0:T(8,128)(2,1)S(1)} %get-tuple-element.60), channel_id=1, source_target_pairs={{0,4},{4,0},{8,12},{12,8},{16,20},{20,16},{24,28},{28,24},{1,5},{5... | collective-permute-start | bytes 491528 | tf_op jit(solution)/shard_map/ppermute | solution.py:601
  27.7 1.0 %collective-permute-done.8.got_ar = bf16[640,128]{1,0:T(8,128)(2,1)S(1)} collective-permute-done((bf16[640,128]{1,0:T(8,128)(2,1)S(1)}, bf16[640,128]{1,0:T(8,128)(2,1)S(1)}, u32[]{:S(2)}, u32[]{:S(2)}) %collective-permute-start.8) | collective-permute-done | bytes 163872 | tf_op jit(solution)/shard_map/ppermute | solution.py:601
  28.7 4.0 %collective-permute-done.9.got_br = bf16[640,128]{1,0:T(8,128)(2,1)S(1)} collective-permute-done((bf16[640,128]{1,0:T(8,128)(2,1)S(1)}, bf16[640,128]{1,0:T(8,128)(2,1)S(1)}, u32[]{:S(2)}, u32[]{:S(2)}) %collective-permute-start.9) | collective-permute-done | bytes 163872 | tf_op jit(solution)/shard_map/ppermute | solution.py:600
  32.8 1.0 %shard_map.178 = (f32[160,1280]{1,0:T(8,128)S(1)}, f32[160,768]{1,0:T(8,128)S(1)}, f32[8,8,128]{2,1,0:T(8,128)S(1)}, f32[8,16,128]{2,1,0:T(8,128)S(1)}) custom-call(s32[7]{0:T(128)S(1)} %stack.31.place_ref.t_ref.edge_ref.x_ref, f32[160,512]{1,0:T(8,128)S(1)} %get-tuple-element.50.pre_p, f32[160,128]{1,0:T(8,128)S(1)} %get-tuple-element.51.up_p, ...), custom_call_target="tpu_custom_call" | custom-call | flops 1000000 | bytes 3244060 | tf_op jit(solution)/shard_map/pallas_call | solution.py:33
  33.8 8.2 %all_to_all.15.sums_ref = f32[8,16,128]{2,1,0:T(8,128)S(1)} all-to-all(f32[8,16,128]{2,1,0:T(8,128)S(1)} %get-tuple-element.64), channel_id=1, replica_groups=mesh['dp'=8,'space'=8,'tensor'=4] {'space'}, dimensions={0} | all-to-all | bytes 131072 | tf_op jit(solution)/shard_map/all_to_all | solution.py:615
  42.0 1.6 %shard_map.179 = (f32[12,8,128]{2,1,0:T(8,128)S(1)}, bf16[160,512]{1,0:T(8,128)(2,1)S(1)}, f32[160,128]{1,0:T(8,128)S(1)}) custom-call(s32[7]{0:T(128)S(1)} %stack.31.place_ref.t_ref.edge_ref.x_ref, f32[160,1280]{1,0:T(8,128)S(1)} %get-tuple-element.62.ext_p, f32[160,768]{1,0:T(8,128)S(1)} %get-tuple-element.63.ext_r, ...), custom_call_target="tpu_custom_call" | custom-call | flops 10000000 | bytes 1799196 | tf_op jit(solution)/shard_map/pallas_call | solution.py:33
  43.8 4.1 %collective-permute-start.11 = (f32[12,8,128]{2,1,0:T(8,128)S(1)}, f32[12,8,128]{2,1,0:T(8,128)S(1)}, u32[]{:S(2)}, u32[]{:S(2)}) collective-permute-start(f32[12,8,128]{2,1,0:T(8,128)S(1)} %get-tuple-element.66.p0), channel_id=1, source_target_pairs={{0,2},{1,3},{2,0},{3,1},{4,6},{5,7},{6,4},{7,5},{8,10},{9,11},{10,... | collective-permute-start | bytes 147464 | tf_op jit(solution)/shard_map/ppermute | solution.py:623
  48.2 1.7 %collective-permute-done.11.p2 = f32[12,8,128]{2,1,0:T(8,128)S(1)} collective-permute-done((f32[12,8,128]{2,1,0:T(8,128)S(1)}, f32[12,8,128]{2,1,0:T(8,128)S(1)}, u32[]{:S(2)}, u32[]{:S(2)}) %collective-permute-start.11) | collective-permute-done | bytes 49184 | tf_op jit(solution)/shard_map/ppermute | solution.py:623
  49.9 1.2 %collective-permute-done.12.p3 = f32[12,8,128]{2,1,0:T(8,128)S(1)} collective-permute-done((f32[12,8,128]{2,1,0:T(8,128)S(1)}, f32[12,8,128]{2,1,0:T(8,128)S(1)}, u32[]{:S(2)}, u32[]{:S(2)}) %collective-permute-start.12) | collective-permute-done | bytes 49184 | tf_op jit(solution)/shard_map/ppermute | solution.py:623
  51.1 1.2 %shard_map.180 = (f32[160,768]{1,0:T(8,128)S(1)}, f32[32,128]{1,0:T(8,128)S(1)}, f32[8,24,128]{2,1,0:T(8,128)S(1)}) custom-call(s32[7]{0:T(128)S(1)} %stack.31.place_ref.t_ref.edge_ref.x_ref, f32[12,8,128]{2,1,0:T(8,128)S(1)} %get-tuple-element.66.p0, f32[12,8,128]{2,1,0:T(8,128)S(1)} %collective-permute-done.10.p1, ...), custom_call_target="tpu_custom_call" | custom-call | flops 10000000 | bytes 2005532 | tf_op jit(solution)/shard_map/pallas_call | solution.py:33
  52.4 9.6 %all_to_all.16.red_ref = f32[8,24,128]{2,1,0:T(8,128)S(1)} all-to-all(f32[8,24,128]{2,1,0:T(8,128)S(1)} %get-tuple-element.72), channel_id=1, replica_groups=mesh['dp'=8,'space'=8,'tensor'=4] {'space'}, dimensions={0} | all-to-all | bytes 196608 | tf_op jit(solution)/shard_map/all_to_all | solution.py:631
  61.9 2.2 %shard_map.181 = (f32[4,40,768]{2,1,0:T(8,128)S(1)}, bf16[4,48,768]{2,1,0:T(8,128)(2,1)S(1)}, f32[32,128]{1,0:T(8,128)S(1)}, f32[1,1]{1,0:T(1,128)}) custom-call(s32[7]{0:T(128)S(1)} %stack.31.place_ref.t_ref.edge_ref.x_ref, f32[160,768]{1,0:T(8,128)S(1)} %get-tuple-element.71.gnorm_ref, f32[160,1280]{1,0:T(8,128)S(1)} %get-tuple-element.62.ext_p, ...), custom_call_target="tpu_custom_call" | custom-call | flops 471859200 | bytes 2965536 | tf_op jit(solution)/shard_map/pallas_call | solution.py:33
  65.0 1.2 %collective-permute-done.13.got_ref = bf16[4,48,768]{2,1,0:T(8,128)(2,1)S(1)} collective-permute-done((bf16[4,48,768]{2,1,0:T(8,128)(2,1)S(1)}, bf16[4,48,768]{2,1,0:T(8,128)(2,1)S(1)}, u32[]{:S(2)}, u32[]{:S(2)}) %collective-permute-start.13) | collective-permute-done | bytes 294944 | tf_op jit(solution)/shard_map/ppermute | solution.py:640
  67.2 1.8 %collective-permute-start.15 = (bf16[48,768]{1,0:T(8,128)(2,1)S(1)}, bf16[48,768]{1,0:T(8,128)(2,1)S(1)}, u32[]{:S(2)}, u32[]{:S(2)}) collective-permute-start(bf16[48,768]{1,0:T(8,128)(2,1)S(1)} %get-tuple-element.81), channel_id=1, source_target_pairs={{0,16},{4,20},{8,24},{12,28},{16,0},{20,4},{24,8},{28,12},{1,17},{... | collective-permute-start | bytes 221192 | tf_op jit(solution)/shard_map/ppermute | solution.py:649
  69.6 2.3 %collective-permute-done.14.r1 = bf16[48,768]{1,0:T(8,128)(2,1)S(1)} collective-permute-done((bf16[48,768]{1,0:T(8,128)(2,1)S(1)}, bf16[48,768]{1,0:T(8,128)(2,1)S(1)}, u32[]{:S(2)}, u32[]{:S(2)}) %collective-permute-start.14) | collective-permute-done | bytes 73760 | tf_op jit(solution)/shard_map/ppermute | solution.py:649
  73.5 15.7 %all_to_all.17.got_ref = bf16[8,56,128]{2,1,0:T(8,128)(2,1)S(1)} all-to-all(bf16[8,56,128]{2,1,0:T(8,128)(2,1)S(1)} %shard_map.183), channel_id=1, replica_groups=mesh['dp'=8,'space'=8,'tensor'=4] {'dp'}, dimensions={0} | all-to-all | bytes 229376 | tf_op jit(solution)/shard_map/all_to_all | solution.py:658
  (50 shorter events, 11.3 us)
Async XLA Ops:
  0.6 13.9 %copy-start = (bf16[9,80,320]{2,1,0:T(8,128)(2,1)S(1)}, bf16[9,80,320]{2,1,0:T(8,128)(2,1)}, u32[]{:S(2)}) copy-start(bf16[9,80,320]{2,1,0:T(8,128)(2,1)} %param.19) | copy-start | bytes 1382404
  1.6 6.5 %collective-permute-start.1 = (bf16[2,4,80,128]{3,2,1,0:T(8,128)(2,1)S(1)}, bf16[2,4,80,128]{3,2,1,0:T(8,128)(2,1)S(1)}, u32[]{:S(2)}, u32[]{:S(2)}) collective-permute-start(bf16[2,4,80,128]{3,2,1,0:T(8,128)(2,1)S(1)} %bitcast.33), channel_id=1, source_target_pairs={{0,3},{1,0},{2,1},{3,2},{4,7},{5,4},{6,5},{7,6},{8,11},{9,8},{10,9... | collective-permute-start | bytes 491528 | tf_op jit(solution)/shard_map/ppermute | solution.py:548
  6.2 6.1 %collective-permute-start.3 = (bf16[2,4,80,128]{3,2,1,0:T(8,128)(2,1)S(1)}, bf16[2,4,80,128]{3,2,1,0:T(8,128)(2,1)S(1)}, u32[]{:S(2)}, u32[]{:S(2)}) collective-permute-start(bf16[2,4,80,128]{3,2,1,0:T(8,128)(2,1)S(1)} %bitcast.30), channel_id=1, source_target_pairs={{0,1},{1,2},{2,3},{3,0},{4,5},{5,6},{6,7},{7,4},{8,9},{9,10},{10,1... | collective-permute-start | bytes 491528 | tf_op jit(solution)/shard_map/ppermute | solution.py:547
  6.3 11.8 %collective-permute-start = (bf16[2,4,80,128]{3,2,1,0:T(8,128)(2,1)S(1)}, bf16[2,4,80,128]{3,2,1,0:T(8,128)(2,1)S(1)}, u32[]{:S(2)}, u32[]{:S(2)}) collective-permute-start(bf16[2,4,80,128]{3,2,1,0:T(8,128)(2,1)S(1)} %bitcast.34), channel_id=1, source_target_pairs={{0,1},{1,2},{2,3},{3,0},{4,5},{5,6},{6,7},{7,4},{8,9},{9,10},{10,1... | collective-permute-start | bytes 491528 | tf_op jit(solution)/shard_map/ppermute | solution.py:547
  8.2 10.0 %collective-permute-start.2 = (bf16[2,4,80,128]{3,2,1,0:T(8,128)(2,1)S(1)}, bf16[2,4,80,128]{3,2,1,0:T(8,128)(2,1)S(1)}, u32[]{:S(2)}, u32[]{:S(2)}) collective-permute-start(bf16[2,4,80,128]{3,2,1,0:T(8,128)(2,1)S(1)} %collective-permute-done.1.f3), channel_id=1, source_target_pairs={{0,3},{1,0},{2,1},{3,2},{4,7},{5,4},{6,5},{7,6},{8,11},{9,8},{10,9... | collective-permute-start | bytes 491528 | tf_op jit(solution)/shard_map/ppermute | solution.py:549
  11.6 12.7 %collective-permute-start.5 = (bf16[2,4,80,128]{3,2,1,0:T(8,128)(2,1)S(1)}, bf16[2,4,80,128]{3,2,1,0:T(8,128)(2,1)S(1)}, u32[]{:S(2)}, u32[]{:S(2)}) collective-permute-start(bf16[2,4,80,128]{3,2,1,0:T(8,128)(2,1)S(1)} %bitcast.31), channel_id=1, source_target_pairs={{0,3},{1,0},{2,1},{3,2},{4,7},{5,4},{6,5},{7,6},{8,11},{9,8},{10,9... | collective-permute-start | bytes 491528 | tf_op jit(solution)/shard_map/ppermute | solution.py:548
  12.3 11.9 %collective-permute-start.4 = (bf16[2,4,80,128]{3,2,1,0:T(8,128)(2,1)S(1)}, bf16[2,4,80,128]{3,2,1,0:T(8,128)(2,1)S(1)}, u32[]{:S(2)}, u32[]{:S(2)}) collective-permute-start(bf16[2,4,80,128]{3,2,1,0:T(8,128)(2,1)S(1)} %collective-permute-done.3.f1), channel_id=1, source_target_pairs={{0,1},{1,2},{2,3},{3,0},{4,5},{5,6},{6,7},{7,4},{8,9},{9,10},{10,1... | collective-permute-start | bytes 491528 | tf_op jit(solution)/shard_map/ppermute | solution.py:549
  13.0 1.5 %copy-start.6 = (f32[80]{0:T(128)S(1)}, f32[80]{0:T(128)}, u32[]{:S(2)}) copy-start(f32[80]{0:T(128)} %param.21) | copy-start | bytes 964
  13.0 1.5 %copy-start.7 = (f32[80]{0:T(128)S(1)}, f32[80]{0:T(128)}, u32[]{:S(2)}) copy-start(f32[80]{0:T(128)} %param.22) | copy-start | bytes 964
  13.0 1.5 %copy-start.8 = (f32[80]{0:T(128)S(1)}, f32[80]{0:T(128)}, u32[]{:S(2)}) copy-start(f32[80]{0:T(128)} %param.23) | copy-start | bytes 964
  13.0 1.5 %copy-start.9 = (f32[80]{0:T(128)S(1)}, f32[80]{0:T(128)}, u32[]{:S(2)}) copy-start(f32[80]{0:T(128)} %param.24) | copy-start | bytes 964
  13.0 1.5 %copy-start.10 = (f32[80]{0:T(128)S(1)}, f32[80]{0:T(128)}, u32[]{:S(2)}) copy-start(f32[80]{0:T(128)} %param.25) | copy-start | bytes 964
  13.1 1.5 %copy-start.11 = (f32[80]{0:T(128)S(1)}, f32[80]{0:T(128)}, u32[]{:S(2)}) copy-start(f32[80]{0:T(128)} %param.26) | copy-start | bytes 964
  20.5 12.3 %collective-permute-start.6 = (bf16[992,128]{1,0:T(8,128)(2,1)S(1)}, bf16[992,128]{1,0:T(8,128)(2,1)S(1)}, u32[]{:S(2)}, u32[]{:S(2)}) collective-permute-start(bf16[992,128]{1,0:T(8,128)(2,1)S(1)} %get-tuple-element.58), channel_id=1, source_target_pairs={{0,4},{4,0},{8,12},{12,8},{16,20},{20,16},{24,28},{28,24},{1,5},{5... | collective-permute-start | bytes 761864 | tf_op jit(solution)/shard_map/ppermute | solution.py:590
  23.0 9.7 %collective-permute-start.7 = (bf16[992,128]{1,0:T(8,128)(2,1)S(1)}, bf16[992,128]{1,0:T(8,128)(2,1)S(1)}, u32[]{:S(2)}, u32[]{:S(2)}) collective-permute-start(bf16[992,128]{1,0:T(8,128)(2,1)S(1)} %get-tuple-element.59), channel_id=1, source_target_pairs={{0,28},{4,8},{8,4},{12,16},{16,12},{20,24},{24,20},{28,0},{1,29},{... | collective-permute-start | bytes 761864 | tf_op jit(solution)/shard_map/ppermute | solution.py:589
  25.9 2.8 %collective-permute-start.8 = (bf16[640,128]{1,0:T(8,128)(2,1)S(1)}, bf16[640,128]{1,0:T(8,128)(2,1)S(1)}, u32[]{:S(2)}, u32[]{:S(2)}) collective-permute-start(bf16[640,128]{1,0:T(8,128)(2,1)S(1)} %get-tuple-element.60), channel_id=1, source_target_pairs={{0,4},{4,0},{8,12},{12,8},{16,20},{20,16},{24,28},{28,24},{1,5},{5... | collective-permute-start | bytes 491528 | tf_op jit(solution)/shard_map/ppermute | solution.py:601
  27.7 5.0 %collective-permute-start.9 = (bf16[640,128]{1,0:T(8,128)(2,1)S(1)}, bf16[640,128]{1,0:T(8,128)(2,1)S(1)}, u32[]{:S(2)}, u32[]{:S(2)}) collective-permute-start(bf16[640,128]{1,0:T(8,128)(2,1)S(1)} %get-tuple-element.61), channel_id=1, source_target_pairs={{0,28},{4,8},{8,4},{12,16},{16,12},{20,24},{24,20},{28,0},{1,29},{... | collective-permute-start | bytes 491528 | tf_op jit(solution)/shard_map/ppermute | solution.py:600
  43.7 4.5 %collective-permute-start.10 = (f32[12,8,128]{2,1,0:T(8,128)S(1)}, f32[12,8,128]{2,1,0:T(8,128)S(1)}, u32[]{:S(2)}, u32[]{:S(2)}) collective-permute-start(f32[12,8,128]{2,1,0:T(8,128)S(1)} %get-tuple-element.66.p0), channel_id=1, source_target_pairs={{0,1},{1,2},{2,3},{3,0},{4,5},{5,6},{6,7},{7,4},{8,9},{9,10},{10,1... | collective-permute-start | bytes 147464 | tf_op jit(solution)/shard_map/ppermute | solution.py:623
  43.8 6.1 %collective-permute-start.11 = (f32[12,8,128]{2,1,0:T(8,128)S(1)}, f32[12,8,128]{2,1,0:T(8,128)S(1)}, u32[]{:S(2)}, u32[]{:S(2)}) collective-permute-start(f32[12,8,128]{2,1,0:T(8,128)S(1)} %get-tuple-element.66.p0), channel_id=1, source_target_pairs={{0,2},{1,3},{2,0},{3,1},{4,6},{5,7},{6,4},{7,5},{8,10},{9,11},{10,... | collective-permute-start | bytes 147464 | tf_op jit(solution)/shard_map/ppermute | solution.py:623
  47.9 3.2 %collective-permute-start.12 = (f32[12,8,128]{2,1,0:T(8,128)S(1)}, f32[12,8,128]{2,1,0:T(8,128)S(1)}, u32[]{:S(2)}, u32[]{:S(2)}) collective-permute-start(f32[12,8,128]{2,1,0:T(8,128)S(1)} %get-tuple-element.66.p0), channel_id=1, source_target_pairs={{0,3},{1,0},{2,1},{3,2},{4,7},{5,4},{6,5},{7,6},{8,11},{9,8},{10,9... | collective-permute-start | bytes 147464 | tf_op jit(solution)/shard_map/ppermute | solution.py:623
  64.1 2.0 %collective-permute-start.13 = (bf16[4,48,768]{2,1,0:T(8,128)(2,1)S(1)}, bf16[4,48,768]{2,1,0:T(8,128)(2,1)S(1)}, u32[]{:S(2)}, u32[]{:S(2)}) collective-permute-start(bf16[4,48,768]{2,1,0:T(8,128)(2,1)S(1)} %get-tuple-element.78), channel_id=1, source_target_pairs={{0,4},{4,0},{8,12},{12,8},{16,20},{20,16},{24,28},{28,24},{1,5},{5... | collective-permute-start | bytes 884744 | tf_op jit(solution)/shard_map/ppermute | solution.py:640
  66.8 5.2 %collective-permute-start.14 = (bf16[48,768]{1,0:T(8,128)(2,1)S(1)}, bf16[48,768]{1,0:T(8,128)(2,1)S(1)}, u32[]{:S(2)}, u32[]{:S(2)}) collective-permute-start(bf16[48,768]{1,0:T(8,128)(2,1)S(1)} %get-tuple-element.80), channel_id=1, source_target_pairs={{0,8},{4,12},{8,16},{12,20},{16,24},{20,28},{24,0},{28,4},{1,9},{5... | collective-permute-start | bytes 221192 | tf_op jit(solution)/shard_map/ppermute | solution.py:649
  67.2 5.5 %collective-permute-start.15 = (bf16[48,768]{1,0:T(8,128)(2,1)S(1)}, bf16[48,768]{1,0:T(8,128)(2,1)S(1)}, u32[]{:S(2)}, u32[]{:S(2)}) collective-permute-start(bf16[48,768]{1,0:T(8,128)(2,1)S(1)} %get-tuple-element.81), channel_id=1, source_target_pairs={{0,16},{4,20},{8,24},{12,28},{16,0},{20,4},{24,8},{28,12},{1,17},{... | collective-permute-start | bytes 221192 | tf_op jit(solution)/shard_map/ppermute | solution.py:649
  68.9 4.5 %collective-permute-start.16 = (bf16[48,768]{1,0:T(8,128)(2,1)S(1)}, bf16[48,768]{1,0:T(8,128)(2,1)S(1)}, u32[]{:S(2)}, u32[]{:S(2)}) collective-permute-start(bf16[48,768]{1,0:T(8,128)(2,1)S(1)} %get-tuple-element.82), channel_id=1, source_target_pairs={{0,24},{4,28},{8,0},{12,4},{16,8},{20,12},{24,16},{28,20},{1,25},{... | collective-permute-start | bytes 221192 | tf_op jit(solution)/shard_map/ppermute | solution.py:649
  (5 other events, 4.3 us)

commit v7 on v4

--- a/solution.py
+++ b/solution.py
@@ -104,11 +104,9 @@
 
 
 def prep_kernel(
-    place_ref, b_p, b_r, gain_p, off_p, gain_r, off_r, w2_p, w2_r, table_ref, noise_ref, w1_p, w1_r,
-    col_ref, lift_ref, drop_ref, rows_ref, w1_p_out, w1_r_out
+    place_ref, b_p, b_r, gain_p, off_p, gain_r, off_r, w2_p, w2_r, table_ref, noise_ref,
+    col_ref, lift_ref, drop_ref, rows_ref
 ):
-    w1_p_out[...] = w1_p[...]
-    w1_r_out[...] = w1_r[...]
     lane = lax.broadcasted_iota(jnp.int32, table_ref.shape, 1)
     shift = jnp.sum(
         jnp.where(lane == place_ref[6], table_ref[...], 0.0), axis=1, keepdims=True
@@ -151,24 +149,28 @@
                 rows_ref[r, slot : slot + 1, :] = noise_ref[im, o, r : r + 1, :]
 
 
-def conv_kernel(last, t_ref, f0, f1, f2, f3, w_ref, col_ref, *refs):
+def conv_kernel(last, t_ref, f0, f1, f2, f3, w_ref, *refs):
     if last:
         pre_ref, up_ref, dn_ref, send_a, send_b, fs_ref = refs
     else:
         noise_ref, pre_ref, up_ref, dn_ref, send_a, send_b, perm_ref, fs_ref = refs
-    t = t_ref[5]
-    bias = 5 if last else 4
+    t = t_ref[0]
     for k in range(4):
         base = pl.multiple_of(lax.rem(t - k + 4, 4) * CH, 16)
         for im in range(2):
             for r in range(ROWS):
                 lo = im * PIX + r * COLS
                 fs_ref[pl.ds(base, CH), lo : lo + COLS] = (f0, f1, f2, f3)[k][im, r]
-    odd = t_ref[3] > 0
+    odd = t_ref[1] > 0
     count = 2 if last else 4
     if not last:
         for index in range(2):
-            first, second = noise_ref[index], noise_ref[2 + index]
+            first, second = [
+                jnp.concatenate(
+                    [noise_ref[im, o, r : r + 1, :] for im in range(2) for o in range(4)], axis=0
+                )
+                for r in (index, 2 + index)
+            ]
             for ref, value in (
                 (send_a, jnp.where(odd, first, second)),
                 (send_b, jnp.where(odd, second, first)),
@@ -204,7 +206,6 @@
             elif r == ROWS:
                 dn_ref[chans, :] = out
             else:
-                out = out + col_ref[chans, bias : bias + 1]
                 pre_ref[chans, r * COLS : (r + 1) * COLS] = out
             outs.append(out)
         for index in range(count):
@@ -232,7 +233,7 @@
 
 
 def stat_kernel(
-    place_ref, pre_p, up_p, dn_p, pre_r, up_r, dn_r, got_ap, got_bp, got_ar, got_br, noise_ref,
+    place_ref, pre_p, up_p, dn_p, pre_r, up_r, dn_r, got_ap, got_bp, got_ar, got_br, noise_ref, col_ref,
     ext_p, ext_r, noise_ext, out_ref
 ):
     odd = place_ref[3] > 0
@@ -250,15 +251,17 @@
 
     columns = []
     first = 0
-    for pre, up, dn, ext, got_a, got_b, halo in (
-        (pre_p, up_p, dn_p, ext_p, got_ap, got_bp, 3),
-        (pre_r, up_r, dn_r, ext_r, got_ar, got_br, 1),
+    for pre, up, dn, ext, got_a, got_b, halo, slot in (
+        (pre_p, up_p, dn_p, ext_p, got_ap, got_bp, 3, 4),
+        (pre_r, up_r, dn_r, ext_r, got_ar, got_br, 1, 5),
     ):
         left, right = (got_a, got_b), (got_b, got_a)
         low = first + halo + 1
+        bias = jnp.broadcast_to(col_ref[:, slot : slot + 1], (2 * CH, COLS))
         rows = [pre[:, r * COLS : (r + 1) * COLS] for r in range(ROWS)]
         rows[0] = rows[0] + jnp.where(top, 0.0, near(left, first + halo, low + 1))
         rows[ROWS - 1] = rows[ROWS - 1] + jnp.where(bottom, 0.0, near(right, first, low))
+        rows = [row + bias for row in rows]
         total = rows[0] + rows[1] + rows[2] + rows[3]
         square = (
             rows[0] * rows[0] + rows[1] * rows[1] + rows[2] * rows[2] + rows[3] * rows[3]
@@ -267,6 +270,8 @@
         before[-1] = near(left, first + halo - 1, low) + up[...]
         after = [got(right, first + 1 + index) for index in range(halo)]
         after[0] = near(right, first + 1, low + 1) + dn[...]
+        before = [row + bias for row in before]
+        after = [row + bias for row in after]
         for index, row in enumerate(before + rows + after):
             ext[:, index * COLS : (index + 1) * COLS] = row
         columns.append(jnp.sum(total, axis=1, keepdims=True))
@@ -529,6 +534,46 @@
 ):
     space = lax.axis_size("space")
     s_index = lax.axis_index("space").astype(jnp.int32)
+    spot = jnp.stack([lax.axis_index("tensor").astype(jnp.int32), s_index & 1])
+
+    def gather(own):
+        return [own] + [lax.ppermute(own, "tensor", ring("tensor", k)) for k in (1, 2, 3)]
+
+    own_p = feat_policy[0].transpose(0, 2, 1, 3)
+    feat_ref, own_p = lax.optimization_barrier((feat_ref, own_p))
+    own_r = feat_ref[0].transpose(0, 2, 1, 3)
+    parts_p = gather(own_p)
+    parts_r = gather(own_r)
+
+    conv_flops = 2 * 9 * C * CH * 2 * PIX
+    wide = arr((2 * CH, PIX), F32)
+    thin = arr((2 * CH, COLS), F32)
+
+    partner = [(i, i ^ 1) for i in range(space)]
+    across = [(i, (i + 1 if i % 2 else i - 1) % space) for i in range(space)]
+    pre_p, up_p, dn_p, to_ap, to_bp, feats = call(
+        functools.partial(conv_kernel, False),
+        [spot, *parts_p, w1_policy.reshape(9 * CH, C), noise[0]],
+        [wide, thin, thin, arr((992, COLS), BF16), arr((992, COLS), BF16), arr((C, 2 * PIX), BF16)],
+        conv_flops,
+        smem=1,
+        scratch=[pltpu.VMEM((C, 2 * PIX), BF16)],
+    )
+    got_bp = lax.ppermute(to_bp, "space", across)
+    got_ap = lax.ppermute(to_ap, "space", partner)
+    own_r, pre_p = lax.optimization_barrier((parts_r[0], pre_p))
+    pre_r, up_r, dn_r, to_ar, to_br = call(
+        functools.partial(conv_kernel, True),
+        [spot, own_r, *parts_r[1:], w1_ref.reshape(9 * CH, C)],
+        [wide, thin, thin, arr((640, COLS), BF16), arr((640, COLS), BF16)],
+        conv_flops,
+        smem=1,
+        scratch=[pltpu.VMEM((C, 2 * PIX), BF16)],
+    )
+    got_br = lax.ppermute(to_br, "space", across)
+    got_ar = lax.ppermute(to_ar, "space", partner)
+
+    pre_r, timestep = lax.optimization_barrier((pre_r, timestep))
     is_top = (s_index == 0).astype(jnp.int32)
     is_bottom = (s_index == space - 1).astype(jnp.int32)
     place = jnp.stack(
@@ -542,64 +587,23 @@
             timestep[0].astype(jnp.int32),
         ]
     )
-
-    def gather(own):
-        return [own] + [lax.ppermute(own, "tensor", ring("tensor", k)) for k in (1, 2, 3)]
-
-    own_p = feat_policy[0].transpose(0, 2, 1, 3)
-    feat_ref, own_p = lax.optimization_barrier((feat_ref, own_p))
-    own_r = feat_ref[0].transpose(0, 2, 1, 3)
-    parts_p = gather(own_p)
-    parts_r = gather(own_r)
-
     vectors = [b1_policy, b1_ref, gn_gain_policy, gn_bias_policy, gn_gain_ref, gn_bias_ref]
-    columns, lift, drop, noise_rows, near_p, near_r = call(
+    columns, lift, drop, noise_rows = call(
         prep_kernel,
-        [place, *[v[None, :] for v in vectors], w2_policy, w2_ref, time_table.T, noise[0],
-         w1_policy.reshape(9 * CH, C), w1_ref.reshape(9 * CH, C)],
+        [place, *[v[None, :] for v in vectors], w2_policy, w2_ref, time_table.T, noise[0]],
         [
             arr((2 * CH, COLS), F32),
             arr((2, 2, 72, CH), BF16),
             arr((2 * CH, 72), BF16),
             arr((ROWS, 8, COLS), F32),
-            arr((9 * CH, C), BF16),
-            arr((9 * CH, C), BF16),
         ],
         10**6,
         smem=1,
     )
 
-    conv_flops = 2 * 9 * C * CH * 2 * PIX
-    wide = arr((2 * CH, PIX), F32)
-    thin = arr((2 * CH, COLS), F32)
-
-    partner = [(i, i ^ 1) for i in range(space)]
-    across = [(i, (i + 1 if i % 2 else i - 1) % space) for i in range(space)]
-    pre_p, up_p, dn_p, to_ap, to_bp, feats = call(
-        functools.partial(conv_kernel, False),
-        [place, *parts_p, near_p, columns, noise_rows],
-        [wide, thin, thin, arr((992, COLS), BF16), arr((992, COLS), BF16), arr((C, 2 * PIX), BF16)],
-        conv_flops,
-        smem=1,
-        scratch=[pltpu.VMEM((C, 2 * PIX), BF16)],
-    )
-    got_bp = lax.ppermute(to_bp, "space", across)
-    got_ap = lax.ppermute(to_ap, "space", partner)
-    own_r, pre_p = lax.optimization_barrier((parts_r[0], pre_p))
-    pre_r, up_r, dn_r, to_ar, to_br = call(
-        functools.partial(conv_kernel, True),
-        [place, own_r, *parts_r[1:], near_r, columns],
-        [wide, thin, thin, arr((640, COLS), BF16), arr((640, COLS), BF16)],
-        conv_flops,
-        smem=1,
-        scratch=[pltpu.VMEM((C, 2 * PIX), BF16)],
-    )
-    got_br = lax.ppermute(to_br, "space", across)
-    got_ar = lax.ppermute(to_ar, "space", partner)
-
     ext_p, ext_r, noise_ext, sums = call(
         stat_kernel,
-        [place, pre_p, up_p, dn_p, pre_r, up_r, dn_r, got_ap, got_bp, got_ar, got_br, noise_rows],
+        [place, pre_p, up_p, dn_p, pre_r, up_r, dn_r, got_ap, got_bp, got_ar, got_br, noise_rows, columns],
         [
             arr((2 * CH, 10 * COLS), F32),
             arr((2 * CH, 6 * COLS), F32),

time: 89.1 us -> 89.9 us (level)
  waiting for transfers between devices: 12.5 us -> 18.2 us
  starting transfers between devices: 22.3 us -> 17.7 us
  local copies, waits for them, and re-layouts: 4.72 us -> 2.69 us
  blocking collectives: 33.4 us -> 34.6 us
    ppermute x6, waiting for transfers between devices: 0.02 us -> 7.53 us  [gather(): lax.ppermute(own, 'tensor', ring('tensor', k))]
    ppermute x3, starting transfers between devices: 4.48 us -> 1.55 us  [body(): lax.ppermute(part, 'tensor', ring('tensor', k))]
    ppermute x1, waiting for transfers between devices: 4.01 us -> 1.87 us  [body(): got_br = lax.ppermute(to_br, 'space', across)]
    unnamed x25, local copies, waits for them, and re-layouts: 3.69 us -> 1.67 us
    ppermute x1, starting transfers between devices: 3.39 us -> 1.55 us  [body(): got_ap = lax.ppermute(to_ap, 'space', partner)]
    ppermute x3, waiting for transfers between devices: 2.67 us -> 3.87 us  [body(): lax.ppermute(part, 'tensor', ring('tensor', k))]
    ppermute x1, starting transfers between devices: 0.01 us -> 1.2 us  [body(): got_bp = lax.ppermute(to_bp, 'space', across)]
  transfers between devices with their start and end apart: 17 -> 17, of which waited for: 8 -> 11; matrix products, arithmetic and copies ran while one was open for 1% -> 1% of each run, Pallas kernels for 6% -> 6%
where the time goes in v7:
time: 89.9 us; the launch traced here: 88.4 us
  blocking collectives  34.6 us (38%)
  waiting for transfers between devices  18.2 us (20%)
  starting transfers between devices  17.7 us (20%)
  Pallas kernels  13 us (14%)
  local copies, waits for them, and re-layouts  2.69 us (3%)
  between operations  2.09 us (2%)
    all_to_all x1, blocking collectives, body(): packed = lax.all_to_all(packed, 'dp', 0, 0, tiled=True)  15.7 us
    pallas_call x10, Pallas kernels, call(): pl.pallas_call(kernel, out_shape=outs, in_specs=[SM] * smem + [VM] * (len...  13 us
    all_to_all x1, blocking collectives, body(): partial = lax.all_to_all(partial, 'space', 0, 0, tiled=True)  9.7 us
    all_to_all x1, blocking collectives, body(): sums = lax.all_to_all(sums, 'space', 0, 0, tiled=True)  9.16 us
    ppermute x6, starting transfers between devices, gather(): lax.ppermute(own, 'tensor', ring('tensor', k))  8.15 us
    ppermute x6, waiting for transfers between devices, gather(): lax.ppermute(own, 'tensor', ring('tensor', k))  7.53 us
    ppermute x3, waiting for transfers between devices, body(): lax.ppermute(part, 'tensor', ring('tensor', k))  3.87 us
    ppermute x3, waiting for transfers between devices, body(): lax.ppermute(sent, 'space', ring('space', 2 * k))  3.75 us
  transfers between devices with their start and end apart: 17, of which 11 were waited for; matrix products, arithmetic and copies ran while one was open for 1% of the time, Pallas kernels for 6%

profile of v7, /device:TPU:1, one launch (start us, length us, event | category | flops | bytes accessed | tf_op | source)
XLA Modules:
  0.0 88.4 jit_solution(11610142552768234322)
XLA Ops:
  0.6 1.0 %copy.24 = bf16[1,2,80,4,128]{4,2,3,1,0:T(8,128)(2,1)S(1)} copy(bf16[1,2,80,4,128]{4,3,2,1,0:T(4,128)(2,1)} %param.16) | data formatting | bytes 327680 | tf_op args[0]
  1.6 3.6 %collective-permute-start.2 = (bf16[2,4,80,128]{3,2,1,0:T(8,128)(2,1)S(1)}, bf16[2,4,80,128]{3,2,1,0:T(8,128)(2,1)S(1)}, u32[]{:S(2)}, u32[]{:S(2)}) collective-permute-start(bf16[2,4,80,128]{3,2,1,0:T(8,128)(2,1)S(1)} %bitcast.32), channel_id=1, source_target_pairs={{0,3},{1,0},{2,1},{3,2},{4,7},{5,4},{6,5},{7,6},{8,11},{9,8},{10,9... | collective-permute-start | bytes 491528 | tf_op jit(solution)/shard_map/ppermute | solution.py:540
  6.3 0.9 %copy.23 = bf16[1,2,80,4,128]{4,2,3,1,0:T(8,128)(2,1)S(1)} copy(bf16[1,2,80,4,128]{4,3,2,1,0:T(4,128)(2,1)} %param.17) | data formatting | bytes 327680 | tf_op jit(solution)/shard_map/optimization_barrier | solution.py:543
  7.3 2.1 %collective-permute-start.5 = (bf16[2,4,80,128]{3,2,1,0:T(8,128)(2,1)S(1)}, bf16[2,4,80,128]{3,2,1,0:T(8,128)(2,1)S(1)}, u32[]{:S(2)}, u32[]{:S(2)}) collective-permute-start(bf16[2,4,80,128]{3,2,1,0:T(8,128)(2,1)S(1)} %bitcast.28), channel_id=1, source_target_pairs={{0,3},{1,0},{2,1},{3,2},{4,7},{5,4},{6,5},{7,6},{8,11},{9,8},{10,9... | collective-permute-start | bytes 491528 | tf_op jit(solution)/shard_map/ppermute | solution.py:540
  9.3 1.4 %collective-permute-start.4 = (bf16[2,4,80,128]{3,2,1,0:T(8,128)(2,1)S(1)}, bf16[2,4,80,128]{3,2,1,0:T(8,128)(2,1)S(1)}, u32[]{:S(2)}, u32[]{:S(2)}) collective-permute-start(bf16[2,4,80,128]{3,2,1,0:T(8,128)(2,1)S(1)} %bitcast.29), channel_id=1, source_target_pairs={{0,2},{1,3},{2,0},{3,1},{4,6},{5,7},{6,4},{7,5},{8,10},{9,11},{10,... | collective-permute-start | bytes 491528 | tf_op jit(solution)/shard_map/ppermute | solution.py:540
  11.6 6.1 %collective-permute-done.f1 = bf16[2,4,80,128]{3,2,1,0:T(8,128)(2,1)S(1)} collective-permute-done((bf16[2,4,80,128]{3,2,1,0:T(8,128)(2,1)S(1)}, bf16[2,4,80,128]{3,2,1,0:T(8,128)(2,1)S(1)}, u32[]{:S(2)}, u32[]{:S(2)}) %collective-permute-start) | collective-permute-done | bytes 163872 | tf_op jit(solution)/shard_map/ppermute | solution.py:540
  17.7 2.3 %shard_map.175 = (f32[160,512]{1,0:T(8,128)S(1)}, f32[160,128]{1,0:T(8,128)S(1)}, f32[160,128]{1,0:T(8,128)S(1)}, bf16[992,128]{1,0:T(8,128)(2,1)S(1)}, bf16[992...) custom-call(s32[2]{0:T(128)S(1)} %pad_add_fusion.t_ref, bf16[2,4,80,128]{3,2,1,0:T(8,128)(2,1)S(1)} %bitcast.35, ...), custom_call_target="tpu_custom_call" | custom-call | flops 471859200 | bytes 2787336 | tf_op jit(solution)/shard_map/pallas_call | solution.py:33
  20.0 1.6 %collective-permute-start.6 = (bf16[992,128]{1,0:T(8,128)(2,1)S(1)}, bf16[992,128]{1,0:T(8,128)(2,1)S(1)}, u32[]{:S(2)}, u32[]{:S(2)}) collective-permute-start(bf16[992,128]{1,0:T(8,128)(2,1)S(1)} %get-tuple-element.56), channel_id=1, source_target_pairs={{0,4},{4,0},{8,12},{12,8},{16,20},{20,16},{24,28},{28,24},{1,5},{5... | collective-permute-start | bytes 761864 | tf_op jit(solution)/shard_map/ppermute | solution.py:563
  21.6 1.2 %collective-permute-start.7 = (bf16[992,128]{1,0:T(8,128)(2,1)S(1)}, bf16[992,128]{1,0:T(8,128)(2,1)S(1)}, u32[]{:S(2)}, u32[]{:S(2)}) collective-permute-start(bf16[992,128]{1,0:T(8,128)(2,1)S(1)} %get-tuple-element.57), channel_id=1, source_target_pairs={{0,28},{4,8},{8,4},{12,16},{16,12},{20,24},{24,20},{28,0},{1,29},{... | collective-permute-start | bytes 761864 | tf_op jit(solution)/shard_map/ppermute | solution.py:562
  23.5 2.4 %shard_map.176 = (f32[160,512]{1,0:T(8,128)S(1)}, f32[160,128]{1,0:T(8,128)S(1)}, f32[160,128]{1,0:T(8,128)S(1)}, bf16[640,128]{1,0:T(8,128)(2,1)}, bf16[640,128]{1,0:T(8,128)(2,1)}) custom-call(s32[2]{0:T(128)S(1)} %pad_add_fusion.t_ref, bf16[2,4,80,128]{3,2,1,0:T(8,128)(2,1)S(1)} %bitcast.31, bf16[2,4,80,128]{3,2,1,0:T(8,128)(2,1)S(1)} %collective-permute-done.3.f1, ...), custom_call_target="tpu_custom_call" | custom-call | flops 471859200 | bytes 1935368 | tf_op jit(solution)/shard_map/pallas_call | solution.py:33
  25.9 1.0 %collective-permute-start.8 = (bf16[640,128]{1,0:T(8,128)(2,1)}, bf16[640,128]{1,0:T(8,128)(2,1)S(1)}, u32[]{:S(2)}, u32[]{:S(2)}) collective-permute-start(bf16[640,128]{1,0:T(8,128)(2,1)} %get-tuple-element.58), channel_id=1, source_target_pairs={{0,4},{4,0},{8,12},{12,8},{16,20},{20,16},{24,28},{28,24},{1,5},{5... | collective-permute-start | bytes 491528 | tf_op jit(solution)/shard_map/ppermute | solution.py:574
  30.3 1.9 %collective-permute-done.9.got_br = bf16[640,128]{1,0:T(8,128)(2,1)S(1)} collective-permute-done((bf16[640,128]{1,0:T(8,128)(2,1)}, bf16[640,128]{1,0:T(8,128)(2,1)S(1)}, u32[]{:S(2)}, u32[]{:S(2)}) %collective-permute-start.9) | collective-permute-done | bytes 163872 | tf_op jit(solution)/shard_map/ppermute | solution.py:573
  32.2 1.1 %shard_map.178 = (f32[160,1280]{1,0:T(8,128)S(1)}, f32[160,768]{1,0:T(8,128)S(1)}, f32[8,8,128]{2,1,0:T(8,128)S(1)}, f32[8,16,128]{2,1,0:T(8,128)S(1)}) custom-call(s32[7]{0:T(128)S(1)} %stack.37.place_ref.edge_ref.x_ref, f32[160,512]{1,0:T(8,128)S(1)} %get-tuple-element.50.pre_p, f32[160,128]{1,0:T(8,128)S(1)} %get-tuple-element.51.up_p, ...), custom_call_target="tpu_custom_call" | custom-call | flops 1000000 | bytes 3325980 | tf_op jit(solution)/shard_map/pallas_call | solution.py:33
  33.3 9.2 %all_to_all.15.sums_ref = f32[8,16,128]{2,1,0:T(8,128)S(1)} all-to-all(f32[8,16,128]{2,1,0:T(8,128)S(1)} %get-tuple-element.64), channel_id=1, replica_groups=mesh['dp'=8,'space'=8,'tensor'=4] {'space'}, dimensions={0} | all-to-all | bytes 131072 | tf_op jit(solution)/shard_map/all_to_all | solution.py:616
  42.4 1.6 %shard_map.179 = (f32[12,8,128]{2,1,0:T(8,128)S(1)}, bf16[160,512]{1,0:T(8,128)(2,1)S(1)}, f32[160,128]{1,0:T(8,128)S(1)}) custom-call(s32[7]{0:T(128)S(1)} %stack.37.place_ref.edge_ref.x_ref, f32[160,1280]{1,0:T(8,128)S(1)} %get-tuple-element.62.ext_p, f32[160,768]{1,0:T(8,128)S(1)} %get-tuple-element.63.ext_r, f32[8,16,128]{2,1,0:T(8,128)S(1)} %all_to_all.15.sums_ref, ...), custom_call_target="tpu_custom_call" | custom-call | flops 10000000 | bytes 1799196 | tf_op jit(solution)/shard_map/pallas_call | solution.py:33
  45.6 1.5 %collective-permute-done.12.p3 = f32[12,8,128]{2,1,0:T(8,128)S(1)} collective-permute-done((f32[12,8,128]{2,1,0:T(8,128)S(1)}, f32[12,8,128]{2,1,0:T(8,128)S(1)}, u32[]{:S(2)}, u32[]{:S(2)}) %collective-permute-start.12) | collective-permute-done | bytes 49184 | tf_op jit(solution)/shard_map/ppermute | solution.py:624
  47.1 1.8 %collective-permute-done.11.p2 = f32[12,8,128]{2,1,0:T(8,128)S(1)} collective-permute-done((f32[12,8,128]{2,1,0:T(8,128)S(1)}, f32[12,8,128]{2,1,0:T(8,128)S(1)}, u32[]{:S(2)}, u32[]{:S(2)}) %collective-permute-start.11) | collective-permute-done | bytes 49184 | tf_op jit(solution)/shard_map/ppermute | solution.py:624
  49.5 1.2 %shard_map.180 = (f32[160,768]{1,0:T(8,128)S(1)}, f32[32,128]{1,0:T(8,128)S(1)}, f32[8,24,128]{2,1,0:T(8,128)S(1)}) custom-call(s32[7]{0:T(128)S(1)} %stack.37.place_ref.edge_ref.x_ref, f32[12,8,128]{2,1,0:T(8,128)S(1)} %get-tuple-element.66.p0, f32[12,8,128]{2,1,0:T(8,128)S(1)} %collective-permute-done.10.p1, f32[12,8,128]{2,1,0:T(8,128)S(1)} %collective-permute-done.11.p2, ...), custom_call_target="tpu_custom_call" | custom-call | flops 10000000 | bytes 2005532 | tf_op jit(solution)/shard_map/pallas_call | solution.py:33
  50.7 9.7 %all_to_all.16.red_ref = f32[8,24,128]{2,1,0:T(8,128)S(1)} all-to-all(f32[8,24,128]{2,1,0:T(8,128)S(1)} %get-tuple-element.72), channel_id=1, replica_groups=mesh['dp'=8,'space'=8,'tensor'=4] {'space'}, dimensions={0} | all-to-all | bytes 196608 | tf_op jit(solution)/shard_map/all_to_all | solution.py:632
  60.4 2.2 %shard_map.181 = (f32[4,40,768]{2,1,0:T(8,128)S(1)}, bf16[4,48,768]{2,1,0:T(8,128)(2,1)S(1)}, f32[32,128]{1,0:T(8,128)S(1)}, f32[1,1]{1,0:T(1,128)}) custom-call(s32[7]{0:T(128)S(1)} %stack.37.place_ref.edge_ref.x_ref, f32[160,768]{1,0:T(8,128)S(1)} %get-tuple-element.71.gnorm_ref, f32[160,1280]{1,0:T(8,128)S(1)} %get-tuple-element.62.ext_p, ...), custom_call_target="tpu_custom_call" | custom-call | flops 471859200 | bytes 2965536 | tf_op jit(solution)/shard_map/pallas_call | solution.py:33
  63.5 1.2 %collective-permute-done.13.got_ref = bf16[4,48,768]{2,1,0:T(8,128)(2,1)S(1)} collective-permute-done((bf16[4,48,768]{2,1,0:T(8,128)(2,1)S(1)}, bf16[4,48,768]{2,1,0:T(8,128)(2,1)S(1)}, u32[]{:S(2)}, u32[]{:S(2)}) %collective-permute-start.13) | collective-permute-done | bytes 294944 | tf_op jit(solution)/shard_map/ppermute | solution.py:641
  65.7 1.8 %collective-permute-start.15 = (bf16[48,768]{1,0:T(8,128)(2,1)S(1)}, bf16[48,768]{1,0:T(8,128)(2,1)S(1)}, u32[]{:S(2)}, u32[]{:S(2)}) collective-permute-start(bf16[48,768]{1,0:T(8,128)(2,1)S(1)} %get-tuple-element.81), channel_id=1, source_target_pairs={{0,16},{4,20},{8,24},{12,28},{16,0},{20,4},{24,8},{28,12},{1,17},{... | collective-permute-start | bytes 221192 | tf_op jit(solution)/shard_map/ppermute | solution.py:650
  68.2 2.3 %collective-permute-done.14.r1 = bf16[48,768]{1,0:T(8,128)(2,1)S(1)} collective-permute-done((bf16[48,768]{1,0:T(8,128)(2,1)S(1)}, bf16[48,768]{1,0:T(8,128)(2,1)S(1)}, u32[]{:S(2)}, u32[]{:S(2)}) %collective-permute-start.14) | collective-permute-done | bytes 73760 | tf_op jit(solution)/shard_map/ppermute | solution.py:650
  72.0 15.7 %all_to_all.17.got_ref = bf16[8,56,128]{2,1,0:T(8,128)(2,1)S(1)} all-to-all(bf16[8,56,128]{2,1,0:T(8,128)(2,1)S(1)} %shard_map.183), channel_id=1, replica_groups=mesh['dp'=8,'space'=8,'tensor'=4] {'dp'}, dimensions={0} | all-to-all | bytes 229376 | tf_op jit(solution)/shard_map/all_to_all | solution.py:659
  (51 shorter events, 11.5 us)
Async XLA Ops:
  0.6 17.0 %copy-start.10 = (bf16[9,80,320]{2,1,0:T(8,128)(2,1)S(1)}, bf16[9,80,320]{2,1,0:T(8,128)(2,1)}, u32[]{:S(2)}) copy-start(bf16[9,80,320]{2,1,0:T(8,128)(2,1)} %param.19) | copy-start | bytes 1382404
  1.6 9.1 %collective-permute-start.2 = (bf16[2,4,80,128]{3,2,1,0:T(8,128)(2,1)S(1)}, bf16[2,4,80,128]{3,2,1,0:T(8,128)(2,1)S(1)}, u32[]{:S(2)}, u32[]{:S(2)}) collective-permute-start(bf16[2,4,80,128]{3,2,1,0:T(8,128)(2,1)S(1)} %bitcast.32), channel_id=1, source_target_pairs={{0,3},{1,0},{2,1},{3,2},{4,7},{5,4},{6,5},{7,6},{8,11},{9,8},{10,9... | collective-permute-start | bytes 491528 | tf_op jit(solution)/shard_map/ppermute | solution.py:540
  5.3 6.4 %collective-permute-start.1 = (bf16[2,4,80,128]{3,2,1,0:T(8,128)(2,1)S(1)}, bf16[2,4,80,128]{3,2,1,0:T(8,128)(2,1)S(1)}, u32[]{:S(2)}, u32[]{:S(2)}) collective-permute-start(bf16[2,4,80,128]{3,2,1,0:T(8,128)(2,1)S(1)} %bitcast.33), channel_id=1, source_target_pairs={{0,2},{1,3},{2,0},{3,1},{4,6},{5,7},{6,4},{7,5},{8,10},{9,11},{10,... | collective-permute-start | bytes 491528 | tf_op jit(solution)/shard_map/ppermute | solution.py:540
  5.6 12.1 %collective-permute-start = (bf16[2,4,80,128]{3,2,1,0:T(8,128)(2,1)S(1)}, bf16[2,4,80,128]{3,2,1,0:T(8,128)(2,1)S(1)}, u32[]{:S(2)}, u32[]{:S(2)}) collective-permute-start(bf16[2,4,80,128]{3,2,1,0:T(8,128)(2,1)S(1)} %bitcast.34), channel_id=1, source_target_pairs={{0,1},{1,2},{2,3},{3,0},{4,5},{5,6},{6,7},{7,4},{8,9},{9,10},{10,1... | collective-permute-start | bytes 491528 | tf_op jit(solution)/shard_map/ppermute | solution.py:540
  7.3 10.4 %copy-start.1 = (f32[1,2,4,4,128]{4,3,2,1,0:T(4,128)S(1)}, f32[1,2,4,4,128]{4,3,2,1,0:T(4,128)}, u32[]{:S(2)}) copy-start(f32[1,2,4,4,128]{4,3,2,1,0:T(4,128)} %param.18) | copy-start | bytes 49156
  7.3 15.5 %collective-permute-start.5 = (bf16[2,4,80,128]{3,2,1,0:T(8,128)(2,1)S(1)}, bf16[2,4,80,128]{3,2,1,0:T(8,128)(2,1)S(1)}, u32[]{:S(2)}, u32[]{:S(2)}) collective-permute-start(bf16[2,4,80,128]{3,2,1,0:T(8,128)(2,1)S(1)} %bitcast.28), channel_id=1, source_target_pairs={{0,3},{1,0},{2,1},{3,2},{4,7},{5,4},{6,5},{7,6},{8,11},{9,8},{10,9... | collective-permute-start | bytes 491528 | tf_op jit(solution)/shard_map/ppermute | solution.py:540
  9.3 13.4 %collective-permute-start.4 = (bf16[2,4,80,128]{3,2,1,0:T(8,128)(2,1)S(1)}, bf16[2,4,80,128]{3,2,1,0:T(8,128)(2,1)S(1)}, u32[]{:S(2)}, u32[]{:S(2)}) collective-permute-start(bf16[2,4,80,128]{3,2,1,0:T(8,128)(2,1)S(1)} %bitcast.29), channel_id=1, source_target_pairs={{0,2},{1,3},{2,0},{3,1},{4,6},{5,7},{6,4},{7,5},{8,10},{9,11},{10,... | collective-permute-start | bytes 491528 | tf_op jit(solution)/shard_map/ppermute | solution.py:540
  10.7 12.7 %collective-permute-start.3 = (bf16[2,4,80,128]{3,2,1,0:T(8,128)(2,1)S(1)}, bf16[2,4,80,128]{3,2,1,0:T(8,128)(2,1)S(1)}, u32[]{:S(2)}, u32[]{:S(2)}) collective-permute-start(bf16[2,4,80,128]{3,2,1,0:T(8,128)(2,1)S(1)} %bitcast.30), channel_id=1, source_target_pairs={{0,1},{1,2},{2,3},{3,0},{4,5},{5,6},{6,7},{7,4},{8,9},{9,10},{10,1... | collective-permute-start | bytes 491528 | tf_op jit(solution)/shard_map/ppermute | solution.py:540
  17.7 5.8 %copy-start.11 = (bf16[9,80,320]{2,1,0:T(8,128)(2,1)S(1)}, bf16[9,80,320]{2,1,0:T(8,128)(2,1)}, u32[]{:S(2)}) copy-start(bf16[9,80,320]{2,1,0:T(8,128)(2,1)} %param.20) | copy-start | bytes 1382404
  20.0 12.2 %collective-permute-start.6 = (bf16[992,128]{1,0:T(8,128)(2,1)S(1)}, bf16[992,128]{1,0:T(8,128)(2,1)S(1)}, u32[]{:S(2)}, u32[]{:S(2)}) collective-permute-start(bf16[992,128]{1,0:T(8,128)(2,1)S(1)} %get-tuple-element.56), channel_id=1, source_target_pairs={{0,4},{4,0},{8,12},{12,8},{16,20},{20,16},{24,28},{28,24},{1,5},{5... | collective-permute-start | bytes 761864 | tf_op jit(solution)/shard_map/ppermute | solution.py:563
  21.6 10.6 %collective-permute-start.7 = (bf16[992,128]{1,0:T(8,128)(2,1)S(1)}, bf16[992,128]{1,0:T(8,128)(2,1)S(1)}, u32[]{:S(2)}, u32[]{:S(2)}) collective-permute-start(bf16[992,128]{1,0:T(8,128)(2,1)S(1)} %get-tuple-element.57), channel_id=1, source_target_pairs={{0,28},{4,8},{8,4},{12,16},{16,12},{20,24},{24,20},{28,0},{1,29},{... | collective-permute-start | bytes 761864 | tf_op jit(solution)/shard_map/ppermute | solution.py:562
  23.4 5.5 %copy-start.6 = (f32[80]{0:T(128)S(1)}, f32[80]{0:T(128)}, u32[]{:S(2)}) copy-start(f32[80]{0:T(128)} %param.23) | copy-start | bytes 964
  23.4 5.5 %copy-start.7 = (f32[80]{0:T(128)S(1)}, f32[80]{0:T(128)}, u32[]{:S(2)}) copy-start(f32[80]{0:T(128)} %param.24) | copy-start | bytes 964
  23.4 5.5 %copy-start.8 = (f32[80]{0:T(128)S(1)}, f32[80]{0:T(128)}, u32[]{:S(2)}) copy-start(f32[80]{0:T(128)} %param.25) | copy-start | bytes 964
  23.5 5.5 %copy-start.9 = (f32[80]{0:T(128)S(1)}, f32[80]{0:T(128)}, u32[]{:S(2)}) copy-start(f32[80]{0:T(128)} %param.26) | copy-start | bytes 964
  25.9 4.4 %collective-permute-start.8 = (bf16[640,128]{1,0:T(8,128)(2,1)}, bf16[640,128]{1,0:T(8,128)(2,1)S(1)}, u32[]{:S(2)}, u32[]{:S(2)}) collective-permute-start(bf16[640,128]{1,0:T(8,128)(2,1)} %get-tuple-element.58), channel_id=1, source_target_pairs={{0,4},{4,0},{8,12},{12,8},{16,20},{20,16},{24,28},{28,24},{1,5},{5... | collective-permute-start | bytes 491528 | tf_op jit(solution)/shard_map/ppermute | solution.py:574
  26.9 5.2 %collective-permute-start.9 = (bf16[640,128]{1,0:T(8,128)(2,1)}, bf16[640,128]{1,0:T(8,128)(2,1)S(1)}, u32[]{:S(2)}, u32[]{:S(2)}) collective-permute-start(bf16[640,128]{1,0:T(8,128)(2,1)} %get-tuple-element.59), channel_id=1, source_target_pairs={{0,28},{4,8},{8,4},{12,16},{16,12},{20,24},{24,20},{28,0},{1,29},{... | collective-permute-start | bytes 491528 | tf_op jit(solution)/shard_map/ppermute | solution.py:573
  44.1 3.0 %collective-permute-start.12 = (f32[12,8,128]{2,1,0:T(8,128)S(1)}, f32[12,8,128]{2,1,0:T(8,128)S(1)}, u32[]{:S(2)}, u32[]{:S(2)}) collective-permute-start(f32[12,8,128]{2,1,0:T(8,128)S(1)} %get-tuple-element.66.p0), channel_id=1, source_target_pairs={{0,3},{1,0},{2,1},{3,2},{4,7},{5,4},{6,5},{7,6},{8,11},{9,8},{10,9... | collective-permute-start | bytes 147464 | tf_op jit(solution)/shard_map/ppermute | solution.py:624
  44.5 4.4 %collective-permute-start.11 = (f32[12,8,128]{2,1,0:T(8,128)S(1)}, f32[12,8,128]{2,1,0:T(8,128)S(1)}, u32[]{:S(2)}, u32[]{:S(2)}) collective-permute-start(f32[12,8,128]{2,1,0:T(8,128)S(1)} %get-tuple-element.66.p0), channel_id=1, source_target_pairs={{0,2},{1,3},{2,0},{3,1},{4,6},{5,7},{6,4},{7,5},{8,10},{9,11},{10,... | collective-permute-start | bytes 147464 | tf_op jit(solution)/shard_map/ppermute | solution.py:624
  44.8 4.7 %collective-permute-start.10 = (f32[12,8,128]{2,1,0:T(8,128)S(1)}, f32[12,8,128]{2,1,0:T(8,128)S(1)}, u32[]{:S(2)}, u32[]{:S(2)}) collective-permute-start(f32[12,8,128]{2,1,0:T(8,128)S(1)} %get-tuple-element.66.p0), channel_id=1, source_target_pairs={{0,1},{1,2},{2,3},{3,0},{4,5},{5,6},{6,7},{7,4},{8,9},{9,10},{10,1... | collective-permute-start | bytes 147464 | tf_op jit(solution)/shard_map/ppermute | solution.py:624
  62.6 2.0 %collective-permute-start.13 = (bf16[4,48,768]{2,1,0:T(8,128)(2,1)S(1)}, bf16[4,48,768]{2,1,0:T(8,128)(2,1)S(1)}, u32[]{:S(2)}, u32[]{:S(2)}) collective-permute-start(bf16[4,48,768]{2,1,0:T(8,128)(2,1)S(1)} %get-tuple-element.78), channel_id=1, source_target_pairs={{0,4},{4,0},{8,12},{12,8},{16,20},{20,16},{24,28},{28,24},{1,5},{5... | collective-permute-start | bytes 884744 | tf_op jit(solution)/shard_map/ppermute | solution.py:641
  65.3 5.2 %collective-permute-start.14 = (bf16[48,768]{1,0:T(8,128)(2,1)S(1)}, bf16[48,768]{1,0:T(8,128)(2,1)S(1)}, u32[]{:S(2)}, u32[]{:S(2)}) collective-permute-start(bf16[48,768]{1,0:T(8,128)(2,1)S(1)} %get-tuple-element.80), channel_id=1, source_target_pairs={{0,8},{4,12},{8,16},{12,20},{16,24},{20,28},{24,0},{28,4},{1,9},{5... | collective-permute-start | bytes 221192 | tf_op jit(solution)/shard_map/ppermute | solution.py:650
  65.7 5.5 %collective-permute-start.15 = (bf16[48,768]{1,0:T(8,128)(2,1)S(1)}, bf16[48,768]{1,0:T(8,128)(2,1)S(1)}, u32[]{:S(2)}, u32[]{:S(2)}) collective-permute-start(bf16[48,768]{1,0:T(8,128)(2,1)S(1)} %get-tuple-element.81), channel_id=1, source_target_pairs={{0,16},{4,20},{8,24},{12,28},{16,0},{20,4},{24,8},{28,12},{1,17},{... | collective-permute-start | bytes 221192 | tf_op jit(solution)/shard_map/ppermute | solution.py:650
  67.4 4.5 %collective-permute-start.16 = (bf16[48,768]{1,0:T(8,128)(2,1)S(1)}, bf16[48,768]{1,0:T(8,128)(2,1)S(1)}, u32[]{:S(2)}, u32[]{:S(2)}) collective-permute-start(bf16[48,768]{1,0:T(8,128)(2,1)S(1)} %get-tuple-element.82), channel_id=1, source_target_pairs={{0,24},{4,28},{8,0},{12,4},{16,8},{20,12},{24,16},{28,20},{1,25},{... | collective-permute-start | bytes 221192 | tf_op jit(solution)/shard_map/ppermute | solution.py:650
  (5 other events, 8.2 us)

commit v8 on v7

--- a/solution.py
+++ b/solution.py
@@ -154,14 +154,14 @@
         pre_ref, up_ref, dn_ref, send_a, send_b, fs_ref = refs
     else:
         noise_ref, pre_ref, up_ref, dn_ref, send_a, send_b, perm_ref, fs_ref = refs
-    t = t_ref[0]
+    t = t_ref[5]
     for k in range(4):
         base = pl.multiple_of(lax.rem(t - k + 4, 4) * CH, 16)
         for im in range(2):
             for r in range(ROWS):
                 lo = im * PIX + r * COLS
                 fs_ref[pl.ds(base, CH), lo : lo + COLS] = (f0, f1, f2, f3)[k][im, r]
-    odd = t_ref[1] > 0
+    odd = t_ref[3] > 0
     count = 2 if last else 4
     if not last:
         for index in range(2):
@@ -534,46 +534,6 @@
 ):
     space = lax.axis_size("space")
     s_index = lax.axis_index("space").astype(jnp.int32)
-    spot = jnp.stack([lax.axis_index("tensor").astype(jnp.int32), s_index & 1])
-
-    def gather(own):
-        return [own] + [lax.ppermute(own, "tensor", ring("tensor", k)) for k in (1, 2, 3)]
-
-    own_p = feat_policy[0].transpose(0, 2, 1, 3)
-    feat_ref, own_p = lax.optimization_barrier((feat_ref, own_p))
-    own_r = feat_ref[0].transpose(0, 2, 1, 3)
-    parts_p = gather(own_p)
-    parts_r = gather(own_r)
-
-    conv_flops = 2 * 9 * C * CH * 2 * PIX
-    wide = arr((2 * CH, PIX), F32)
-    thin = arr((2 * CH, COLS), F32)
-
-    partner = [(i, i ^ 1) for i in range(space)]
-    across = [(i, (i + 1 if i % 2 else i - 1) % space) for i in range(space)]
-    pre_p, up_p, dn_p, to_ap, to_bp, feats = call(
-        functools.partial(conv_kernel, False),
-        [spot, *parts_p, w1_policy.reshape(9 * CH, C), noise[0]],
-        [wide, thin, thin, arr((992, COLS), BF16), arr((992, COLS), BF16), arr((C, 2 * PIX), BF16)],
-        conv_flops,
-        smem=1,
-        scratch=[pltpu.VMEM((C, 2 * PIX), BF16)],
-    )
-    got_bp = lax.ppermute(to_bp, "space", across)
-    got_ap = lax.ppermute(to_ap, "space", partner)
-    own_r, pre_p = lax.optimization_barrier((parts_r[0], pre_p))
-    pre_r, up_r, dn_r, to_ar, to_br = call(
-        functools.partial(conv_kernel, True),
-        [spot, own_r, *parts_r[1:], w1_ref.reshape(9 * CH, C)],
-        [wide, thin, thin, arr((640, COLS), BF16), arr((640, COLS), BF16)],
-        conv_flops,
-        smem=1,
-        scratch=[pltpu.VMEM((C, 2 * PIX), BF16)],
-    )
-    got_br = lax.ppermute(to_br, "space", across)
-    got_ar = lax.ppermute(to_ar, "space", partner)
-
-    pre_r, timestep = lax.optimization_barrier((pre_r, timestep))
     is_top = (s_index == 0).astype(jnp.int32)
     is_bottom = (s_index == space - 1).astype(jnp.int32)
     place = jnp.stack(
@@ -587,6 +547,45 @@
             timestep[0].astype(jnp.int32),
         ]
     )
+
+    def gather(own):
+        return [own] + [lax.ppermute(own, "tensor", ring("tensor", k)) for k in (3, 2, 1)][::-1]
+
+    own_p = feat_policy[0].transpose(0, 2, 1, 3)
+    feat_ref, own_p = lax.optimization_barrier((feat_ref, own_p))
+    own_r = feat_ref[0].transpose(0, 2, 1, 3)
+    parts_p = gather(own_p)
+    parts_r = gather(own_r)
+
+    conv_flops = 2 * 9 * C * CH * 2 * PIX
+    wide = arr((2 * CH, PIX), F32)
+    thin = arr((2 * CH, COLS), F32)
+
+    partner = [(i, i ^ 1) for i in range(space)]
+    across = [(i, (i + 1 if i % 2 else i - 1) % space) for i in range(space)]
+    pre_p, up_p, dn_p, to_ap, to_bp, feats = call(
+        functools.partial(conv_kernel, False),
+        [place, *parts_p, w1_policy.reshape(9 * CH, C), noise[0]],
+        [wide, thin, thin, arr((992, COLS), BF16), arr((992, COLS), BF16), arr((C, 2 * PIX), BF16)],
+        conv_flops,
+        smem=1,
+        scratch=[pltpu.VMEM((C, 2 * PIX), BF16)],
+    )
+    got_bp = lax.ppermute(to_bp, "space", across)
+    got_ap = lax.ppermute(to_ap, "space", partner)
+    own_r, pre_p = lax.optimization_barrier((parts_r[0], pre_p))
+    pre_r, up_r, dn_r, to_ar, to_br = call(
+        functools.partial(conv_kernel, True),
+        [place, own_r, *parts_r[1:], w1_ref.reshape(9 * CH, C)],
+        [wide, thin, thin, arr((640, COLS), BF16), arr((640, COLS), BF16)],
+        conv_flops,
+        smem=1,
+        scratch=[pltpu.VMEM((C, 2 * PIX), BF16)],
+    )
+    got_br = lax.ppermute(to_br, "space", across)
+    got_ar = lax.ppermute(to_ar, "space", partner)
+
+    pre_r, b1_policy = lax.optimization_barrier((pre_r, b1_policy))
     vectors = [b1_policy, b1_ref, gn_gain_policy, gn_bias_policy, gn_gain_ref, gn_bias_ref]
     columns, lift, drop, noise_rows = call(
         prep_kernel,

time: 89.9 us -> 89.1 us (level)
    ppermute x6, waiting for transfers between devices: 7.53 us -> 6.21 us  [gather(): lax.ppermute(own, 'tensor', ring('tensor', k))]
    ppermute x1, waiting for transfers between devices: 1.87 us -> 2.99 us  [body(): got_br = lax.ppermute(to_br, 'space', across)]
  transfers between devices with their start and end apart: 17 -> 17, of which waited for: 11 -> 10; matrix products, arithmetic and copies ran while one was open for 1% -> 1% of each run, Pallas kernels for 6% -> 5%
where the time goes in v8:
time: 89.1 us; the launch traced here: 87.6 us
  blocking collectives  34.6 us (39%)
  waiting for transfers between devices  18 us (20%)
  starting transfers between devices  17.9 us (20%)
  Pallas kernels  12.3 us (14%)
  local copies, waits for them, and re-layouts  2.67 us (3%)
  between operations  2.11 us (2%)
    all_to_all x1, blocking collectives, body(): packed = lax.all_to_all(packed, 'dp', 0, 0, tiled=True)  15.7 us
    pallas_call x10, Pallas kernels, call(): pl.pallas_call(kernel, out_shape=outs, in_specs=[SM] * smem + [VM] * (len...  12.3 us
    all_to_all x1, blocking collectives, body(): partial = lax.all_to_all(partial, 'space', 0, 0, tiled=True)  9.7 us
    all_to_all x1, blocking collectives, body(): sums = lax.all_to_all(sums, 'space', 0, 0, tiled=True)  9.15 us
    ppermute x6, starting transfers between devices, gather(): lax.ppermute(own, 'tensor', ring('tensor', k))  8.15 us
    ppermute x6, waiting for transfers between devices, gather(): lax.ppermute(own, 'tensor', ring('tensor', k))  6.21 us
    ppermute x3, waiting for transfers between devices, body(): lax.ppermute(part, 'tensor', ring('tensor', k))  3.87 us
    ppermute x3, waiting for transfers between devices, body(): lax.ppermute(sent, 'space', ring('space', 2 * k))  3.75 us
  transfers between devices with their start and end apart: 17, of which 10 were waited for; matrix products, arithmetic and copies ran while one was open for 1% of the time, Pallas kernels for 5%

profile of v8, /device:TPU:1, one launch (start us, length us, event | category | flops | bytes accessed | tf_op | source)
XLA Modules:
  0.0 87.6 jit_solution(6886227117416407178)
XLA Ops:
  0.6 1.0 %copy.24 = bf16[1,2,80,4,128]{4,2,3,1,0:T(8,128)(2,1)S(1)} copy(bf16[1,2,80,4,128]{4,3,2,1,0:T(4,128)(2,1)} %param.16) | data formatting | bytes 327680 | tf_op args[0]
  1.6 3.6 %collective-permute-start.2 = (bf16[2,4,80,128]{3,2,1,0:T(8,128)(2,1)S(1)}, bf16[2,4,80,128]{3,2,1,0:T(8,128)(2,1)S(1)}, u32[]{:S(2)}, u32[]{:S(2)}) collective-permute-start(bf16[2,4,80,128]{3,2,1,0:T(8,128)(2,1)S(1)} %bitcast.32), channel_id=1, source_target_pairs={{0,3},{1,0},{2,1},{3,2},{4,7},{5,4},{6,5},{7,6},{8,11},{9,8},{10,9... | collective-permute-start | bytes 491528 | tf_op jit(solution)/shard_map/ppermute | solution.py:552
  6.3 0.9 %copy.23 = bf16[1,2,80,4,128]{4,2,3,1,0:T(8,128)(2,1)S(1)} copy(bf16[1,2,80,4,128]{4,3,2,1,0:T(4,128)(2,1)} %param.17) | data formatting | bytes 327680 | tf_op jit(solution)/shard_map/optimization_barrier | solution.py:555
  7.3 2.1 %collective-permute-start.5 = (bf16[2,4,80,128]{3,2,1,0:T(8,128)(2,1)S(1)}, bf16[2,4,80,128]{3,2,1,0:T(8,128)(2,1)S(1)}, u32[]{:S(2)}, u32[]{:S(2)}) collective-permute-start(bf16[2,4,80,128]{3,2,1,0:T(8,128)(2,1)S(1)} %bitcast.28), channel_id=1, source_target_pairs={{0,3},{1,0},{2,1},{3,2},{4,7},{5,4},{6,5},{7,6},{8,11},{9,8},{10,9... | collective-permute-start | bytes 491528 | tf_op jit(solution)/shard_map/ppermute | solution.py:552
  9.3 1.4 %collective-permute-start.4 = (bf16[2,4,80,128]{3,2,1,0:T(8,128)(2,1)S(1)}, bf16[2,4,80,128]{3,2,1,0:T(8,128)(2,1)S(1)}, u32[]{:S(2)}, u32[]{:S(2)}) collective-permute-start(bf16[2,4,80,128]{3,2,1,0:T(8,128)(2,1)S(1)} %bitcast.29), channel_id=1, source_target_pairs={{0,2},{1,3},{2,0},{3,1},{4,6},{5,7},{6,4},{7,5},{8,10},{9,11},{10,... | collective-permute-start | bytes 491528 | tf_op jit(solution)/shard_map/ppermute | solution.py:552
  12.1 5.5 %collective-permute-done.f1 = bf16[2,4,80,128]{3,2,1,0:T(8,128)(2,1)S(1)} collective-permute-done((bf16[2,4,80,128]{3,2,1,0:T(8,128)(2,1)S(1)}, bf16[2,4,80,128]{3,2,1,0:T(8,128)(2,1)S(1)}, u32[]{:S(2)}, u32[]{:S(2)}) %collective-permute-start) | collective-permute-done | bytes 163872 | tf_op jit(solution)/shard_map/ppermute | solution.py:552
  17.7 2.3 %shard_map.175 = (f32[160,512]{1,0:T(8,128)S(1)}, f32[160,128]{1,0:T(8,128)S(1)}, f32[160,128]{1,0:T(8,128)S(1)}, bf16[992,128]{1,0:T(8,128)(2,1)S(1)}, bf16[992...) custom-call(s32[7]{0:T(128)S(1)} %stack.31.t_ref.place_ref.edge_ref.x_ref, bf16[2,4,80,128]{3,2,1,0:T(8,128)(2,1)S(1)} %bitcast.35, ...), custom_call_target="tpu_custom_call" | custom-call | flops 471859200 | bytes 2787356 | tf_op jit(solution)/shard_map/pallas_call | solution.py:33
  20.0 1.6 %collective-permute-start.6 = (bf16[992,128]{1,0:T(8,128)(2,1)S(1)}, bf16[992,128]{1,0:T(8,128)(2,1)S(1)}, u32[]{:S(2)}, u32[]{:S(2)}) collective-permute-start(bf16[992,128]{1,0:T(8,128)(2,1)S(1)} %get-tuple-element.55), channel_id=1, source_target_pairs={{0,4},{4,0},{8,12},{12,8},{16,20},{20,16},{24,28},{28,24},{1,5},{5... | collective-permute-start | bytes 761864 | tf_op jit(solution)/shard_map/ppermute | solution.py:575
  21.6 1.2 %collective-permute-start.7 = (bf16[992,128]{1,0:T(8,128)(2,1)S(1)}, bf16[992,128]{1,0:T(8,128)(2,1)S(1)}, u32[]{:S(2)}, u32[]{:S(2)}) collective-permute-start(bf16[992,128]{1,0:T(8,128)(2,1)S(1)} %get-tuple-element.56), channel_id=1, source_target_pairs={{0,28},{4,8},{8,4},{12,16},{16,12},{20,24},{24,20},{28,0},{1,29},{... | collective-permute-start | bytes 761864 | tf_op jit(solution)/shard_map/ppermute | solution.py:574
  23.5 1.7 %shard_map.176 = (f32[160,512]{1,0:T(8,128)S(1)}, f32[160,128]{1,0:T(8,128)S(1)}, f32[160,128]{1,0:T(8,128)S(1)}, bf16[640,128]{1,0:T(8,128)(2,1)S(1)}, bf16[640,128]{1,0:T(8,128)(2,1)S(1)}) custom-call(s32[7]{0:T(128)S(1)} %stack.31.t_ref.place_ref.edge_ref.x_ref, bf16[2,4,80,128]{3,2,1,0:T(8,128)(2,1)S(1)} %bitcast.31, ...), custom_call_target="tpu_custom_call" | custom-call | flops 471859200 | bytes 1935388 | tf_op jit(solution)/shard_map/pallas_call | solution.py:33
  25.2 1.1 %collective-permute-start.8 = (bf16[640,128]{1,0:T(8,128)(2,1)S(1)}, bf16[640,128]{1,0:T(8,128)(2,1)S(1)}, u32[]{:S(2)}, u32[]{:S(2)}) collective-permute-start(bf16[640,128]{1,0:T(8,128)(2,1)S(1)} %get-tuple-element.57), channel_id=1, source_target_pairs={{0,4},{4,0},{8,12},{12,8},{16,20},{20,16},{24,28},{28,24},{1,5},{5... | collective-permute-start | bytes 491528 | tf_op jit(solution)/shard_map/ppermute | solution.py:586
  28.4 3.0 %collective-permute-done.9.got_br = bf16[640,128]{1,0:T(8,128)(2,1)S(1)} collective-permute-done((bf16[640,128]{1,0:T(8,128)(2,1)S(1)}, bf16[640,128]{1,0:T(8,128)(2,1)S(1)}, u32[]{:S(2)}, u32[]{:S(2)}) %collective-permute-start.9) | collective-permute-done | bytes 163872 | tf_op jit(solution)/shard_map/ppermute | solution.py:585
  31.4 1.1 %shard_map.178 = (f32[160,1280]{1,0:T(8,128)S(1)}, f32[160,768]{1,0:T(8,128)S(1)}, f32[8,8,128]{2,1,0:T(8,128)S(1)}, f32[8,16,128]{2,1,0:T(8,128)S(1)}) custom-call(s32[7]{0:T(128)S(1)} %stack.31.t_ref.place_ref.edge_ref.x_ref, f32[160,512]{1,0:T(8,128)S(1)} %get-tuple-element.47.pre_p, f32[160,128]{1,0:T(8,128)S(1)} %get-tuple-element.48.up_p, ...), custom_call_target="tpu_custom_call" | custom-call | flops 1000000 | bytes 3325980 | tf_op jit(solution)/shard_map/pallas_call | solution.py:33
  32.5 9.2 %all_to_all.15.sums_ref = f32[8,16,128]{2,1,0:T(8,128)S(1)} all-to-all(f32[8,16,128]{2,1,0:T(8,128)S(1)} %get-tuple-element.64), channel_id=1, replica_groups=mesh['dp'=8,'space'=8,'tensor'=4] {'space'}, dimensions={0} | all-to-all | bytes 131072 | tf_op jit(solution)/shard_map/all_to_all | solution.py:615
  41.6 1.6 %shard_map.179 = (f32[12,8,128]{2,1,0:T(8,128)S(1)}, bf16[160,512]{1,0:T(8,128)(2,1)S(1)}, f32[160,128]{1,0:T(8,128)S(1)}) custom-call(s32[7]{0:T(128)S(1)} %stack.31.t_ref.place_ref.edge_ref.x_ref, f32[160,1280]{1,0:T(8,128)S(1)} %get-tuple-element.62.ext_p, f32[160,768]{1,0:T(8,128)S(1)} %get-tuple-element.63.ext_r, ...), custom_call_target="tpu_custom_call" | custom-call | flops 10000000 | bytes 1799196 | tf_op jit(solution)/shard_map/pallas_call | solution.py:33
  44.8 1.5 %collective-permute-done.12.p3 = f32[12,8,128]{2,1,0:T(8,128)S(1)} collective-permute-done((f32[12,8,128]{2,1,0:T(8,128)S(1)}, f32[12,8,128]{2,1,0:T(8,128)S(1)}, u32[]{:S(2)}, u32[]{:S(2)}) %collective-permute-start.12) | collective-permute-done | bytes 49184 | tf_op jit(solution)/shard_map/ppermute | solution.py:623
  46.3 1.8 %collective-permute-done.11.p2 = f32[12,8,128]{2,1,0:T(8,128)S(1)} collective-permute-done((f32[12,8,128]{2,1,0:T(8,128)S(1)}, f32[12,8,128]{2,1,0:T(8,128)S(1)}, u32[]{:S(2)}, u32[]{:S(2)}) %collective-permute-start.11) | collective-permute-done | bytes 49184 | tf_op jit(solution)/shard_map/ppermute | solution.py:623
  48.7 1.2 %shard_map.180 = (f32[160,768]{1,0:T(8,128)S(1)}, f32[32,128]{1,0:T(8,128)S(1)}, f32[8,24,128]{2,1,0:T(8,128)S(1)}) custom-call(s32[7]{0:T(128)S(1)} %stack.31.t_ref.place_ref.edge_ref.x_ref, f32[12,8,128]{2,1,0:T(8,128)S(1)} %get-tuple-element.66.p0, f32[12,8,128]{2,1,0:T(8,128)S(1)} %collective-permute-done.10.p1, ...), custom_call_target="tpu_custom_call" | custom-call | flops 10000000 | bytes 2005532 | tf_op jit(solution)/shard_map/pallas_call | solution.py:33
  49.9 9.7 %all_to_all.16.red_ref = f32[8,24,128]{2,1,0:T(8,128)S(1)} all-to-all(f32[8,24,128]{2,1,0:T(8,128)S(1)} %get-tuple-element.72), channel_id=1, replica_groups=mesh['dp'=8,'space'=8,'tensor'=4] {'space'}, dimensions={0} | all-to-all | bytes 196608 | tf_op jit(solution)/shard_map/all_to_all | solution.py:631
  59.6 2.2 %shard_map.181 = (f32[4,40,768]{2,1,0:T(8,128)S(1)}, bf16[4,48,768]{2,1,0:T(8,128)(2,1)S(1)}, f32[32,128]{1,0:T(8,128)S(1)}, f32[1,1]{1,0:T(1,128)}) custom-call(s32[7]{0:T(128)S(1)} %stack.31.t_ref.place_ref.edge_ref.x_ref, f32[160,768]{1,0:T(8,128)S(1)} %get-tuple-element.71.gnorm_ref, f32[160,1280]{1,0:T(8,128)S(1)} %get-tuple-element.62.ext_p, ...), custom_call_target="tpu_custom_call" | custom-call | flops 471859200 | bytes 2965536 | tf_op jit(solution)/shard_map/pallas_call | solution.py:33
  62.7 1.2 %collective-permute-done.13.got_ref = bf16[4,48,768]{2,1,0:T(8,128)(2,1)S(1)} collective-permute-done((bf16[4,48,768]{2,1,0:T(8,128)(2,1)S(1)}, bf16[4,48,768]{2,1,0:T(8,128)(2,1)S(1)}, u32[]{:S(2)}, u32[]{:S(2)}) %collective-permute-start.13) | collective-permute-done | bytes 294944 | tf_op jit(solution)/shard_map/ppermute | solution.py:640
  64.9 1.8 %collective-permute-start.15 = (bf16[48,768]{1,0:T(8,128)(2,1)S(1)}, bf16[48,768]{1,0:T(8,128)(2,1)S(1)}, u32[]{:S(2)}, u32[]{:S(2)}) collective-permute-start(bf16[48,768]{1,0:T(8,128)(2,1)S(1)} %get-tuple-element.81), channel_id=1, source_target_pairs={{0,16},{4,20},{8,24},{12,28},{16,0},{20,4},{24,8},{28,12},{1,17},{... | collective-permute-start | bytes 221192 | tf_op jit(solution)/shard_map/ppermute | solution.py:649
  67.4 2.3 %collective-permute-done.14.r1 = bf16[48,768]{1,0:T(8,128)(2,1)S(1)} collective-permute-done((bf16[48,768]{1,0:T(8,128)(2,1)S(1)}, bf16[48,768]{1,0:T(8,128)(2,1)S(1)}, u32[]{:S(2)}, u32[]{:S(2)}) %collective-permute-start.14) | collective-permute-done | bytes 73760 | tf_op jit(solution)/shard_map/ppermute | solution.py:649
  71.2 15.7 %all_to_all.17.got_ref = bf16[8,56,128]{2,1,0:T(8,128)(2,1)S(1)} all-to-all(bf16[8,56,128]{2,1,0:T(8,128)(2,1)S(1)} %shard_map.183), channel_id=1, replica_groups=mesh['dp'=8,'space'=8,'tensor'=4] {'dp'}, dimensions={0} | all-to-all | bytes 229376 | tf_op jit(solution)/shard_map/all_to_all | solution.py:658
  (50 shorter events, 10.7 us)
Async XLA Ops:
  0.6 17.0 %copy-start.10 = (bf16[9,80,320]{2,1,0:T(8,128)(2,1)S(1)}, bf16[9,80,320]{2,1,0:T(8,128)(2,1)}, u32[]{:S(2)}) copy-start(bf16[9,80,320]{2,1,0:T(8,128)(2,1)} %param.19) | copy-start | bytes 1382404
  1.6 9.1 %collective-permute-start.2 = (bf16[2,4,80,128]{3,2,1,0:T(8,128)(2,1)S(1)}, bf16[2,4,80,128]{3,2,1,0:T(8,128)(2,1)S(1)}, u32[]{:S(2)}, u32[]{:S(2)}) collective-permute-start(bf16[2,4,80,128]{3,2,1,0:T(8,128)(2,1)S(1)} %bitcast.32), channel_id=1, source_target_pairs={{0,3},{1,0},{2,1},{3,2},{4,7},{5,4},{6,5},{7,6},{8,11},{9,8},{10,9... | collective-permute-start | bytes 491528 | tf_op jit(solution)/shard_map/ppermute | solution.py:552
  5.3 6.9 %collective-permute-start.1 = (bf16[2,4,80,128]{3,2,1,0:T(8,128)(2,1)S(1)}, bf16[2,4,80,128]{3,2,1,0:T(8,128)(2,1)S(1)}, u32[]{:S(2)}, u32[]{:S(2)}) collective-permute-start(bf16[2,4,80,128]{3,2,1,0:T(8,128)(2,1)S(1)} %bitcast.33), channel_id=1, source_target_pairs={{0,2},{1,3},{2,0},{3,1},{4,6},{5,7},{6,4},{7,5},{8,10},{9,11},{10,... | collective-permute-start | bytes 491528 | tf_op jit(solution)/shard_map/ppermute | solution.py:552
  5.6 12.1 %collective-permute-start = (bf16[2,4,80,128]{3,2,1,0:T(8,128)(2,1)S(1)}, bf16[2,4,80,128]{3,2,1,0:T(8,128)(2,1)S(1)}, u32[]{:S(2)}, u32[]{:S(2)}) collective-permute-start(bf16[2,4,80,128]{3,2,1,0:T(8,128)(2,1)S(1)} %bitcast.34), channel_id=1, source_target_pairs={{0,1},{1,2},{2,3},{3,0},{4,5},{5,6},{6,7},{7,4},{8,9},{9,10},{10,1... | collective-permute-start | bytes 491528 | tf_op jit(solution)/shard_map/ppermute | solution.py:552
  7.3 15.5 %collective-permute-start.5 = (bf16[2,4,80,128]{3,2,1,0:T(8,128)(2,1)S(1)}, bf16[2,4,80,128]{3,2,1,0:T(8,128)(2,1)S(1)}, u32[]{:S(2)}, u32[]{:S(2)}) collective-permute-start(bf16[2,4,80,128]{3,2,1,0:T(8,128)(2,1)S(1)} %bitcast.28), channel_id=1, source_target_pairs={{0,3},{1,0},{2,1},{3,2},{4,7},{5,4},{6,5},{7,6},{8,11},{9,8},{10,9... | collective-permute-start | bytes 491528 | tf_op jit(solution)/shard_map/ppermute | solution.py:552
  9.3 13.4 %collective-permute-start.4 = (bf16[2,4,80,128]{3,2,1,0:T(8,128)(2,1)S(1)}, bf16[2,4,80,128]{3,2,1,0:T(8,128)(2,1)S(1)}, u32[]{:S(2)}, u32[]{:S(2)}) collective-permute-start(bf16[2,4,80,128]{3,2,1,0:T(8,128)(2,1)S(1)} %bitcast.29), channel_id=1, source_target_pairs={{0,2},{1,3},{2,0},{3,1},{4,6},{5,7},{6,4},{7,5},{8,10},{9,11},{10,... | collective-permute-start | bytes 491528 | tf_op jit(solution)/shard_map/ppermute | solution.py:552
  10.7 12.7 %collective-permute-start.3 = (bf16[2,4,80,128]{3,2,1,0:T(8,128)(2,1)S(1)}, bf16[2,4,80,128]{3,2,1,0:T(8,128)(2,1)S(1)}, u32[]{:S(2)}, u32[]{:S(2)}) collective-permute-start(bf16[2,4,80,128]{3,2,1,0:T(8,128)(2,1)S(1)} %bitcast.30), channel_id=1, source_target_pairs={{0,1},{1,2},{2,3},{3,0},{4,5},{5,6},{6,7},{7,4},{8,9},{9,10},{10,1... | collective-permute-start | bytes 491528 | tf_op jit(solution)/shard_map/ppermute | solution.py:552
  10.7 6.9 %copy-start.1 = (f32[1,2,4,4,128]{4,3,2,1,0:T(4,128)S(1)}, f32[1,2,4,4,128]{4,3,2,1,0:T(4,128)}, u32[]{:S(2)}) copy-start(f32[1,2,4,4,128]{4,3,2,1,0:T(4,128)} %param.18) | copy-start | bytes 49156
  17.7 5.8 %copy-start.11 = (bf16[9,80,320]{2,1,0:T(8,128)(2,1)S(1)}, bf16[9,80,320]{2,1,0:T(8,128)(2,1)}, u32[]{:S(2)}) copy-start(bf16[9,80,320]{2,1,0:T(8,128)(2,1)} %param.20) | copy-start | bytes 1382404
  20.0 11.4 %collective-permute-start.6 = (bf16[992,128]{1,0:T(8,128)(2,1)S(1)}, bf16[992,128]{1,0:T(8,128)(2,1)S(1)}, u32[]{:S(2)}, u32[]{:S(2)}) collective-permute-start(bf16[992,128]{1,0:T(8,128)(2,1)S(1)} %get-tuple-element.55), channel_id=1, source_target_pairs={{0,4},{4,0},{8,12},{12,8},{16,20},{20,16},{24,28},{28,24},{1,5},{5... | collective-permute-start | bytes 761864 | tf_op jit(solution)/shard_map/ppermute | solution.py:575
  21.6 9.8 %collective-permute-start.7 = (bf16[992,128]{1,0:T(8,128)(2,1)S(1)}, bf16[992,128]{1,0:T(8,128)(2,1)S(1)}, u32[]{:S(2)}, u32[]{:S(2)}) collective-permute-start(bf16[992,128]{1,0:T(8,128)(2,1)S(1)} %get-tuple-element.56), channel_id=1, source_target_pairs={{0,28},{4,8},{8,4},{12,16},{16,12},{20,24},{24,20},{28,0},{1,29},{... | collective-permute-start | bytes 761864 | tf_op jit(solution)/shard_map/ppermute | solution.py:574
  23.4 3.5 %copy-start = (f32[1000,80]{0,1:T(8,128)S(1)}, f32[1000,80]{0,1:T(8,128)}, u32[]{:S(2)}) copy-start(f32[1000,80]{0,1:T(8,128)} %param.29) | copy-start | bytes 960004
  23.4 3.5 %copy-start.5 = (f32[80]{0:T(128)S(1)}, f32[80]{0:T(128)}, u32[]{:S(2)}) copy-start(f32[80]{0:T(128)} %param.22) | copy-start | bytes 964
  23.4 3.5 %copy-start.6 = (f32[80]{0:T(128)S(1)}, f32[80]{0:T(128)}, u32[]{:S(2)}) copy-start(f32[80]{0:T(128)} %param.23) | copy-start | bytes 964
  23.4 3.5 %copy-start.7 = (f32[80]{0:T(128)S(1)}, f32[80]{0:T(128)}, u32[]{:S(2)}) copy-start(f32[80]{0:T(128)} %param.24) | copy-start | bytes 964
  25.2 3.2 %collective-permute-start.8 = (bf16[640,128]{1,0:T(8,128)(2,1)S(1)}, bf16[640,128]{1,0:T(8,128)(2,1)S(1)}, u32[]{:S(2)}, u32[]{:S(2)}) collective-permute-start(bf16[640,128]{1,0:T(8,128)(2,1)S(1)} %get-tuple-element.57), channel_id=1, source_target_pairs={{0,4},{4,0},{8,12},{12,8},{16,20},{20,16},{24,28},{28,24},{1,5},{5... | collective-permute-start | bytes 491528 | tf_op jit(solution)/shard_map/ppermute | solution.py:586
  26.3 5.0 %collective-permute-start.9 = (bf16[640,128]{1,0:T(8,128)(2,1)S(1)}, bf16[640,128]{1,0:T(8,128)(2,1)S(1)}, u32[]{:S(2)}, u32[]{:S(2)}) collective-permute-start(bf16[640,128]{1,0:T(8,128)(2,1)S(1)} %get-tuple-element.58), channel_id=1, source_target_pairs={{0,28},{4,8},{8,4},{12,16},{16,12},{20,24},{24,20},{28,0},{1,29},{... | collective-permute-start | bytes 491528 | tf_op jit(solution)/shard_map/ppermute | solution.py:585
  43.3 3.0 %collective-permute-start.12 = (f32[12,8,128]{2,1,0:T(8,128)S(1)}, f32[12,8,128]{2,1,0:T(8,128)S(1)}, u32[]{:S(2)}, u32[]{:S(2)}) collective-permute-start(f32[12,8,128]{2,1,0:T(8,128)S(1)} %get-tuple-element.66.p0), channel_id=1, source_target_pairs={{0,3},{1,0},{2,1},{3,2},{4,7},{5,4},{6,5},{7,6},{8,11},{9,8},{10,9... | collective-permute-start | bytes 147464 | tf_op jit(solution)/shard_map/ppermute | solution.py:623
  43.7 4.4 %collective-permute-start.11 = (f32[12,8,128]{2,1,0:T(8,128)S(1)}, f32[12,8,128]{2,1,0:T(8,128)S(1)}, u32[]{:S(2)}, u32[]{:S(2)}) collective-permute-start(f32[12,8,128]{2,1,0:T(8,128)S(1)} %get-tuple-element.66.p0), channel_id=1, source_target_pairs={{0,2},{1,3},{2,0},{3,1},{4,6},{5,7},{6,4},{7,5},{8,10},{9,11},{10,... | collective-permute-start | bytes 147464 | tf_op jit(solution)/shard_map/ppermute | solution.py:623
  44.0 4.7 %collective-permute-start.10 = (f32[12,8,128]{2,1,0:T(8,128)S(1)}, f32[12,8,128]{2,1,0:T(8,128)S(1)}, u32[]{:S(2)}, u32[]{:S(2)}) collective-permute-start(f32[12,8,128]{2,1,0:T(8,128)S(1)} %get-tuple-element.66.p0), channel_id=1, source_target_pairs={{0,1},{1,2},{2,3},{3,0},{4,5},{5,6},{6,7},{7,4},{8,9},{9,10},{10,1... | collective-permute-start | bytes 147464 | tf_op jit(solution)/shard_map/ppermute | solution.py:623
  61.9 2.0 %collective-permute-start.13 = (bf16[4,48,768]{2,1,0:T(8,128)(2,1)S(1)}, bf16[4,48,768]{2,1,0:T(8,128)(2,1)S(1)}, u32[]{:S(2)}, u32[]{:S(2)}) collective-permute-start(bf16[4,48,768]{2,1,0:T(8,128)(2,1)S(1)} %get-tuple-element.78), channel_id=1, source_target_pairs={{0,4},{4,0},{8,12},{12,8},{16,20},{20,16},{24,28},{28,24},{1,5},{5... | collective-permute-start | bytes 884744 | tf_op jit(solution)/shard_map/ppermute | solution.py:640
  64.5 5.2 %collective-permute-start.14 = (bf16[48,768]{1,0:T(8,128)(2,1)S(1)}, bf16[48,768]{1,0:T(8,128)(2,1)S(1)}, u32[]{:S(2)}, u32[]{:S(2)}) collective-permute-start(bf16[48,768]{1,0:T(8,128)(2,1)S(1)} %get-tuple-element.80), channel_id=1, source_target_pairs={{0,8},{4,12},{8,16},{12,20},{16,24},{20,28},{24,0},{28,4},{1,9},{5... | collective-permute-start | bytes 221192 | tf_op jit(solution)/shard_map/ppermute | solution.py:649
  64.9 5.5 %collective-permute-start.15 = (bf16[48,768]{1,0:T(8,128)(2,1)S(1)}, bf16[48,768]{1,0:T(8,128)(2,1)S(1)}, u32[]{:S(2)}, u32[]{:S(2)}) collective-permute-start(bf16[48,768]{1,0:T(8,128)(2,1)S(1)} %get-tuple-element.81), channel_id=1, source_target_pairs={{0,16},{4,20},{8,24},{12,28},{16,0},{20,4},{24,8},{28,12},{1,17},{... | collective-permute-start | bytes 221192 | tf_op jit(solution)/shard_map/ppermute | solution.py:649
  66.7 4.5 %collective-permute-start.16 = (bf16[48,768]{1,0:T(8,128)(2,1)S(1)}, bf16[48,768]{1,0:T(8,128)(2,1)S(1)}, u32[]{:S(2)}, u32[]{:S(2)}) collective-permute-start(bf16[48,768]{1,0:T(8,128)(2,1)S(1)} %get-tuple-element.82), channel_id=1, source_target_pairs={{0,24},{4,28},{8,0},{12,4},{16,8},{20,12},{24,16},{28,20},{1,25},{... | collective-permute-start | bytes 221192 | tf_op jit(solution)/shard_map/ppermute | solution.py:649
  (5 other events, 11.4 us)

commit v9 on v8

--- a/solution.py
+++ b/solution.py
@@ -6,6 +6,7 @@
 from jax.experimental import pallas as pl
 from jax.experimental.pallas import tpu as pltpu
 from jax.sharding import PartitionSpec as P
+
 
 C = 320
 GROUPS = 32
@@ -549,7 +550,10 @@
     )
 
     def gather(own):
-        return [own] + [lax.ppermute(own, "tensor", ring("tensor", k)) for k in (3, 2, 1)][::-1]
+        parts = [own]
+        for k in (1, 2, 3):
+            parts.append(lax.ppermute(own, "tensor", ring("tensor", k)))
+        return parts
 
     own_p = feat_policy[0].transpose(0, 2, 1, 3)
     feat_ref, own_p = lax.optimization_barrier((feat_ref, own_p))

time: 89.1 us -> 89.1 us (level)
  no operation moved by 1% of the time
where the time goes in v9:
time: 89.1 us; the launch traced here: 87.6 us
  blocking collectives  34.6 us (39%)
  waiting for transfers between devices  18 us (20%)
  starting transfers between devices  17.9 us (20%)
  Pallas kernels  12.3 us (14%)
  local copies, waits for them, and re-layouts  2.67 us (3%)
  between operations  2.11 us (2%)
    all_to_all x1, blocking collectives, body(): packed = lax.all_to_all(packed, 'dp', 0, 0, tiled=True)  15.7 us
    pallas_call x10, Pallas kernels, call(): pl.pallas_call(kernel, out_shape=outs, in_specs=[SM] * smem + [VM] * (len...  12.3 us
    all_to_all x1, blocking collectives, body(): partial = lax.all_to_all(partial, 'space', 0, 0, tiled=True)  9.7 us
    all_to_all x1, blocking collectives, body(): sums = lax.all_to_all(sums, 'space', 0, 0, tiled=True)  9.15 us
    ppermute x6, starting transfers between devices, gather(): parts.append(lax.ppermute(own, 'tensor', ring('tensor', k)))  8.15 us
    ppermute x6, waiting for transfers between devices, gather(): parts.append(lax.ppermute(own, 'tensor', ring('tensor', k)))  6.21 us
    ppermute x3, waiting for transfers between devices, body(): lax.ppermute(part, 'tensor', ring('tensor', k))  3.87 us
    ppermute x3, waiting for transfers between devices, body(): lax.ppermute(sent, 'space', ring('space', 2 * k))  3.75 us
  transfers between devices with their start and end apart: 17, of which 10 were waited for; matrix products, arithmetic and copies ran while one was open for 1% of the time, Pallas kernels for 5%

profile of v9, /device:TPU:1, one launch (start us, length us, event | category | flops | bytes accessed | tf_op | source)
XLA Modules:
  0.0 87.6 jit_solution(6886227117416407178)
XLA Ops:
  0.6 1.0 %copy.24 = bf16[1,2,80,4,128]{4,2,3,1,0:T(8,128)(2,1)S(1)} copy(bf16[1,2,80,4,128]{4,3,2,1,0:T(4,128)(2,1)} %param.16) | data formatting | bytes 327680 | tf_op args[0]
  1.6 3.6 %collective-permute-start.2 = (bf16[2,4,80,128]{3,2,1,0:T(8,128)(2,1)S(1)}, bf16[2,4,80,128]{3,2,1,0:T(8,128)(2,1)S(1)}, u32[]{:S(2)}, u32[]{:S(2)}) collective-permute-start(bf16[2,4,80,128]{3,2,1,0:T(8,128)(2,1)S(1)} %bitcast.32), channel_id=1, source_target_pairs={{0,3},{1,0},{2,1},{3,2},{4,7},{5,4},{6,5},{7,6},{8,11},{9,8},{10,9... | collective-permute-start | bytes 491528 | tf_op jit(solution)/shard_map/ppermute | solution.py:555
  6.3 0.9 %copy.23 = bf16[1,2,80,4,128]{4,2,3,1,0:T(8,128)(2,1)S(1)} copy(bf16[1,2,80,4,128]{4,3,2,1,0:T(4,128)(2,1)} %param.17) | data formatting | bytes 327680 | tf_op jit(solution)/shard_map/optimization_barrier | solution.py:559
  7.3 2.1 %collective-permute-start.5 = (bf16[2,4,80,128]{3,2,1,0:T(8,128)(2,1)S(1)}, bf16[2,4,80,128]{3,2,1,0:T(8,128)(2,1)S(1)}, u32[]{:S(2)}, u32[]{:S(2)}) collective-permute-start(bf16[2,4,80,128]{3,2,1,0:T(8,128)(2,1)S(1)} %bitcast.28), channel_id=1, source_target_pairs={{0,3},{1,0},{2,1},{3,2},{4,7},{5,4},{6,5},{7,6},{8,11},{9,8},{10,9... | collective-permute-start | bytes 491528 | tf_op jit(solution)/shard_map/ppermute | solution.py:555
  9.3 1.4 %collective-permute-start.4 = (bf16[2,4,80,128]{3,2,1,0:T(8,128)(2,1)S(1)}, bf16[2,4,80,128]{3,2,1,0:T(8,128)(2,1)S(1)}, u32[]{:S(2)}, u32[]{:S(2)}) collective-permute-start(bf16[2,4,80,128]{3,2,1,0:T(8,128)(2,1)S(1)} %bitcast.29), channel_id=1, source_target_pairs={{0,2},{1,3},{2,0},{3,1},{4,6},{5,7},{6,4},{7,5},{8,10},{9,11},{10,... | collective-permute-start | bytes 491528 | tf_op jit(solution)/shard_map/ppermute | solution.py:555
  12.1 5.5 %collective-permute-done.f1 = bf16[2,4,80,128]{3,2,1,0:T(8,128)(2,1)S(1)} collective-permute-done((bf16[2,4,80,128]{3,2,1,0:T(8,128)(2,1)S(1)}, bf16[2,4,80,128]{3,2,1,0:T(8,128)(2,1)S(1)}, u32[]{:S(2)}, u32[]{:S(2)}) %collective-permute-start) | collective-permute-done | bytes 163872 | tf_op jit(solution)/shard_map/ppermute | solution.py:555
  17.7 2.3 %shard_map.175 = (f32[160,512]{1,0:T(8,128)S(1)}, f32[160,128]{1,0:T(8,128)S(1)}, f32[160,128]{1,0:T(8,128)S(1)}, bf16[992,128]{1,0:T(8,128)(2,1)S(1)}, bf16[992...) custom-call(s32[7]{0:T(128)S(1)} %stack.31.t_ref.place_ref.edge_ref.x_ref, bf16[2,4,80,128]{3,2,1,0:T(8,128)(2,1)S(1)} %bitcast.35, ...), custom_call_target="tpu_custom_call" | custom-call | flops 471859200 | bytes 2787356 | tf_op jit(solution)/shard_map/pallas_call | solution.py:34
  20.0 1.6 %collective-permute-start.6 = (bf16[992,128]{1,0:T(8,128)(2,1)S(1)}, bf16[992,128]{1,0:T(8,128)(2,1)S(1)}, u32[]{:S(2)}, u32[]{:S(2)}) collective-permute-start(bf16[992,128]{1,0:T(8,128)(2,1)S(1)} %get-tuple-element.55), channel_id=1, source_target_pairs={{0,4},{4,0},{8,12},{12,8},{16,20},{20,16},{24,28},{28,24},{1,5},{5... | collective-permute-start | bytes 761864 | tf_op jit(solution)/shard_map/ppermute | solution.py:579
  21.6 1.2 %collective-permute-start.7 = (bf16[992,128]{1,0:T(8,128)(2,1)S(1)}, bf16[992,128]{1,0:T(8,128)(2,1)S(1)}, u32[]{:S(2)}, u32[]{:S(2)}) collective-permute-start(bf16[992,128]{1,0:T(8,128)(2,1)S(1)} %get-tuple-element.56), channel_id=1, source_target_pairs={{0,28},{4,8},{8,4},{12,16},{16,12},{20,24},{24,20},{28,0},{1,29},{... | collective-permute-start | bytes 761864 | tf_op jit(solution)/shard_map/ppermute | solution.py:578
  23.5 1.7 %shard_map.176 = (f32[160,512]{1,0:T(8,128)S(1)}, f32[160,128]{1,0:T(8,128)S(1)}, f32[160,128]{1,0:T(8,128)S(1)}, bf16[640,128]{1,0:T(8,128)(2,1)S(1)}, bf16[640,128]{1,0:T(8,128)(2,1)S(1)}) custom-call(s32[7]{0:T(128)S(1)} %stack.31.t_ref.place_ref.edge_ref.x_ref, bf16[2,4,80,128]{3,2,1,0:T(8,128)(2,1)S(1)} %bitcast.31, ...), custom_call_target="tpu_custom_call" | custom-call | flops 471859200 | bytes 1935388 | tf_op jit(solution)/shard_map/pallas_call | solution.py:34
  25.2 1.1 %collective-permute-start.8 = (bf16[640,128]{1,0:T(8,128)(2,1)S(1)}, bf16[640,128]{1,0:T(8,128)(2,1)S(1)}, u32[]{:S(2)}, u32[]{:S(2)}) collective-permute-start(bf16[640,128]{1,0:T(8,128)(2,1)S(1)} %get-tuple-element.57), channel_id=1, source_target_pairs={{0,4},{4,0},{8,12},{12,8},{16,20},{20,16},{24,28},{28,24},{1,5},{5... | collective-permute-start | bytes 491528 | tf_op jit(solution)/shard_map/ppermute | solution.py:590
  28.4 3.0 %collective-permute-done.9.got_br = bf16[640,128]{1,0:T(8,128)(2,1)S(1)} collective-permute-done((bf16[640,128]{1,0:T(8,128)(2,1)S(1)}, bf16[640,128]{1,0:T(8,128)(2,1)S(1)}, u32[]{:S(2)}, u32[]{:S(2)}) %collective-permute-start.9) | collective-permute-done | bytes 163872 | tf_op jit(solution)/shard_map/ppermute | solution.py:589
  31.4 1.1 %shard_map.178 = (f32[160,1280]{1,0:T(8,128)S(1)}, f32[160,768]{1,0:T(8,128)S(1)}, f32[8,8,128]{2,1,0:T(8,128)S(1)}, f32[8,16,128]{2,1,0:T(8,128)S(1)}) custom-call(s32[7]{0:T(128)S(1)} %stack.31.t_ref.place_ref.edge_ref.x_ref, f32[160,512]{1,0:T(8,128)S(1)} %get-tuple-element.47.pre_p, f32[160,128]{1,0:T(8,128)S(1)} %get-tuple-element.48.up_p, ...), custom_call_target="tpu_custom_call" | custom-call | flops 1000000 | bytes 3325980 | tf_op jit(solution)/shard_map/pallas_call | solution.py:34
  32.5 9.2 %all_to_all.15.sums_ref = f32[8,16,128]{2,1,0:T(8,128)S(1)} all-to-all(f32[8,16,128]{2,1,0:T(8,128)S(1)} %get-tuple-element.64), channel_id=1, replica_groups=mesh['dp'=8,'space'=8,'tensor'=4] {'space'}, dimensions={0} | all-to-all | bytes 131072 | tf_op jit(solution)/shard_map/all_to_all | solution.py:619
  41.6 1.6 %shard_map.179 = (f32[12,8,128]{2,1,0:T(8,128)S(1)}, bf16[160,512]{1,0:T(8,128)(2,1)S(1)}, f32[160,128]{1,0:T(8,128)S(1)}) custom-call(s32[7]{0:T(128)S(1)} %stack.31.t_ref.place_ref.edge_ref.x_ref, f32[160,1280]{1,0:T(8,128)S(1)} %get-tuple-element.62.ext_p, f32[160,768]{1,0:T(8,128)S(1)} %get-tuple-element.63.ext_r, ...), custom_call_target="tpu_custom_call" | custom-call | flops 10000000 | bytes 1799196 | tf_op jit(solution)/shard_map/pallas_call | solution.py:34
  44.8 1.5 %collective-permute-done.12.p3 = f32[12,8,128]{2,1,0:T(8,128)S(1)} collective-permute-done((f32[12,8,128]{2,1,0:T(8,128)S(1)}, f32[12,8,128]{2,1,0:T(8,128)S(1)}, u32[]{:S(2)}, u32[]{:S(2)}) %collective-permute-start.12) | collective-permute-done | bytes 49184 | tf_op jit(solution)/shard_map/ppermute | solution.py:627
  46.3 1.8 %collective-permute-done.11.p2 = f32[12,8,128]{2,1,0:T(8,128)S(1)} collective-permute-done((f32[12,8,128]{2,1,0:T(8,128)S(1)}, f32[12,8,128]{2,1,0:T(8,128)S(1)}, u32[]{:S(2)}, u32[]{:S(2)}) %collective-permute-start.11) | collective-permute-done | bytes 49184 | tf_op jit(solution)/shard_map/ppermute | solution.py:627
  48.7 1.2 %shard_map.180 = (f32[160,768]{1,0:T(8,128)S(1)}, f32[32,128]{1,0:T(8,128)S(1)}, f32[8,24,128]{2,1,0:T(8,128)S(1)}) custom-call(s32[7]{0:T(128)S(1)} %stack.31.t_ref.place_ref.edge_ref.x_ref, f32[12,8,128]{2,1,0:T(8,128)S(1)} %get-tuple-element.66.p0, f32[12,8,128]{2,1,0:T(8,128)S(1)} %collective-permute-done.10.p1, ...), custom_call_target="tpu_custom_call" | custom-call | flops 10000000 | bytes 2005532 | tf_op jit(solution)/shard_map/pallas_call | solution.py:34
  49.9 9.7 %all_to_all.16.red_ref = f32[8,24,128]{2,1,0:T(8,128)S(1)} all-to-all(f32[8,24,128]{2,1,0:T(8,128)S(1)} %get-tuple-element.72), channel_id=1, replica_groups=mesh['dp'=8,'space'=8,'tensor'=4] {'space'}, dimensions={0} | all-to-all | bytes 196608 | tf_op jit(solution)/shard_map/all_to_all | solution.py:635
  59.6 2.2 %shard_map.181 = (f32[4,40,768]{2,1,0:T(8,128)S(1)}, bf16[4,48,768]{2,1,0:T(8,128)(2,1)S(1)}, f32[32,128]{1,0:T(8,128)S(1)}, f32[1,1]{1,0:T(1,128)}) custom-call(s32[7]{0:T(128)S(1)} %stack.31.t_ref.place_ref.edge_ref.x_ref, f32[160,768]{1,0:T(8,128)S(1)} %get-tuple-element.71.gnorm_ref, f32[160,1280]{1,0:T(8,128)S(1)} %get-tuple-element.62.ext_p, ...), custom_call_target="tpu_custom_call" | custom-call | flops 471859200 | bytes 2965536 | tf_op jit(solution)/shard_map/pallas_call | solution.py:34
  62.7 1.2 %collective-permute-done.13.got_ref = bf16[4,48,768]{2,1,0:T(8,128)(2,1)S(1)} collective-permute-done((bf16[4,48,768]{2,1,0:T(8,128)(2,1)S(1)}, bf16[4,48,768]{2,1,0:T(8,128)(2,1)S(1)}, u32[]{:S(2)}, u32[]{:S(2)}) %collective-permute-start.13) | collective-permute-done | bytes 294944 | tf_op jit(solution)/shard_map/ppermute | solution.py:644
  64.9 1.8 %collective-permute-start.15 = (bf16[48,768]{1,0:T(8,128)(2,1)S(1)}, bf16[48,768]{1,0:T(8,128)(2,1)S(1)}, u32[]{:S(2)}, u32[]{:S(2)}) collective-permute-start(bf16[48,768]{1,0:T(8,128)(2,1)S(1)} %get-tuple-element.81), channel_id=1, source_target_pairs={{0,16},{4,20},{8,24},{12,28},{16,0},{20,4},{24,8},{28,12},{1,17},{... | collective-permute-start | bytes 221192 | tf_op jit(solution)/shard_map/ppermute | solution.py:653
  67.4 2.3 %collective-permute-done.14.r1 = bf16[48,768]{1,0:T(8,128)(2,1)S(1)} collective-permute-done((bf16[48,768]{1,0:T(8,128)(2,1)S(1)}, bf16[48,768]{1,0:T(8,128)(2,1)S(1)}, u32[]{:S(2)}, u32[]{:S(2)}) %collective-permute-start.14) | collective-permute-done | bytes 73760 | tf_op jit(solution)/shard_map/ppermute | solution.py:653
  71.2 15.7 %all_to_all.17.got_ref = bf16[8,56,128]{2,1,0:T(8,128)(2,1)S(1)} all-to-all(bf16[8,56,128]{2,1,0:T(8,128)(2,1)S(1)} %shard_map.183), channel_id=1, replica_groups=mesh['dp'=8,'space'=8,'tensor'=4] {'dp'}, dimensions={0} | all-to-all | bytes 229376 | tf_op jit(solution)/shard_map/all_to_all | solution.py:662
  (50 shorter events, 10.7 us)
Async XLA Ops:
  0.6 17.0 %copy-start.10 = (bf16[9,80,320]{2,1,0:T(8,128)(2,1)S(1)}, bf16[9,80,320]{2,1,0:T(8,128)(2,1)}, u32[]{:S(2)}) copy-start(bf16[9,80,320]{2,1,0:T(8,128)(2,1)} %param.19) | copy-start | bytes 1382404
  1.6 9.1 %collective-permute-start.2 = (bf16[2,4,80,128]{3,2,1,0:T(8,128)(2,1)S(1)}, bf16[2,4,80,128]{3,2,1,0:T(8,128)(2,1)S(1)}, u32[]{:S(2)}, u32[]{:S(2)}) collective-permute-start(bf16[2,4,80,128]{3,2,1,0:T(8,128)(2,1)S(1)} %bitcast.32), channel_id=1, source_target_pairs={{0,3},{1,0},{2,1},{3,2},{4,7},{5,4},{6,5},{7,6},{8,11},{9,8},{10,9... | collective-permute-start | bytes 491528 | tf_op jit(solution)/shard_map/ppermute | solution.py:555
  5.3 6.9 %collective-permute-start.1 = (bf16[2,4,80,128]{3,2,1,0:T(8,128)(2,1)S(1)}, bf16[2,4,80,128]{3,2,1,0:T(8,128)(2,1)S(1)}, u32[]{:S(2)}, u32[]{:S(2)}) collective-permute-start(bf16[2,4,80,128]{3,2,1,0:T(8,128)(2,1)S(1)} %bitcast.33), channel_id=1, source_target_pairs={{0,2},{1,3},{2,0},{3,1},{4,6},{5,7},{6,4},{7,5},{8,10},{9,11},{10,... | collective-permute-start | bytes 491528 | tf_op jit(solution)/shard_map/ppermute | solution.py:555
  5.6 12.1 %collective-permute-start = (bf16[2,4,80,128]{3,2,1,0:T(8,128)(2,1)S(1)}, bf16[2,4,80,128]{3,2,1,0:T(8,128)(2,1)S(1)}, u32[]{:S(2)}, u32[]{:S(2)}) collective-permute-start(bf16[2,4,80,128]{3,2,1,0:T(8,128)(2,1)S(1)} %bitcast.34), channel_id=1, source_target_pairs={{0,1},{1,2},{2,3},{3,0},{4,5},{5,6},{6,7},{7,4},{8,9},{9,10},{10,1... | collective-permute-start | bytes 491528 | tf_op jit(solution)/shard_map/ppermute | solution.py:555
  7.3 15.5 %collective-permute-start.5 = (bf16[2,4,80,128]{3,2,1,0:T(8,128)(2,1)S(1)}, bf16[2,4,80,128]{3,2,1,0:T(8,128)(2,1)S(1)}, u32[]{:S(2)}, u32[]{:S(2)}) collective-permute-start(bf16[2,4,80,128]{3,2,1,0:T(8,128)(2,1)S(1)} %bitcast.28), channel_id=1, source_target_pairs={{0,3},{1,0},{2,1},{3,2},{4,7},{5,4},{6,5},{7,6},{8,11},{9,8},{10,9... | collective-permute-start | bytes 491528 | tf_op jit(solution)/shard_map/ppermute | solution.py:555
  9.3 13.4 %collective-permute-start.4 = (bf16[2,4,80,128]{3,2,1,0:T(8,128)(2,1)S(1)}, bf16[2,4,80,128]{3,2,1,0:T(8,128)(2,1)S(1)}, u32[]{:S(2)}, u32[]{:S(2)}) collective-permute-start(bf16[2,4,80,128]{3,2,1,0:T(8,128)(2,1)S(1)} %bitcast.29), channel_id=1, source_target_pairs={{0,2},{1,3},{2,0},{3,1},{4,6},{5,7},{6,4},{7,5},{8,10},{9,11},{10,... | collective-permute-start | bytes 491528 | tf_op jit(solution)/shard_map/ppermute | solution.py:555
  10.7 12.7 %collective-permute-start.3 = (bf16[2,4,80,128]{3,2,1,0:T(8,128)(2,1)S(1)}, bf16[2,4,80,128]{3,2,1,0:T(8,128)(2,1)S(1)}, u32[]{:S(2)}, u32[]{:S(2)}) collective-permute-start(bf16[2,4,80,128]{3,2,1,0:T(8,128)(2,1)S(1)} %bitcast.30), channel_id=1, source_target_pairs={{0,1},{1,2},{2,3},{3,0},{4,5},{5,6},{6,7},{7,4},{8,9},{9,10},{10,1... | collective-permute-start | bytes 491528 | tf_op jit(solution)/shard_map/ppermute | solution.py:555
  10.7 6.9 %copy-start.1 = (f32[1,2,4,4,128]{4,3,2,1,0:T(4,128)S(1)}, f32[1,2,4,4,128]{4,3,2,1,0:T(4,128)}, u32[]{:S(2)}) copy-start(f32[1,2,4,4,128]{4,3,2,1,0:T(4,128)} %param.18) | copy-start | bytes 49156
  17.7 5.8 %copy-start.11 = (bf16[9,80,320]{2,1,0:T(8,128)(2,1)S(1)}, bf16[9,80,320]{2,1,0:T(8,128)(2,1)}, u32[]{:S(2)}) copy-start(bf16[9,80,320]{2,1,0:T(8,128)(2,1)} %param.20) | copy-start | bytes 1382404
  20.0 11.4 %collective-permute-start.6 = (bf16[992,128]{1,0:T(8,128)(2,1)S(1)}, bf16[992,128]{1,0:T(8,128)(2,1)S(1)}, u32[]{:S(2)}, u32[]{:S(2)}) collective-permute-start(bf16[992,128]{1,0:T(8,128)(2,1)S(1)} %get-tuple-element.55), channel_id=1, source_target_pairs={{0,4},{4,0},{8,12},{12,8},{16,20},{20,16},{24,28},{28,24},{1,5},{5... | collective-permute-start | bytes 761864 | tf_op jit(solution)/shard_map/ppermute | solution.py:579
  21.6 9.8 %collective-permute-start.7 = (bf16[992,128]{1,0:T(8,128)(2,1)S(1)}, bf16[992,128]{1,0:T(8,128)(2,1)S(1)}, u32[]{:S(2)}, u32[]{:S(2)}) collective-permute-start(bf16[992,128]{1,0:T(8,128)(2,1)S(1)} %get-tuple-element.56), channel_id=1, source_target_pairs={{0,28},{4,8},{8,4},{12,16},{16,12},{20,24},{24,20},{28,0},{1,29},{... | collective-permute-start | bytes 761864 | tf_op jit(solution)/shard_map/ppermute | solution.py:578
  23.4 3.5 %copy-start = (f32[1000,80]{0,1:T(8,128)S(1)}, f32[1000,80]{0,1:T(8,128)}, u32[]{:S(2)}) copy-start(f32[1000,80]{0,1:T(8,128)} %param.29) | copy-start | bytes 960004
  23.4 3.5 %copy-start.5 = (f32[80]{0:T(128)S(1)}, f32[80]{0:T(128)}, u32[]{:S(2)}) copy-start(f32[80]{0:T(128)} %param.22) | copy-start | bytes 964
  23.4 3.5 %copy-start.6 = (f32[80]{0:T(128)S(1)}, f32[80]{0:T(128)}, u32[]{:S(2)}) copy-start(f32[80]{0:T(128)} %param.23) | copy-start | bytes 964
  23.4 3.5 %copy-start.7 = (f32[80]{0:T(128)S(1)}, f32[80]{0:T(128)}, u32[]{:S(2)}) copy-start(f32[80]{0:T(128)} %param.24) | copy-start | bytes 964
  25.2 3.2 %collective-permute-start.8 = (bf16[640,128]{1,0:T(8,128)(2,1)S(1)}, bf16[640,128]{1,0:T(8,128)(2,1)S(1)}, u32[]{:S(2)}, u32[]{:S(2)}) collective-permute-start(bf16[640,128]{1,0:T(8,128)(2,1)S(1)} %get-tuple-element.57), channel_id=1, source_target_pairs={{0,4},{4,0},{8,12},{12,8},{16,20},{20,16},{24,28},{28,24},{1,5},{5... | collective-permute-start | bytes 491528 | tf_op jit(solution)/shard_map/ppermute | solution.py:590
  26.3 5.0 %collective-permute-start.9 = (bf16[640,128]{1,0:T(8,128)(2,1)S(1)}, bf16[640,128]{1,0:T(8,128)(2,1)S(1)}, u32[]{:S(2)}, u32[]{:S(2)}) collective-permute-start(bf16[640,128]{1,0:T(8,128)(2,1)S(1)} %get-tuple-element.58), channel_id=1, source_target_pairs={{0,28},{4,8},{8,4},{12,16},{16,12},{20,24},{24,20},{28,0},{1,29},{... | collective-permute-start | bytes 491528 | tf_op jit(solution)/shard_map/ppermute | solution.py:589
  43.3 3.0 %collective-permute-start.12 = (f32[12,8,128]{2,1,0:T(8,128)S(1)}, f32[12,8,128]{2,1,0:T(8,128)S(1)}, u32[]{:S(2)}, u32[]{:S(2)}) collective-permute-start(f32[12,8,128]{2,1,0:T(8,128)S(1)} %get-tuple-element.66.p0), channel_id=1, source_target_pairs={{0,3},{1,0},{2,1},{3,2},{4,7},{5,4},{6,5},{7,6},{8,11},{9,8},{10,9... | collective-permute-start | bytes 147464 | tf_op jit(solution)/shard_map/ppermute | solution.py:627
  43.7 4.4 %collective-permute-start.11 = (f32[12,8,128]{2,1,0:T(8,128)S(1)}, f32[12,8,128]{2,1,0:T(8,128)S(1)}, u32[]{:S(2)}, u32[]{:S(2)}) collective-permute-start(f32[12,8,128]{2,1,0:T(8,128)S(1)} %get-tuple-element.66.p0), channel_id=1, source_target_pairs={{0,2},{1,3},{2,0},{3,1},{4,6},{5,7},{6,4},{7,5},{8,10},{9,11},{10,... | collective-permute-start | bytes 147464 | tf_op jit(solution)/shard_map/ppermute | solution.py:627
  44.0 4.7 %collective-permute-start.10 = (f32[12,8,128]{2,1,0:T(8,128)S(1)}, f32[12,8,128]{2,1,0:T(8,128)S(1)}, u32[]{:S(2)}, u32[]{:S(2)}) collective-permute-start(f32[12,8,128]{2,1,0:T(8,128)S(1)} %get-tuple-element.66.p0), channel_id=1, source_target_pairs={{0,1},{1,2},{2,3},{3,0},{4,5},{5,6},{6,7},{7,4},{8,9},{9,10},{10,1... | collective-permute-start | bytes 147464 | tf_op jit(solution)/shard_map/ppermute | solution.py:627
  61.9 2.0 %collective-permute-start.13 = (bf16[4,48,768]{2,1,0:T(8,128)(2,1)S(1)}, bf16[4,48,768]{2,1,0:T(8,128)(2,1)S(1)}, u32[]{:S(2)}, u32[]{:S(2)}) collective-permute-start(bf16[4,48,768]{2,1,0:T(8,128)(2,1)S(1)} %get-tuple-element.78), channel_id=1, source_target_pairs={{0,4},{4,0},{8,12},{12,8},{16,20},{20,16},{24,28},{28,24},{1,5},{5... | collective-permute-start | bytes 884744 | tf_op jit(solution)/shard_map/ppermute | solution.py:644
  64.5 5.2 %collective-permute-start.14 = (bf16[48,768]{1,0:T(8,128)(2,1)S(1)}, bf16[48,768]{1,0:T(8,128)(2,1)S(1)}, u32[]{:S(2)}, u32[]{:S(2)}) collective-permute-start(bf16[48,768]{1,0:T(8,128)(2,1)S(1)} %get-tuple-element.80), channel_id=1, source_target_pairs={{0,8},{4,12},{8,16},{12,20},{16,24},{20,28},{24,0},{28,4},{1,9},{5... | collective-permute-start | bytes 221192 | tf_op jit(solution)/shard_map/ppermute | solution.py:653
  64.9 5.5 %collective-permute-start.15 = (bf16[48,768]{1,0:T(8,128)(2,1)S(1)}, bf16[48,768]{1,0:T(8,128)(2,1)S(1)}, u32[]{:S(2)}, u32[]{:S(2)}) collective-permute-start(bf16[48,768]{1,0:T(8,128)(2,1)S(1)} %get-tuple-element.81), channel_id=1, source_target_pairs={{0,16},{4,20},{8,24},{12,28},{16,0},{20,4},{24,8},{28,12},{1,17},{... | collective-permute-start | bytes 221192 | tf_op jit(solution)/shard_map/ppermute | solution.py:653
  66.7 4.5 %collective-permute-start.16 = (bf16[48,768]{1,0:T(8,128)(2,1)S(1)}, bf16[48,768]{1,0:T(8,128)(2,1)S(1)}, u32[]{:S(2)}, u32[]{:S(2)}) collective-permute-start(bf16[48,768]{1,0:T(8,128)(2,1)S(1)} %get-tuple-element.82), channel_id=1, source_target_pairs={{0,24},{4,28},{8,0},{12,4},{16,8},{20,12},{24,16},{28,20},{1,25},{... | collective-permute-start | bytes 221192 | tf_op jit(solution)/shard_map/ppermute | solution.py:653
  (5 other events, 11.4 us)
